TPU v7x, 32 devices: a whole 2x2x4 slice. The times are simulated.
32 devices in a mesh: ctx: 4 (over x, core), fsdp: 8 (over z, y).
Axes of the slice: x: 2, y: 2, z: 4, core: 2. Of those that a mesh axis runs over, the one named last changes fastest.
Arguments:
- tokens_in: bfloat16 [8, 1024, 1600], P('fsdp', 'ctx'), may hold values from -6 to 6
- group_order: int32 [8], replicated, may hold values from 0 to 7, each once
- out_grad: bfloat16 [8, 1024, 1600], P('fsdp', 'ctx'), may hold values from -6 to 6
- w_qkv: bfloat16 [1600, 4800], P('fsdp'), may hold values from -0.15625 to 0.15625
- w_attn_out: bfloat16 [1600, 1600], P('fsdp'), may hold values from -0.625 to 0.625
- b_query: bfloat16 [1600], P('fsdp'), may hold values from -3 to 3
- b_value: bfloat16 [1600], P('fsdp'), may hold values from -3 to 3
- b_attn_out: bfloat16 [1600], P('fsdp'), may hold values from -3 to 3
- w_fc: bfloat16 [1600, 6400], P('fsdp'), may hold values from -0.15625 to 0.15625
- w_proj: bfloat16 [6400, 1600], P('fsdp'), may hold values from -0.078125 to 0.078125
- b_fc: bfloat16 [6400], P('fsdp'), may hold values from -3 to 3
- b_proj: bfloat16 [1600], P('fsdp'), may hold values from -3 to 3
- ln1_gain: bfloat16 [1600], P('fsdp'), may hold values from 0.5 to 1.5
- ln1_bias: bfloat16 [1600], P('fsdp'), may hold values from -2 to 2
- ln2_gain: bfloat16 [1600], P('fsdp'), may hold values from 0.5 to 1.5
- ln2_bias: bfloat16 [1600], P('fsdp'), may hold values from -2 to 2
Outputs:
- tokens_out: bfloat16 [8, 1024, 1600], P('fsdp', 'ctx')
- grad_tokens: float32 [8, 1024, 1600], P('fsdp', 'ctx')
- grad_w_qkv: float32 [1600, 4800], P('fsdp')
- grad_w_attn_out: float32 [1600, 1600], P('fsdp')
- grad_b_query: float32 [1600], P('fsdp')
- grad_b_value: float32 [1600], P('fsdp')
- grad_b_attn_out: float32 [1600], P('fsdp')
- grad_w_fc: float32 [1600, 6400], P('fsdp')
- grad_w_proj: float32 [6400, 1600], P('fsdp')
- grad_b_fc: float32 [6400], P('fsdp')
- grad_b_proj: float32 [1600], P('fsdp')
- grad_ln1_gain: float32 [1600], P('fsdp')
- grad_ln1_bias: float32 [1600], P('fsdp')
- grad_ln2_gain: float32 [1600], P('fsdp')
- grad_ln2_bias: float32 [1600], P('fsdp')
Inputs may be any that keep to these rules, and one draw needn't show every extreme that they name: group_order is a permutation: each of the 8 groups of a sequence is stored at exactly one slot.
All inputs are finite; a program needn't handle non-finite values.
Results may differ from a plain program's by a relative error of at most 0.02.
Values may be sent and summed in bfloat16 or wider, within the bound.
No kernel may reach another device: no remote copies, remote signals or barrier semaphores. Data moves between devices by JAX's collectives and lax.ppermute only.
A program may use at most 384 MiB of HBM per device.

v0:
```python
import jax
import jax.numpy as jnp
from jax import lax
from jax.sharding import PartitionSpec as P

H = 25
GROUP = 128


norm_eps = 1e-05
masked_low = -1e30


def shifted(block, axis, distance):
    devices = range(lax.axis_size(axis))
    route = [((i - distance) % len(devices), i) for i in devices]
    return lax.ppermute(block, axis, route)


def layer_norm(values, norm_gain, norm_shift):
    centre = values - jnp.mean(values, axis=-1, keepdims=True)
    spread = jnp.mean(centre * centre, axis=-1, keepdims=True)
    return centre * lax.rsqrt(spread + norm_eps) * norm_gain + norm_shift


def gelu_tanh(values):
    return (
        0.5
        * values
        * (1.0 + jnp.tanh(0.7978845608028654 * (values + 0.044715 * values * values * values)))
    )


def outer_sum(left_op, right_op):
    return lax.dot_general(
        left_op, right_op, (((0,), (0,)), ((), ())), preferred_element_type=jnp.float32
    )


def back_product(left_op, right_op):
    return lax.dot_general(
        left_op, right_op, (((1,), (1,)), ((), ())), preferred_element_type=jnp.float32
    )


def block_positions(group_order, owner_index):
    slot_groups = lax.dynamic_slice_in_dim(group_order, 2 * owner_index, 2)
    offsets = jnp.arange(GROUP, dtype=jnp.int32)
    return (slot_groups[:, None] * GROUP + offsets[None, :]).reshape(-1)


def block_scores(queries, key_block, query_places, key_places):
    scale_factor = queries.shape[2] ** (-0.5)
    scores = (
        jnp.einsum("qhd,khd->hqk", queries, key_block, preferred_element_type=jnp.float32)
        * scale_factor
    )
    allowed = query_places[:, None] >= key_places[None, :]
    return (scores, allowed)


def stat_update(softmax_stats, scores, allowed):
    row_peak, row_mass = softmax_stats
    masked = jnp.where(allowed[None], scores, masked_low)
    new_peak = jnp.maximum(row_peak, jnp.max(masked, axis=2))
    weights = jnp.where(allowed[None], jnp.exp(masked - new_peak[:, :, None]), 0.0)
    return (new_peak, row_mass * jnp.exp(row_peak - new_peak) + jnp.sum(weights, axis=2))


def block_probs(scores, allowed, log_mass):
    return jnp.exp(jnp.where(allowed[None], scores - log_mass[:, :, None], masked_low))


def block_output(queries, pair_block, query_places, key_places, log_mass):
    scores, allowed = block_scores(queries, pair_block[:, 0], query_places, key_places)
    probs_low = block_probs(scores, allowed, log_mass).astype(jnp.bfloat16)
    return jnp.einsum(
        "hqk,khd->qhd", probs_low, pair_block[:, 1], preferred_element_type=jnp.float32
    )


def block_grads(queries, pair_block, query_places, key_places, log_mass, grad_attended, row_delta):
    key_block = pair_block[:, 0]
    value_block = pair_block[:, 1]
    scale_factor = queries.shape[2] ** (-0.5)
    scores, allowed = block_scores(queries, key_block, query_places, key_places)
    probs_full = block_probs(scores, allowed, log_mass)
    probs_low = probs_full.astype(jnp.bfloat16)
    grad_probs = jnp.einsum(
        "qhd,khd->hqk", grad_attended, value_block, preferred_element_type=jnp.float32
    )
    grad_scores = (probs_full * (grad_probs - row_delta[:, :, None]) * scale_factor).astype(
        jnp.bfloat16
    )
    grad_queries = jnp.einsum(
        "hqk,khd->qhd", grad_scores, key_block, preferred_element_type=jnp.float32
    )
    grad_keys = jnp.einsum("hqk,qhd->khd", grad_scores, queries, preferred_element_type=jnp.float32)
    grad_values = jnp.einsum(
        "hqk,qhd->khd", probs_low, grad_attended, preferred_element_type=jnp.float32
    )
    return (grad_queries, jnp.stack([grad_keys, grad_values], axis=1))


def per_device(
    tokens_in,
    group_order,
    out_grad,
    w_qkv,
    w_attn_out,
    b_query,
    b_value,
    b_attn_out,
    w_fc,
    w_proj,
    b_fc,
    b_proj,
    ln1_gain,
    ln1_bias,
    ln2_gain,
    ln2_bias,
):
    cycle_size = lax.axis_size("ctx")
    cycle_index = lax.axis_index("ctx")
    tokens = tokens_in[0].astype(jnp.float32)
    row_count = tokens.shape[0]
    model_width = tokens.shape[1]
    head_count = H
    head_dim = model_width // head_count
    qkv_full, attn_out_full, query_bias, value_bias, attn_out_bias, gain_one, shift_one = (
        lax.all_gather(w_qkv, "fsdp", axis=0, tiled=True),
        lax.all_gather(w_attn_out, "fsdp", axis=0, tiled=True),
        lax.all_gather(b_query, "fsdp", axis=0, tiled=True),
        lax.all_gather(b_value, "fsdp", axis=0, tiled=True),
        lax.all_gather(b_attn_out, "fsdp", axis=0, tiled=True),
        lax.all_gather(ln1_gain, "fsdp", axis=0, tiled=True),
        lax.all_gather(ln1_bias, "fsdp", axis=0, tiled=True),
    )
    normed, norm_pull = jax.vjp(
        layer_norm, tokens, gain_one.astype(jnp.float32), shift_one.astype(jnp.float32)
    )
    normed_low = normed.astype(jnp.bfloat16)
    mixed_all = jnp.dot(normed_low, qkv_full, preferred_element_type=jnp.float32)
    queries = (
        (mixed_all[:, :model_width] + query_bias.astype(jnp.float32))
        .astype(jnp.bfloat16)
        .reshape(row_count, head_count, head_dim)
    )
    pair_bias = jnp.concatenate(
        [jnp.zeros((model_width,), jnp.float32), value_bias.astype(jnp.float32)]
    )
    pair_local = (
        (mixed_all[:, model_width:] + pair_bias)
        .astype(jnp.bfloat16)
        .reshape(row_count, 2, head_count, head_dim)
    )
    query_places = block_positions(group_order, cycle_index)
    empty_peak = jnp.full((head_count, row_count), masked_low, jnp.float32)
    empty_mass = jnp.zeros((head_count, row_count), jnp.float32)
    first_scores, first_allowed = block_scores(
        queries, pair_local[:, 0], query_places, query_places
    )
    softmax_stats = stat_update((empty_peak, empty_mass), first_scores, first_allowed)

    def key_turn(cycle_turn, cycle_state):
        key_block, stats_now = cycle_state
        key_block = shifted(key_block, "ctx", 1)
        owner_index = (cycle_index - cycle_turn) % cycle_size
        scores, allowed = block_scores(
            queries, key_block, query_places, block_positions(group_order, owner_index)
        )
        return (key_block, stat_update(stats_now, scores, allowed))

    moved_keys, softmax_stats = lax.fori_loop(
        1, cycle_size, key_turn, (pair_local[:, 0], softmax_stats)
    )
    log_mass = softmax_stats[0] + jnp.log(softmax_stats[1])
    attended = block_output(queries, pair_local, query_places, query_places, log_mass)

    def pair_turn(cycle_turn, cycle_state):
        pair_block, output_now = cycle_state
        pair_block = shifted(pair_block, "ctx", 1)
        owner_index = (cycle_index - cycle_turn) % cycle_size
        return (
            pair_block,
            output_now
            + block_output(
                queries,
                pair_block,
                query_places,
                block_positions(group_order, owner_index),
                log_mass,
            ),
        )

    moved_pairs, attended = lax.fori_loop(1, cycle_size, pair_turn, (pair_local, attended))
    attended_low = attended.reshape(row_count, model_width).astype(jnp.bfloat16)
    branch = jnp.dot(
        attended_low, attn_out_full, preferred_element_type=jnp.float32
    ) + attn_out_bias.astype(jnp.float32)
    middle = tokens + branch
    fc_full, proj_full, fc_bias, proj_bias, gain_two, shift_two = (
        lax.all_gather(w_fc, "fsdp", axis=0, tiled=True),
        lax.all_gather(w_proj, "fsdp", axis=0, tiled=True),
        lax.all_gather(b_fc, "fsdp", axis=0, tiled=True),
        lax.all_gather(b_proj, "fsdp", axis=0, tiled=True),
        lax.all_gather(ln2_gain, "fsdp", axis=0, tiled=True),
        lax.all_gather(ln2_bias, "fsdp", axis=0, tiled=True),
    )
    normed_two, norm_two_pull = jax.vjp(
        layer_norm, middle, gain_two.astype(jnp.float32), shift_two.astype(jnp.float32)
    )
    normed_two_low = normed_two.astype(jnp.bfloat16)
    before = jnp.dot(normed_two_low, fc_full, preferred_element_type=jnp.float32) + fc_bias.astype(
        jnp.float32
    )
    activated, gelu_pull = jax.vjp(gelu_tanh, before)
    activated_low = activated.astype(jnp.bfloat16)
    branch_two = jnp.dot(
        activated_low, proj_full, preferred_element_type=jnp.float32
    ) + proj_bias.astype(jnp.float32)
    tokens_out = (middle + branch_two).astype(jnp.bfloat16)[None]
    fc_back, proj_back = (
        lax.all_gather(w_fc, "fsdp", axis=0, tiled=True),
        lax.all_gather(w_proj, "fsdp", axis=0, tiled=True),
    )
    grad_low = out_grad[0]
    grad_out = grad_low.astype(jnp.float32)
    grad_proj = outer_sum(activated_low, grad_low)
    grad_proj_bias = jnp.sum(grad_out, axis=0)
    (grad_before,) = gelu_pull(back_product(grad_low, proj_back))
    before_low = grad_before.astype(jnp.bfloat16)
    grad_fc = outer_sum(normed_two_low, before_low)
    grad_fc_bias = jnp.sum(before_low.astype(jnp.float32), axis=0)
    grad_middle_norm, grad_gain_two, grad_shift_two = norm_two_pull(
        back_product(before_low, fc_back)
    )
    grad_middle = grad_out + grad_middle_norm
    shard_fc, shard_proj, shard_fc_bias, shard_proj_bias, shard_gain_two, shard_shift_two = (
        lax.psum_scatter(
            grad_fc.astype(jnp.bfloat16), "fsdp", scatter_dimension=0, tiled=True
        ).astype(jnp.float32),
        lax.psum_scatter(
            grad_proj.astype(jnp.bfloat16), "fsdp", scatter_dimension=0, tiled=True
        ).astype(jnp.float32),
        lax.psum_scatter(
            grad_fc_bias.astype(jnp.bfloat16), "fsdp", scatter_dimension=0, tiled=True
        ).astype(jnp.float32),
        lax.psum_scatter(
            grad_proj_bias.astype(jnp.bfloat16), "fsdp", scatter_dimension=0, tiled=True
        ).astype(jnp.float32),
        lax.psum_scatter(
            grad_gain_two.astype(jnp.bfloat16), "fsdp", scatter_dimension=0, tiled=True
        ).astype(jnp.float32),
        lax.psum_scatter(
            grad_shift_two.astype(jnp.bfloat16), "fsdp", scatter_dimension=0, tiled=True
        ).astype(jnp.float32),
    )
    qkv_back, attn_out_back = (
        lax.all_gather(w_qkv, "fsdp", axis=0, tiled=True),
        lax.all_gather(w_attn_out, "fsdp", axis=0, tiled=True),
    )
    middle_low = grad_middle.astype(jnp.bfloat16)
    grad_attn_out = outer_sum(attended_low, middle_low)
    grad_attn_out_bias = jnp.sum(middle_low.astype(jnp.float32), axis=0)
    grad_attended = (
        back_product(middle_low, attn_out_back)
        .astype(jnp.bfloat16)
        .reshape(row_count, head_count, head_dim)
    )
    row_delta = jnp.einsum("qhd,qhd->hq", grad_attended.astype(jnp.float32), attended)

    def send_grads(grad_block):
        return shifted(grad_block.astype(jnp.bfloat16), "ctx", 1).astype(grad_block.dtype)

    grad_query_acc, grad_pair = block_grads(
        queries, pair_local, query_places, query_places, log_mass, grad_attended, row_delta
    )

    def back_turn(cycle_turn, cycle_state):
        pair_block, grad_block, query_now = cycle_state
        grad_block = send_grads(grad_block)
        pair_block = shifted(pair_block, "ctx", 1)
        owner_index = (cycle_index - cycle_turn) % cycle_size
        more_query, more_pair = block_grads(
            queries,
            pair_block,
            query_places,
            block_positions(group_order, owner_index),
            log_mass,
            grad_attended,
            row_delta,
        )
        return (pair_block, grad_block + more_pair, query_now + more_query)

    last_pair, grad_pair, grad_query_acc = lax.fori_loop(
        1, cycle_size, back_turn, (pair_local, grad_pair, grad_query_acc)
    )
    grad_pair = send_grads(grad_pair)
    grad_mixed_low = jnp.concatenate(
        [
            grad_query_acc.astype(jnp.bfloat16).reshape(row_count, model_width),
            grad_pair.astype(jnp.bfloat16).reshape(row_count, 2 * model_width),
        ],
        axis=1,
    )
    grad_qkv = outer_sum(normed_low, grad_mixed_low)
    grad_query_bias = jnp.sum(grad_mixed_low[:, :model_width].astype(jnp.float32), axis=0)
    grad_value_bias = jnp.sum(grad_mixed_low[:, 2 * model_width :].astype(jnp.float32), axis=0)
    grad_tokens_norm, grad_gain_one, grad_shift_one = norm_pull(
        back_product(grad_mixed_low, qkv_back)
    )
    grad_tokens = (grad_middle + grad_tokens_norm)[None]
    (
        shard_qkv,
        shard_attn_out,
        shard_query_bias,
        shard_value_bias,
        shard_attn_out_bias,
        shard_gain_one,
        shard_shift_one,
    ) = (
        lax.psum_scatter(
            grad_qkv.astype(jnp.bfloat16), "fsdp", scatter_dimension=0, tiled=True
        ).astype(jnp.float32),
        lax.psum_scatter(
            grad_attn_out.astype(jnp.bfloat16), "fsdp", scatter_dimension=0, tiled=True
        ).astype(jnp.float32),
        lax.psum_scatter(
            grad_query_bias.astype(jnp.bfloat16), "fsdp", scatter_dimension=0, tiled=True
        ).astype(jnp.float32),
        lax.psum_scatter(
            grad_value_bias.astype(jnp.bfloat16), "fsdp", scatter_dimension=0, tiled=True
        ).astype(jnp.float32),
        lax.psum_scatter(
            grad_attn_out_bias.astype(jnp.bfloat16), "fsdp", scatter_dimension=0, tiled=True
        ).astype(jnp.float32),
        lax.psum_scatter(
            grad_gain_one.astype(jnp.bfloat16), "fsdp", scatter_dimension=0, tiled=True
        ).astype(jnp.float32),
        lax.psum_scatter(
            grad_shift_one.astype(jnp.bfloat16), "fsdp", scatter_dimension=0, tiled=True
        ).astype(jnp.float32),
    )
    summed = (
        lax.psum(shard_qkv.astype(jnp.bfloat16), "ctx").astype(jnp.float32),
        lax.psum(shard_attn_out.astype(jnp.bfloat16), "ctx").astype(jnp.float32),
        lax.psum(shard_query_bias.astype(jnp.bfloat16), "ctx").astype(jnp.float32),
        lax.psum(shard_value_bias.astype(jnp.bfloat16), "ctx").astype(jnp.float32),
        lax.psum(shard_attn_out_bias.astype(jnp.bfloat16), "ctx").astype(jnp.float32),
        lax.psum(shard_fc.astype(jnp.bfloat16), "ctx").astype(jnp.float32),
        lax.psum(shard_proj.astype(jnp.bfloat16), "ctx").astype(jnp.float32),
        lax.psum(shard_fc_bias.astype(jnp.bfloat16), "ctx").astype(jnp.float32),
        lax.psum(shard_proj_bias.astype(jnp.bfloat16), "ctx").astype(jnp.float32),
        lax.psum(shard_gain_one.astype(jnp.bfloat16), "ctx").astype(jnp.float32),
        lax.psum(shard_shift_one.astype(jnp.bfloat16), "ctx").astype(jnp.float32),
        lax.psum(shard_gain_two.astype(jnp.bfloat16), "ctx").astype(jnp.float32),
        lax.psum(shard_shift_two.astype(jnp.bfloat16), "ctx").astype(jnp.float32),
    )
    return (
        tokens_out,
        grad_tokens,
        summed[0],
        summed[1],
        summed[2],
        summed[3],
        summed[4],
        summed[5],
        summed[6],
        summed[7],
        summed[8],
        summed[9],
        summed[10],
        summed[11],
        summed[12],
    )


def solution(mesh):
    placed = (
        P("fsdp", "ctx", None),
        P(),
        P("fsdp", "ctx", None),
        P("fsdp", None),
        P("fsdp", None),
        P("fsdp"),
        P("fsdp"),
        P("fsdp"),
        P("fsdp", None),
        P("fsdp", None),
        P("fsdp"),
        P("fsdp"),
        P("fsdp"),
        P("fsdp"),
        P("fsdp"),
        P("fsdp"),
    )
    return jax.shard_map(
        per_device,
        mesh=mesh,
        in_specs=placed,
        out_specs=(
            P("fsdp", "ctx", None),
            P("fsdp", "ctx", None),
            P("fsdp", None),
            P("fsdp", None),
            P("fsdp"),
            P("fsdp"),
            P("fsdp"),
            P("fsdp", None),
            P("fsdp", None),
            P("fsdp"),
            P("fsdp"),
            P("fsdp"),
            P("fsdp"),
            P("fsdp"),
            P("fsdp"),
        ),
        check_vma=False,
    )
```

profile of v0, /device:TPU:0, one launch (start us, length us, event | category | flops | bytes accessed | tf_op | source)
XLA Modules:
  0.0 2478.8 jit_solution(9812996042900565081)
XLA Ops:
  14.1 41.0 %all-reduce.22 = (bf16[1600]{0:T(1024)(128)(2,1)S(1)}, bf16[1600]{0:T(1024)(128)(2,1)S(1)}, bf16[1600]{0:T(1024)(128)(2,1)S(1)}, bf16[1600]{0:T(1024)(128)(2,1)S...) all-reduce(bf16[1600]{0:T(1024)(128)(2,1)S(1)} %dynamic-update-slic, ...), channel_id=1, replica_groups=mesh['ctx'=4,'fsdp'=8] {'fsdp'}, use_global_device_ids=true, to_apply=%add.2 | all-reduce | flops 17600 | bytes 70400
  56.1 170.6 %all-gather.5.cloned.1.call-done = bf16[1600,4800]{1,0:T(8,128)(2,1)} async-done(((bf16[200,4800]{1,0:T(8,128)(2,1)}), bf16[1600,4800]{1,0:T(8,128)(2,1)}) %all-gather.5.cloned.1.call-update) | async-done | bytes 15360016 | tf_op jit(solution)/shard_map/all_gather | solution.py:131
  226.7 14.8 fusion.79
  255.9 47.1 %while.58 = (s32[]{:T(128)}, bf16[256,25,64]{0,2,1:T(8,128)(2,1)}, f32[25,256]{1,0:T(8,128)S(1)}, f32[25,256]{1,0:T(8,128)S(1)}, s32[]{:T(128)}, /*index=5*/s32[...) while((s32[]{:T(128)}, bf16[256,25,64]{0,2,1:T(8,128)(2,1)}, ...), condition=%wide.region_7.8_spmd.clone, body=%wide.region_4.7_spmd.clone.sunk | while | flops 222901264 | bytes 20194680 | solution.py:174
  308.8 84.4 %while.59 = (s32[]{:T(128)}, bf16[256,2,25,64]{0,3,2,1:T(8,128)(2,1)}, f32[256,25,64]{0,2,1:T(8,128)}, s32[]{:T(128)}, s32[8]{0:T(128)S(1)}, /*index=5*/bf16[256...) while((s32[]{:T(128)}, ...), condition=%wide.region_9.10_spmd.clone, body=%wide.region_8.9_spmd.clone.sunk | while | flops 426459680 | bytes 15725944 | solution.py:196
  309.1 20.5 collective-permute-done.1
  337.1 20.5 collective-permute-done.1
  365.2 20.5 collective-permute-done.1
  401.2 305.6 %all-gather.9.cloned.1.call-done = bf16[1600,6400]{1,0:T(8,128)(2,1)} async-done(((bf16[200,6400]{1,0:T(8,128)(2,1)}), bf16[1600,6400]{1,0:T(8,128)(2,1)}) %all-gather.9.cloned.1.call-update) | async-done | bytes 20480016 | tf_op jit(solution)/shard_map/all_gather | solution.py:203
  719.1 396.9 %all-gather.11.cloned.1.call-done = bf16[6400,1600]{1,0:T(8,128)(2,1)} async-done(((bf16[800,1600]{1,0:T(8,128)(2,1)}), bf16[6400,1600]{1,0:T(8,128)(2,1)}) %all-gather.11.cloned.1.call-update) | async-done | bytes 20480016 | tf_op jit(solution)/shard_map/all_gather | solution.py:204
  1116.0 15.6 fusion.88
  1131.7 14.0 multiply_reduce_fusion
  1165.3 125.2 %while.60 = (s32[]{:T(128)}, bf16[256,2,25,64]{0,3,2,1:T(8,128)(2,1)}, bf16[256,2,25,64]{0,3,2,1:T(8,128)(2,1)}, f32[256,25,64]{0,2,1:T(8,128)}, s32[]{:T(128)},...) while((s32[]{:T(128)}, ...), condition=%wide.region_15.16_spmd.clone, body=%wide.region_14.15_spmd.clone.sunk | while | flops 1070350848 | bytes 81393160 | solution.py:296
  1167.4 18.8 collective-permute-done.2
  1209.1 18.8 collective-permute-done.2
  1250.7 18.8 collective-permute-done.2
  1292.2 19.0 collective-permute-done.4
  1335.0 13.7 convolution_convert_fusion
  1362.6 209.1 %reduce-scatter.9.cloned.1.call-done = bf16[200,4800]{1,0:T(8,128)(2,1)} async-done(((bf16[1600,4800]{1,0:T(8,128)(2,1)}), bf16[200,4800]{1,0:T(8,128)(2,1)}) %reduce-scatter.9.cloned.1.call-update) | async-done | bytes 1920016 | tf_op jit(solution)/shard_map/reduce_scatter | solution.py:323
  1571.7 390.8 %reduce-scatter.15.cloned.1.call-done = bf16[200,6400]{1,0:T(8,128)(2,1)} async-done(((bf16[1600,6400]{1,0:T(8,128)(2,1)}), bf16[200,6400]{1,0:T(8,128)(2,1)}) %reduce-scatter.15.cloned.1.call-update) | async-done | bytes 2560016
  1962.4 351.4 %reduce-scatter.11.cloned.1.call-done = bf16[800,1600]{1,0:T(8,128)(2,1)} async-done(((bf16[6400,1600]{1,0:T(8,128)(2,1)}), bf16[800,1600]{1,0:T(8,128)(2,1)}) %reduce-scatter.11.cloned.1.call-update) | async-done | bytes 2560016 | tf_op jit(solution)/shard_map/reduce_scatter | solution.py:243
  2315.4 35.7 %all-reduce.21 = (bf16[1600]{0:T(1024)(128)(2,1)S(1)}, bf16[1600]{0:T(1024)(128)(2,1)S(1)}, bf16[1600]{0:T(1024)(128)(2,1)S(1)}, bf16[1600]{0:T(1024)(128)(2,1)S...) all-reduce(bf16[1600]{0:T(1024)(128)(2,1)S(1)} %dynamic-update-slic, ...), channel_id=1, replica_groups=mesh['ctx'=4,'fsdp'=8] {'fsdp'}, use_global_device_ids=true, to_apply=%add.9 | all-reduce | flops 20800 | bytes 83200
  2367.8 17.4 fusion.44
  2385.2 76.2 %all-reduce.27.cloned.1.call-done = (bf16[200,4800]{1,0:T(8,128)(2,1)}, bf16[200,1600]{1,0:T(8,128)(2,1)}, bf16[200,6400]{1,0:T(8,128)(2,1)}, bf16[800,1600]{1,0:T(8,128)(2,1)}) async-done(((bf16[200,4800]{1,0:T(8,128)(2,1)}, bf16[200,1600]{1,0:T(8,128)(2,1)}, bf16[200,6400]{1,0:T(8,128)(2,1)}, bf16[800,1600]{1,0:T(8,128)(2,1)}), (bf16[200,4800]{1,0:T(8,128)(2,1)}, bf16[200,1600]{1,0:T(8,128)(2,1)}, ...) | async-done | bytes 7680016 | tf_op jit(solution)/shard_map/psum | solution.py:346
  (325 shorter events, 271.0 us)
Async XLA Ops:
  7.2 219.5 %all-gather.5.cloned.1.call-start = ((), (), s32[]{:S(2)}) async-start(), calls=%async_computation.4 | async-start | bytes 17510400 | tf_op jit(solution)/shard_map/all_gather | solution.py:131
  8.0 387.7 %all-gather.7.cloned.1.call-start = ((), (), s32[]{:S(2)}) async-start(), calls=%async_computation.5 | async-start | bytes 5990400 | tf_op jit(solution)/shard_map/all_gather | solution.py:132
  8.8 697.9 %all-gather.9.cloned.1.call-start = ((), (), s32[]{:S(2)}) async-start(), calls=%async_computation.6 | async-start | bytes 23040000 | tf_op jit(solution)/shard_map/all_gather | solution.py:203
  9.5 1106.5 %all-gather.11.cloned.1.call-start = ((), (), s32[]{:S(2)}) async-start(), calls=%async_computation.7 | async-start | bytes 23961600 | tf_op jit(solution)/shard_map/all_gather | solution.py:204
  10.1 1352.5 %reduce-scatter.13.cloned.1.call-start = ((), (), s32[]{:S(2)}) async-start(), calls=%async_computation.10 | async-start | bytes 5990400
  55.1 186.4 %copy-start.23 = (f32[1600]{0:T(1024)}, f32[1600]{0:T(1024)S(1)}, u32[]{:S(2)}) copy-start(f32[1600]{0:T(1024)S(1)} %convert_element_type.234) | copy-start | bytes 19204
  255.9 12.0 collective-permute-start
  271.6 12.0 collective-permute-start
  287.3 12.0 collective-permute-start
  308.8 20.8 collective-permute-start.1
  336.9 20.8 collective-permute-start.1
  365.0 20.8 collective-permute-start.1
  400.9 744.8 %copy-start.2 = (f32[256,1600]{0,1:T(8,128)}, f32[256,1600]{0,1:T(8,128)S(1)}, u32[]{:S(2)}) copy-start(f32[256,1600]{0,1:T(8,128)S(1)} %get-tuple-element.873) | copy-start | bytes 4915204
  1163.9 407.8 %reduce-scatter.9.cloned.1.call-start = ((), (), s32[]{:S(2)}) async-start(), calls=%async_computation.8 | async-start | bytes 17510400 | tf_op jit(solution)/shard_map/reduce_scatter | solution.py:323
  1165.5 20.8 collective-permute-start.2
  1165.5 38.4 %collective-permute-start.3 = (bf16[256,2,25,64]{0,3,2,1:T(8,128)(2,1)}, bf16[256,2,25,64]{0,3,2,1:T(8,128)(2,1)}, u32[]{:S(2)}, u32[]{:S(2)}) collective-permute-start(bf16[256,2,25,64]{0,3,2,1:T(8,128)(2,1)} %get-tuple-element.1158), channel_id=1, source_target_pairs={{24,0},{0,8},{8,16},{16,24},{25,1},{1,9},{9,17},{17,25},{26,2},{2,... | collective-permute-start | bytes 4915208 | tf_op jit(solution)/shard_map/while/body/eval_jaxpr/ppermute | solution.py:17
  1207.2 20.8 collective-permute-start.2
  1207.2 38.4 %collective-permute-start.3 = (bf16[256,2,25,64]{0,3,2,1:T(8,128)(2,1)}, bf16[256,2,25,64]{0,3,2,1:T(8,128)(2,1)}, u32[]{:S(2)}, u32[]{:S(2)}) collective-permute-start(bf16[256,2,25,64]{0,3,2,1:T(8,128)(2,1)} %get-tuple-element.1158), channel_id=1, source_target_pairs={{24,0},{0,8},{8,16},{16,24},{25,1},{1,9},{9,17},{17,25},{26,2},{2,... | collective-permute-start | bytes 4915208 | tf_op jit(solution)/shard_map/while/body/eval_jaxpr/ppermute | solution.py:17
  1248.8 20.8 collective-permute-start.2
  1248.8 38.4 %collective-permute-start.3 = (bf16[256,2,25,64]{0,3,2,1:T(8,128)(2,1)}, bf16[256,2,25,64]{0,3,2,1:T(8,128)(2,1)}, u32[]{:S(2)}, u32[]{:S(2)}) collective-permute-start(bf16[256,2,25,64]{0,3,2,1:T(8,128)(2,1)} %get-tuple-element.1158), channel_id=1, source_target_pairs={{24,0},{0,8},{8,16},{16,24},{25,1},{1,9},{9,17},{17,25},{26,2},{2,... | collective-permute-start | bytes 4915208 | tf_op jit(solution)/shard_map/while/body/eval_jaxpr/ppermute | solution.py:17
  1290.5 20.8 collective-permute-start.4
  1319.6 642.8 %reduce-scatter.15.cloned.1.call-start = ((), (), s32[]{:S(2)}) async-start(), calls=%async_computation.11 | async-start | bytes 23040000
  1333.8 980.0 %reduce-scatter.11.cloned.1.call-start = ((), (), s32[]{:S(2)}) async-start(), calls=%async_computation.9 | async-start | bytes 23961600 | tf_op jit(solution)/shard_map/reduce_scatter | solution.py:243
  1348.7 1112.7 %all-reduce.27.cloned.1.call-start = ((), (), s32[]{:S(2)}) async-start(), calls=%async_computation.12 | async-start | bytes 15667200 | tf_op jit(solution)/shard_map/psum | solution.py:346
  (54 other events, 1641.1 us)
Sparse Core Ops, SparseCore 0:
  10.2 216.4 all-gather.4
  228.9 85.4 all-gather.6
  315.9 390.7 all-gather.8
  708.1 407.8 all-gather.10
  1164.0 123.9 reduce-scatter.12
  1319.7 251.9 reduce-scatter.8
  1575.2 387.1 reduce-scatter.14
  1966.1 347.7 reduce-scatter.10
  2316.5 144.8 all-reduce.26
where the time goes:
time: 2480 us
  waiting for transfers between devices  2100 us (85%)
  matrix products  193 us (8%)
  blocking collectives  83.8 us (3%)
  other arithmetic  53 us (2%)
  local copies, waits for them, and re-layouts  28.2 us (1%)
    all_gather x1, waiting for transfers between devices, per_device(): lax.all_gather(w_proj, 'fsdp', axis=0, tiled=True)  397 us
    unnamed x11, waiting for transfers between devices  393 us
    reduce_scatter x1, waiting for transfers between devices, per_device(): lax.psum_scatter(grad_proj.astype(jnp.bfloat16), 'fsdp', scatter_dimensio...  351 us
    all_gather x1, waiting for transfers between devices, per_device(): lax.all_gather(w_fc, 'fsdp', axis=0, tiled=True)  306 us
    reduce_scatter x1, waiting for transfers between devices, per_device(): lax.psum_scatter(grad_qkv.astype(jnp.bfloat16), 'fsdp', scatter_dimension...  209 us
    ppermute x13, waiting for transfers between devices, shifted(): return lax.ppermute(block, axis, route)  195 us
    all_gather x1, waiting for transfers between devices, per_device(): lax.all_gather(w_qkv, 'fsdp', axis=0, tiled=True)  171 us
    unnamed x2, blocking collectives  76.7 us
  transfers between devices with their start and end apart: 22, of which 20 were waited for; matrix products, arithmetic and copies ran while one was open for 8% of the time, Pallas kernels for 0%

commit v1 on v0

v1 whole, which is shorter than its diff:
```python
import jax
import jax.numpy as jnp
import numpy as np
from jax import lax
from jax.experimental import pallas as pl
from jax.experimental.pallas import tpu as pltpu
from jax.sharding import PartitionSpec as P

H = 25
HD = 64
GROUP = 128
QB = 256
PAIR = 2 * HD
SLOTS = 7
norm_eps = 1e-05
masked_low = -1e30
f32 = jnp.float32
bf16 = jnp.bfloat16


def outer_sum(left_op, right_op):
    return lax.dot_general(
        left_op, right_op, (((0,), (0,)), ((), ())), preferred_element_type=f32
    )


def back_product(left_op, right_op):
    return lax.dot_general(
        left_op, right_op, (((1,), (1,)), ((), ())), preferred_element_type=f32
    )


def product(left_op, right_op):
    return jnp.dot(left_op, right_op, preferred_element_type=f32)


def added(*terms):
    total = terms[0].astype(f32)
    for term in terms[1:]:
        total = total + term.astype(f32)
    return total


def ctx_swap(block, bit):
    return lax.ppermute(block, "ctx", [(i, i ^ bit) for i in range(lax.axis_size("ctx"))])


def gather_ctx(block):
    near = ctx_swap(block, 1)
    far = ctx_swap(block, 2)
    return [block, near, far, ctx_swap(far, 1)]


def scatter_ctx(parts):
    got = ctx_swap(jnp.stack([parts[1], parts[3]]), 1)
    onward = added(parts[2], got[1]).astype(bf16)
    return added(parts[0], got[0], ctx_swap(onward, 2))


def plane_of(count):
    return count // 2, 2


def gather_shards(block):
    count = lax.axis_size("fsdp")
    if count != 8:
        return lax.all_gather(block, "fsdp", axis=0, tiled=False)
    rows, cols = plane_of(count)
    me = lax.axis_index("fsdp")
    row, col = me // cols, me % cols

    def side(value, keep):
        pairs = [(r * 2 + c, r * 2 + 1 - c) for r in range(rows) if keep(r) for c in (0, 1)]
        return lax.ppermute(value, "fsdp", pairs)

    up, down = [block], [block]
    side_up, side_down = [side(block, lambda r: True)], [None]
    for s in range(1, rows):
        up.append(
            lax.ppermute(
                up[-1],
                "fsdp",
                [(r * 2 + c, r * 2 + 2 + c) for r in range(s - 1, rows - 1) for c in (0, 1)],
            )
        )
        down.append(
            lax.ppermute(
                down[-1],
                "fsdp",
                [(r * 2 + 2 + c, r * 2 + c) for r in range(rows - s) for c in (0, 1)],
            )
        )
        side_up.append(side(up[s], lambda r: r >= s))
        side_down.append(side(down[s], lambda r: r < rows - s))
    whole = jnp.zeros((rows, cols) + block.shape, block.dtype)

    def put(whole, value, r, c):
        return lax.dynamic_update_slice(whole, value[None, None], (r, c, 0, 0))

    whole = put(whole, block, row, col)
    whole = put(whole, side_up[0], row, 1 - col)
    for s in range(1, rows):
        whole = put(whole, jnp.where(row >= s, up[s], down[rows - s]), (row - s) % rows, col)
        whole = put(
            whole, jnp.where(row >= s, side_up[s], side_down[rows - s]), (row - s) % rows, 1 - col
        )
    return whole.reshape((count,) + block.shape)


def scatter_shards(blocks):
    count = lax.axis_size("fsdp")
    if count != 8:
        return lax.psum_scatter(blocks, "fsdp", scatter_dimension=0, tiled=False).astype(f32)
    rows, cols = plane_of(count)
    me = lax.axis_index("fsdp")
    row, col = me // cols, me % cols
    grid = blocks.reshape((rows, cols) + blocks.shape[1:])

    def pick(r, c):
        return lax.dynamic_slice(grid, (r, c, 0, 0), (1, 1) + blocks.shape[1:])[0, 0]

    order = [sorted(range(rows), key=lambda t: (-abs(t - r), -t)) for r in range(rows)]
    table = jnp.asarray(np.array(order, np.int32))
    sums = []
    for k in range(rows):
        target = lax.dynamic_index_in_dim(
            lax.dynamic_index_in_dim(table, row, 0, False), k, 0, False
        )
        got = lax.ppermute(pick(target, 1 - col), "fsdp", [(i, i ^ 1) for i in range(count)])
        sums.append(added(got, pick(target, col)))

    def chosen(offset):
        value = None
        for r in range(rows):
            if 0 <= r + offset < rows:
                found = sums[order[r].index(r + offset)]
                value = found if value is None else jnp.where(row == r, found, value)
        return value

    up = down = None
    for s in range(1, rows):
        d = rows - s
        send_up = chosen(d) if up is None else added(chosen(d), up)
        send_down = chosen(-d) if down is None else added(chosen(-d), down)
        up = lax.ppermute(
            send_up.astype(bf16),
            "fsdp",
            [(r * 2 + c, r * 2 + 2 + c) for r in range(s) for c in (0, 1)],
        )
        down = lax.ppermute(
            send_down.astype(bf16),
            "fsdp",
            [(r * 2 + c, r * 2 - 2 + c) for r in range(d, rows) for c in (0, 1)],
        )
    return added(sums[-1], up, down)


def gather_small(vector):
    count = lax.axis_size("fsdp")
    me = lax.axis_index("fsdp")
    held = vector[None]
    bit = 1
    while bit < count:
        got = lax.ppermute(held, "fsdp", [(i, i ^ bit) for i in range(count)])
        low = (me & bit) == 0
        held = jnp.concatenate([jnp.where(low, held, got), jnp.where(low, got, held)], axis=0)
        bit *= 2
    return held


def reduce_small(table):
    count = lax.axis_size("fsdp")
    me = lax.axis_index("fsdp")
    held = table
    bit = count // 2
    while bit:
        halves = held.reshape(2, bit, -1)
        high = (me & bit) != 0
        keep = jnp.where(high, halves[1], halves[0])
        give = jnp.where(high, halves[0], halves[1])
        held = keep + lax.ppermute(give, "fsdp", [(i, i ^ bit) for i in range(count)])
        bit //= 2
    held = held[0]
    held = held + ctx_swap(held, 1)
    return held + ctx_swap(held, 2)


def norm_stats(values):
    centre = values - jnp.mean(values, axis=-1, keepdims=True)
    scale = lax.rsqrt(jnp.mean(centre * centre, axis=-1, keepdims=True) + norm_eps)
    return centre * scale, scale


def norm_back(grad, unit, scale, gain):
    inner = grad * gain
    back = scale * (
        inner
        - jnp.mean(inner, axis=-1, keepdims=True)
        - unit * jnp.mean(inner * unit, axis=-1, keepdims=True)
    )
    return back, jnp.sum(grad * unit, axis=0), jnp.sum(grad, axis=0)


def across(left_op, right_op, left_dim, right_dim):
    return lax.dot_general(
        left_op, right_op, (((left_dim,), (right_dim,)), ((), ())), preferred_element_type=f32
    )


def head_columns(which, last):
    if last:
        return [slice(t * HD, (t + 1) * HD) for t in range(3)]
    return [slice(t * PAIR + which * HD, t * PAIR + (which + 1) * HD) for t in range(3)]


def diagonal_kept():
    shape = (QB, QB)
    return lax.broadcasted_iota(jnp.int32, shape, 0) <= lax.broadcasted_iota(jnp.int32, shape, 1)


def attend_head(which, last, qkv_ref, out_ref, mass_ref):
    at_q, at_k, at_v = head_columns(which, last)
    length = qkv_ref.shape[0]
    queries = qkv_ref[:, at_q] * bf16(HD**-0.5)
    keys = qkv_ref[:, at_k]
    values_t = qkv_ref[:, at_v].T
    kept = diagonal_kept()
    for i in range(length // QB):
        rows = slice(i * QB, (i + 1) * QB)
        mine = queries[rows]
        diag = jnp.where(kept, across(keys[rows], mine, 1, 1), masked_low)
        peak = jnp.max(diag, axis=0, keepdims=True)
        if i:
            rest = across(keys[: i * QB], mine, 1, 1)
            peak = jnp.maximum(peak, jnp.max(rest, axis=0, keepdims=True))
        diag = jnp.exp(diag - peak)
        mass = jnp.sum(diag, axis=0, keepdims=True)
        out = across(values_t[:, rows], diag.astype(bf16), 1, 0)
        if i:
            rest = jnp.exp(rest - peak)
            mass = mass + jnp.sum(rest, axis=0, keepdims=True)
            out = out + across(values_t[:, : i * QB], rest.astype(bf16), 1, 0)
        out = out / mass
        out_ref[rows, which * HD : (which + 1) * HD] = out.T.astype(bf16)
        mass_ref[0, which : which + 1, rows] = peak + jnp.log(mass)


def attend_kernel(qkv_ref, out_ref, mass_ref):
    pair = pl.program_id(0)
    final = pl.num_programs(0) - 1

    @pl.when(pair < final)
    def _():
        for which in range(2):
            attend_head(which, False, qkv_ref, out_ref, mass_ref)

    @pl.when(pair == final)
    def _():
        out_ref[...] = jnp.zeros_like(out_ref)
        mass_ref[...] = jnp.zeros_like(mass_ref)
        attend_head(0, True, qkv_ref, out_ref, mass_ref)


def attend_back_head(which, last, qkv_ref, grad_ref, mass_ref, out_ref, key_acc, value_acc):
    at_q, at_k, at_v = head_columns(which, last)
    length = qkv_ref.shape[0]
    queries = qkv_ref[:, at_q] * bf16(HD**-0.5)
    keys = qkv_ref[:, at_k]
    keys_t = keys.T
    values = qkv_ref[:, at_v]
    grads = grad_ref[:, which * HD : (which + 1) * HD]
    kept = diagonal_kept()
    for i in range(length // QB):
        rows = slice(i * QB, (i + 1) * QB)
        mine = queries[rows]
        grad = grads[rows]
        mass = mass_ref[0, which : which + 1, rows]
        spans = [(rows, True)] + ([(slice(0, i * QB), False)] if i else [])
        probs, both, delta = [], [], None
        for span, diagonal in spans:
            scores = across(keys[span], mine, 1, 1)
            if diagonal:
                scores = jnp.where(kept, scores, masked_low)
            prob = jnp.exp(scores - mass)
            prod = prob * across(values[span], grad, 1, 1)
            part = jnp.sum(prod, axis=0, keepdims=True)
            delta = part if delta is None else delta + part
            probs.append(prob)
            both.append(prod)
        query_t = None
        for (span, diagonal), prob, prod in zip(spans, probs, both):
            grad_scores = (prod - prob * delta).astype(bf16)
            part = across(keys_t[:, span], grad_scores, 1, 0)
            query_t = part if query_t is None else query_t + part
            key_part = across(grad_scores, mine, 1, 0)
            value_part = across(prob.astype(bf16), grad, 1, 0)
            if diagonal:
                key_acc[span, :] = key_part
                value_acc[span, :] = value_part
            else:
                key_acc[span, :] += key_part
                value_acc[span, :] += value_part
        out_ref[rows, at_q] = (query_t * HD**-0.5).T.astype(bf16)
    out_ref[:, at_k] = key_acc[...].astype(bf16)
    out_ref[:, at_v] = value_acc[...].astype(bf16)


def attend_back_kernel(qkv_ref, grad_ref, mass_ref, out_ref, key_acc, value_acc):
    pair = pl.program_id(0)
    final = pl.num_programs(0) - 1
    refs = (qkv_ref, grad_ref, mass_ref, out_ref, key_acc, value_acc)

    @pl.when(pair < final)
    def _():
        for which in range(2):
            attend_back_head(which, False, *refs)

    @pl.when(pair == final)
    def _():
        out_ref[...] = jnp.zeros_like(out_ref)
        attend_back_head(0, True, *refs)


def attend(qkv):
    length = qkv.shape[0]
    pairs = (SLOTS + 1) // 2
    area = SLOTS * length * (length + QB) // 2
    return pl.pallas_call(
        attend_kernel,
        grid=(pairs,),
        in_specs=[pl.BlockSpec((length, 3 * PAIR), lambda p: (0, p))],
        out_specs=[
            pl.BlockSpec((length, PAIR), lambda p: (0, p)),
            pl.BlockSpec((1, 8, length), lambda p: (p, 0, 0)),
        ],
        out_shape=[
            jax.ShapeDtypeStruct((length, pairs * PAIR), bf16),
            jax.ShapeDtypeStruct((pairs, 8, length), f32),
        ],
        compiler_params=pltpu.CompilerParams(vmem_limit_bytes=40 << 20),
        cost_estimate=pl.CostEstimate(
            flops=4 * area * HD * 4, transcendentals=area, bytes_accessed=8 << 20
        ),
        name="attend",
    )(qkv)


def attend_back(qkv, grad, mass):
    length = qkv.shape[0]
    pairs = (SLOTS + 1) // 2
    area = SLOTS * length * (length + QB) // 2
    return pl.pallas_call(
        attend_back_kernel,
        grid=(pairs,),
        in_specs=[
            pl.BlockSpec((length, 3 * PAIR), lambda p: (0, p)),
            pl.BlockSpec((length, PAIR), lambda p: (0, p)),
            pl.BlockSpec((1, 8, length), lambda p: (p, 0, 0)),
        ],
        out_specs=pl.BlockSpec((length, 3 * PAIR), lambda p: (0, p)),
        out_shape=jax.ShapeDtypeStruct((length, pairs * 3 * PAIR), bf16),
        scratch_shapes=[pltpu.VMEM((length, HD), f32), pltpu.VMEM((length, HD), f32)],
        compiler_params=pltpu.CompilerParams(vmem_limit_bytes=40 << 20),
        cost_estimate=pl.CostEstimate(
            flops=10 * area * HD * 4, transcendentals=area, bytes_accessed=12 << 20
        ),
        name="attend_back",
    )(qkv, grad, mass)


def head_slice(matrix, rank, part_count):
    rows = matrix.shape[0]
    width = matrix.shape[1] // part_count
    span = SLOTS * HD
    parts = [
        jnp.pad(matrix[:, t * width : (t + 1) * width], ((0, 0), (0, 4 * span - width)))
        for t in range(part_count)
    ]
    return [lax.dynamic_slice(part, (0, rank * span), (rows, span)) for part in parts]


def to_pairs(parts):
    pieces = []
    for p in range(SLOTS // 2):
        pieces += [part[:, p * PAIR : (p + 1) * PAIR] for part in parts]
    pieces += [part[:, (SLOTS - 1) * HD :] for part in parts]
    return jnp.concatenate(pieces, axis=1)


def from_pairs(matrix):
    whole = SLOTS // 2
    parts = []
    for t in range(3):
        pieces = [
            matrix[:, (3 * p + t) * PAIR : (3 * p + t + 1) * PAIR] for p in range(whole)
        ]
        start = 3 * whole * PAIR + t * HD
        pieces.append(matrix[:, start : start + HD])
        parts.append(jnp.concatenate(pieces, axis=1))
    return parts


def per_device(
    tokens_in,
    group_order,
    out_grad,
    w_qkv,
    w_attn_out,
    b_query,
    b_value,
    b_attn_out,
    w_fc,
    w_proj,
    b_fc,
    b_proj,
    ln1_gain,
    ln1_bias,
    ln2_gain,
    ln2_bias,
):
    ctx = lax.axis_size("ctx")
    shards = lax.axis_size("fsdp")
    rank = lax.axis_index("ctx")
    tokens = tokens_in[0].astype(f32)
    count, width = tokens.shape
    length = count * ctx
    span = SLOTS * HD
    padded = (SLOTS + 1) // 2 * 3 * PAIR
    shard_rows = w_qkv.shape[0]
    unit_rows = w_proj.shape[0] // ctx
    quarter = width // ctx
    peers = [rank ^ k for k in range(ctx)]

    def groups_of(owner):
        return [
            lax.dynamic_index_in_dim(group_order, owner * 2 + j, 0, False) for j in range(2)
        ]

    def sorted_rows(blocks):
        whole = jnp.zeros((length // GROUP, GROUP, blocks[0].shape[1]), blocks[0].dtype)
        for k, block in enumerate(blocks):
            for j, slot in enumerate(groups_of(peers[k])):
                piece = block[j * GROUP : (j + 1) * GROUP][None]
                whole = lax.dynamic_update_slice(whole, piece, (slot, 0, 0))
        return whole.reshape(length, -1)

    def rows_of(matrix, owner):
        return jnp.concatenate(
            [
                lax.dynamic_slice(matrix, (slot * GROUP, 0), (GROUP, matrix.shape[1]))
                for slot in groups_of(owner)
            ],
            axis=0,
        )

    small = gather_small(
        jnp.concatenate(
            [b_query, b_value, b_attn_out, b_proj, ln1_gain, ln1_bias, ln2_gain, ln2_bias, b_fc]
        )
    ).astype(f32)
    vectors = [
        small[:, t * shard_rows : (t + 1) * shard_rows].reshape(-1) for t in range(8)
    ]
    bias_q, bias_v, bias_o, bias_p, gain_one, shift_one, gain_two, shift_two = vectors
    bias_fc = lax.dynamic_index_in_dim(
        small[:, 8 * shard_rows :].reshape(shards, ctx, unit_rows), rank, 1, False
    ).reshape(-1)

    qkv_block = to_pairs(head_slice(w_qkv, rank, 3))
    out_block = lax.dynamic_slice(w_attn_out, (0, rank * quarter), (shard_rows, quarter))
    fc_block = jnp.concatenate(
        [
            lax.dynamic_slice(
                w_fc, (0, (i * ctx + rank) * unit_rows), (shard_rows, unit_rows)
            )
            for i in range(shards)
        ],
        axis=1,
    )
    proj_block = lax.dynamic_slice(w_proj, (rank * unit_rows, 0), (unit_rows, width))

    qkv_weights = gather_shards(qkv_block).reshape(width, 3 * span)
    qkv_weights = jnp.pad(qkv_weights, ((0, 0), (0, padded - 3 * span)))
    out_quarters = gather_ctx(gather_shards(out_block).reshape(width, quarter))
    out_weights = jnp.zeros((ctx, width, quarter), bf16)
    for k in range(ctx):
        out_weights = lax.dynamic_update_slice(out_weights, out_quarters[k][None], (peers[k], 0, 0))
    out_weights = jnp.concatenate([out_weights[k] for k in range(ctx)], axis=1)
    fc_weights = gather_shards(fc_block).reshape(width, shards * unit_rows)
    proj_weights = gather_shards(proj_block).reshape(shards * unit_rows, width)

    unit_one, scale_one = norm_stats(tokens)
    normed_one = (unit_one * gain_one + shift_one).astype(bf16)
    normed_all = sorted_rows(gather_ctx(normed_one))
    none = jnp.zeros((1, span), f32)

    def my_bias(vector):
        return lax.dynamic_slice(
            jnp.pad(vector, (0, ctx * span - width)), (rank * span,), (span,)
        )[None]

    bias_mixed = jnp.pad(
        to_pairs([my_bias(bias_q), none, my_bias(bias_v)]), ((0, 0), (0, padded - 3 * span))
    )
    mixed = (product(normed_all, qkv_weights) + bias_mixed).astype(bf16)
    attended_mine, mass = attend(mixed)
    attended_mine = attended_mine[:, :span]
    attended = jnp.zeros((count, ctx * span), bf16)
    for k in range(ctx):
        got = rows_of(attended_mine, peers[k])
        if k:
            got = ctx_swap(got, k)
        attended = lax.dynamic_update_slice(attended, got, (0, peers[k] * span))
    attended = attended[:, :width]
    middle = tokens + product(attended, out_weights) + bias_o

    unit_two, scale_two = norm_stats(middle)
    normed_two = (unit_two * gain_two + shift_two).astype(bf16)
    normed_two_all = jnp.concatenate(gather_ctx(normed_two), axis=0)
    grad_low = out_grad[0]
    grad_all = jnp.concatenate(gather_ctx(grad_low), axis=0)
    before = product(normed_two_all, fc_weights) + bias_fc
    inner = jnp.tanh(0.7978845608028654 * (before + 0.044715 * before * before * before))
    activated = (0.5 * before * (1.0 + inner)).astype(bf16)
    slope = 0.5 * (1.0 + inner) + 0.5 * before * (1.0 - inner * inner) * (
        0.7978845608028654 * (1.0 + 3 * 0.044715 * before * before)
    )
    branch_two = product(activated, proj_weights).astype(bf16)
    branch_two = scatter_ctx([branch_two[k * count : (k + 1) * count] for k in range(ctx)])
    tokens_out = (middle + branch_two + bias_p).astype(bf16)[None]

    grad_proj = outer_sum(activated, grad_all).astype(bf16)
    shard_proj = scatter_shards(grad_proj.reshape(shards, unit_rows, width))
    before_low = (back_product(grad_all, proj_weights) * slope).astype(bf16)
    grad_fc = outer_sum(normed_two_all, before_low).astype(bf16)
    shard_fc = scatter_shards(grad_fc.reshape(shards, shard_rows, shards * unit_rows))
    grad_two = back_product(before_low, fc_weights).astype(bf16)
    grad_two = scatter_ctx([grad_two[k * count : (k + 1) * count] for k in range(ctx)])
    grad_out = grad_low.astype(f32)
    grad_norm, grad_gain_two, grad_shift_two = norm_back(grad_two, unit_two, scale_two, gain_two)
    grad_middle = grad_out + grad_norm
    middle_low = grad_middle.astype(bf16)

    grad_attended = back_product(middle_low, out_weights).astype(bf16)
    grad_attended = jnp.pad(grad_attended, ((0, 0), (0, ctx * span - width)))
    grad_blocks = []
    for k in range(ctx):
        got = lax.dynamic_slice(grad_attended, (0, peers[k] * span), (count, span))
        grad_blocks.append(ctx_swap(got, k) if k else got)
    grad_heads = jnp.pad(sorted_rows(grad_blocks), ((0, 0), (0, padded // 3 - span)))
    grad_attn_out = outer_sum(attended, middle_low).astype(bf16)
    grad_attn_out = scatter_ctx(
        [
            lax.dynamic_slice(grad_attn_out, (0, peers[k] * quarter), (width, quarter))
            for k in range(ctx)
        ]
    ).astype(bf16)
    shard_attn_out = scatter_shards(grad_attn_out.reshape(shards, shard_rows, quarter))
    grad_mixed = attend_back(mixed, grad_heads, mass)
    grad_qkv = outer_sum(normed_all, grad_mixed)[:, : 3 * span].astype(bf16)
    shard_qkv = scatter_shards(grad_qkv.reshape(shards, shard_rows, 3 * span))
    grad_one = back_product(grad_mixed, qkv_weights).astype(bf16)
    grad_one = scatter_ctx([rows_of(grad_one, peers[k]) for k in range(ctx)])
    grad_norm, grad_gain_one, grad_shift_one = norm_back(grad_one, unit_one, scale_one, gain_one)
    grad_tokens = (grad_middle + grad_norm)[None]

    bias_sums = from_pairs(jnp.sum(grad_mixed.astype(f32), axis=0, keepdims=True))

    def all_heads(vector):
        whole = jnp.zeros((ctx * span,), f32)
        return lax.dynamic_update_slice(whole, vector.reshape(-1), (rank * span,))[:width]

    grad_bias_fc = lax.dynamic_update_slice(
        jnp.zeros((shards, ctx, unit_rows), f32),
        jnp.sum(before_low.astype(f32), axis=0).reshape(shards, 1, unit_rows),
        (0, rank, 0),
    )
    small_grads = [
        all_heads(bias_sums[0]),
        all_heads(bias_sums[2]),
        jnp.sum(middle_low.astype(f32), axis=0),
        jnp.sum(grad_out, axis=0),
        grad_gain_one,
        grad_shift_one,
        grad_gain_two,
        grad_shift_two,
        grad_bias_fc,
    ]
    summed = reduce_small(
        jnp.concatenate([value.reshape(shards, -1) for value in small_grads], axis=1)
    )
    shares = [summed[t * shard_rows : (t + 1) * shard_rows] for t in range(8)]
    share_fc = summed[8 * shard_rows :]

    def all_ranks(share):
        whole = jnp.zeros((ctx,) + share.shape, bf16)
        for k, block in enumerate(gather_ctx(share.astype(bf16))):
            whole = lax.dynamic_update_slice(whole, block[None], (peers[k], 0, 0))
        return whole

    whole_proj = all_ranks(shard_proj).reshape(ctx * unit_rows, width).astype(f32)
    whole_fc = all_ranks(shard_fc)
    whole_fc = jnp.concatenate(
        [
            whole_fc[r][:, i * unit_rows : (i + 1) * unit_rows]
            for i in range(shards)
            for r in range(ctx)
        ],
        axis=1,
    ).astype(f32)
    whole_attn_out = all_ranks(shard_attn_out)
    whole_attn_out = jnp.concatenate([whole_attn_out[r] for r in range(ctx)], axis=1).astype(f32)
    whole_qkv = all_ranks(shard_qkv)
    columns = [from_pairs(whole_qkv[r]) for r in range(ctx)]
    whole_qkv = jnp.concatenate(
        [
            jnp.concatenate([columns[r][t] for r in range(ctx)], axis=1)[:, :width]
            for t in range(3)
        ],
        axis=1,
    ).astype(f32)

    return (
        tokens_out,
        grad_tokens,
        whole_qkv,
        whole_attn_out,
        shares[0],
        shares[1],
        shares[2],
        whole_fc,
        whole_proj,
        share_fc,
        shares[3],
        shares[4],
        shares[5],
        shares[6],
        shares[7],
    )


def solution(mesh):
    placed = (
        P("fsdp", "ctx", None),
        P(),
        P("fsdp", "ctx", None),
        P("fsdp", None),
        P("fsdp", None),
        P("fsdp"),
        P("fsdp"),
        P("fsdp"),
        P("fsdp", None),
        P("fsdp", None),
        P("fsdp"),
        P("fsdp"),
        P("fsdp"),
        P("fsdp"),
        P("fsdp"),
        P("fsdp"),
    )
    return jax.shard_map(
        per_device,
        mesh=mesh,
        in_specs=placed,
        out_specs=(
            P("fsdp", "ctx", None),
            P("fsdp", "ctx", None),
            P("fsdp", None),
            P("fsdp", None),
            P("fsdp"),
            P("fsdp"),
            P("fsdp"),
            P("fsdp", None),
            P("fsdp", None),
            P("fsdp"),
            P("fsdp"),
            P("fsdp"),
            P("fsdp"),
            P("fsdp"),
            P("fsdp"),
        ),
        check_vma=False,
    )
```

time: 2480 us -> 1180 us (0.48); the launches traced: 2480 us -> 1150 us
  waiting for transfers between devices: 2100 us -> 187 us
  local copies, waits for them, and re-layouts: 28.2 us -> 467 us
  starting transfers between devices: 5.18 us -> 245 us
  matrix products: 193 us -> 88.7 us
  blocking collectives: 83.8 us -> 0 us
  other arithmetic: 53 us -> 102 us
  Pallas kernels: 0 us -> 31.9 us
    all_gather x4 -> x0, waiting for transfers between devices: 873 us -> none  [the longest x1 397 us: per_device(): lax.all_gather(w_proj, 'fsdp', axis=0, tiled=True)]
    reduce_scatter x2 -> x0, waiting for transfers between devices: 560 us -> none  [the longest x1 351 us: per_device(): lax.psum_scatter(grad_proj.astype(jnp.bfloat16), 'fsdp', scatter_dimensio...]
    unnamed x11 -> x0, waiting for transfers between devices: 393 us -> none
    dynamic_update_slice x0 -> x53, local copies, waits for them, and re-layouts: none -> 261 us  [the longest x16 162 us: sorted_rows(): whole = lax.dynamic_update_slice(whole, piece, (slot, 0, 0))]
    ppermute x13 -> x138, starting transfers between devices: 4.82 us -> 245 us  [the longest x28 69.2 us: side(): return lax.ppermute(value, 'fsdp', pairs)]
    broadcast_in_dim x0 -> x44, local copies, waits for them, and re-layouts: none -> 92.6 us  [the longest x24 75 us: sorted_rows(): piece = block[j * GROUP:(j + 1) * GROUP][None]]
    dot_general x31 -> x4, matrix products: 110 us -> 31.1 us  [product(): return jnp.dot(left_op, right_op, preferred_element_type=f32)]
    unnamed x2 -> x0, blocking collectives: 76.7 us -> none
  transfers between devices with their start and end apart: 22 -> 138, of which waited for: 20 -> 35; matrix products, arithmetic and copies ran while one was open for 8% -> 53% of each run, Pallas kernels for 0% -> 3%
where the time goes in v1:
time: 1180 us; the launch traced here: 1150 us
  local copies, waits for them, and re-layouts  467 us (40%)
  starting transfers between devices  245 us (21%)
  waiting for transfers between devices  187 us (16%)
  other arithmetic  102 us (9%)
  matrix products  88.7 us (8%)
  Pallas kernels  31.9 us (3%)
  between operations  31.9 us (3%)
    dynamic_update_slice x16, local copies, waits for them, and re-layouts, sorted_rows(): whole = lax.dynamic_update_slice(whole, piece, (slot, 0, 0))  162 us
    broadcast_in_dim x24, local copies, waits for them, and re-layouts, sorted_rows(): piece = block[j * GROUP:(j + 1) * GROUP][None]  75 us
    ppermute x28, starting transfers between devices, side(): return lax.ppermute(value, 'fsdp', pairs)  69.2 us
    dynamic_update_slice x14, local copies, waits for them, and re-layouts, put(): return lax.dynamic_update_slice(whole, value[None, None], (r, c, 0, 0))  67.7 us
    ppermute x12, starting transfers between devices, scatter_shards(): lax.ppermute(send_up.astype(bf16), 'fsdp', [(r * 2 + c, r * 2 + 2 + c) fo...  62.5 us
    ppermute x40, waiting for transfers between devices, ctx_swap(): lax.ppermute(block, 'ctx', [(i, i ^ bit) for i in range(lax.axis_size('ct...  56.6 us
    ppermute x28, waiting for transfers between devices, side(): return lax.ppermute(value, 'fsdp', pairs)  45.2 us
    ppermute x16, waiting for transfers between devices, scatter_shards(): lax.ppermute(pick(target, 1 - col), 'fsdp', [(i, i ^ 1) for i in range(co...  43 us
  transfers between devices with their start and end apart: 138, of which 35 were waited for; matrix products, arithmetic and copies ran while one was open for 53% of the time, Pallas kernels for 3%

profile of v1, /device:TPU:0, one launch (start us, length us, event | category | flops | bytes accessed | tf_op | source)
XLA Modules:
  0.0 1153.7 jit_solution(16893043033221300916)
XLA Ops:
  111.0 21.6 %dynamic_update_slice.225 = bf16[8,128,1600]{1,0,2:T(8,128)(2,1)} dynamic-update-slice(bf16[8,128,1600]{1,0,2:T(8,128)(2,1)} %broadcast_in_dim.255, bf16[1,128,1600]{1,0,2:T(2,128)(2,1)S(1)} %copy.116, s32[]{:T(128)S(6)} %select_n.805, s32[]{:T(128)} %constant.337.clone.1, s32[]{:T(128)} %constant.337.clone.1) | dynamic-update-slice | bytes 819204 | tf_op jit(solution)/shard_map/dynamic_update_slice | solution.py:444
  132.6 21.6 %dynamic_update_slice.226 = bf16[8,128,1600]{1,0,2:T(8,128)(2,1)} dynamic-update-slice(bf16[8,128,1600]{1,0,2:T(8,128)(2,1)} %dynamic_update_slice.225, bf16[1,128,1600]{1,0,2:T(2,128)(2,1)} %copy.117, s32[]{:T(128)S(6)} %select_n.807, s32[]{:T(128)} %constant.337.clone.1, s32[]{:T(128)} %constant.337.clone.1) | dynamic-update-slice | bytes 819204 | tf_op jit(solution)/shard_map/dynamic_update_slice | solution.py:444
  168.5 8.8 collective-permute-done.26
  303.4 18.6 %dynamic_update_slice.227 = bf16[8,128,1600]{1,0,2:T(8,128)(2,1)S(1)} dynamic-update-slice(bf16[8,128,1600]{1,0,2:T(8,128)(2,1)S(1)} %copy-done.28, bf16[1,128,1600]{1,0,2:T(2,128)(2,1)} %copy.118, s32[]{:T(128)S(6)} %select_n.809, s32[]{:T(128)} %constant.337.clone.1, s32[]{:T(128)} %constant.337.clone.1) | dynamic-update-slice | bytes 819204 | tf_op jit(solution)/shard_map/dynamic_update_slice | solution.py:444
  322.0 18.6 %dynamic_update_slice.228 = bf16[8,128,1600]{1,0,2:T(8,128)(2,1)S(1)} dynamic-update-slice(bf16[8,128,1600]{1,0,2:T(8,128)(2,1)S(1)} %dynamic_update_slice.227, bf16[1,128,1600]{1,0,2:T(2,128)(2,1)} %copy.119, s32[]{:T(128)S(6)} %select_n.811, s32[]{:T(128)} %constant.337.clone.1, s32[]{:T(128)} %constant.337.clone.1) | dynamic-update-slice | bytes 819204 | tf_op jit(solution)/shard_map/dynamic_update_slice | solution.py:444
  340.6 18.6 %dynamic_update_slice.229 = bf16[8,128,1600]{1,0,2:T(8,128)(2,1)S(1)} dynamic-update-slice(bf16[8,128,1600]{1,0,2:T(8,128)(2,1)S(1)} %dynamic_update_slice.228, bf16[1,128,1600]{1,0,2:T(2,128)(2,1)} %copy.120, s32[]{:T(128)S(6)} %select_n.813, s32[]{:T(128)} %constant.337.clone.1, s32[]{:T(128)} %constant.337.clone.1) | dynamic-update-slice | bytes 819204 | tf_op jit(solution)/shard_map/dynamic_update_slice | solution.py:444
  359.2 18.6 %dynamic_update_slice.230 = bf16[8,128,1600]{1,0,2:T(8,128)(2,1)S(1)} dynamic-update-slice(bf16[8,128,1600]{1,0,2:T(8,128)(2,1)S(1)} %dynamic_update_slice.229, bf16[1,128,1600]{1,0,2:T(2,128)(2,1)} %copy.121, s32[]{:T(128)S(6)} %select_n.815, s32[]{:T(128)} %constant.337.clone.1, s32[]{:T(128)} %constant.337.clone.1) | dynamic-update-slice | bytes 819204 | tf_op jit(solution)/shard_map/dynamic_update_slice | solution.py:444
  407.5 18.6 %dynamic_update_slice.231 = bf16[8,128,1600]{1,0,2:T(8,128)(2,1)S(1)} dynamic-update-slice(bf16[8,128,1600]{1,0,2:T(8,128)(2,1)S(1)} %dynamic_update_slice.230, bf16[1,128,1600]{1,0,2:T(2,128)(2,1)} %copy.122, s32[]{:T(128)S(6)} %select_n.817, s32[]{:T(128)} %constant.337.clone.1, s32[]{:T(128)} %constant.337.clone.1) | dynamic-update-slice | bytes 819204 | tf_op jit(solution)/shard_map/dynamic_update_slice | solution.py:444
  426.1 18.6 %dynamic_update_slice.232 = bf16[8,128,1600]{1,0,2:T(8,128)(2,1)S(1)} dynamic-update-slice(bf16[8,128,1600]{1,0,2:T(8,128)(2,1)S(1)} %dynamic_update_slice.231, bf16[1,128,1600]{1,0,2:T(2,128)(2,1)} %copy.123, s32[]{:T(128)S(6)} %select_n.819, s32[]{:T(128)} %constant.337.clone.1, s32[]{:T(128)} %constant.337.clone.1) | dynamic-update-slice | bytes 819204 | tf_op jit(solution)/shard_map/dynamic_update_slice | solution.py:444
  506.4 12.9 %attend.1 = (bf16[1024,512]{1,0:T(8,128)(2,1)S(1)}, f32[4,8,1024]{2,1,0:T(8,128)S(1)}) custom-call(bf16[1024,1536]{1,0:T(8,128)(2,1)S(1)} %add_convert_fusion.qkv_ref), custom_call_target="tpu_custom_call" | custom-call | flops 4697620480 | bytes 8388608 | tf_op jit(solution)/shard_map/attend/pallas_call | solution.py:328
  539.6 15.9 %collective-permute-start.59 = (bf16[200,1600]{1,0:T(8,128)(2,1)}, bf16[200,1600]{1,0:T(8,128)(2,1)}, u32[]{:S(2)}, u32[]{:S(2)}) collective-permute-start(bf16[200,1600]{1,0:T(8,128)(2,1)} %collective-permute-done.55), channel_id=1, source_target_pairs={{2,3},{3,2},{4,5},{5,4},{6,7},{7,6},{10,11},{11,10},{12,13},{13,12... | collective-permute-start | bytes 1920008 | tf_op jit(solution)/shard_map/ppermute | solution.py:74
  570.4 9.8 collective-permute-done.60
  611.4 11.3 collective-permute-done.63
  630.5 12.1 %collective-permute-done.39 = bf16[256,1600]{0,1:T(8,128)(2,1)S(1)} collective-permute-done((bf16[256,1600]{0,1:T(8,128)(2,1)S(1)}, bf16[256,1600]{0,1:T(8,128)(2,1)S(1)}, u32[]{:S(2)}, u32[]{:S(2)}) %collective-permute-start.39) | collective-permute-done | bytes 819232 | tf_op jit(solution)/shard_map/ppermute | solution.py:45
  653.5 12.6 %convolution_convert_fusion.4 = bf16[1024,1600]{0,1:T(8,128)(2,1)} fusion(bf16[1600,1600]{1,0:T(8,128)(2,1)} %bitcast.60, f32[1024,1600]{0,1:T(8,128)} %fusion.72, f32[1600]{0:T(1024)S(1)} %copy-done.77), kind=kOutput, calls=%fused_computation.25 | convolution fusion | flops 5260902400 | bytes 14956800 | tf_op jit(solution)/shard_map/dot_general | solution.py:34
  666.1 14.9 %convert_reduce_fusion = (f32[1600]{0:T(1024)S(1)}, bf16[1024,1600]{0,1:T(8,128)(2,1)S(1)}) fusion(f32[1024,1600]{0,1:T(8,128)} %fusion.72, f32[1600]{0:T(1024)S(1)} %copy-done.77, bf16[1600,1600]{1,0:T(8,128)(2,1)} %bitcast.60, bf16[256,1600]{0,1:T(8,128)(2,1)S(1)} %collective-permute-done.71, bf16[256,1600]{0,1:T(8,128)(2,1)} %collective-permute-done.70, ...), kind=kOutput, calls=%fused_computation.14 | convolution fusion | flops 5292030464 | bytes 18240000 | tf_op jit(solution)/shard_map/dot_general | solution.py:28
  703.8 11.5 convolution_convert_fusion
  725.8 22.5 %collective-permute-done.128 = bf16[200,1600]{1,0:T(8,128)(2,1)S(1)} collective-permute-done((bf16[200,1600]{1,0:T(8,128)(2,1)S(1)}, bf16[200,1600]{1,0:T(8,128)(2,1)S(1)}, u32[]{:S(2)}, u32[]{:S(2)}) %collective-permute-start.128) | collective-permute-done | bytes 640032 | tf_op jit(solution)/shard_map/ppermute | solution.py:129
  780.0 9.2 collective-permute-start.130
  806.3 10.8 collective-permute-done.73
  817.1 9.3 collective-permute-start.118
  902.3 19.0 %attend_back.1 = bf16[1024,1536]{1,0:T(8,128)(2,1)S(1)} custom-call(bf16[1024,1536]{1,0:T(8,128)(2,1)S(1)} %add_convert_fusion.qkv_ref, bf16[1024,512]{1,0:T(8,128)(2,1)S(1)} %pad.41.grad_ref, f32[4,8,1024]{2,1,0:T(8,128)S(1)} %get-tuple-element.18.mass_ref), custom_call_target="tpu_custom_call" | custom-call | flops 11744051200 | bytes 12582912 | tf_op jit(solution)/shard_map/attend_back/pallas_call | solution.py:352
  955.4 11.1 collective-permute-done.82
  1058.4 24.7 %collective-permute-done.111 = f32[2400]{0:T(1024)S(1)} collective-permute-done((f32[2400]{0:T(1024)S(1)}, f32[2400]{0:T(1024)S(1)}, u32[]{:S(2)}, u32[]{:S(2)}) %collective-permute-start.111) | collective-permute-done | bytes 9632 | tf_op jit(solution)/shard_map/ppermute | solution.py:45
  (741 shorter events, 750.7 us)
Async XLA Ops:
  2.6 154.4 %collective-permute-start.22 = (bf16[200,400]{1,0:T(8,128)(2,1)}, bf16[200,400]{1,0:T(8,128)(2,1)}, u32[]{:S(2)}, u32[]{:S(2)}) collective-permute-start(bf16[200,400]{1,0:T(8,128)(2,1)} %constant_dynamic-slice_fusion.27), channel_id=1, source_target_pairs={{0,1},{1,0},{2,3},{3,2},{4,5},{5,4},{6,7},{7,6},{8,9},{9,8},{10,11... | collective-permute-start | bytes 480008 | tf_op jit(solution)/shard_map/ppermute | solution.py:74
  5.5 150.0 %collective-permute-start.23 = (bf16[200,400]{1,0:T(8,128)(2,1)}, bf16[200,400]{1,0:T(8,128)(2,1)}, u32[]{:S(2)}, u32[]{:S(2)}) collective-permute-start(bf16[200,400]{1,0:T(8,128)(2,1)} %constant_dynamic-slice_fusion.27), channel_id=1, source_target_pairs={{0,2},{1,3},{2,4},{3,5},{4,6},{5,7},{8,10},{9,11},{10,12},{11,13},... | collective-permute-start | bytes 480008 | tf_op jit(solution)/shard_map/ppermute | solution.py:80
  9.7 144.5 %collective-permute-start.24 = (bf16[200,400]{1,0:T(8,128)(2,1)}, bf16[200,400]{1,0:T(8,128)(2,1)}, u32[]{:S(2)}, u32[]{:S(2)}) collective-permute-start(bf16[200,400]{1,0:T(8,128)(2,1)} %constant_dynamic-slice_fusion.27), channel_id=1, source_target_pairs={{2,0},{3,1},{4,2},{5,3},{6,4},{7,5},{10,8},{11,9},{12,10},{13,11},... | collective-permute-start | bytes 480008 | tf_op jit(solution)/shard_map/ppermute | solution.py:87
  24.4 173.7 %collective-permute-start.6 = (bf16[200,1344]{1,0:T(8,128)(2,1)}, bf16[200,1344]{1,0:T(8,128)(2,1)}, u32[]{:S(2)}, u32[]{:S(2)}) collective-permute-start(bf16[200,1344]{1,0:T(8,128)(2,1)} %concatenate.76), channel_id=1, source_target_pairs={{0,1},{1,0},{2,3},{3,2},{4,5},{5,4},{6,7},{7,6},{8,9},{9,8},{10,11... | collective-permute-start | bytes 1612808 | tf_op jit(solution)/shard_map/ppermute | solution.py:74
  88.4 123.7 %collective-permute-start.8 = (bf16[200,1344]{1,0:T(8,128)(2,1)}, bf16[200,1344]{1,0:T(8,128)(2,1)}, u32[]{:S(2)}, u32[]{:S(2)}) collective-permute-start(bf16[200,1344]{1,0:T(8,128)(2,1)} %concatenate.76), channel_id=1, source_target_pairs={{2,0},{3,1},{4,2},{5,3},{6,4},{7,5},{10,8},{11,9},{12,10},{13,11},... | collective-permute-start | bytes 1612808 | tf_op jit(solution)/shard_map/ppermute | solution.py:87
  181.6 87.5 %collective-permute-start.43 = (bf16[200,1600]{1,0:T(8,128)(2,1)}, bf16[200,1600]{1,0:T(8,128)(2,1)}, u32[]{:S(2)}, u32[]{:S(2)}) collective-permute-start(bf16[200,1600]{1,0:T(8,128)(2,1)} %concatenate.84), channel_id=1, source_target_pairs={{2,0},{3,1},{4,2},{5,3},{6,4},{7,5},{10,8},{11,9},{12,10},{13,11},... | collective-permute-start | bytes 1920008 | tf_op jit(solution)/shard_map/ppermute | solution.py:87
  198.1 71.5 %collective-permute-start.4 = (bf16[256,1600]{0,1:T(8,128)(2,1)}, bf16[256,1600]{0,1:T(8,128)(2,1)}, u32[]{:S(2)}, u32[]{:S(2)}) collective-permute-start(bf16[256,1600]{0,1:T(8,128)(2,1)} %fusion.34), channel_id=1, source_target_pairs={{0,16},{8,24},{16,0},{24,8},{1,17},{9,25},{17,1},{25,9},{2,18},{10... | collective-permute-start | bytes 2457608 | tf_op jit(solution)/shard_map/ppermute | solution.py:45
  216.6 161.3 %collective-permute-start.7 = (bf16[200,1344]{1,0:T(8,128)(2,1)}, bf16[200,1344]{1,0:T(8,128)(2,1)}, u32[]{:S(2)}, u32[]{:S(2)}) collective-permute-start(bf16[200,1344]{1,0:T(8,128)(2,1)} %concatenate.76), channel_id=1, source_target_pairs={{0,2},{1,3},{2,4},{3,5},{4,6},{5,7},{8,10},{9,11},{10,12},{11,13},... | collective-permute-start | bytes 1612808 | tf_op jit(solution)/shard_map/ppermute | solution.py:80
  269.1 175.6 %collective-permute-start.35 = (bf16[1600,400]{0,1:T(8,128)(2,1)}, bf16[1600,400]{0,1:T(8,128)(2,1)}, u32[]{:S(2)}, u32[]{:S(2)}) collective-permute-start(bf16[1600,400]{0,1:T(8,128)(2,1)} %reshape_reshape.25), channel_id=1, source_target_pairs={{0,8},{8,0},{16,24},{24,16},{1,9},{9,1},{17,25},{25,17},{2,10},{10... | collective-permute-start | bytes 3840008 | tf_op jit(solution)/shard_map/ppermute | solution.py:45
  269.6 120.3 %collective-permute-start.44 = (bf16[200,1600]{1,0:T(8,128)(2,1)}, bf16[200,1600]{1,0:T(8,128)(2,1)}, u32[]{:S(2)}, u32[]{:S(2)}) collective-permute-start(bf16[200,1600]{1,0:T(8,128)(2,1)} %collective-permute-done.43), channel_id=1, source_target_pairs={{2,0},{3,1},{4,2},{5,3},{10,8},{11,9},{12,10},{13,11},{18,16},{19,... | collective-permute-start | bytes 1920008 | tf_op jit(solution)/shard_map/ppermute | solution.py:87
  270.9 113.2 %collective-permute-start.10 = (bf16[200,1344]{1,0:T(8,128)(2,1)}, bf16[200,1344]{1,0:T(8,128)(2,1)}, u32[]{:S(2)}, u32[]{:S(2)}) collective-permute-start(bf16[200,1344]{1,0:T(8,128)(2,1)} %collective-permute-done.9), channel_id=1, source_target_pairs={{2,0},{3,1},{10,8},{11,9},{18,16},{19,17},{26,24},{27,25}} | collective-permute-start | bytes 1612808 | tf_op jit(solution)/shard_map/ppermute | solution.py:87
  273.6 116.8 %collective-permute-start.5 = (bf16[256,1600]{0,1:T(8,128)(2,1)}, bf16[256,1600]{0,1:T(8,128)(2,1)}, u32[]{:S(2)}, u32[]{:S(2)}) collective-permute-start(bf16[256,1600]{0,1:T(8,128)(2,1)} %collective-permute-done.4), channel_id=1, source_target_pairs={{0,8},{8,0},{16,24},{24,16},{1,9},{9,1},{17,25},{25,17},{2,10},{10... | collective-permute-start | bytes 2457608 | tf_op jit(solution)/shard_map/ppermute | solution.py:45
  377.8 70.7 %collective-permute-start.42 = (bf16[200,1600]{1,0:T(8,128)(2,1)}, bf16[200,1600]{1,0:T(8,128)(2,1)}, u32[]{:S(2)}, u32[]{:S(2)}) collective-permute-start(bf16[200,1600]{1,0:T(8,128)(2,1)} %concatenate.84), channel_id=1, source_target_pairs={{0,2},{1,3},{2,4},{3,5},{4,6},{5,7},{8,10},{9,11},{10,12},{11,13},... | collective-permute-start | bytes 1920008 | tf_op jit(solution)/shard_map/ppermute | solution.py:80
  384.1 136.2 %collective-permute-start.55 = (bf16[200,1600]{1,0:T(8,128)(2,1)}, bf16[200,1600]{1,0:T(8,128)(2,1)}, u32[]{:S(2)}, u32[]{:S(2)}) collective-permute-start(bf16[200,1600]{1,0:T(8,128)(2,1)} %get-tuple-element.38), channel_id=1, source_target_pairs={{0,2},{1,3},{2,4},{3,5},{4,6},{5,7},{8,10},{9,11},{10,12},{11,13},... | collective-permute-start | bytes 1920008 | tf_op jit(solution)/shard_map/ppermute | solution.py:80
  476.9 81.8 %collective-permute-start.46 = (bf16[200,1600]{1,0:T(8,128)(2,1)}, bf16[200,1600]{1,0:T(8,128)(2,1)}, u32[]{:S(2)}, u32[]{:S(2)}) collective-permute-start(bf16[200,1600]{1,0:T(8,128)(2,1)} %collective-permute-done.42), channel_id=1, source_target_pairs={{2,3},{3,2},{4,5},{5,4},{6,7},{7,6},{10,11},{11,10},{12,13},{13,12... | collective-permute-start | bytes 1920008 | tf_op jit(solution)/shard_map/ppermute | solution.py:74
  489.8 69.7 %collective-permute-start.48 = (bf16[200,1600]{1,0:T(8,128)(2,1)}, bf16[200,1600]{1,0:T(8,128)(2,1)}, u32[]{:S(2)}, u32[]{:S(2)}) collective-permute-start(bf16[200,1600]{1,0:T(8,128)(2,1)} %collective-permute-done.42), channel_id=1, source_target_pairs={{2,4},{3,5},{4,6},{5,7},{10,12},{11,13},{12,14},{13,15},{18,20},{1... | collective-permute-start | bytes 1920008 | tf_op jit(solution)/shard_map/ppermute | solution.py:80
  535.1 107.8 %collective-permute-start.70 = (bf16[256,1600]{0,1:T(8,128)(2,1)}, bf16[256,1600]{0,1:T(8,128)(2,1)}, u32[]{:S(2)}, u32[]{:S(2)}) collective-permute-start(bf16[256,1600]{0,1:T(8,128)(2,1)} %bitcast.460), channel_id=1, source_target_pairs={{0,16},{8,24},{16,0},{24,8},{1,17},{9,25},{17,1},{25,9},{2,18},{10... | collective-permute-start | bytes 2457608 | tf_op jit(solution)/shard_map/ppermute | solution.py:45
  691.6 82.6 %collective-permute-start.72 = (bf16[2,256,1600]{1,2,0:T(8,128)(2,1)}, bf16[2,256,1600]{1,2,0:T(8,128)(2,1)}, u32[]{:S(2)}, u32[]{:S(2)}) collective-permute-start(bf16[2,256,1600]{1,2,0:T(8,128)(2,1)} %pad_maximum_fusion.5), channel_id=1, source_target_pairs={{0,8},{8,0},{16,24},{24,16},{1,9},{9,1},{17,25},{25,17},{2,10},{10... | collective-permute-start | bytes 4915208 | tf_op jit(solution)/shard_map/ppermute | solution.py:45
  800.6 66.1 %collective-permute-start.125 = (bf16[200,1600]{1,0:T(8,128)(2,1)}, bf16[200,1600]{1,0:T(8,128)(2,1)}, u32[]{:S(2)}, u32[]{:S(2)}) collective-permute-start(bf16[200,1600]{1,0:T(8,128)(2,1)} %get-tuple-element.49), channel_id=1, source_target_pairs={{0,1},{1,0},{2,3},{3,2},{4,5},{5,4},{6,7},{7,6},{8,9},{9,8},{10,11... | collective-permute-start | bytes 1920008 | tf_op jit(solution)/shard_map/ppermute | solution.py:129
  867.1 175.2 %collective-permute-start.92 = (bf16[2,1600,400]{1,2,0:T(8,128)(2,1)}, bf16[2,1600,400]{1,2,0:T(8,128)(2,1)}, u32[]{:S(2)}, u32[]{:S(2)}) collective-permute-start(bf16[2,1600,400]{1,2,0:T(8,128)(2,1)} %pad_maximum_fusion.3), channel_id=1, source_target_pairs={{0,8},{8,0},{16,24},{24,16},{1,9},{9,1},{17,25},{25,17},{2,10},{10... | collective-permute-start | bytes 7680008 | tf_op jit(solution)/shard_map/ppermute | solution.py:45
  874.6 76.2 %collective-permute-start.122 = (bf16[200,1600]{1,0:T(8,128)(2,1)}, bf16[200,1600]{1,0:T(8,128)(2,1)}, u32[]{:S(2)}, u32[]{:S(2)}) collective-permute-start(bf16[200,1600]{1,0:T(8,128)(2,1)} %get-tuple-element.30), channel_id=1, source_target_pairs={{0,8},{8,0},{16,24},{24,16},{1,9},{9,1},{17,25},{25,17},{2,10},{10... | collective-permute-start | bytes 1920008 | tf_op jit(solution)/shard_map/ppermute | solution.py:45
  879.3 74.3 %collective-permute-start.123 = (bf16[200,1600]{1,0:T(8,128)(2,1)}, bf16[200,1600]{1,0:T(8,128)(2,1)}, u32[]{:S(2)}, u32[]{:S(2)}) collective-permute-start(bf16[200,1600]{1,0:T(8,128)(2,1)} %get-tuple-element.30), channel_id=1, source_target_pairs={{0,16},{8,24},{16,0},{24,8},{1,17},{9,25},{17,1},{25,9},{2,18},{10... | collective-permute-start | bytes 1920008 | tf_op jit(solution)/shard_map/ppermute | solution.py:45
  882.6 89.6 %collective-permute-start.135 = (bf16[200,1600]{1,0:T(8,128)(2,1)}, bf16[200,1600]{1,0:T(8,128)(2,1)}, u32[]{:S(2)}, u32[]{:S(2)}) collective-permute-start(bf16[200,1600]{1,0:T(8,128)(2,1)} %get-tuple-element.28), channel_id=1, source_target_pairs={{0,8},{8,0},{16,24},{24,16},{1,9},{9,1},{17,25},{25,17},{2,10},{10... | collective-permute-start | bytes 1920008 | tf_op jit(solution)/shard_map/ppermute | solution.py:45
  887.8 87.1 %collective-permute-start.136 = (bf16[200,1600]{1,0:T(8,128)(2,1)}, bf16[200,1600]{1,0:T(8,128)(2,1)}, u32[]{:S(2)}, u32[]{:S(2)}) collective-permute-start(bf16[200,1600]{1,0:T(8,128)(2,1)} %get-tuple-element.28), channel_id=1, source_target_pairs={{0,16},{8,24},{16,0},{24,8},{1,17},{9,25},{17,1},{25,9},{2,18},{10... | collective-permute-start | bytes 1920008 | tf_op jit(solution)/shard_map/ppermute | solution.py:45
  (207 other events, 3469.9 us)

commit v2 on v1

v2 whole, which is shorter than its diff:
```python
import functools

import jax
import jax.numpy as jnp
import numpy as np
from jax import lax
from jax.experimental import pallas as pl
from jax.experimental.layout import Layout, with_layout_constraint
from jax.experimental.pallas import tpu as pltpu
from jax.sharding import PartitionSpec as P

H = 25
HD = 64
GROUP = 128
QB = 256
PAIR = 2 * HD
RANKS = 4
BASE = H // RANKS
SLOTS = H - (RANKS - 1) * BASE
norm_eps = 1e-05
masked_low = -1e30
f32 = jnp.float32
bf16 = jnp.bfloat16


def outer_sum(left_op, right_op):
    return lax.dot_general(
        left_op, right_op, (((0,), (0,)), ((), ())), preferred_element_type=f32
    )


def back_product(left_op, right_op):
    return lax.dot_general(
        left_op, right_op, (((1,), (1,)), ((), ())), preferred_element_type=f32
    )


def product(left_op, right_op):
    return jnp.dot(left_op, right_op, preferred_element_type=f32)


def added(*terms):
    total = terms[0].astype(f32)
    for term in terms[1:]:
        total = total + term.astype(f32)
    return total


def row_major(matrix):
    return with_layout_constraint(matrix, Layout(major_to_minor=tuple(range(matrix.ndim))))


def after(value, *others):
    return lax.optimization_barrier((value,) + others)[0]


PEERS = (0, 2, 1, 3)


def ctx_swap(block, bit):
    pairs = [(i, i ^ bit) for i in range(lax.axis_size("ctx"))]
    return row_major(lax.ppermute(row_major(block), "ctx", pairs))


def gather_ctx(block):
    far = ctx_swap(block, 2)
    near = ctx_swap(block, 1)
    return [block, far, near, ctx_swap(far, 1)]


def scatter_near(matrix):
    half = matrix.shape[0] // 2
    quarter = half // 2
    got = ctx_swap(matrix[half:], 1)
    onward = added(matrix[quarter:half], got[quarter:]).astype(bf16)
    return added(matrix[:quarter], got[:quarter]), onward


def scatter_far(kept, onward):
    return added(kept, ctx_swap(onward, 2))


def exchange_near(matrix):
    half = matrix.shape[0] // 2
    quarter = half // 2
    got = ctx_swap(matrix[half:], 1)
    return matrix[:quarter], got[:quarter], jnp.concatenate([matrix[quarter:half], got[quarter:]])


def exchange_far(mine, near, onward):
    quarter = mine.shape[0]
    got = ctx_swap(onward, 2)
    return [mine, got[:quarter], near, got[quarter:]]


RING = (0, 2, 4, 6, 7, 5, 3, 1)
HALF = len(RING) // 2


def ring_hop(value, step):
    count = len(RING)
    pairs = [(RING[q], RING[(q + step) % count]) for q in range(count)]
    return row_major(lax.ppermute(row_major(value), "fsdp", pairs))


def ring_owners():
    place = jnp.asarray(np.argsort(np.array(RING)).astype(np.int32))
    mine = lax.dynamic_index_in_dim(place, lax.axis_index("fsdp"), 0, False)
    offsets = np.array([0, -1, 1, -2, 2, -3, 3, 4], np.int32)
    return jnp.take(jnp.asarray(np.array(RING, np.int32)), (mine + offsets) % len(RING))


def on_ring():
    return lax.axis_size("fsdp") == len(RING)


def upper_part(rows):
    return rows // 16 * 8


class Gather:
    def __init__(self, block):
        self.block = block
        self.cut = upper_part(block.shape[0])
        self.pieces = [block]
        self.forth = self.back = block

    def hop(self, *gate):
        if not on_ring():
            return
        k = (len(self.pieces) + 1) // 2
        forth, back = self.forth, self.back
        if k == HALF:
            forth, back = forth[: self.cut], back[self.cut :]
        if gate:
            forth, back = after(forth, *gate), after(back, *gate)
        self.forth, self.back = ring_hop(forth, 1), ring_hop(back, -1)
        self.pieces += [self.forth, self.back]

    def arrived(self):
        return (self.forth, self.back) if on_ring() else ()

    def result(self, owners, columns, rows):
        if not on_ring():
            whole = lax.all_gather(self.block, "fsdp", axis=0, tiled=False)
            return [whole[:, top : top + n, c : c + w] for c, w, top, n in columns]
        return collect(self.pieces, owners, self.cut, columns)


def collect_kernel(cut, columns, owners, *refs):
    pieces = refs[: 2 * HALF + 1]
    outs = refs[2 * HALF + 1 : 2 * HALF + 1 + len(columns)]
    sems = refs[-1]
    copies = []
    for out, (start, width, top, rows) in zip(outs, columns):
        for j, piece in enumerate(pieces):
            first = cut if j == 2 * HALF else 0
            low = max(top, first)
            high = min(top + rows, first + piece.shape[0])
            if low < high:
                copies.append(
                    pltpu.make_async_copy(
                        piece.at[pl.ds(low - first, high - low), pl.ds(start, width)],
                        out.at[owners[min(j, 2 * HALF - 1)], pl.ds(low - top, high - low)],
                        sems.at[len(copies)],
                    )
                )
    for copy in copies:
        copy.start()
    for copy in copies:
        copy.wait()


def collect(pieces, owners, cut, columns):
    shapes = [(len(RING), rows, width) for _, width, _, rows in columns]
    return pl.pallas_call(
        functools.partial(collect_kernel, cut, columns),
        grid_spec=pltpu.PrefetchScalarGridSpec(
            num_scalar_prefetch=1,
            grid=(1,),
            in_specs=[pl.BlockSpec(memory_space=pl.ANY)] * len(pieces),
            out_specs=[pl.BlockSpec(shape, lambda i, t: (0, 0, 0)) for shape in shapes],
            scratch_shapes=[pltpu.SemaphoreType.DMA((len(pieces) * len(columns),))],
        ),
        out_shape=[jax.ShapeDtypeStruct(shape, pieces[0].dtype) for shape in shapes],
        compiler_params=pltpu.CompilerParams(vmem_limit_bytes=40 << 20),
        cost_estimate=pl.CostEstimate(flops=0, transcendentals=0, bytes_accessed=12 << 20),
        name="collect",
    )(owners, *pieces)


class Scatter:
    def __init__(self, blocks, owners):
        self.blocks, self.owners = blocks, owners
        self.cut = upper_part(blocks.shape[1])
        self.next = HALF
        self.forth = self.back = None

    def part(self, offset):
        where = {0: 0, 4: 7}.get(offset, 2 * abs(offset) - (offset < 0))
        return lax.dynamic_index_in_dim(self.blocks, self.owners[where], 0, False)

    def hop(self, *gate):
        if not on_ring():
            return
        k, cut = self.next, self.cut
        if k == HALF:
            far = self.part(HALF)
            ahead, behind = far[:cut], far[cut:]
        else:
            ahead, behind = self.part(k), self.part(-k)
            forth, back = self.forth, self.back
            if gate:
                forth, back = after(forth, *gate), after(back, *gate)
            if k == HALF - 1:
                ahead = jnp.concatenate([added(ahead[:cut], forth).astype(bf16), ahead[cut:]])
                behind = jnp.concatenate([behind[:cut], added(behind[cut:], back).astype(bf16)])
            else:
                ahead = added(ahead, forth).astype(bf16)
                behind = added(behind, back).astype(bf16)
        self.next -= 1
        self.forth, self.back = ring_hop(ahead, 1), ring_hop(behind, -1)

    def result(self):
        if not on_ring():
            return lax.psum_scatter(
                self.blocks, "fsdp", scatter_dimension=0, tiled=False
            ).astype(f32)
        return added(self.part(0), self.forth, self.back)


def reduce_small(table):
    count = lax.axis_size("fsdp")
    me = lax.axis_index("fsdp")
    held = table
    bit = count // 2
    while bit:
        halves = held.reshape(2, bit, -1)
        high = (me & bit) != 0
        keep = jnp.where(high, halves[1], halves[0])
        give = jnp.where(high, halves[0], halves[1])
        held = keep + lax.ppermute(give, "fsdp", [(i, i ^ bit) for i in range(count)])
        bit //= 2
    held = held[0]
    held = held + ctx_swap(held, 1)
    return held + ctx_swap(held, 2)


def norm_stats(values):
    centre = values - jnp.mean(values, axis=-1, keepdims=True)
    scale = lax.rsqrt(jnp.mean(centre * centre, axis=-1, keepdims=True) + norm_eps)
    return centre * scale, scale


def norm_back(grad, unit, scale, gain):
    inner = grad * gain
    back = scale * (
        inner
        - jnp.mean(inner, axis=-1, keepdims=True)
        - unit * jnp.mean(inner * unit, axis=-1, keepdims=True)
    )
    return back, jnp.sum(grad * unit, axis=0), jnp.sum(grad, axis=0)


def across(left_op, right_op, left_dim, right_dim):
    return lax.dot_general(
        left_op, right_op, (((left_dim,), (right_dim,)), ((), ())), preferred_element_type=f32
    )


def diagonal_kept():
    shape = (QB, QB)
    return lax.broadcasted_iota(jnp.int32, shape, 0) <= lax.broadcasted_iota(jnp.int32, shape, 1)


def sorted_tile(table, ref, columns):
    groups = ref.shape[0] // GROUP
    return jnp.concatenate(
        [ref[pl.ds(pl.multiple_of(table[g], GROUP), GROUP), columns] for g in range(groups)],
        axis=0,
    )


def put_sorted(table, ref, columns, first, value):
    for j in range(value.shape[0] // GROUP):
        start = pl.multiple_of(table[first + j], GROUP)
        ref[pl.ds(start, GROUP), columns] = value[j * GROUP : (j + 1) * GROUP]


def split_heads(tiles, last):
    if last:
        return [(tiles[0][:, :HD], tiles[0][:, HD:], tiles[1][:, :HD])]
    return [tuple(t[:, w * HD : (w + 1) * HD] for t in tiles) for w in range(2)]


def pair_columns(pair, last):
    if last:
        start = SLOTS // 2 * 3 * PAIR
        return [slice(start, start + PAIR), slice(start + PAIR, start + 2 * PAIR)]
    return [pl.ds(pl.multiple_of(pair * 3 * PAIR + t * PAIR, PAIR), PAIR) for t in range(3)]


def attend_pair(pair, last, table, qkv_ref, out_ref, mass_ref):
    tiles = [sorted_tile(table, qkv_ref, c) for c in pair_columns(pair, last)]
    heads = split_heads(tiles, last)
    length = qkv_ref.shape[0]
    kept = diagonal_kept()
    ready = [(q * bf16(HD**-0.5), k, v.T) for q, k, v in heads]
    for i in range(length // QB):
        rows = slice(i * QB, (i + 1) * QB)
        outs = []
        for w, (queries, keys, values_t) in enumerate(ready):
            mine = queries[rows]
            diag = jnp.where(kept, across(keys[rows], mine, 1, 1), masked_low)
            peak = jnp.max(diag, axis=0, keepdims=True)
            if i:
                rest = across(keys[: i * QB], mine, 1, 1)
                peak = jnp.maximum(peak, jnp.max(rest, axis=0, keepdims=True))
            diag = jnp.exp(diag - peak)
            mass = jnp.sum(diag, axis=0, keepdims=True)
            out = across(values_t[:, rows], diag.astype(bf16), 1, 0)
            if i:
                rest = jnp.exp(rest - peak)
                mass = mass + jnp.sum(rest, axis=0, keepdims=True)
                out = out + across(values_t[:, : i * QB], rest.astype(bf16), 1, 0)
            outs.append(out / mass)
            mass_ref[0, w : w + 1, rows] = peak + jnp.log(mass)
        if last:
            outs.append(jnp.zeros_like(outs[0]))
        tile = jnp.concatenate(outs, axis=0).T.astype(bf16)
        put_sorted(table, out_ref, slice(None), 2 * i, tile)


def attend_kernel(table, qkv_ref, out_ref, mass_ref):
    pair = pl.program_id(0)
    final = pl.num_programs(0) - 1

    @pl.when(pair < final)
    def _():
        attend_pair(pair, False, table, qkv_ref, out_ref, mass_ref)

    @pl.when(pair == final)
    def _():
        mass_ref[...] = jnp.zeros_like(mass_ref)

        @pl.when(table[table.shape[0] - 1] == 0)
        def _():
            out_ref[...] = jnp.zeros_like(out_ref)

        @pl.when(table[table.shape[0] - 1] != 0)
        def _():
            attend_pair(pair, True, table, qkv_ref, out_ref, mass_ref)


def attend_back_pair(pair, last, table, qkv_ref, grad_ref, mass_ref, out_ref, acc):
    places = pair_columns(pair, last)
    heads = split_heads([sorted_tile(table, qkv_ref, c) for c in places], last)
    grads = sorted_tile(table, grad_ref, slice(None))
    length = qkv_ref.shape[0]
    kept = diagonal_kept()
    ready = [
        (q * bf16(HD**-0.5), k, k.T, v, grads[:, w * HD : (w + 1) * HD])
        for w, (q, k, v) in enumerate(heads)
    ]
    for i in range(length // QB):
        rows = slice(i * QB, (i + 1) * QB)
        query_tiles = []
        for w, (queries, keys, keys_t, values, grads_w) in enumerate(ready):
            mine = queries[rows]
            grad = grads_w[rows]
            mass = mass_ref[0, w : w + 1, rows]
            spans = [(rows, True)] + ([(slice(0, i * QB), False)] if i else [])
            probs, both, delta = [], [], None
            for span, diagonal in spans:
                scores = across(keys[span], mine, 1, 1)
                if diagonal:
                    scores = jnp.where(kept, scores, masked_low)
                prob = jnp.exp(scores - mass)
                prod = prob * across(values[span], grad, 1, 1)
                part = jnp.sum(prod, axis=0, keepdims=True)
                delta = part if delta is None else delta + part
                probs.append(prob)
                both.append(prod)
            query_t = None
            for (span, diagonal), prob, prod in zip(spans, probs, both):
                grad_scores = (prod - prob * delta).astype(bf16)
                part = across(keys_t[:, span], grad_scores, 1, 0)
                query_t = part if query_t is None else query_t + part
                key_part = across(grad_scores, mine, 1, 0)
                value_part = across(prob.astype(bf16), grad, 1, 0)
                if diagonal:
                    acc[2 * w, span, :] = key_part
                    acc[2 * w + 1, span, :] = value_part
                else:
                    acc[2 * w, span, :] += key_part
                    acc[2 * w + 1, span, :] += value_part
            query_tiles.append(query_t * HD**-0.5)
        if last:
            query_tiles.append(jnp.zeros_like(query_tiles[0]))
        tile = jnp.concatenate(query_tiles, axis=0).T
        if last:
            tile = jnp.concatenate([tile[:, :HD], jnp.zeros_like(tile[:, HD:])], axis=1)
        put_sorted(table, out_ref, places[0], 2 * i, tile.astype(bf16))
    if last:
        old = sorted_tile(table, out_ref, places[0])
        tile = jnp.concatenate([old[:, :HD], acc[0].astype(bf16)], axis=1)
        put_sorted(table, out_ref, places[0], 0, tile)
        tile = jnp.concatenate([acc[1].astype(bf16), jnp.zeros((length, HD), bf16)], axis=1)
        put_sorted(table, out_ref, places[1], 0, tile)
    else:
        for t in range(2):
            tile = jnp.concatenate([acc[t].astype(bf16), acc[2 + t].astype(bf16)], axis=1)
            put_sorted(table, out_ref, places[1 + t], 0, tile)


def attend_back_kernel(table, qkv_ref, grad_ref, mass_ref, out_ref, acc):
    pair = pl.program_id(0)
    final = pl.num_programs(0) - 1
    refs = (table, qkv_ref, grad_ref, mass_ref, out_ref, acc)

    @pl.when(pair < final)
    def _():
        attend_back_pair(pair, False, *refs)

    @pl.when(pair == final)
    def _():
        @pl.when(table[table.shape[0] - 1] == 0)
        def _():
            for columns in pair_columns(pair, True):
                out_ref[:, columns] = jnp.zeros((out_ref.shape[0], PAIR), bf16)

        @pl.when(table[table.shape[0] - 1] != 0)
        def _():
            attend_back_pair(pair, True, *refs)


def attend(table, qkv):
    length, columns = qkv.shape
    pairs = (SLOTS + 1) // 2
    area = SLOTS * length * (length + QB) // 2
    return pl.pallas_call(
        attend_kernel,
        grid_spec=pltpu.PrefetchScalarGridSpec(
            num_scalar_prefetch=1,
            grid=(pairs,),
            in_specs=[pl.BlockSpec((length, columns), lambda p, t: (0, 0))],
            out_specs=[
                pl.BlockSpec((length, PAIR), lambda p, t: (0, p)),
                pl.BlockSpec((1, 8, length), lambda p, t: (p, 0, 0)),
            ],
        ),
        out_shape=[
            jax.ShapeDtypeStruct((length, pairs * PAIR), bf16),
            jax.ShapeDtypeStruct((pairs, 8, length), f32),
        ],
        compiler_params=pltpu.CompilerParams(vmem_limit_bytes=40 << 20),
        cost_estimate=pl.CostEstimate(
            flops=4 * area * HD * 4, transcendentals=area, bytes_accessed=8 << 20
        ),
        name="attend",
    )(table, qkv)


def attend_back(table, qkv, grad, mass):
    length, columns = qkv.shape
    pairs = (SLOTS + 1) // 2
    area = SLOTS * length * (length + QB) // 2
    return pl.pallas_call(
        attend_back_kernel,
        grid_spec=pltpu.PrefetchScalarGridSpec(
            num_scalar_prefetch=1,
            grid=(pairs,),
            in_specs=[
                pl.BlockSpec((length, columns), lambda p, t: (0, 0)),
                pl.BlockSpec((length, PAIR), lambda p, t: (0, p)),
                pl.BlockSpec((1, 8, length), lambda p, t: (p, 0, 0)),
            ],
            out_specs=pl.BlockSpec((length, columns), lambda p, t: (0, 0)),
            scratch_shapes=[pltpu.VMEM((4, length, HD), f32)],
        ),
        out_shape=jax.ShapeDtypeStruct((length, columns), bf16),
        compiler_params=pltpu.CompilerParams(vmem_limit_bytes=40 << 20),
        cost_estimate=pl.CostEstimate(
            flops=10 * area * HD * 4, transcendentals=area, bytes_accessed=12 << 20
        ),
        name="attend_back",
    )(table, qkv, grad, mass)


def head_slice(matrix, rank, part_count):
    width = matrix.shape[1] // part_count
    return [
        lax.dynamic_slice(
            matrix, (0, t * width + rank * BASE * HD), (matrix.shape[0], SLOTS * HD)
        )
        for t in range(part_count)
    ]


def to_pairs(parts):
    pieces = []
    for p in range(SLOTS // 2):
        pieces += [part[:, p * PAIR : (p + 1) * PAIR] for part in parts]
    pieces += [part[:, (SLOTS - 1) * HD :] for part in parts]
    pieces.append(jnp.zeros((parts[0].shape[0], HD), parts[0].dtype))
    return jnp.concatenate(pieces, axis=1)


def from_pairs(matrix, part, last):
    pieces = [
        matrix[:, (3 * p + part) * PAIR : (3 * p + part + 1) * PAIR] for p in range(SLOTS // 2)
    ]
    if last:
        start = 3 * (SLOTS // 2) * PAIR + part * HD
        pieces.append(matrix[:, start : start + HD])
    return pieces


def per_device(
    tokens_in,
    group_order,
    out_grad,
    w_qkv,
    w_attn_out,
    b_query,
    b_value,
    b_attn_out,
    w_fc,
    w_proj,
    b_fc,
    b_proj,
    ln1_gain,
    ln1_bias,
    ln2_gain,
    ln2_bias,
):
    ctx = lax.axis_size("ctx")
    shards = lax.axis_size("fsdp")
    rank = lax.axis_index("ctx")
    tokens = tokens_in[0].astype(f32)
    count, width = tokens.shape
    span = SLOTS * HD
    step = BASE * HD
    mixed_width = (3 * span + PAIR - 1) // PAIR * PAIR
    attn_width = mixed_width + span
    shard_rows = w_qkv.shape[0]
    unit_rows = w_proj.shape[0] // ctx
    peers = [rank ^ bit for bit in PEERS]
    owners = ring_owners() if on_ring() else None

    def by_rank(blocks):
        whole = jnp.zeros((ctx,) + blocks[0].shape, blocks[0].dtype)
        for peer, block in zip(peers, blocks):
            whole = lax.dynamic_update_slice(whole, block[None], (peer,) + (0,) * block.ndim)
        return row_major(whole)

    def columns_of(blocks):
        return jnp.concatenate(
            [blocks[r][:, :step] for r in range(ctx - 1)] + [blocks[ctx - 1]], axis=1
        )

    def windows(matrix):
        return jnp.concatenate(
            [
                row_major(lax.dynamic_slice(matrix, (0, peer * step), (matrix.shape[0], span)))
                for peer in peers
            ]
        )

    slots = jnp.argsort(group_order).astype(jnp.int32)
    place = jnp.take(jnp.asarray(np.argsort(np.array(PEERS)).astype(np.int32)), (slots // 2) ^ rank)
    slot_rows = (place * 2 + slots % 2) * GROUP
    table = jnp.concatenate([slot_rows, (rank == ctx - 1).astype(jnp.int32)[None]])

    vectors = jnp.concatenate(
        [b_query, b_value, b_attn_out, b_proj, ln1_gain, ln1_bias, ln2_gain, ln2_bias, b_fc]
    )
    vector_rows = (vectors.shape[0] + attn_width * 8 - 1) // (attn_width * 8) * 8
    vector_block = jnp.pad(vectors, (0, vector_rows * attn_width - vectors.shape[0]))
    attn_block = jnp.concatenate(
        [
            to_pairs(head_slice(w_qkv, rank, 3)),
            lax.dynamic_slice(w_attn_out, (0, rank * step), (shard_rows, span)),
        ],
        axis=1,
    )
    attn_block = jnp.concatenate([attn_block, vector_block.reshape(vector_rows, attn_width)])
    fc_block = jnp.concatenate(
        [
            lax.dynamic_slice(
                w_fc, (0, (i * ctx + rank) * unit_rows), (shard_rows, unit_rows)
            )
            for i in range(shards)
        ],
        axis=1,
    )
    proj_block = lax.dynamic_slice(w_proj, (rank * unit_rows, 0), (unit_rows, width))
    attn_gather = Gather(attn_block)
    attn_gather.hop()
    tokens_all = row_major(jnp.concatenate(gather_ctx(tokens_in[0])))
    attn_gather.hop()
    attn_gather.hop()
    fc_gather = Gather(after(fc_block, *attn_gather.arrived()))
    proj_gather = Gather(after(proj_block, *attn_gather.arrived()))
    attn_gather.hop()
    grad_all = row_major(
        jnp.concatenate(gather_ctx(after(out_grad[0], *attn_gather.arrived())))
    )
    for _ in range(HALF):
        fc_gather.hop()
        proj_gather.hop()

    qkv_weights, out_columns, small = attn_gather.result(
        owners,
        (
            (0, mixed_width, 0, shard_rows),
            (mixed_width, span, 0, shard_rows),
            (0, attn_width, shard_rows, vector_rows),
        ),
        None,
    )
    qkv_weights = qkv_weights.reshape(width, mixed_width)
    small = small.reshape(shards, -1).astype(f32)
    bias_q, bias_v, bias_o, bias_p, gain_one, shift_one, gain_two, shift_two = [
        small[:, t * shard_rows : (t + 1) * shard_rows].reshape(-1) for t in range(8)
    ]
    units = ctx * unit_rows
    bias_fc = lax.dynamic_index_in_dim(
        small[:, 8 * shard_rows : 8 * shard_rows + units].reshape(shards, ctx, unit_rows),
        rank,
        1,
        False,
    ).reshape(-1)

    normed_all = row_major(
        (norm_stats(tokens_all.astype(f32))[0] * gain_one + shift_one).astype(bf16)
    )

    def my_bias(vector):
        return lax.dynamic_slice(vector, (rank * step,), (span,))[None]

    bias_mixed = to_pairs([my_bias(bias_q), jnp.zeros((1, span), f32), my_bias(bias_v)])
    mixed = row_major((product(normed_all, qkv_weights) + bias_mixed).astype(bf16))
    attended_mine, mass = attend(table, mixed)
    out_windows = by_rank(gather_ctx(out_columns.reshape(width, span)))
    out_weights = row_major(columns_of(out_windows))
    attended = exchange_far(*exchange_near(row_major(attended_mine[:, :span])))
    attended = row_major(columns_of(by_rank(attended)))
    middle = tokens + product(attended, out_weights) + bias_o

    unit_two, scale_two = norm_stats(middle)
    normed_two = row_major((unit_two * gain_two + shift_two).astype(bf16))
    normed_two_all = row_major(jnp.concatenate(gather_ctx(normed_two)))
    (fc_weights,) = fc_gather.result(owners, ((0, shards * unit_rows, 0, shard_rows),), None)
    (proj_weights,) = proj_gather.result(owners, ((0, width, 0, unit_rows),), None)
    fc_weights = fc_weights.reshape(width, -1)
    proj_weights = proj_weights.reshape(-1, width)
    before = product(normed_two_all, fc_weights) + bias_fc
    inner = jnp.tanh(0.7978845608028654 * (before + 0.044715 * before * before * before))
    activated = row_major((0.5 * before * (1.0 + inner)).astype(bf16))
    slope = 0.5 * (1.0 + inner) + 0.5 * before * (1.0 - inner * inner) * (
        0.7978845608028654 * (1.0 + 3 * 0.044715 * before * before)
    )

    grad_proj = row_major(outer_sum(activated, grad_all).astype(bf16))
    proj_scatter = Scatter(grad_proj.reshape(shards, unit_rows, width), owners)
    proj_scatter.hop()
    before_low = row_major(
        (back_product(after(grad_all, grad_proj), proj_weights) * slope).astype(bf16)
    )
    grad_two = row_major(back_product(before_low, fc_weights).astype(bf16))
    proj_scatter.hop()
    kept_two, onward_two = scatter_near(grad_two)
    grad_fc = row_major(outer_sum(normed_two_all, after(before_low, grad_two)).astype(bf16))
    fc_scatter = Scatter(grad_fc.reshape(shards, shard_rows, shards * unit_rows), owners)
    fc_scatter.hop()
    proj_scatter.hop(onward_two)
    fc_scatter.hop(onward_two)
    grad_two = scatter_far(kept_two, onward_two)
    grad_out = out_grad[0].astype(f32)
    grad_norm, grad_gain_two, grad_shift_two = norm_back(grad_two, unit_two, scale_two, gain_two)
    grad_middle = grad_out + grad_norm
    middle_low = row_major(grad_middle.astype(bf16))
    proj_scatter.hop(middle_low)
    fc_scatter.hop(middle_low)

    grad_attended = row_major(back_product(middle_low, out_weights).astype(bf16))
    heads_near = exchange_near(windows(grad_attended))
    grad_heads = jnp.concatenate(exchange_far(*heads_near))
    grad_heads = jnp.pad(grad_heads, ((0, 0), (0, PAIR - span % PAIR)))
    grad_mixed = attend_back(table, mixed, grad_heads, mass)
    fc_scatter.hop(grad_heads)
    grad_qkv = row_major(outer_sum(normed_all, grad_mixed).astype(bf16))
    qkv_scatter = Scatter(grad_qkv.reshape(shards, shard_rows, mixed_width), owners)
    qkv_scatter.hop()
    grad_one = row_major(
        back_product(after(grad_mixed, grad_qkv), qkv_weights).astype(bf16)
    )
    kept_one, onward_one = scatter_near(grad_one)
    qkv_scatter.hop()
    grad_attn_out = row_major(
        outer_sum(attended, after(middle_low, onward_one)).astype(bf16)
    )
    kept_out, onward_out = scatter_near(windows(grad_attn_out))
    qkv_scatter.hop()
    grad_one = scatter_far(kept_one, onward_one)
    grad_attn_out = row_major(scatter_far(kept_out, onward_out).astype(bf16))
    out_scatter = Scatter(grad_attn_out.reshape(shards, shard_rows, span), owners)
    out_scatter.hop()
    qkv_scatter.hop()
    out_scatter.hop()
    out_scatter.hop()
    out_scatter.hop()

    unit_one, scale_one = norm_stats(tokens)
    grad_norm, grad_gain_one, grad_shift_one = norm_back(grad_one, unit_one, scale_one, gain_one)
    grad_tokens = (grad_middle + grad_norm)[None]

    branch_two = row_major(product(activated, after(proj_weights, grad_qkv)).astype(bf16))
    branch_two = scatter_far(*scatter_near(branch_two))
    tokens_out = (middle + branch_two + bias_p).astype(bf16)[None]

    bias_sums = jnp.sum(grad_mixed.astype(f32), axis=0, keepdims=True)

    def all_heads(part):
        mine = jnp.concatenate(from_pairs(bias_sums, part, True), axis=1)
        return lax.dynamic_update_slice(jnp.zeros((1, width), f32), mine, (0, rank * step))

    grad_bias_fc = lax.dynamic_update_slice(
        jnp.zeros((shards, ctx, unit_rows), f32),
        jnp.sum(before_low.astype(f32), axis=0).reshape(shards, 1, unit_rows),
        (0, rank, 0),
    )
    small_grads = [
        all_heads(0),
        all_heads(2),
        jnp.sum(middle_low.astype(f32), axis=0),
        jnp.sum(grad_out, axis=0),
        grad_gain_one,
        grad_shift_one,
        grad_gain_two,
        grad_shift_two,
        grad_bias_fc,
    ]
    summed = reduce_small(
        jnp.concatenate([value.reshape(shards, -1) for value in small_grads], axis=1)
    )
    shares = [summed[t * shard_rows : (t + 1) * shard_rows] for t in range(8)]
    share_fc = summed[8 * shard_rows :]

    shard_ff = jnp.stack([fc_scatter.result(), proj_scatter.result()]).astype(bf16)
    whole_ff = gather_ctx(after(shard_ff, grad_qkv))
    whole_proj = by_rank([g[1] for g in whole_ff]).reshape(ctx * unit_rows, width).astype(f32)
    whole_fc = by_rank([g[0] for g in whole_ff])
    whole_fc = jnp.concatenate(
        [
            whole_fc[r][:, i * unit_rows : (i + 1) * unit_rows]
            for i in range(shards)
            for r in range(ctx)
        ],
        axis=1,
    ).astype(f32)
    shard_attn = jnp.concatenate([qkv_scatter.result(), out_scatter.result()], axis=1)
    whole_attn = by_rank(gather_ctx(shard_attn.astype(bf16)))
    whole_attn_out = columns_of(whole_attn[:, :, mixed_width:]).astype(f32)
    whole_qkv = jnp.concatenate(
        [
            piece
            for t in range(3)
            for r in range(ctx)
            for piece in from_pairs(whole_attn[r], t, r == ctx - 1)
        ],
        axis=1,
    ).astype(f32)

    return (
        tokens_out,
        grad_tokens,
        whole_qkv,
        whole_attn_out,
        shares[0],
        shares[1],
        shares[2],
        whole_fc,
        whole_proj,
        share_fc,
        shares[3],
        shares[4],
        shares[5],
        shares[6],
        shares[7],
    )


def solution(mesh):
    placed = (
        P("fsdp", "ctx", None),
        P(),
        P("fsdp", "ctx", None),
        P("fsdp", None),
        P("fsdp", None),
        P("fsdp"),
        P("fsdp"),
        P("fsdp"),
        P("fsdp", None),
        P("fsdp", None),
        P("fsdp"),
        P("fsdp"),
        P("fsdp"),
        P("fsdp"),
        P("fsdp"),
        P("fsdp"),
    )
    return jax.shard_map(
        per_device,
        mesh=mesh,
        in_specs=placed,
        out_specs=(
            P("fsdp", "ctx", None),
            P("fsdp", "ctx", None),
            P("fsdp", None),
            P("fsdp", None),
            P("fsdp"),
            P("fsdp"),
            P("fsdp"),
            P("fsdp", None),
            P("fsdp", None),
            P("fsdp"),
            P("fsdp"),
            P("fsdp"),
            P("fsdp"),
            P("fsdp"),
            P("fsdp"),
        ),
        check_vma=False,
    )
```

time: 1180 us -> 792 us (0.67); the launches traced: 1150 us -> 784 us
  local copies, waits for them, and re-layouts: 467 us -> 215 us
  starting transfers between devices: 245 us -> 86.3 us
  waiting for transfers between devices: 187 us -> 225 us
  between operations: 31.9 us -> 18.5 us
    dynamic_update_slice x52 -> x18, local copies, waits for them, and re-layouts: 261 us -> 22.8 us  [the longest x16 22.5 us: by_rank(): lax.dynamic_update_slice(whole, block[None], (peer,) + (0,) * block.ndim)]
    ppermute x135 -> x88, starting transfers between devices: 239 us -> 82.4 us  [the longest x56 60.6 us: ring_hop(): return row_major(lax.ppermute(row_major(value), 'fsdp', pairs))]
    broadcast_in_dim x43 -> x5, local copies, waits for them, and re-layouts: 92.6 us -> 0.81 us  [the longest x3 0.8 us: by_rank(): whole = jnp.zeros((ctx,) + blocks[0].shape, blocks[0].dtype)]
    ppermute x0 -> x16, local copies, waits for them, and re-layouts: none -> 39.4 us  [ctx_swap(): return row_major(lax.ppermute(row_major(block), 'ctx', pairs))]
    ppermute x135 -> x88, waiting for transfers between devices: 184 us -> 220 us  [the longest x56 148 us: ring_hop(): return row_major(lax.ppermute(row_major(value), 'fsdp', pairs))]
    dynamic_update_slice x22 -> x3, other arithmetic: 33.6 us -> 0.15 us  [the longest x1 0.1 us: by_rank(): lax.dynamic_update_slice(whole, block[None], (peer,) + (0,) * block.ndim)]
    unnamed x186 -> x214, local copies, waits for them, and re-layouts: 14.7 us -> 42.4 us
    slice x10 -> x43, local copies, waits for them, and re-layouts: 15.6 us -> 31.6 us  [the longest x4 9.9 us: scatter_near(): return (added(matrix[:quarter], got[:quarter]), onward)]
  transfers between devices with their start and end apart: 138 -> 91, of which waited for: 35 -> 31; matrix products, arithmetic and copies ran while one was open for 53% -> 38% of each run, Pallas kernels for 3% -> 3%
where the time goes in v2:
time: 792 us; the launch traced here: 784 us
  waiting for transfers between devices  225 us (28%)
  local copies, waits for them, and re-layouts  215 us (27%)
  other arithmetic  102 us (13%)
  matrix products  99.9 us (13%)
  starting transfers between devices  86.3 us (11%)
  Pallas kernels  36.7 us (5%)
  between operations  18.5 us (2%)
    ppermute x56, waiting for transfers between devices, ring_hop(): return row_major(lax.ppermute(row_major(value), 'fsdp', pairs))  148 us
    ppermute x32, waiting for transfers between devices, ctx_swap(): return row_major(lax.ppermute(row_major(block), 'ctx', pairs))  71.9 us
    ppermute x56, starting transfers between devices, ring_hop(): return row_major(lax.ppermute(row_major(value), 'fsdp', pairs))  60.6 us
    unnamed x214, local copies, waits for them, and re-layouts  42.4 us
    ppermute x16, local copies, waits for them, and re-layouts, ctx_swap(): return row_major(lax.ppermute(row_major(block), 'ctx', pairs))  39.4 us
    dot_general x4, matrix products, product(): return jnp.dot(left_op, right_op, preferred_element_type=f32)  34.5 us
    dot_general x4, matrix products, outer_sum(): lax.dot_general(left_op, right_op, (((0,), (0,)), ((), ())), preferred_el...  33.3 us
    dot_general x4, matrix products, back_product(): lax.dot_general(left_op, right_op, (((1,), (1,)), ((), ())), preferred_el...  32.1 us
  transfers between devices with their start and end apart: 91, of which 31 were waited for; matrix products, arithmetic and copies ran while one was open for 38% of the time, Pallas kernels for 3%

profile of v2, /device:TPU:0, one launch (start us, length us, event | category | flops | bytes accessed | tf_op | source)
XLA Modules:
  0.0 784.3 jit_solution(7310810224854875206)
XLA Ops:
  24.7 11.1 %collective-permute-done.3.refs_1_ = bf16[208,1856]{1,0:T(8,128)(2,1)} collective-permute-done((bf16[208,1856]{1,0:T(8,128)(2,1)S(1)}, bf16[208,1856]{1,0:T(8,128)(2,1)}, u32[]{:S(2)}, u32[]{:S(2)}) %collective-permute-start.3) | collective-permute-done | bytes 772128 | tf_op jit(solution)/shard_map/ppermute | solution.py:103
  40.9 14.2 %collective-permute-done.5.refs_3_ = bf16[208,1856]{1,0:T(8,128)(2,1)} collective-permute-done((bf16[208,1856]{1,0:T(8,128)(2,1)}, bf16[208,1856]{1,0:T(8,128)(2,1)}, u32[]{:S(2)}, u32[]{:S(2)}) %collective-permute-start.5) | collective-permute-done | bytes 772128 | tf_op jit(solution)/shard_map/ppermute | solution.py:103
  94.1 11.1 %add_convert_fusion.qkv_ref = bf16[1024,1408]{1,0:T(8,128)(2,1)S(1)} fusion(bf16[1600,1408]{1,0:T(8,128)(2,1)} %bitcast.272, f32[1408]{0:T(1024)S(1)} %reduce, f32[1600]{0:T(1024)S(1)} %add.457, f32[1600]{0:T(1024)S(1)} %mul.220, f32[1024]{0:T(1024)S(1)} %add_rsqrt_fusion, f32[1024]{0:T(1024)S(1)} %broadcast_multiply_fusion, bf16[256,1600]{1,0:T(8,128)(2,1)} %copy.53, ...), kind=kOutput, calls=%fused_computation.27 | convolution fusion | flops 4637917184 | bytes 10692608 | tf_op jit(solution)/shard_map/dot_general | solution.py:39
  105.2 11.6 %attend.1 = (bf16[1024,512]{1,0:T(8,128)(2,1)S(1)}, f32[4,8,1024]{2,1,0:T(8,128)S(1)}) custom-call(s32[9]{0:T(128)S(1)} %pad_add_fusion.table, bf16[1024,1408]{1,0:T(8,128)(2,1)S(1)} %add_convert_fusion.qkv_ref), custom_call_target="tpu_custom_call" | custom-call | flops 4697620480 | bytes 8388608 | tf_op jit(solution)/shard_map/attend/pallas_call | solution.py:441
  142.4 28.5 %collective-permute-done.12 = bf16[512,448]{1,0:T(8,128)(2,1)S(1)} collective-permute-done((bf16[512,448]{1,0:T(8,128)(2,1)S(1)}, bf16[512,448]{1,0:T(8,128)(2,1)S(1)}, u32[]{:S(2)}, u32[]{:S(2)}) %collective-permute-start.12) | collective-permute-done | bytes 458784 | tf_op jit(solution)/shard_map/ppermute | solution.py:62
  214.8 8.7 %collective-permute-done.30.refs_4_ = bf16[200,1600]{1,0:T(8,128)(2,1)} collective-permute-done((bf16[200,1600]{1,0:T(8,128)(2,1)}, bf16[200,1600]{1,0:T(8,128)(2,1)}, u32[]{:S(2)}, u32[]{:S(2)}) %collective-permute-start.30) | collective-permute-done | bytes 640032 | tf_op jit(solution)/shard_map/ppermute | solution.py:103
  225.5 12.2 %collective-permute-done.22.refs_4_ = bf16[200,1600]{1,0:T(8,128)(2,1)} collective-permute-done((bf16[200,1600]{1,0:T(8,128)(2,1)S(1)}, bf16[200,1600]{1,0:T(8,128)(2,1)}, u32[]{:S(2)}, u32[]{:S(2)}) %collective-permute-start.22) | collective-permute-done | bytes 640032 | tf_op jit(solution)/shard_map/ppermute | solution.py:103
  239.7 12.2 %collective-permute-done.32.refs_6_ = bf16[200,1600]{1,0:T(8,128)(2,1)S(1)} collective-permute-done((bf16[200,1600]{1,0:T(8,128)(2,1)}, bf16[200,1600]{1,0:T(8,128)(2,1)S(1)}, u32[]{:S(2)}, u32[]{:S(2)}) %collective-permute-start.32) | collective-permute-done | bytes 640032 | tf_op jit(solution)/shard_map/ppermute | solution.py:103
  311.8 13.0 %fusion.60 = f32[1024,1600]{1,0:T(8,128)} fusion(bf16[1600,1600]{1,0:T(8,128)(2,1)} %bitcast.268, bf16[256,1600]{1,0:T(8,128)(2,1)} %copy.66, bf16[256,1600]{1,0:T(8,128)(2,1)} %copy.64, bf16[256,1600]{1,0:T(8,128)(2,1)} %copy.62, bf16[256,1600]{1,0:T(8,128)(2,1)S(1)} %copy-done.55), kind=kOutput, calls=%fused_computation.163 | convolution fusion | flops 5255987200 | bytes 14950400 | tf_op jit(solution)/shard_map/dot_general | solution.py:39
  324.9 12.9 %convolution_convert_fusion.3 = bf16[1600,1600]{1,0:T(8,128)(2,1)} fusion(f32[1024,1600]{1,0:T(8,128)} %fusion.60, f32[1600]{0:T(1024)S(1)} %add.484, bf16[256,1600]{1,0:T(8,128)(2,1)S(1)} %copy-done.58, bf16[256,1600]{1,0:T(8,128)(2,1)S(1)} %copy-done.57, bf16[256,1600]{1,0:T(8,128)(2,1)S(1)} %copy-done.56, bf16[256,1600]{1,0:T(8,128)(2,1)S(1)} %bitcast.280), kind=kOutput, calls=%fused_computation.11 | convolution fusion | flops 5274931200 | bytes 14956800 | tf_op jit(solution)/shard_map/dot_general | solution.py:27
  337.8 12.6 %convert_reduce_fusion.1 = (f32[1600]{0:T(1024)S(1)}, bf16[1024,1600]{1,0:T(8,128)(2,1)}) fusion(f32[1024,1600]{1,0:T(8,128)} %fusion.60, f32[1600]{0:T(1024)S(1)} %add.484, bf16[1024,1600]{1,0:T(8,128)(2,1)S(1)} %copy-done.59, bf16[1600,1600]{1,0:T(8,128)(2,1)S(1)} %bitcast.264), kind=kOutput, calls=%fused_computation.24 | convolution fusion | flops 5278923264 | bytes 18240000 | tf_op jit(solution)/shard_map/dot_general | solution.py:33
  350.4 8.7 %convolution_convert_fusion.6 = bf16[1024,1600]{1,0:T(8,128)(2,1)S(1)} fusion(bf16[1024,1600]{1,0:T(8,128)(2,1)} %get-tuple-element.53, bf16[1600,1600]{1,0:T(8,128)(2,1)S(1)} %bitcast.271), kind=kOutput, calls=%fused_computation.31 | convolution fusion | flops 5244518400 | bytes 11673600 | tf_op jit(solution)/shard_map/dot_general | solution.py:33
  368.2 9.2 %convolution_convert_fusion.1 = bf16[1600,1600]{1,0:T(8,128)(2,1)S(1)} fusion(bf16[1024,1600]{1,0:T(8,128)(2,1)} %get-tuple-element.53, bf16[256,1600]{1,0:T(8,128)(2,1)} %copy.66, bf16[256,1600]{1,0:T(8,128)(2,1)} %copy.64, bf16[256,1600]{1,0:T(8,128)(2,1)} %copy.62, bf16[256,1600]{1,0:T(8,128)(2,1)} %add_convert_fusion.7), kind=kOutput, calls=%fused_computation.9 | convolution fusion | flops 5258547200 | bytes 11673600 | tf_op jit(solution)/shard_map/dot_general | solution.py:27
  393.4 9.0 %collective-permute-done.81 = bf16[200,1600]{1,0:T(8,128)(2,1)} collective-permute-done((bf16[200,1600]{1,0:T(8,128)(2,1)}, bf16[200,1600]{1,0:T(8,128)(2,1)}, u32[]{:S(2)}, u32[]{:S(2)}) %collective-permute-start.81) | collective-permute-done | bytes 640032 | tf_op jit(solution)/shard_map/ppermute | solution.py:103
  440.9 9.5 %collective-permute-done.86 = bf16[200,1600]{1,0:T(8,128)(2,1)S(1)} collective-permute-done((bf16[200,1600]{1,0:T(8,128)(2,1)S(1)}, bf16[200,1600]{1,0:T(8,128)(2,1)S(1)}, u32[]{:S(2)}, u32[]{:S(2)}) %collective-permute-start.86) | collective-permute-done | bytes 640032 | tf_op jit(solution)/shard_map/ppermute | solution.py:103
  454.0 16.5 %attend_back.1 = bf16[1024,1408]{1,0:T(8,128)(2,1)S(1)} custom-call(s32[9]{0:T(128)S(1)} %pad_add_fusion.table, bf16[1024,1408]{1,0:T(8,128)(2,1)S(1)} %copy-done.27, bf16[1024,512]{1,0:T(8,128)(2,1)S(1)} %fusion.51.grad_ref, f32[4,8,1024]{2,1,0:T(8,128)S(1)} %get-tuple-element.49.mass_ref), custom_call_target="tpu_custom_call" | custom-call | flops 11744051200 | bytes 12582912 | tf_op jit(solution)/shard_map/attend_back/pallas_call | solution.py:468
  470.6 8.3 %convolution_convert_fusion = bf16[1600,1408]{1,0:T(8,128)(2,1)} fusion(bf16[1024,1408]{1,0:T(8,128)(2,1)S(1)} %attend_back.1, f32[1600]{0:T(1024)S(1)} %copy-done.89, f32[1600]{0:T(1024)S(1)} %mul.220, f32[1024]{0:T(1024)S(1)} %copy-done.91, f32[1024]{0:T(1024)S(1)} %copy-done.86, bf16[256,1600]{1,0:T(8,128)(2,1)S(1)} %copy-done.50, ...), kind=kOutput, calls=%fused_computation.8 | convolution fusion | flops 4637286400 | bytes 10686976 | tf_op jit(solution)/shard_map/dot_general | solution.py:27
  479.5 8.4 %convolution_convert_fusion.5 = bf16[1024,1600]{1,0:T(8,128)(2,1)S(1)} fusion(bf16[1600,1600]{1,0:T(8,128)(2,1)S(1)} %bitcast.267, f32[1024,1600]{1,0:T(8,128)S(1)} %bitcast.322, f32[1600]{0:T(1024)S(1)} %add.484), kind=kOutput, calls=%fused_computation.30 | convolution fusion | flops 5260902400 | bytes 14956800 | tf_op jit(solution)/shard_map/dot_general | solution.py:39
  492.1 8.8 %convolution_convert_fusion.4 = bf16[1024,1600]{1,0:T(8,128)(2,1)S(1)} fusion(bf16[1024,1408]{1,0:T(8,128)(2,1)} %copy-done.6, bf16[1600,1408]{1,0:T(8,128)(2,1)} %bitcast.273), kind=kOutput, calls=%fused_computation.29 | convolution fusion | flops 4615372800 | bytes 10665984 | tf_op jit(solution)/shard_map/dot_general | solution.py:33
  524.8 13.5 %collective-permute-done.78 = bf16[200,1600]{1,0:T(8,128)(2,1)S(1)} collective-permute-done((bf16[200,1600]{1,0:T(8,128)(2,1)S(1)}, bf16[200,1600]{1,0:T(8,128)(2,1)S(1)}, u32[]{:S(2)}, u32[]{:S(2)}) %collective-permute-start.78) | collective-permute-done | bytes 640032 | tf_op jit(solution)/shard_map/ppermute | solution.py:103
  544.3 9.7 %collective-permute-done.47 = bf16[200,1408]{1,0:T(8,128)(2,1)S(1)} collective-permute-done((bf16[200,1408]{1,0:T(8,128)(2,1)S(1)}, bf16[200,1408]{1,0:T(8,128)(2,1)S(1)}, u32[]{:S(2)}, u32[]{:S(2)}) %collective-permute-start.47) | collective-permute-done | bytes 563232 | tf_op jit(solution)/shard_map/ppermute | solution.py:103
  555.7 9.8 %collective-permute-done.75 = bf16[200,1600]{1,0:T(8,128)(2,1)S(1)} collective-permute-done((bf16[200,1600]{1,0:T(8,128)(2,1)S(1)}, bf16[200,1600]{1,0:T(8,128)(2,1)S(1)}, u32[]{:S(2)}, u32[]{:S(2)}) %collective-permute-start.75) | collective-permute-done | bytes 640032 | tf_op jit(solution)/shard_map/ppermute | solution.py:103
  616.4 17.8 %collective-permute-done.45 = bf16[256,1600]{0,1:T(8,128)(2,1)} collective-permute-done((bf16[256,1600]{0,1:T(8,128)(2,1)}, bf16[256,1600]{0,1:T(8,128)(2,1)}, u32[]{:S(2)}, u32[]{:S(2)}) %collective-permute-start.45) | collective-permute-done | bytes 819232 | tf_op jit(solution)/shard_map/ppermute | solution.py:62
  692.9 23.3 %collective-permute-done.55 = bf16[1600,448]{0,1:T(8,128)(2,1)} collective-permute-done((bf16[1600,448]{0,1:T(8,128)(2,1)}, bf16[1600,448]{0,1:T(8,128)(2,1)}, u32[]{:S(2)}, u32[]{:S(2)}) %collective-permute-start.55) | collective-permute-done | bytes 1433632 | tf_op jit(solution)/shard_map/ppermute | solution.py:62
  (648 shorter events, 465.0 us)
Async XLA Ops:
  19.9 40.1 %collective-permute-start.1 = (bf16[256,1600]{0,1:T(8,128)(2,1)}, bf16[256,1600]{0,1:T(8,128)(2,1)}, u32[]{:S(2)}, u32[]{:S(2)}) collective-permute-start(bf16[256,1600]{0,1:T(8,128)(2,1)} %bitcast.316), channel_id=1, source_target_pairs={{0,8},{8,0},{16,24},{24,16},{1,9},{9,1},{17,25},{25,17},{2,10},{10... | collective-permute-start | bytes 2457608 | tf_op jit(solution)/shard_map/ppermute | solution.py:62
  124.4 47.5 %collective-permute-start.13 = (bf16[1600,448]{0,1:T(8,128)(2,1)}, bf16[1600,448]{0,1:T(8,128)(2,1)}, u32[]{:S(2)}, u32[]{:S(2)}) collective-permute-start(bf16[1600,448]{0,1:T(8,128)(2,1)} %copy.54), channel_id=1, source_target_pairs={{0,16},{8,24},{16,0},{24,8},{1,17},{9,25},{17,1},{25,9},{2,18},{10... | collective-permute-start | bytes 4300808 | tf_op jit(solution)/shard_map/ppermute | solution.py:62
  130.5 57.9 %collective-permute-start.27 = (bf16[200,1600]{1,0:T(8,128)(2,1)S(1)}, bf16[200,1600]{1,0:T(8,128)(2,1)S(1)}, u32[]{:S(2)}, u32[]{:S(2)}) collective-permute-start(bf16[200,1600]{1,0:T(8,128)(2,1)S(1)} %constant_dynamic-slice_fusion.15.refs_0_), channel_id=1, source_target_pairs={{0,2},{2,4},{4,6},{6,7},{7,5},{5,3},{3,1},{1,0},{8,10},{10,12},{12... | collective-permute-start | bytes 1920008 | tf_op jit(solution)/shard_map/ppermute | solution.py:103
  132.2 72.8 %collective-permute-start.28 = (bf16[200,1600]{1,0:T(8,128)(2,1)S(1)}, bf16[200,1600]{1,0:T(8,128)(2,1)}, u32[]{:S(2)}, u32[]{:S(2)}) collective-permute-start(bf16[200,1600]{1,0:T(8,128)(2,1)S(1)} %constant_dynamic-slice_fusion.15.refs_0_), channel_id=1, source_target_pairs={{0,1},{2,0},{4,2},{6,4},{7,6},{5,7},{3,5},{1,3},{8,9},{10,8},{12,1... | collective-permute-start | bytes 1920008 | tf_op jit(solution)/shard_map/ppermute | solution.py:103
  132.6 72.7 %collective-permute-start.19 = (bf16[200,1600]{1,0:T(8,128)(2,1)}, bf16[200,1600]{1,0:T(8,128)(2,1)}, u32[]{:S(2)}, u32[]{:S(2)}) collective-permute-start(bf16[200,1600]{1,0:T(8,128)(2,1)} %concatenate.118.refs_0_), channel_id=1, source_target_pairs={{0,2},{2,4},{4,6},{6,7},{7,5},{5,3},{3,1},{1,0},{8,10},{10,12},{12... | collective-permute-start | bytes 1920008 | tf_op jit(solution)/shard_map/ppermute | solution.py:103
  139.0 31.8 %collective-permute-start.12 = (bf16[512,448]{1,0:T(8,128)(2,1)S(1)}, bf16[512,448]{1,0:T(8,128)(2,1)S(1)}, u32[]{:S(2)}, u32[]{:S(2)}) collective-permute-start(bf16[512,448]{1,0:T(8,128)(2,1)S(1)} %pad_maximum_fusion.19), channel_id=1, source_target_pairs={{0,16},{8,24},{16,0},{24,8},{1,17},{9,25},{17,1},{25,9},{2,18},{10... | collective-permute-start | bytes 1376264 | tf_op jit(solution)/shard_map/ppermute | solution.py:62
  214.2 37.7 %collective-permute-start.16 = (bf16[256,1600]{0,1:T(8,128)(2,1)}, bf16[256,1600]{0,1:T(8,128)(2,1)}, u32[]{:S(2)}, u32[]{:S(2)}) collective-permute-start(bf16[256,1600]{0,1:T(8,128)(2,1)} %copy.61), channel_id=1, source_target_pairs={{0,16},{8,24},{16,0},{24,8},{1,17},{9,25},{17,1},{25,9},{2,18},{10... | collective-permute-start | bytes 2457608 | tf_op jit(solution)/shard_map/ppermute | solution.py:62
  237.7 44.5 %collective-permute-start.37 = (bf16[256,1600]{0,1:T(8,128)(2,1)}, bf16[256,1600]{0,1:T(8,128)(2,1)}, u32[]{:S(2)}, u32[]{:S(2)}) collective-permute-start(bf16[256,1600]{0,1:T(8,128)(2,1)} %collective-permute-done.35), channel_id=1, source_target_pairs={{0,8},{8,0},{16,24},{24,16},{1,9},{9,1},{17,25},{25,17},{2,10},{10... | collective-permute-start | bytes 2457608 | tf_op jit(solution)/shard_map/ppermute | solution.py:62
  239.1 41.9 %collective-permute-start.24 = (bf16[200,1600]{1,0:T(8,128)(2,1)}, bf16[200,1600]{1,0:T(8,128)(2,1)S(1)}, u32[]{:S(2)}, u32[]{:S(2)}) collective-permute-start(bf16[200,1600]{1,0:T(8,128)(2,1)} %collective-permute-done.22.refs_4_), channel_id=1, source_target_pairs={{0,1},{2,0},{4,2},{6,4},{7,6},{5,7},{3,5},{1,3},{8,9},{10,8},{12,1... | collective-permute-start | bytes 1920008 | tf_op jit(solution)/shard_map/ppermute | solution.py:103
  251.9 55.5 %collective-permute-start.17 = (bf16[256,1600]{0,1:T(8,128)(2,1)}, bf16[256,1600]{0,1:T(8,128)(2,1)}, u32[]{:S(2)}, u32[]{:S(2)}) collective-permute-start(bf16[256,1600]{0,1:T(8,128)(2,1)} %copy.61), channel_id=1, source_target_pairs={{0,8},{8,0},{16,24},{24,16},{1,9},{9,1},{17,25},{25,17},{2,10},{10... | collective-permute-start | bytes 2457608 | tf_op jit(solution)/shard_map/ppermute | solution.py:62
  251.9 57.6 %collective-permute-start.18 = (bf16[256,1600]{0,1:T(8,128)(2,1)}, bf16[256,1600]{0,1:T(8,128)(2,1)}, u32[]{:S(2)}, u32[]{:S(2)}) collective-permute-start(bf16[256,1600]{0,1:T(8,128)(2,1)} %collective-permute-done.16), channel_id=1, source_target_pairs={{0,8},{8,0},{16,24},{24,16},{1,9},{9,1},{17,25},{25,17},{2,10},{10... | collective-permute-start | bytes 2457608 | tf_op jit(solution)/shard_map/ppermute | solution.py:62
  254.0 32.0 %collective-permute-start.33 = (bf16[96,1600]{1,0:T(8,128)(2,1)S(1)}, bf16[96,1600]{1,0:T(8,128)(2,1)S(1)}, u32[]{:S(2)}, u32[]{:S(2)}) collective-permute-start(bf16[96,1600]{1,0:T(8,128)(2,1)S(1)} %slice.1102), channel_id=1, source_target_pairs={{0,2},{2,4},{4,6},{6,7},{7,5},{5,3},{3,1},{1,0},{8,10},{10,12},{12... | collective-permute-start | bytes 921608 | tf_op jit(solution)/shard_map/ppermute | solution.py:103
  433.5 107.2 %collective-permute-start.83 = (bf16[200,1600]{1,0:T(8,128)(2,1)}, bf16[200,1600]{1,0:T(8,128)(2,1)}, u32[]{:S(2)}, u32[]{:S(2)}) collective-permute-start(bf16[200,1600]{1,0:T(8,128)(2,1)} %get-tuple-element.131), channel_id=1, source_target_pairs={{0,2},{2,4},{4,6},{6,7},{7,5},{5,3},{3,1},{1,0},{8,10},{10,12},{12... | collective-permute-start | bytes 1920008 | tf_op jit(solution)/shard_map/ppermute | solution.py:103
  437.6 69.0 %collective-permute-start.74 = (bf16[200,1600]{1,0:T(8,128)(2,1)}, bf16[200,1600]{1,0:T(8,128)(2,1)}, u32[]{:S(2)}, u32[]{:S(2)}) collective-permute-start(bf16[200,1600]{1,0:T(8,128)(2,1)} %fusion.39), channel_id=1, source_target_pairs={{0,2},{2,4},{4,6},{6,7},{7,5},{5,3},{3,1},{1,0},{8,10},{10,12},{12... | collective-permute-start | bytes 1920008 | tf_op jit(solution)/shard_map/ppermute | solution.py:103
  452.5 89.7 %collective-permute-start.87 = (bf16[200,1600]{1,0:T(8,128)(2,1)}, bf16[200,1600]{1,0:T(8,128)(2,1)S(1)}, u32[]{:S(2)}, u32[]{:S(2)}) collective-permute-start(bf16[200,1600]{1,0:T(8,128)(2,1)} %fusion.32), channel_id=1, source_target_pairs={{0,1},{2,0},{4,2},{6,4},{7,6},{5,7},{3,5},{1,3},{8,9},{10,8},{12,1... | collective-permute-start | bytes 1920008 | tf_op jit(solution)/shard_map/ppermute | solution.py:103
  492.1 96.0 %collective-permute-start.42 = (bf16[512,1600]{0,1:T(8,128)(2,1)}, bf16[512,1600]{0,1:T(8,128)(2,1)}, u32[]{:S(2)}, u32[]{:S(2)}) collective-permute-start(bf16[512,1600]{0,1:T(8,128)(2,1)} %copy.79), channel_id=1, source_target_pairs={{0,8},{8,0},{16,24},{24,16},{1,9},{9,1},{17,25},{25,17},{2,10},{10... | collective-permute-start | bytes 4915208 | tf_op jit(solution)/shard_map/ppermute | solution.py:62
  505.0 76.9 %collective-permute-start.44 = (bf16[512,1600]{0,1:T(8,128)(2,1)}, bf16[512,1600]{0,1:T(8,128)(2,1)}, u32[]{:S(2)}, u32[]{:S(2)}) collective-permute-start(bf16[512,1600]{0,1:T(8,128)(2,1)} %copy.83), channel_id=1, source_target_pairs={{0,8},{8,0},{16,24},{24,16},{1,9},{9,1},{17,25},{25,17},{2,10},{10... | collective-permute-start | bytes 4915208 | tf_op jit(solution)/shard_map/ppermute | solution.py:62
  569.1 97.8 %collective-permute-start.88 = (bf16[2,200,1600]{2,1,0:T(8,128)(2,1)}, bf16[2,200,1600]{2,1,0:T(8,128)(2,1)}, u32[]{:S(2)}, u32[]{:S(2)}) collective-permute-start(bf16[2,200,1600]{2,1,0:T(8,128)(2,1)} %pad_maximum_fusion.5), channel_id=1, source_target_pairs={{0,16},{8,24},{16,0},{24,8},{1,17},{9,25},{17,1},{25,9},{2,18},{10... | collective-permute-start | bytes 3840008 | tf_op jit(solution)/shard_map/ppermute | solution.py:62
  579.9 34.3 %collective-permute-start.52 = (bf16[200,1408]{1,0:T(8,128)(2,1)}, bf16[200,1408]{1,0:T(8,128)(2,1)}, u32[]{:S(2)}, u32[]{:S(2)}) collective-permute-start(bf16[200,1408]{1,0:T(8,128)(2,1)} %get-tuple-element.140), channel_id=1, source_target_pairs={{0,1},{2,0},{4,2},{6,4},{7,6},{5,7},{3,5},{1,3},{8,9},{10,8},{12,1... | collective-permute-start | bytes 1689608 | tf_op jit(solution)/shard_map/ppermute | solution.py:103
  580.3 81.5 %collective-permute-start.49 = (bf16[200,1408]{1,0:T(8,128)(2,1)}, bf16[200,1408]{1,0:T(8,128)(2,1)}, u32[]{:S(2)}, u32[]{:S(2)}) collective-permute-start(bf16[200,1408]{1,0:T(8,128)(2,1)} %get-tuple-element.139), channel_id=1, source_target_pairs={{0,2},{2,4},{4,6},{6,7},{7,5},{5,3},{3,1},{1,0},{8,10},{10,12},{12... | collective-permute-start | bytes 1689608 | tf_op jit(solution)/shard_map/ppermute | solution.py:103
  592.8 59.8 %collective-permute-start.43 = (bf16[256,1600]{0,1:T(8,128)(2,1)}, bf16[256,1600]{0,1:T(8,128)(2,1)}, u32[]{:S(2)}, u32[]{:S(2)}) collective-permute-start(bf16[256,1600]{0,1:T(8,128)(2,1)} %copy.81), channel_id=1, source_target_pairs={{0,16},{8,24},{16,0},{24,8},{1,17},{9,25},{17,1},{25,9},{2,18},{10... | collective-permute-start | bytes 2457608 | tf_op jit(solution)/shard_map/ppermute | solution.py:62
  597.5 36.7 %collective-permute-start.45 = (bf16[256,1600]{0,1:T(8,128)(2,1)}, bf16[256,1600]{0,1:T(8,128)(2,1)}, u32[]{:S(2)}, u32[]{:S(2)}) collective-permute-start(bf16[256,1600]{0,1:T(8,128)(2,1)} %copy.85), channel_id=1, source_target_pairs={{0,16},{8,24},{16,0},{24,8},{1,17},{9,25},{17,1},{25,9},{2,18},{10... | collective-permute-start | bytes 2457608 | tf_op jit(solution)/shard_map/ppermute | solution.py:62
  614.2 52.8 %collective-permute-start.54 = (bf16[3200,448]{0,1:T(8,128)(2,1)}, bf16[3200,448]{0,1:T(8,128)(2,1)}, u32[]{:S(2)}, u32[]{:S(2)}) collective-permute-start(bf16[3200,448]{0,1:T(8,128)(2,1)} %copy.87), channel_id=1, source_target_pairs={{0,8},{8,0},{16,24},{24,16},{1,9},{9,1},{17,25},{25,17},{2,10},{10... | collective-permute-start | bytes 8601608 | tf_op jit(solution)/shard_map/ppermute | solution.py:62
  680.9 35.3 %collective-permute-start.55 = (bf16[1600,448]{0,1:T(8,128)(2,1)}, bf16[1600,448]{0,1:T(8,128)(2,1)}, u32[]{:S(2)}, u32[]{:S(2)}) collective-permute-start(bf16[1600,448]{0,1:T(8,128)(2,1)} %copy.89), channel_id=1, source_target_pairs={{0,16},{8,24},{16,0},{24,8},{1,17},{9,25},{17,1},{25,9},{2,18},{10... | collective-permute-start | bytes 4300808 | tf_op jit(solution)/shard_map/ppermute | solution.py:62
  (168 other events, 2391.7 us)

commit v3 on v2

--- a/solution.py
+++ b/solution.py
@@ -19,6 +19,8 @@
 SLOTS = H - (RANKS - 1) * BASE
 norm_eps = 1e-05
 masked_low = -1e30
+LIGHT = pl.CostEstimate(flops=1 << 20, transcendentals=0, bytes_accessed=1 << 16)
+VMEM_LIMIT = 56 << 20
 f32 = jnp.float32
 bf16 = jnp.bfloat16
 
@@ -57,9 +59,16 @@
 PEERS = (0, 2, 1, 3)
 
 
+def tiled(block):
+    if block.ndim != 2 or block.shape[0] % 8:
+        return block
+    return block.reshape(-1, 8, block.shape[1])
+
+
 def ctx_swap(block, bit):
     pairs = [(i, i ^ bit) for i in range(lax.axis_size("ctx"))]
-    return row_major(lax.ppermute(row_major(block), "ctx", pairs))
+    got = row_major(lax.ppermute(row_major(tiled(block)), "ctx", pairs))
+    return got.reshape(block.shape)
 
 
 def gather_ctx(block):
@@ -68,23 +77,36 @@
     return [block, far, near, ctx_swap(far, 1)]
 
 
-def scatter_near(matrix):
+def halves(matrix):
     half = matrix.shape[0] // 2
-    quarter = half // 2
-    got = ctx_swap(matrix[half:], 1)
-    onward = added(matrix[quarter:half], got[quarter:]).astype(bf16)
-    return added(matrix[:quarter], got[:quarter]), onward
-
-
-def scatter_far(kept, onward):
-    return added(kept, ctx_swap(onward, 2))
-
-
-def exchange_near(matrix):
-    half = matrix.shape[0] // 2
-    quarter = half // 2
-    got = ctx_swap(matrix[half:], 1)
-    return matrix[:quarter], got[:quarter], jnp.concatenate([matrix[quarter:half], got[quarter:]])
+    return matrix[:half], matrix[half:]
+
+
+def pair_add_kernel(keep, got, kept, onward):
+    rows = kept.shape[0]
+    kept[...] = added(keep[:rows], got[:rows])
+    onward[...] = added(keep[rows:], got[rows:]).astype(bf16)
+
+
+def scatter_near(keep, give, *gates):
+    rows, columns = keep.shape
+    half = (rows // 2, columns)
+    return call(
+        pair_add_kernel,
+        "pair_add",
+        1,
+        (keep, ctx_swap(give, 1)),
+        [whole(keep.shape)] * 2,
+        [(half, f32), (half, bf16)],
+        [whole(half)] * 2,
+        gates=gates,
+    )
+
+
+def exchange_near(keep, give):
+    quarter = keep.shape[0] // 2
+    got = ctx_swap(give, 1)
+    return keep[:quarter], got[:quarter], jnp.concatenate([keep[quarter:], got[quarter:]])
 
 
 def exchange_far(mine, near, onward):
@@ -140,11 +162,11 @@
     def arrived(self):
         return (self.forth, self.back) if on_ring() else ()
 
-    def result(self, owners, columns, rows):
+    def result(self, owners, columns, gates=()):
         if not on_ring():
             whole = lax.all_gather(self.block, "fsdp", axis=0, tiled=False)
             return [whole[:, top : top + n, c : c + w] for c, w, top, n in columns]
-        return collect(self.pieces, owners, self.cut, columns)
+        return collect(self.pieces, owners, self.cut, columns, gates)
 
 
 def collect_kernel(cut, columns, owners, *refs):
@@ -171,22 +193,67 @@
         copy.wait()
 
 
-def collect(pieces, owners, cut, columns):
+def collect(pieces, owners, cut, columns, gates):
     shapes = [(len(RING), rows, width) for _, width, _, rows in columns]
-    return pl.pallas_call(
+    return call(
         functools.partial(collect_kernel, cut, columns),
-        grid_spec=pltpu.PrefetchScalarGridSpec(
-            num_scalar_prefetch=1,
-            grid=(1,),
-            in_specs=[pl.BlockSpec(memory_space=pl.ANY)] * len(pieces),
-            out_specs=[pl.BlockSpec(shape, lambda i, t: (0, 0, 0)) for shape in shapes],
-            scratch_shapes=[pltpu.SemaphoreType.DMA((len(pieces) * len(columns),))],
-        ),
-        out_shape=[jax.ShapeDtypeStruct(shape, pieces[0].dtype) for shape in shapes],
-        compiler_params=pltpu.CompilerParams(vmem_limit_bytes=40 << 20),
-        cost_estimate=pl.CostEstimate(flops=0, transcendentals=0, bytes_accessed=12 << 20),
-        name="collect",
-    )(owners, *pieces)
+        "collect",
+        1,
+        pieces,
+        [pl.BlockSpec(memory_space=pl.ANY)] * len(pieces),
+        [(shape, pieces[0].dtype) for shape in shapes],
+        [whole(shape) for shape in shapes],
+        [pltpu.SemaphoreType.DMA((len(pieces) * len(columns),))],
+        owners,
+        gates,
+    )
+
+
+PLACE = {0: 0, -1: 1, 1: 2, -2: 3, 2: 4, -3: 5, 3: 6, 4: 7}
+
+
+def ring_part_kernel(distance, cut, owners, *refs):
+    if distance == HALF:
+        far, ahead, behind = refs
+        ahead[...] = far[:cut]
+        behind[...] = far[cut:]
+    elif distance == 0:
+        own, forth, back, out = refs
+        out[...] = added(own[...], forth[...], back[...]).astype(bf16)
+    else:
+        mine_ahead, mine_behind, forth, back, ahead, behind = refs
+        if distance == HALF - 1:
+            ahead[:cut] = added(mine_ahead[:cut], forth[...]).astype(bf16)
+            ahead[cut:] = mine_ahead[cut:]
+            behind[:cut] = mine_behind[:cut]
+            behind[cut:] = added(mine_behind[cut:], back[...]).astype(bf16)
+        else:
+            ahead[...] = added(mine_ahead[...], forth[...]).astype(bf16)
+            behind[...] = added(mine_behind[...], back[...]).astype(bf16)
+
+
+def ring_part(blocks, owners, distance, cut, moved, gates=()):
+    rows, columns = blocks.shape[1:]
+    distances = (distance,) if distance in (0, HALF) else (distance, -distance)
+    if distance == HALF:
+        shapes = [(cut, columns), (rows - cut, columns)]
+    else:
+        shapes = [(rows, columns)] * len(distances)
+    places = [PLACE[d] for d in distances]
+    return call(
+        functools.partial(ring_part_kernel, distance, cut),
+        "ring_part",
+        1,
+        (*[blocks] * len(places), *moved),
+        [
+            pl.BlockSpec((None, rows, columns), lambda i, t, p=p: (t[p], 0, 0)) for p in places
+        ]
+        + [whole(value.shape) for value in moved],
+        [(shape, bf16) for shape in shapes],
+        [whole(shape) for shape in shapes],
+        table=owners,
+        gates=gates,
+    )
 
 
 class Scatter:
@@ -194,39 +261,21 @@
         self.blocks, self.owners = blocks, owners
         self.cut = upper_part(blocks.shape[1])
         self.next = HALF
-        self.forth = self.back = None
-
-    def part(self, offset):
-        where = {0: 0, 4: 7}.get(offset, 2 * abs(offset) - (offset < 0))
-        return lax.dynamic_index_in_dim(self.blocks, self.owners[where], 0, False)
+        self.moved = self.given = ()
 
     def hop(self, *gate):
         if not on_ring():
             return
-        k, cut = self.next, self.cut
-        if k == HALF:
-            far = self.part(HALF)
-            ahead, behind = far[:cut], far[cut:]
-        else:
-            ahead, behind = self.part(k), self.part(-k)
-            forth, back = self.forth, self.back
-            if gate:
-                forth, back = after(forth, *gate), after(back, *gate)
-            if k == HALF - 1:
-                ahead = jnp.concatenate([added(ahead[:cut], forth).astype(bf16), ahead[cut:]])
-                behind = jnp.concatenate([behind[:cut], added(behind[cut:], back).astype(bf16)])
-            else:
-                ahead = added(ahead, forth).astype(bf16)
-                behind = added(behind, back).astype(bf16)
+        self.given = ring_part(
+            self.blocks, self.owners, self.next, self.cut, self.moved, gate
+        )
+        self.moved = [ring_hop(self.given[0], 1), ring_hop(self.given[1], -1)]
         self.next -= 1
-        self.forth, self.back = ring_hop(ahead, 1), ring_hop(behind, -1)
-
-    def result(self):
+
+    def result(self, *gate):
         if not on_ring():
-            return lax.psum_scatter(
-                self.blocks, "fsdp", scatter_dimension=0, tiled=False
-            ).astype(f32)
-        return added(self.part(0), self.forth, self.back)
+            return lax.psum_scatter(self.blocks, "fsdp", scatter_dimension=0, tiled=False)
+        return ring_part(self.blocks, self.owners, 0, self.cut, self.moved, gate)[0]
 
 
 def reduce_small(table):
@@ -434,67 +483,524 @@
             attend_back_pair(pair, True, *refs)
 
 
-def attend(table, qkv):
+def attend(table, qkv, gates):
     length, columns = qkv.shape
     pairs = (SLOTS + 1) // 2
-    area = SLOTS * length * (length + QB) // 2
-    return pl.pallas_call(
+    return call(
         attend_kernel,
-        grid_spec=pltpu.PrefetchScalarGridSpec(
-            num_scalar_prefetch=1,
-            grid=(pairs,),
-            in_specs=[pl.BlockSpec((length, columns), lambda p, t: (0, 0))],
-            out_specs=[
-                pl.BlockSpec((length, PAIR), lambda p, t: (0, p)),
-                pl.BlockSpec((1, 8, length), lambda p, t: (p, 0, 0)),
-            ],
-        ),
-        out_shape=[
-            jax.ShapeDtypeStruct((length, pairs * PAIR), bf16),
-            jax.ShapeDtypeStruct((pairs, 8, length), f32),
+        "attend",
+        pairs,
+        (qkv,),
+        [whole((length, columns))],
+        [((length, pairs * PAIR), bf16), ((pairs, 8, length), f32)],
+        [
+            pl.BlockSpec((length, PAIR), lambda p, t: (0, p)),
+            pl.BlockSpec((1, 8, length), lambda p, t: (p, 0, 0)),
         ],
-        compiler_params=pltpu.CompilerParams(vmem_limit_bytes=40 << 20),
-        cost_estimate=pl.CostEstimate(
-            flops=4 * area * HD * 4, transcendentals=area, bytes_accessed=8 << 20
-        ),
-        name="attend",
-    )(table, qkv)
-
-
-def attend_back(table, qkv, grad, mass):
+        table=table,
+        gates=gates,
+    )
+
+
+def attend_back(table, qkv, grad, mass, gates):
     length, columns = qkv.shape
     pairs = (SLOTS + 1) // 2
-    area = SLOTS * length * (length + QB) // 2
+    return call(
+        attend_back_kernel,
+        "attend_back",
+        pairs,
+        (qkv, grad, mass),
+        [
+            whole((length, columns)),
+            pl.BlockSpec((length, PAIR), lambda p, t: (0, p)),
+            pl.BlockSpec((1, 8, length), lambda p, t: (p, 0, 0)),
+        ],
+        [((length, columns), bf16)],
+        [whole((length, columns))],
+        [pltpu.VMEM((4, length, HD), f32)],
+        table,
+        gates,
+    )[0]
+
+
+def whole(shape):
+    return pl.BlockSpec(shape, lambda *_: (0,) * len(shape))
+
+
+def rows_spec(rows, columns):
+    return pl.BlockSpec((rows, columns), lambda i, *_: (i, 0))
+
+
+def call(kernel, name, grid, operands, specs, outs, out_specs, scratch=(), table=None, gates=()):
+    tables = () if table is None else (table,)
+    first = len(tables) + len(operands)
+    count = len(gates)
+
+    def body(*refs):
+        kernel(*refs[:first], *refs[first + count :])
+
     return pl.pallas_call(
-        attend_back_kernel,
+        body,
         grid_spec=pltpu.PrefetchScalarGridSpec(
-            num_scalar_prefetch=1,
-            grid=(pairs,),
-            in_specs=[
-                pl.BlockSpec((length, columns), lambda p, t: (0, 0)),
-                pl.BlockSpec((length, PAIR), lambda p, t: (0, p)),
-                pl.BlockSpec((1, 8, length), lambda p, t: (p, 0, 0)),
-            ],
-            out_specs=pl.BlockSpec((length, columns), lambda p, t: (0, 0)),
-            scratch_shapes=[pltpu.VMEM((4, length, HD), f32)],
+            num_scalar_prefetch=len(tables),
+            grid=(grid,),
+            in_specs=list(specs) + [pl.BlockSpec(memory_space=pl.ANY)] * count,
+            out_specs=out_specs,
+            scratch_shapes=list(scratch),
         ),
-        out_shape=jax.ShapeDtypeStruct((length, columns), bf16),
-        compiler_params=pltpu.CompilerParams(vmem_limit_bytes=40 << 20),
-        cost_estimate=pl.CostEstimate(
-            flops=10 * area * HD * 4, transcendentals=area, bytes_accessed=12 << 20
-        ),
-        name="attend_back",
-    )(table, qkv, grad, mass)
-
-
-def head_slice(matrix, rank, part_count):
-    width = matrix.shape[1] // part_count
-    return [
-        lax.dynamic_slice(
-            matrix, (0, t * width + rank * BASE * HD), (matrix.shape[0], SLOTS * HD)
+        out_shape=[jax.ShapeDtypeStruct(shape, kind) for shape, kind in outs],
+        compiler_params=pltpu.CompilerParams(vmem_limit_bytes=VMEM_LIMIT),
+        cost_estimate=LIGHT,
+        name=name,
+    )(*tables, *operands, *gates)
+
+
+def pick_block(refs, held):
+    for j, ref in enumerate(refs):
+
+        @pl.when(pl.program_id(0) == j)
+        def _(ref=ref):
+            held[...] = ref[...]
+
+
+def norm_mixed_kernel(*refs):
+    blocks, (gain, shift, weights, bias, normed, mixed, held) = refs[:4], refs[4:]
+    pick_block(blocks, held)
+    unit, _ = norm_stats(held[...].astype(f32))
+    low = (unit * gain[...] + shift[...]).astype(bf16)
+    normed[...] = low
+    mixed[...] = (product(low, weights[...]) + bias[...]).astype(bf16)
+
+
+def norm_mixed(blocks, gain, shift, weights, bias):
+    count, width = blocks[0].shape
+    mixed_width = weights.shape[1]
+    length = count * len(blocks)
+    return call(
+        norm_mixed_kernel,
+        "norm_mixed",
+        len(blocks),
+        (*blocks, gain[None], shift[None], weights, bias),
+        [whole((count, width))] * len(blocks)
+        + [whole((1, width))] * 2
+        + [whole(weights.shape), whole((1, mixed_width))],
+        [((length, width), bf16), ((length, mixed_width), bf16)],
+        [rows_spec(count, width), rows_spec(count, mixed_width)],
+        [pltpu.VMEM((count, width), bf16)],
+    )
+
+
+def join_kernel(table, *refs):
+    pieces, out, sems, last_sem = refs[:4], refs[4], refs[5], refs[6]
+    step, span = BASE * HD, SLOTS * HD
+    width = out.shape[1]
+    rest = span - step
+    last = len(pieces) - 1
+
+    def copies(j):
+        start = pl.multiple_of(table[j] * step, PAIR)
+        main = pltpu.make_async_copy(
+            pieces[j].at[:, pl.ds(0, step)], out.at[:, pl.ds(start, step)], sems.at[j]
         )
-        for t in range(part_count)
+        tail = pltpu.make_async_copy(
+            pieces[j].at[:, pl.ds(step, rest)], out.at[:, pl.ds(width - rest, rest)], last_sem.at[0]
+        )
+        return main, tail
+
+    for j in range(len(pieces)):
+        main, tail = copies(j)
+        main.start()
+
+        @pl.when(table[j] == last)
+        def _(tail=tail):
+            tail.start()
+
+    for j in range(len(pieces)):
+        main, tail = copies(j)
+        main.wait()
+
+        @pl.when(table[j] == last)
+        def _(tail=tail):
+            tail.wait()
+
+
+def join_windows(table, pieces, width):
+    rows = pieces[0].shape[0]
+    return call(
+        join_kernel,
+        "join_windows",
+        1,
+        pieces,
+        [pl.BlockSpec(memory_space=pl.ANY)] * len(pieces),
+        [((rows, width), pieces[0].dtype)],
+        [whole((rows, width))],
+        [pltpu.SemaphoreType.DMA((len(pieces),)), pltpu.SemaphoreType.DMA((1,))],
+        table,
+    )[0]
+
+
+def attn_out_kernel(table, *refs):
+    pieces, rest = refs[:4], refs[4:]
+    weights, tokens, bias, gain, shift, middle, normed, attended = rest
+    step, span = BASE * HD, SLOTS * HD
+    width = attended.shape[1]
+    for j, piece in enumerate(pieces):
+        start = pl.multiple_of(table[j] * step, PAIR)
+        attended[:, pl.ds(start, step)] = piece[:, :step]
+
+        @pl.when(table[j] == len(pieces) - 1)
+        def _(piece=piece):
+            attended[:, width - (span - step) :] = piece[:, step:]
+
+    value = tokens[...].astype(f32) + product(attended[...], weights[...]) + bias[...]
+    middle[...] = value
+    unit, _ = norm_stats(value)
+    normed[...] = (unit * gain[...] + shift[...]).astype(bf16)
+
+
+def attn_out(table, pieces, weights, tokens, bias, gain, shift):
+    count, width = tokens.shape
+    return call(
+        attn_out_kernel,
+        "attn_out",
+        1,
+        (*pieces, weights, tokens, bias[None], gain[None], shift[None]),
+        [whole(piece.shape) for piece in pieces]
+        + [whole(weights.shape), whole((count, width))]
+        + [whole((1, width))] * 3,
+        [((count, width), f32), ((count, width), bf16), ((count, width), bf16)],
+        [whole((count, width))] * 3,
+        table=table,
+    )
+
+
+def up_kernel(*refs):
+    blocks, (weights, bias, activated, slope, normed, held) = refs[:4], refs[4:]
+    pick_block(blocks, held)
+    normed[...] = held[...]
+    before = product(held[...], weights[...]) + bias[...]
+    square = before * before
+    inner = jnp.tanh(before * (0.7978845608028654 + 0.7978845608028654 * 0.044715 * square))
+    half = 0.5 * (1.0 + inner)
+    activated[...] = (before * half).astype(bf16)
+    slope[...] = (
+        half
+        + 0.5
+        * before
+        * (1.0 - inner * inner)
+        * (0.7978845608028654 + 3 * 0.7978845608028654 * 0.044715 * square)
+    ).astype(bf16)
+
+
+def feed_up(blocks, weights, bias):
+    count, width = blocks[0].shape
+    units = weights.shape[1]
+    length = count * len(blocks)
+    return call(
+        up_kernel,
+        "feed_up",
+        len(blocks),
+        (*blocks, weights, bias[None]),
+        [whole((count, width))] * len(blocks) + [whole(weights.shape), whole((1, units))],
+        [((length, units), bf16), ((length, units), bf16), ((length, width), bf16)],
+        [rows_spec(count, units), rows_spec(count, units), rows_spec(count, width)],
+        [pltpu.VMEM((count, width), bf16)],
+    )
+
+
+def back_kernel(*refs):
+    blocks, (down, slope, low, sums, held) = refs[:4], refs[4:]
+    pick_block(blocks, held)
+    value = (back_product(held[...], down[...]) * slope[...].astype(f32)).astype(bf16)
+    low[...] = value
+
+    @pl.when(pl.program_id(0) == 0)
+    def _():
+        sums[...] = jnp.zeros_like(sums)
+
+    sums[...] += jnp.sum(value.astype(f32), axis=0, keepdims=True)
+
+
+def feed_back(blocks, down, slope, gates):
+    count, width = blocks[0].shape
+    units = slope.shape[1]
+    length = count * len(blocks)
+    return call(
+        back_kernel,
+        "feed_back",
+        len(blocks),
+        (*blocks, down, slope),
+        [whole((count, width))] * len(blocks) + [whole(down.shape), rows_spec(count, units)],
+        [((length, units), bf16), ((1, units), f32)],
+        [rows_spec(count, units), whole((1, units))],
+        [pltpu.VMEM((count, width), bf16)],
+        gates=gates,
+    )
+
+
+def plain_back_kernel(left, right, out):
+    out[...] = back_product(left[...], right[...]).astype(bf16)
+
+
+def plain_back(left, right, name, gates):
+    length, inner = left.shape
+    width = right.shape[0]
+    return call(
+        plain_back_kernel,
+        name,
+        length // QB,
+        (left, right),
+        [rows_spec(QB, inner), whole(right.shape)],
+        [((length, width), bf16)],
+        [rows_spec(QB, width)],
+        gates=gates,
+    )[0]
+
+
+VECTOR_ROWS = 8
+FC_START = 2 * PAIR
+
+
+def attn_block_kernel(place, qkv, out_weights, *refs):
+    vectors, bias_fc, block = refs[:VECTOR_ROWS], refs[VECTOR_ROWS], refs[VECTOR_ROWS + 1]
+    step, span = BASE * HD, SLOTS * HD
+    width = out_weights.shape[1]
+    rows = qkv.shape[0]
+    parts = []
+    for t in range(3):
+        skip = t * width % PAIR
+        start = pl.multiple_of(place[0] * step + (t * width - skip), PAIR)
+        parts.append(qkv[:, pl.ds(start, span + skip)][:, skip:])
+    for p in range(SLOTS // 2):
+        for t in range(3):
+            first = (3 * p + t) * PAIR
+            block[:rows, first : first + PAIR] = parts[t][:, p * PAIR : (p + 1) * PAIR]
+    rest = [part[:, (SLOTS - 1) * HD :] for part in parts] + [jnp.zeros((rows, HD), bf16)]
+    first = 3 * (SLOTS // 2) * PAIR
+    for p in range(2):
+        block[:rows, first + p * PAIR : first + (p + 1) * PAIR] = jnp.concatenate(
+            rest[2 * p : 2 * p + 2], axis=1
+        )
+    start = pl.multiple_of(place[0] * step, PAIR)
+    block[:rows, first + 2 * PAIR :] = out_weights[:, pl.ds(start, span)]
+    block[rows:, :] = jnp.zeros((VECTOR_ROWS, block.shape[1]), bf16)
+    lines = jnp.stack([vector[...].astype(f32) for vector in vectors])
+    block[rows:, : lines.shape[1]] = lines.astype(bf16)
+    units = bias_fc.shape[0]
+    line = jnp.broadcast_to(bias_fc[...].astype(f32)[None], (VECTOR_ROWS, units))
+    block[rows:, FC_START : FC_START + units] = line.astype(bf16)
+
+
+def form_attn_block(place, qkv, out_weights, vectors, bias_fc):
+    rows = qkv.shape[0]
+    columns = 3 * (SLOTS // 2) * PAIR + 2 * PAIR + SLOTS * HD
+    vectors = [*vectors, bias_fc]
+    return call(
+        attn_block_kernel,
+        "form_attn_block",
+        1,
+        (qkv, out_weights, *vectors),
+        [whole(value.shape) for value in (qkv, out_weights, *vectors)],
+        [((rows + VECTOR_ROWS, columns), bf16)],
+        [whole((rows + VECTOR_ROWS, columns))],
+        table=place,
+    )[0]
+
+
+def whole_rows_kernel(table, *refs):
+    pieces, out, held = refs[:4], refs[4], refs[5]
+    pick_block(pieces, held)
+    out[...] = held[...].astype(f32)
+
+
+def whole_rows(table, pieces, gates):
+    rows, width = pieces[0].shape
+    return call(
+        whole_rows_kernel,
+        "whole_rows",
+        len(pieces),
+        pieces,
+        [whole((rows, width))] * len(pieces),
+        [((len(pieces), rows, width), f32)],
+        [pl.BlockSpec((None, rows, width), lambda i, t: (t[i], 0, 0))],
+        [pltpu.VMEM((rows, width), bf16)],
+        table,
+        gates,
+    )[0].reshape(-1, width)
+
+
+def put_windows(table, held, outs):
+    for j in range(2 * len(outs)):
+        start = pl.multiple_of(table[j] * BASE * HD, PAIR)
+        outs[j // 2][j % 2] = held[:, pl.ds(start, SLOTS * HD)]
+
+
+def norm_two_kernel(table, *refs):
+    kept, far, middle, grad_out, gain, weights, grad_middle, low, keep, give, sums, held = refs
+    grad = kept[...] + far[...].astype(f32)
+    unit, scale = norm_stats(middle[...])
+    back, grad_gain, grad_shift = norm_back(grad, unit, scale, gain[...])
+    out = grad_out[...].astype(f32)
+    value = out + back
+    grad_middle[...] = value
+    value_low = value.astype(bf16)
+    low[...] = value_low
+    held[...] = back_product(value_low, weights[...]).astype(bf16)
+    put_windows(table, held, (keep, give))
+    sums[0:1, :] = grad_gain[None]
+    sums[1:2, :] = grad_shift[None]
+    sums[2:3, :] = jnp.sum(value_low.astype(f32), axis=0, keepdims=True)
+    sums[3:4, :] = jnp.sum(out, axis=0, keepdims=True)
+
+
+def norm_two_back(table, kept, far, middle, grad_out, gain, weights, gates):
+    count, width = middle.shape
+    half = (2, count, SLOTS * HD)
+    return call(
+        norm_two_kernel,
+        "norm_two_back",
+        1,
+        (kept, far, middle, grad_out, gain[None], weights),
+        [whole((count, width))] * 4 + [whole((1, width)), whole(weights.shape)],
+        [
+            ((count, width), f32),
+            ((count, width), bf16),
+            (half, bf16),
+            (half, bf16),
+            ((4, width), f32),
+        ],
+        [
+            whole((count, width)),
+            whole((count, width)),
+            whole(half),
+            whole(half),
+            whole((4, width)),
+        ],
+        [pltpu.VMEM((count, width), bf16)],
+        table,
+        gates=gates,
+    )
+
+
+def norm_one_kernel(kept, far, tokens, grad_middle, gain, grad_tokens, sums):
+    grad = kept[...] + far[...].astype(f32)
+    unit, scale = norm_stats(tokens[...].astype(f32))
+    back, grad_gain, grad_shift = norm_back(grad, unit, scale, gain[...])
+    grad_tokens[...] = grad_middle[...] + back
+    sums[0:1, :] = grad_gain[None]
+    sums[1:2, :] = grad_shift[None]
+
+
+def norm_one_back(kept, far, tokens, grad_middle, gain, gates):
+    shape = kept.shape
+    return call(
+        norm_one_kernel,
+        "norm_one_back",
+        1,
+        (kept, far, tokens, grad_middle, gain[None]),
+        [whole(shape)] * 4 + [whole((1, shape[1]))],
+        [(shape, f32), ((2, shape[1]), f32)],
+        [whole(shape), whole((2, shape[1]))],
+        gates=gates,
+    )
+
+
+def out_grad_kernel(table, attended, low, keep, give, held):
+    held[...] = outer_sum(attended[...], low[...]).astype(bf16)
+    put_windows(table, held, (keep, give))
+
+
+def out_weight_grad(table, attended, low, gates):
+    count, width = attended.shape
+    half = (2, width, SLOTS * HD)
+    return call(
+        out_grad_kernel,
+        "out_weight_grad",
+        1,
+        (attended, low),
+        [whole((count, width))] * 2,
+        [(half, bf16)] * 2,
+        [whole(half)] * 2,
+        [pltpu.VMEM((width, width), bf16)],
+        table,
+        gates=gates,
+    )
+
+
+def whole_fc_kernel(table, *refs):
+    pieces, out, held, sems = refs[:4], refs[4], refs[5], refs[6]
+    copies = [
+        pltpu.make_async_copy(piece, held.at[table[j]], sems.at[j])
+        for j, piece in enumerate(pieces)
     ]
+    for copy in copies:
+        copy.start()
+    for copy in copies:
+        copy.wait()
+    ranks = len(pieces)
+    units = pieces[0].shape[0]
+    for r in range(ranks):
+        for i in range(pieces[0].shape[1] // units):
+            first = (i * ranks + r) * units
+            out[:, first : first + units] = held[r, :, i * units : (i + 1) * units].astype(f32)
+
+
+def whole_fc(table, pieces, gates):
+    rows, width = pieces[0].shape
+    ranks = len(pieces)
+    return call(
+        whole_fc_kernel,
+        "whole_fc",
+        1,
+        pieces,
+        [pl.BlockSpec(memory_space=pl.ANY)] * ranks,
+        [((rows, ranks * width), f32)],
+        [whole((rows, ranks * width))],
+        [pltpu.VMEM((ranks, rows, width), bf16), pltpu.SemaphoreType.DMA((ranks,))],
+        table,
+        gates,
+    )[0]
+
+
+def whole_qkv_kernel(table, *refs):
+    pieces, out, held, sems = refs[:4], refs[4], refs[5], refs[6]
+    copies = [
+        pltpu.make_async_copy(piece, held.at[table[j]], sems.at[j])
+        for j, piece in enumerate(pieces)
+    ]
+    for copy in copies:
+        copy.start()
+    for copy in copies:
+        copy.wait()
+    width = out.shape[1] // 3
+    for rank in range(len(pieces)):
+        for part in range(3):
+            start = part * width + rank * BASE * HD
+            for p in range(SLOTS // 2):
+                tile = held[rank, :, (3 * p + part) * PAIR : (3 * p + part + 1) * PAIR]
+                out[:, start + p * PAIR : start + (p + 1) * PAIR] = tile.astype(f32)
+            if rank == len(pieces) - 1:
+                first = 3 * (SLOTS // 2) * PAIR + part * HD
+                tile = held[rank, :, first : first + HD]
+                out[:, start + BASE * HD : start + SLOTS * HD] = tile.astype(f32)
+
+
+def whole_qkv(table, pieces, width):
+    rows = pieces[0].shape[0]
+    return call(
+        whole_qkv_kernel,
+        "whole_qkv",
+        1,
+        pieces,
+        [pl.BlockSpec(memory_space=pl.ANY)] * len(pieces),
+        [((rows, 3 * width), f32)],
+        [whole((rows, 3 * width))],
+        [
+            pltpu.VMEM((len(pieces),) + pieces[0].shape, bf16),
+            pltpu.SemaphoreType.DMA((len(pieces),)),
+        ],
+        table,
+    )[0]
 
 
 def to_pairs(parts):
@@ -548,43 +1054,25 @@
     peers = [rank ^ bit for bit in PEERS]
     owners = ring_owners() if on_ring() else None
 
-    def by_rank(blocks):
-        whole = jnp.zeros((ctx,) + blocks[0].shape, blocks[0].dtype)
-        for peer, block in zip(peers, blocks):
-            whole = lax.dynamic_update_slice(whole, block[None], (peer,) + (0,) * block.ndim)
-        return row_major(whole)
-
-    def columns_of(blocks):
-        return jnp.concatenate(
-            [blocks[r][:, :step] for r in range(ctx - 1)] + [blocks[ctx - 1]], axis=1
-        )
-
-    def windows(matrix):
-        return jnp.concatenate(
-            [
-                row_major(lax.dynamic_slice(matrix, (0, peer * step), (matrix.shape[0], span)))
-                for peer in peers
-            ]
-        )
+    peer_table = jnp.stack(peers).astype(jnp.int32)
 
     slots = jnp.argsort(group_order).astype(jnp.int32)
     place = jnp.take(jnp.asarray(np.argsort(np.array(PEERS)).astype(np.int32)), (slots // 2) ^ rank)
     slot_rows = (place * 2 + slots % 2) * GROUP
     table = jnp.concatenate([slot_rows, (rank == ctx - 1).astype(jnp.int32)[None]])
 
-    vectors = jnp.concatenate(
-        [b_query, b_value, b_attn_out, b_proj, ln1_gain, ln1_bias, ln2_gain, ln2_bias, b_fc]
-    )
-    vector_rows = (vectors.shape[0] + attn_width * 8 - 1) // (attn_width * 8) * 8
-    vector_block = jnp.pad(vectors, (0, vector_rows * attn_width - vectors.shape[0]))
-    attn_block = jnp.concatenate(
-        [
-            to_pairs(head_slice(w_qkv, rank, 3)),
-            lax.dynamic_slice(w_attn_out, (0, rank * step), (shard_rows, span)),
-        ],
-        axis=1,
-    )
-    attn_block = jnp.concatenate([attn_block, vector_block.reshape(vector_rows, attn_width)])
+    attn_block = form_attn_block(
+        rank[None].astype(jnp.int32),
+        w_qkv,
+        w_attn_out,
+        (b_query, b_value, b_attn_out, b_proj, ln1_gain, ln1_bias, ln2_gain, ln2_bias),
+        b_fc,
+    )
+    own_tokens = tokens_in[0]
+    own_grad = out_grad[0]
+    attn_gather = Gather(attn_block)
+    attn_gather.hop()
+    w_fc = after(w_fc, attn_block)
     fc_block = jnp.concatenate(
         [
             lax.dynamic_slice(
@@ -595,130 +1083,162 @@
         axis=1,
     )
     proj_block = lax.dynamic_slice(w_proj, (rank * unit_rows, 0), (unit_rows, width))
-    attn_gather = Gather(attn_block)
+    feed_block = jnp.concatenate([fc_block, proj_block])
+    token_blocks = gather_ctx(own_tokens)
+    grad_blocks = gather_ctx(after(own_grad, token_blocks[1]))
     attn_gather.hop()
-    tokens_all = row_major(jnp.concatenate(gather_ctx(tokens_in[0])))
+    attn_gather.hop(feed_block)
+    feed_gather = Gather(after(feed_block, *attn_gather.arrived()))
+    feed_gather.hop()
     attn_gather.hop()
-    attn_gather.hop()
-    fc_gather = Gather(after(fc_block, *attn_gather.arrived()))
-    proj_gather = Gather(after(proj_block, *attn_gather.arrived()))
-    attn_gather.hop()
-    grad_all = row_major(
-        jnp.concatenate(gather_ctx(after(out_grad[0], *attn_gather.arrived())))
-    )
-    for _ in range(HALF):
-        fc_gather.hop()
-        proj_gather.hop()
 
     qkv_weights, out_columns, small = attn_gather.result(
         owners,
         (
             (0, mixed_width, 0, shard_rows),
             (mixed_width, span, 0, shard_rows),
-            (0, attn_width, shard_rows, vector_rows),
+            (0, attn_width, shard_rows, VECTOR_ROWS),
         ),
-        None,
+        feed_gather.arrived(),
     )
     qkv_weights = qkv_weights.reshape(width, mixed_width)
-    small = small.reshape(shards, -1).astype(f32)
+    small = small.astype(f32)
     bias_q, bias_v, bias_o, bias_p, gain_one, shift_one, gain_two, shift_two = [
-        small[:, t * shard_rows : (t + 1) * shard_rows].reshape(-1) for t in range(8)
+        small[:, t, :shard_rows].reshape(-1) for t in range(VECTOR_ROWS)
     ]
-    units = ctx * unit_rows
     bias_fc = lax.dynamic_index_in_dim(
-        small[:, 8 * shard_rows : 8 * shard_rows + units].reshape(shards, ctx, unit_rows),
+        small[:, 0, FC_START : FC_START + ctx * unit_rows].reshape(shards, ctx, unit_rows),
         rank,
         1,
         False,
     ).reshape(-1)
 
-    normed_all = row_major(
-        (norm_stats(tokens_all.astype(f32))[0] * gain_one + shift_one).astype(bf16)
-    )
-
     def my_bias(vector):
         return lax.dynamic_slice(vector, (rank * step,), (span,))[None]
 
     bias_mixed = to_pairs([my_bias(bias_q), jnp.zeros((1, span), f32), my_bias(bias_v)])
-    mixed = row_major((product(normed_all, qkv_weights) + bias_mixed).astype(bf16))
-    attended_mine, mass = attend(table, mixed)
-    out_windows = by_rank(gather_ctx(out_columns.reshape(width, span)))
-    out_weights = row_major(columns_of(out_windows))
-    attended = exchange_far(*exchange_near(row_major(attended_mine[:, :span])))
-    attended = row_major(columns_of(by_rank(attended)))
-    middle = tokens + product(attended, out_weights) + bias_o
-
-    unit_two, scale_two = norm_stats(middle)
-    normed_two = row_major((unit_two * gain_two + shift_two).astype(bf16))
-    normed_two_all = row_major(jnp.concatenate(gather_ctx(normed_two)))
-    (fc_weights,) = fc_gather.result(owners, ((0, shards * unit_rows, 0, shard_rows),), None)
-    (proj_weights,) = proj_gather.result(owners, ((0, width, 0, unit_rows),), None)
+    normed_all, mixed = norm_mixed(
+        [after(token_blocks[0], grad_blocks[3])] + token_blocks[1:],
+        gain_one,
+        shift_one,
+        qkv_weights,
+        bias_mixed,
+    )
+    attended_mine, mass = attend(table, mixed, feed_gather.arrived())
+    feed_gather.hop()
+    out_blocks = gather_ctx(out_columns.reshape(width, span))
+    out_weights = join_windows(peer_table, out_blocks, width)
+    pieces = exchange_far(
+        *exchange_near(*halves(after(row_major(attended_mine[:, :span]), out_blocks[1])))
+    )
+    middle, normed_two, attended = attn_out(
+        peer_table,
+        pieces,
+        out_weights,
+        after(own_tokens, *feed_gather.arrived()),
+        bias_o,
+        gain_two,
+        shift_two,
+    )
+    feed_gather.hop()
+
+    normed_far = ctx_swap(normed_two, 2)
+    normed_blocks = [
+        normed_two,
+        normed_far,
+        ctx_swap(normed_two, 1),
+    ]
+    feed_gather.hop()
+    normed_blocks.append(ctx_swap(after(normed_far, *feed_gather.arrived()), 1))
+    grad_all = row_major(jnp.concatenate([after(grad_blocks[0], normed_two)] + grad_blocks[1:]))
+    fc_weights, proj_weights = feed_gather.result(
+        owners, ((0, width, 0, shard_rows), (0, width, shard_rows, unit_rows))
+    )
     fc_weights = fc_weights.reshape(width, -1)
     proj_weights = proj_weights.reshape(-1, width)
-    before = product(normed_two_all, fc_weights) + bias_fc
-    inner = jnp.tanh(0.7978845608028654 * (before + 0.044715 * before * before * before))
-    activated = row_major((0.5 * before * (1.0 + inner)).astype(bf16))
-    slope = 0.5 * (1.0 + inner) + 0.5 * before * (1.0 - inner * inner) * (
-        0.7978845608028654 * (1.0 + 3 * 0.044715 * before * before)
+    activated, slope, normed_two_all = feed_up(
+        [after(normed_blocks[0], grad_all)] + normed_blocks[1:], fc_weights, bias_fc
     )
 
     grad_proj = row_major(outer_sum(activated, grad_all).astype(bf16))
     proj_scatter = Scatter(grad_proj.reshape(shards, unit_rows, width), owners)
     proj_scatter.hop()
-    before_low = row_major(
-        (back_product(after(grad_all, grad_proj), proj_weights) * slope).astype(bf16)
-    )
-    grad_two = row_major(back_product(before_low, fc_weights).astype(bf16))
+    before_low, grad_bias_fc = feed_back(grad_blocks, proj_weights, slope, proj_scatter.given)
+    proj_scatter.hop(before_low)
+    grad_two = plain_back(before_low, fc_weights, "feed_back_two", proj_scatter.given)
+    kept_two, onward_two = scatter_near(*halves(grad_two))
     proj_scatter.hop()
-    kept_two, onward_two = scatter_near(grad_two)
-    grad_fc = row_major(outer_sum(normed_two_all, after(before_low, grad_two)).astype(bf16))
+    branch_two = row_major(
+        product(after(activated, *proj_scatter.given), proj_weights).astype(bf16)
+    )
+    grad_fc = row_major(
+        outer_sum(after(normed_two_all, onward_two, *proj_scatter.given), before_low).astype(bf16)
+    )
+    far_two = ctx_swap(onward_two, 2)
+    kept_branch, onward_branch = scatter_near(*halves(branch_two))
     fc_scatter = Scatter(grad_fc.reshape(shards, shard_rows, shards * unit_rows), owners)
     fc_scatter.hop()
-    proj_scatter.hop(onward_two)
-    fc_scatter.hop(onward_two)
-    grad_two = scatter_far(kept_two, onward_two)
-    grad_out = out_grad[0].astype(f32)
-    grad_norm, grad_gain_two, grad_shift_two = norm_back(grad_two, unit_two, scale_two, gain_two)
-    grad_middle = grad_out + grad_norm
-    middle_low = row_major(grad_middle.astype(bf16))
-    proj_scatter.hop(middle_low)
-    fc_scatter.hop(middle_low)
-
-    grad_attended = row_major(back_product(middle_low, out_weights).astype(bf16))
-    heads_near = exchange_near(windows(grad_attended))
-    grad_heads = jnp.concatenate(exchange_far(*heads_near))
-    grad_heads = jnp.pad(grad_heads, ((0, 0), (0, PAIR - span % PAIR)))
-    grad_mixed = attend_back(table, mixed, grad_heads, mass)
-    fc_scatter.hop(grad_heads)
-    grad_qkv = row_major(outer_sum(normed_all, grad_mixed).astype(bf16))
+    proj_scatter.hop(*fc_scatter.given)
+    grad_middle, middle_low, heads_keep, heads_give, sums_two = norm_two_back(
+        peer_table,
+        kept_two,
+        far_two,
+        middle,
+        own_grad,
+        gain_two,
+        out_weights,
+        (onward_branch, *fc_scatter.given, *proj_scatter.given),
+    )
+    far_branch = ctx_swap(after(onward_branch, far_two), 2)
+    fc_scatter.hop()
+
+    heads_near = exchange_near(heads_keep.reshape(-1, span), heads_give.reshape(-1, span))
+    out_keep, out_give = out_weight_grad(
+        peer_table,
+        attended,
+        middle_low,
+        (*heads_near[1:], *fc_scatter.given, *proj_scatter.moved),
+    )
+    heads_far = exchange_far(heads_near[0], heads_near[1], after(heads_near[2], far_branch))
+    grad_heads = jnp.pad(jnp.concatenate(heads_far), ((0, 0), (0, PAIR - span % PAIR)))
+    tokens_out = (middle + added(kept_branch, far_branch) + bias_p).astype(bf16)[None]
+    kept_out, onward_out = scatter_near(
+        out_keep.reshape(-1, span), after(out_give.reshape(-1, span), heads_far[1])
+    )
+    grad_mixed = attend_back(table, mixed, grad_heads, mass, (out_give,))
+    far_out = ctx_swap(onward_out, 2)
+    fc_scatter.hop(grad_mixed)
+    grad_qkv = row_major(
+        outer_sum(normed_all, after(grad_mixed, onward_out, *fc_scatter.given)).astype(bf16)
+    )
     qkv_scatter = Scatter(grad_qkv.reshape(shards, shard_rows, mixed_width), owners)
     qkv_scatter.hop()
-    grad_one = row_major(
-        back_product(after(grad_mixed, grad_qkv), qkv_weights).astype(bf16)
-    )
-    kept_one, onward_one = scatter_near(grad_one)
-    qkv_scatter.hop()
-    grad_attn_out = row_major(
-        outer_sum(attended, after(middle_low, onward_one)).astype(bf16)
-    )
-    kept_out, onward_out = scatter_near(windows(grad_attn_out))
-    qkv_scatter.hop()
-    grad_one = scatter_far(kept_one, onward_one)
-    grad_attn_out = row_major(scatter_far(kept_out, onward_out).astype(bf16))
+    fc_scatter.hop(*qkv_scatter.given)
+    qkv_scatter.hop(*fc_scatter.given)
+    grad_one = plain_back(
+        grad_mixed, qkv_weights, "mixed_back", (far_out, *fc_scatter.given, *qkv_scatter.given)
+    )
+    kept_one, onward_one = scatter_near(*halves(grad_one))
+    shard_proj = proj_scatter.result(onward_one)
+    grad_attn_out = added(kept_out, far_out).astype(bf16)
     out_scatter = Scatter(grad_attn_out.reshape(shards, shard_rows, span), owners)
-    out_scatter.hop()
-    qkv_scatter.hop()
-    out_scatter.hop()
-    out_scatter.hop()
-    out_scatter.hop()
-
-    unit_one, scale_one = norm_stats(tokens)
-    grad_norm, grad_gain_one, grad_shift_one = norm_back(grad_one, unit_one, scale_one, gain_one)
-    grad_tokens = (grad_middle + grad_norm)[None]
-
-    branch_two = row_major(product(activated, after(proj_weights, grad_qkv)).astype(bf16))
-    branch_two = scatter_far(*scatter_near(branch_two))
-    tokens_out = (middle + branch_two + bias_p).astype(bf16)[None]
+    out_scatter.hop(onward_one)
+    far_one = ctx_swap(onward_one, 2)
+    proj_pieces = gather_ctx(after(shard_proj, far_one))
+    qkv_scatter.hop(*fc_scatter.moved)
+    out_scatter.hop(*qkv_scatter.given)
+    fc_pieces = gather_ctx(after(fc_scatter.result(*qkv_scatter.given), proj_pieces[1]))
+    grad_tokens, sums_one = norm_one_back(
+        kept_one, far_one, own_tokens, grad_middle, gain_one, qkv_scatter.given
+    )
+    grad_tokens = grad_tokens[None]
+    qkv_scatter.hop(far_one)
+    out_scatter.hop(*qkv_scatter.given)
+    grad_w_proj = whole_rows(peer_table, proj_pieces, qkv_scatter.given)
+    shard_qkv = qkv_scatter.result(proj_pieces[1])
+    out_scatter.hop(shard_qkv)
+    qkv_pieces = gather_ctx(after(shard_qkv, fc_pieces[1]))
+    grad_w_fc = whole_fc(peer_table, fc_pieces, (shard_qkv,))
 
     bias_sums = jnp.sum(grad_mixed.astype(f32), axis=0, keepdims=True)
 
@@ -728,18 +1248,18 @@
 
     grad_bias_fc = lax.dynamic_update_slice(
         jnp.zeros((shards, ctx, unit_rows), f32),
-        jnp.sum(before_low.astype(f32), axis=0).reshape(shards, 1, unit_rows),
+        grad_bias_fc.reshape(shards, 1, unit_rows),
         (0, rank, 0),
     )
     small_grads = [
         all_heads(0),
         all_heads(2),
-        jnp.sum(middle_low.astype(f32), axis=0),
-        jnp.sum(grad_out, axis=0),
-        grad_gain_one,
-        grad_shift_one,
-        grad_gain_two,
-        grad_shift_two,
+        sums_two[2],
+        sums_two[3],
+        sums_one[0],
+        sums_one[1],
+        sums_two[0],
+        sums_two[1],
         grad_bias_fc,
     ]
     summed = reduce_small(
@@ -748,41 +1268,19 @@
     shares = [summed[t * shard_rows : (t + 1) * shard_rows] for t in range(8)]
     share_fc = summed[8 * shard_rows :]
 
-    shard_ff = jnp.stack([fc_scatter.result(), proj_scatter.result()]).astype(bf16)
-    whole_ff = gather_ctx(after(shard_ff, grad_qkv))
-    whole_proj = by_rank([g[1] for g in whole_ff]).reshape(ctx * unit_rows, width).astype(f32)
-    whole_fc = by_rank([g[0] for g in whole_ff])
-    whole_fc = jnp.concatenate(
-        [
-            whole_fc[r][:, i * unit_rows : (i + 1) * unit_rows]
-            for i in range(shards)
-            for r in range(ctx)
-        ],
-        axis=1,
-    ).astype(f32)
-    shard_attn = jnp.concatenate([qkv_scatter.result(), out_scatter.result()], axis=1)
-    whole_attn = by_rank(gather_ctx(shard_attn.astype(bf16)))
-    whole_attn_out = columns_of(whole_attn[:, :, mixed_width:]).astype(f32)
-    whole_qkv = jnp.concatenate(
-        [
-            piece
-            for t in range(3)
-            for r in range(ctx)
-            for piece in from_pairs(whole_attn[r], t, r == ctx - 1)
-        ],
-        axis=1,
-    ).astype(f32)
+    whole_attn_out = join_windows(peer_table, gather_ctx(out_scatter.result()), width).astype(f32)
+    grad_w_qkv = whole_qkv(peer_table, qkv_pieces, width)
 
     return (
         tokens_out,
         grad_tokens,
-        whole_qkv,
+        grad_w_qkv,
         whole_attn_out,
         shares[0],
         shares[1],
         shares[2],
-        whole_fc,
-        whole_proj,
+        grad_w_fc,
+        grad_w_proj,
         share_fc,
         shares[3],
         shares[4],

time: 792 us -> 633 us (0.80)
  Pallas kernels: 36.7 us -> 244 us
  local copies, waits for them, and re-layouts: 215 us -> 67.6 us
  other arithmetic: 102 us -> 16.7 us
  matrix products: 99.9 us -> 39.2 us
  waiting for transfers between devices: 225 us -> 173 us
  between operations: 18.5 us -> 1.81 us
    pallas_call x5 -> x43, Pallas kernels: 36.7 us -> 244 us  [call(): pl.pallas_call(body, grid_spec=pltpu.PrefetchScalarGridSpec(num_scalar_pr...]
    convert_element_type x30 -> x3, other arithmetic: 51.4 us -> 6.86 us  [the longest x1 3.64 us: per_device(): grad_attn_out = added(kept_out, far_out).astype(bf16)]
    ppermute x16 -> x0, local copies, waits for them, and re-layouts: 39.4 us -> none  [ctx_swap(): return row_major(lax.ppermute(row_major(block), 'ctx', pairs))]
    ppermute x32 -> x38, waiting for transfers between devices: 71.9 us -> 39.1 us  [ctx_swap(): got = row_major(lax.ppermute(row_major(tiled(block)), 'ctx', pairs))]
    dot_general x4 -> x0, matrix products: 32.1 us -> none  [back_product(): lax.dot_general(left_op, right_op, (((1,), (1,)), ((), ())), preferred_el...]
    dot_general x4 -> x1, matrix products: 34.5 us -> 8.39 us  [product(): return jnp.dot(left_op, right_op, preferred_element_type=f32)]
    slice x34 -> x6, local copies, waits for them, and re-layouts: 28.2 us -> 5.4 us  [the longest x1 1.76 us: exchange_near(): keep[quarter:]]
    another operation x17 -> x19, local copies, waits for them, and re-layouts: 28 us -> 5.44 us  [the longest x1 0.69 us: feed_up(): bias[None]]
  transfers between devices with their start and end apart: 91 -> 89, of which waited for: 31 -> 31; matrix products, arithmetic and copies ran while one was open for 38% -> 14% of each run, Pallas kernels for 3% -> 33%
where the time goes in v3:
time: 633 us; the launch traced here: 628 us
  Pallas kernels  244 us (39%)
  waiting for transfers between devices  173 us (27%)
  starting transfers between devices  85.8 us (14%)
  local copies, waits for them, and re-layouts  67.6 us (11%)
  matrix products  39.2 us (6%)
  other arithmetic  16.7 us (3%)
    pallas_call x43, Pallas kernels, call(): pl.pallas_call(body, grid_spec=pltpu.PrefetchScalarGridSpec(num_scalar_pr...  244 us
    ppermute x48, waiting for transfers between devices, ring_hop(): return row_major(lax.ppermute(row_major(value), 'fsdp', pairs))  130 us
    ppermute x48, starting transfers between devices, ring_hop(): return row_major(lax.ppermute(row_major(value), 'fsdp', pairs))  61.4 us
    ppermute x38, waiting for transfers between devices, ctx_swap(): got = row_major(lax.ppermute(row_major(tiled(block)), 'ctx', pairs))  39.1 us
    dot_general x3, matrix products, outer_sum(): lax.dot_general(left_op, right_op, (((0,), (0,)), ((), ())), preferred_el...  30.8 us
    unnamed x150, local copies, waits for them, and re-layouts  28.8 us
    ppermute x38, starting transfers between devices, ctx_swap(): got = row_major(lax.ppermute(row_major(tiled(block)), 'ctx', pairs))  21.9 us
  transfers between devices with their start and end apart: 89, of which 31 were waited for; matrix products, arithmetic and copies ran while one was open for 14% of the time, Pallas kernels for 33%

profile of v3, /device:TPU:0, one launch (start us, length us, event | category | flops | bytes accessed | tf_op | source)
XLA Modules:
  0.0 627.7 jit_solution(15474970304331069996)
XLA Ops:
  6.7 18.1 %collective-permute-done.6.refs_3_ = bf16[208,1856]{1,0:T(8,128)(2,1)} collective-permute-done((bf16[208,1856]{1,0:T(8,128)(2,1)}, bf16[208,1856]{1,0:T(8,128)(2,1)}, u32[]{:S(2)}, u32[]{:S(2)}) %collective-permute-start.6) | collective-permute-done | bytes 772128 | tf_op jit(solution)/shard_map/ppermute | solution.py:125
  36.2 7.9 %collective-permute-done.8.refs_5_ = bf16[208,1856]{1,0:T(8,128)(2,1)} collective-permute-done((bf16[208,1856]{1,0:T(8,128)(2,1)}, bf16[208,1856]{1,0:T(8,128)(2,1)}, u32[]{:S(2)}, u32[]{:S(2)}) %collective-permute-start.8) | collective-permute-done | bytes 772128 | tf_op jit(solution)/shard_map/ppermute | solution.py:125
  49.5 13.1 %collective-permute-done.10.refs_7_ = bf16[208,1856]{1,0:T(8,128)(2,1)} collective-permute-done((bf16[208,1856]{1,0:T(8,128)(2,1)}, bf16[208,1856]{1,0:T(8,128)(2,1)}, u32[]{:S(2)}, u32[]{:S(2)}) %collective-permute-start.10) | collective-permute-done | bytes 772128 | tf_op jit(solution)/shard_map/ppermute | solution.py:125
  74.3 26.7 %collective-permute-done.12.refs_9_ = bf16[104,1856]{1,0:T(8,128)(2,1)} collective-permute-done((bf16[104,1856]{1,0:T(8,128)(2,1)S(1)}, bf16[104,1856]{1,0:T(8,128)(2,1)}, u32[]{:S(2)}, u32[]{:S(2)}) %collective-permute-start.12) | collective-permute-done | bytes 386080 | tf_op jit(solution)/shard_map/ppermute | solution.py:125
  119.2 12.6 %norm_mixed.1 = (bf16[1024,1600]{1,0:T(8,128)(2,1)}, bf16[1024,1408]{1,0:T(8,128)(2,1)}) custom-call(bf16[256,1600]{1,0:T(8,128)(2,1)} %bitcast.150, bf16[256,1600]{1,0:T(8,128)(2,1)} %bitcast.8.refs_1_, bf16[256,1600]{1,0:T(8,128)(2,1)} %bitcast.183, bf16[256,1600]{1,0:T(8,128)(2,1)} %bitcast.184, f32[1,1600]{1,0:T(1,128)} %broadcast_in_dim_reshape_squeeze.18.refs_4_, ...), custom_call_target="tpu_custom_call" | custom-call | flops 1048576 | bytes 65536 | tf_op jit(solution)/shard_map/norm_mixed/pallas_call | solution.py:542
  131.7 14.0 %attend.1 = (bf16[1024,512]{1,0:T(8,128)(2,1)}, f32[4,8,1024]{2,1,0:T(8,128)}) custom-call(s32[9]{0:T(128)} %pad_add_fusion.1.refs_0_, bf16[1024,1408]{1,0:T(8,128)(2,1)} %get-tuple-element.111.refs_1_, bf16[400,1600]{1,0:T(8,128)(2,1)} %collective-permute-done.13.refs_10_.refs_2_, bf16[400,1600]{1,0:T(8,128)(2,1)} %collective-permute-done.14.refs_11_.refs_3_), custom_call_target="tpu_custom_call" | custom-call | flops 1048576 | bytes 65536 | tf_op jit(solution)/shard_map/attend/pallas_call | solution.py:542
  157.8 9.3 %collective-permute-done.17 = bf16[64,8,448]{2,1,0:T(8,128)(2,1)} collective-permute-done((bf16[64,8,448]{2,1,0:T(8,128)(2,1)}, bf16[64,8,448]{2,1,0:T(8,128)(2,1)}, u32[]{:S(2)}, u32[]{:S(2)}) %collective-permute-start.17) | collective-permute-done | bytes 458784 | tf_op jit(solution)/shard_map/ppermute | solution.py:70
  186.4 13.0 %collective-permute-done.26.refs_8_ = bf16[200,1600]{1,0:T(8,128)(2,1)S(1)} collective-permute-done((bf16[200,1600]{1,0:T(8,128)(2,1)S(1)}, bf16[200,1600]{1,0:T(8,128)(2,1)S(1)}, u32[]{:S(2)}, u32[]{:S(2)}) %collective-permute-start.26) | collective-permute-done | bytes 640032 | tf_op jit(solution)/shard_map/ppermute | solution.py:125
  206.2 8.8 %collect.3 = (bf16[8,200,1600]{2,1,0:T(8,128)(2,1)}, bf16[8,200,1600]{2,1,0:T(8,128)(2,1)}) custom-call(s32[8]{0:T(128)} %and_select_fusion.refs_0_, bf16[400,1600]{1,0:T(8,128)(2,1)} %copy-done.13, bf16[400,1600]{1,0:T(8,128)(2,1)} %collective-permute-done.13.refs_10_.refs_2_, bf16[400,1600]{1,0:T(8,128)(2,1)} %collective-permute-done.14.refs_11_.refs_3_, ...), custom_call_target="tpu_custom_call" | custom-call | flops 1048576 | bytes 65536 | tf_op jit(solution)/shard_map/collect/pallas_call | solution.py:542
  215.0 14.4 %feed_up.1 = (bf16[1024,1600]{1,0:T(8,128)(2,1)}, bf16[1024,1600]{1,0:T(8,128)(2,1)}, bf16[1024,1600]{1,0:T(8,128)(2,1)}) custom-call(bf16[256,1600]{1,0:T(8,128)(2,1)} %get-tuple-element.119.refs_0_, bf16[256,1600]{1,0:T(8,128)(2,1)} %bitcast.31.refs_1_, bf16[256,1600]{1,0:T(8,128)(2,1)} %bitcast.32.refs_2_, bf16[256,1600]{1,0:T(8,128)(2,1)} %bitcast.34.refs_3_, ...), custom_call_target="tpu_custom_call" | custom-call | flops 1048576 | bytes 65536 | tf_op jit(solution)/shard_map/feed_up/pallas_call | solution.py:542
  229.4 11.2 %convolution_convert_fusion.2 = bf16[1600,1600]{1,0:T(8,128)(2,1)} fusion(bf16[1024,1600]{1,0:T(8,128)(2,1)} %get-tuple-element.132, bf16[256,1600]{1,0:T(8,128)(2,1)} %bitcast.10.refs_3_, bf16[256,1600]{1,0:T(8,128)(2,1)} %bitcast.29.refs_2_, bf16[256,1600]{1,0:T(8,128)(2,1)} %bitcast.28.refs_1_, bf16[256,1600]{1,0:T(8,128)(2,1)S(1)} %bitcast.157), kind=kOutput, calls=%fused_computation.4 | convolution fusion | flops 5258547200 | bytes 11673600 | tf_op jit(solution)/shard_map/dot_general | solution.py:29
  244.7 11.4 %collective-permute-start.30 = (bf16[96,1600]{1,0:T(8,128)(2,1)}, bf16[96,1600]{1,0:T(8,128)(2,1)S(1)}, u32[]{:S(2)}, u32[]{:S(2)}) collective-permute-start(bf16[96,1600]{1,0:T(8,128)(2,1)} %get-tuple-element.123.refs_6_), channel_id=1, source_target_pairs={{0,2},{2,4},{4,6},{6,7},{7,5},{5,3},{3,1},{1,0},{8,10},{10,12},{12... | collective-permute-start | bytes 921608 | tf_op jit(solution)/shard_map/ppermute | solution.py:125
  256.1 12.9 %feed_back.1 = (bf16[1024,1600]{1,0:T(8,128)(2,1)}, f32[1,1600]{1,0:T(1,128)}) custom-call(bf16[256,1600]{1,0:T(8,128)(2,1)} %bitcast.158, bf16[256,1600]{1,0:T(8,128)(2,1)} %bitcast.28.refs_1_, bf16[256,1600]{1,0:T(8,128)(2,1)} %bitcast.29.refs_2_, bf16[256,1600]{1,0:T(8,128)(2,1)} %bitcast.10.refs_3_, bf16[1600,1600]{1,0:T(8,128)(2,1)} %bitcast.161, ...), custom_call_target="tpu_custom_call" | custom-call | flops 1048576 | bytes 65536 | tf_op jit(solution)/shard_map/feed_back/pallas_call | solution.py:542
  275.2 11.1 %feed_back_two.1 = bf16[1024,1600]{1,0:T(8,128)(2,1)} custom-call(bf16[1024,1600]{1,0:T(8,128)(2,1)} %get-tuple-element.127.refs_5_.refs_0_, bf16[1600,1600]{1,0:T(8,128)(2,1)} %bitcast.145, bf16[200,1600]{1,0:T(8,128)(2,1)} %get-tuple-element.128.refs_2_, bf16[200,1600]{1,0:T(8,128)(2,1)} %get-tuple-element.129.refs_3_), custom_call_target="tpu_custom_call" | custom-call | flops 1048576 | bytes 65536 | tf_op jit(solution)/shard_map/feed_back_two/pallas_call | solution.py:542
  297.1 8.4 %convolution_convert_fusion.3 = bf16[1024,1600]{1,0:T(8,128)(2,1)S(1)} fusion(bf16[1024,1600]{1,0:T(8,128)(2,1)} %get-tuple-element.132, bf16[1600,1600]{1,0:T(8,128)(2,1)S(1)} %bitcast.164), kind=kOutput, calls=%fused_computation.6 | convolution fusion | flops 5244518400 | bytes 11673600 | tf_op jit(solution)/shard_map/dot_general | solution.py:41
  314.2 10.7 %convolution_convert_fusion.1 = bf16[1600,1600]{1,0:T(8,128)(2,1)} fusion(bf16[1024,1600]{1,0:T(8,128)(2,1)} %get-tuple-element.139, bf16[1024,1600]{1,0:T(8,128)(2,1)S(1)} %copy-done.7), kind=kOutput, calls=%fused_computation.3 | convolution fusion | flops 5245440000 | bytes 11673600 | tf_op jit(solution)/shard_map/dot_general | solution.py:29
  337.7 9.0 %norm_two_back.1 = (f32[256,1600]{1,0:T(8,128)}, bf16[256,1600]{1,0:T(8,128)(2,1)}, bf16[2,256,448]{2,1,0:T(8,128)(2,1)}, bf16[2,256,448]{2,1,0:T(8,128)(2,1)}, f32[4,1600]{1,0:T(4,128)}) custom-call(s32[4]{0:T(128)} %pad_add_fusion.refs_0_, f32[256,1600]{1,0:T(8,128)} %get-tuple-element.137.refs_1_, bf16[256,1600]{1,0:T(8,128)(2,1)} %bitcast.187, ...), custom_call_target="tpu_custom_call" | custom-call | flops 1048576 | bytes 65536 | tf_op jit(solution)/shard_map/norm_two_back/pallas_call | solution.py:542
  353.8 17.2 %collective-permute-done.42.refs_3_ = bf16[96,1600]{1,0:T(8,128)(2,1)S(1)} collective-permute-done((bf16[96,1600]{1,0:T(8,128)(2,1)S(1)}, bf16[96,1600]{1,0:T(8,128)(2,1)S(1)}, u32[]{:S(2)}, u32[]{:S(2)}) %collective-permute-start.42) | collective-permute-done | bytes 307232 | tf_op jit(solution)/shard_map/ppermute | solution.py:125
  399.7 20.0 %attend_back.1.refs_5_.refs_0_ = bf16[1024,1408]{1,0:T(8,128)(2,1)} custom-call(s32[9]{0:T(128)} %pad_add_fusion.1.refs_0_, bf16[1024,1408]{1,0:T(8,128)(2,1)} %get-tuple-element.111.refs_1_, bf16[1024,512]{1,0:T(8,128)(2,1)} %fusion.6.refs_2_, f32[4,8,1024]{2,1,0:T(8,128)} %get-tuple-element.147.refs_3_, bf16[2,1600,448]{2,1,0:T(8,128)(2,1)} %get-tuple-element.152.refs_4_), custom_call_target="tpu_custom_call" | custom-call | flops 1048576 | bytes 65536 | tf_op jit(solution)/shard_map/attend_back/pallas_call | solution.py:542
  426.4 8.8 %convolution_convert_fusion = bf16[1600,1408]{1,0:T(8,128)(2,1)} fusion(bf16[1024,1600]{1,0:T(8,128)(2,1)} %get-tuple-element.158, bf16[1024,1408]{1,0:T(8,128)(2,1)S(1)} %copy-done.4), kind=kOutput, calls=%fused_computation.2 | convolution fusion | flops 4615987200 | bytes 10665984 | tf_op jit(solution)/shard_map/dot_general | solution.py:29
  453.9 9.9 %mixed_back.1 = bf16[1024,1600]{1,0:T(8,128)(2,1)} custom-call(bf16[1024,1408]{1,0:T(8,128)(2,1)} %attend_back.1.refs_5_.refs_0_, bf16[1600,1408]{1,0:T(8,128)(2,1)} %bitcast.147, bf16[1600,448]{1,0:T(8,128)(2,1)} %bitcast.160, bf16[200,1600]{1,0:T(8,128)(2,1)} %get-tuple-element.162.refs_5_.refs_3_, bf16[200,1600]{1,0:T(8,128)(2,1)} %get-tuple-element.163.refs_6_.refs_4_, ...), custom_call_target="tpu_custom_call" | custom-call | flops 1048576 | bytes 65536 | tf_op jit(solution)/shard_map/mixed_back/pallas_call | solution.py:542
  487.7 8.0 %collective-permute-done.58.refs_5_.refs_2_ = bf16[200,1600]{1,0:T(8,128)(2,1)S(1)} collective-permute-done((bf16[200,1600]{1,0:T(8,128)(2,1)}, bf16[200,1600]{1,0:T(8,128)(2,1)S(1)}, u32[]{:S(2)}, u32[]{:S(2)}) %collective-permute-start.58) | collective-permute-done | bytes 640032 | tf_op jit(solution)/shard_map/ppermute | solution.py:125
  499.2 8.7 %collective-permute-done.56.refs_3_ = bf16[200,1408]{1,0:T(8,128)(2,1)} collective-permute-done((bf16[200,1408]{1,0:T(8,128)(2,1)}, bf16[200,1408]{1,0:T(8,128)(2,1)}, u32[]{:S(2)}, u32[]{:S(2)}) %collective-permute-start.56) | collective-permute-done | bytes 563232 | tf_op jit(solution)/shard_map/ppermute | solution.py:125
  572.1 15.2 %collective-permute-done.65 = bf16[25,8,1600]{2,1,0:T(8,128)(2,1)S(1)} collective-permute-done((bf16[25,8,1600]{2,1,0:T(8,128)(2,1)S(1)}, bf16[25,8,1600]{2,1,0:T(8,128)(2,1)S(1)}, u32[]{:S(2)}, u32[]{:S(2)}) %collective-permute-start.65) | collective-permute-done | bytes 640032 | tf_op jit(solution)/shard_map/ppermute | solution.py:70
  (449 shorter events, 325.4 us)
Async XLA Ops:
  63.7 37.3 %collective-permute-start.13 = (bf16[400,1600]{1,0:T(8,128)(2,1)S(1)}, bf16[400,1600]{1,0:T(8,128)(2,1)}, u32[]{:S(2)}, u32[]{:S(2)}) collective-permute-start(bf16[400,1600]{1,0:T(8,128)(2,1)S(1)} %pad_maximum_fusion.1.refs_1_), channel_id=1, source_target_pairs={{0,2},{2,4},{4,6},{6,7},{7,5},{5,3},{3,1},{1,0},{8,10},{10,12},{12... | collective-permute-start | bytes 3840008 | tf_op jit(solution)/shard_map/ppermute | solution.py:125
  64.3 36.6 %collective-permute-start.14 = (bf16[400,1600]{1,0:T(8,128)(2,1)S(1)}, bf16[400,1600]{1,0:T(8,128)(2,1)}, u32[]{:S(2)}, u32[]{:S(2)}) collective-permute-start(bf16[400,1600]{1,0:T(8,128)(2,1)S(1)} %pad_maximum_fusion.1.refs_1_), channel_id=1, source_target_pairs={{0,1},{2,0},{4,2},{6,4},{7,6},{5,7},{3,5},{1,3},{8,9},{10,8},{12,1... | collective-permute-start | bytes 3840008 | tf_op jit(solution)/shard_map/ppermute | solution.py:125
  66.9 44.4 %collective-permute-start.2 = (bf16[32,8,1600]{2,1,0:T(8,128)(2,1)}, bf16[32,8,1600]{2,1,0:T(8,128)(2,1)}, u32[]{:S(2)}, u32[]{:S(2)}) collective-permute-start(bf16[32,8,1600]{2,1,0:T(8,128)(2,1)} %collective-permute-done.1), channel_id=1, source_target_pairs={{0,8},{8,0},{16,24},{24,16},{1,9},{9,1},{17,25},{25,17},{2,10},{10... | collective-permute-start | bytes 2457608 | tf_op jit(solution)/shard_map/ppermute | solution.py:70
  67.9 33.0 %collective-permute-start.12 = (bf16[104,1856]{1,0:T(8,128)(2,1)S(1)}, bf16[104,1856]{1,0:T(8,128)(2,1)}, u32[]{:S(2)}, u32[]{:S(2)}) collective-permute-start(bf16[104,1856]{1,0:T(8,128)(2,1)S(1)} %slice.340), channel_id=1, source_target_pairs={{0,1},{2,0},{4,2},{6,4},{7,6},{5,7},{3,5},{1,3},{8,9},{10,8},{12,1... | collective-permute-start | bytes 1158152 | tf_op jit(solution)/shard_map/ppermute | solution.py:125
  70.8 30.1 %collective-permute-start.11 = (bf16[104,1856]{1,0:T(8,128)(2,1)}, bf16[104,1856]{1,0:T(8,128)(2,1)}, u32[]{:S(2)}, u32[]{:S(2)}) collective-permute-start(bf16[104,1856]{1,0:T(8,128)(2,1)} %slice.339), channel_id=1, source_target_pairs={{0,2},{2,4},{4,6},{6,7},{7,5},{5,3},{3,1},{1,0},{8,10},{10,12},{12... | collective-permute-start | bytes 1158152 | tf_op jit(solution)/shard_map/ppermute | solution.py:125
  107.3 38.5 %collective-permute-start.15 = (bf16[200,8,448]{2,1,0:T(8,128)(2,1)}, bf16[200,8,448]{2,1,0:T(8,128)(2,1)}, u32[]{:S(2)}, u32[]{:S(2)}) collective-permute-start(bf16[200,8,448]{2,1,0:T(8,128)(2,1)} %bitcast.17), channel_id=1, source_target_pairs={{0,16},{8,24},{16,0},{24,8},{1,17},{9,25},{17,1},{25,9},{2,18},{10... | collective-permute-start | bytes 4300808 | tf_op jit(solution)/shard_map/ppermute | solution.py:70
  109.8 37.7 %collective-permute-start.20 = (bf16[400,1600]{1,0:T(8,128)(2,1)}, bf16[400,1600]{1,0:T(8,128)(2,1)}, u32[]{:S(2)}, u32[]{:S(2)}) collective-permute-start(bf16[400,1600]{1,0:T(8,128)(2,1)} %collective-permute-done.13.refs_10_.refs_2_), channel_id=1, source_target_pairs={{0,2},{2,4},{4,6},{6,7},{7,5},{5,3},{3,1},{1,0},{8,10},{10,12},{12... | collective-permute-start | bytes 3840008 | tf_op jit(solution)/shard_map/ppermute | solution.py:125
  111.3 37.7 %collective-permute-start.21 = (bf16[400,1600]{1,0:T(8,128)(2,1)}, bf16[400,1600]{1,0:T(8,128)(2,1)}, u32[]{:S(2)}, u32[]{:S(2)}) collective-permute-start(bf16[400,1600]{1,0:T(8,128)(2,1)} %collective-permute-done.14.refs_11_.refs_3_), channel_id=1, source_target_pairs={{0,1},{2,0},{4,2},{6,4},{7,6},{5,7},{3,5},{1,3},{8,9},{10,8},{12,1... | collective-permute-start | bytes 3840008 | tf_op jit(solution)/shard_map/ppermute | solution.py:125
  147.5 36.6 %collective-permute-start.25 = (bf16[400,1600]{1,0:T(8,128)(2,1)}, bf16[400,1600]{1,0:T(8,128)(2,1)S(1)}, u32[]{:S(2)}, u32[]{:S(2)}) collective-permute-start(bf16[400,1600]{1,0:T(8,128)(2,1)} %collective-permute-done.20.refs_4_), channel_id=1, source_target_pairs={{0,2},{2,4},{4,6},{6,7},{7,5},{5,3},{3,1},{1,0},{8,10},{10,12},{12... | collective-permute-start | bytes 3840008 | tf_op jit(solution)/shard_map/ppermute | solution.py:125
  149.0 36.2 %collective-permute-start.27 = (bf16[400,1600]{1,0:T(8,128)(2,1)}, bf16[400,1600]{1,0:T(8,128)(2,1)S(1)}, u32[]{:S(2)}, u32[]{:S(2)}) collective-permute-start(bf16[400,1600]{1,0:T(8,128)(2,1)} %collective-permute-done.21.refs_5_), channel_id=1, source_target_pairs={{0,1},{2,0},{4,2},{6,4},{7,6},{5,7},{3,5},{1,3},{8,9},{10,8},{12,1... | collective-permute-start | bytes 3840008 | tf_op jit(solution)/shard_map/ppermute | solution.py:125
  186.4 28.6 %collective-permute-start.24 = (bf16[32,8,1600]{2,1,0:T(8,128)(2,1)}, bf16[32,8,1600]{2,1,0:T(8,128)(2,1)}, u32[]{:S(2)}, u32[]{:S(2)}) collective-permute-start(bf16[32,8,1600]{2,1,0:T(8,128)(2,1)} %bitcast.186), channel_id=1, source_target_pairs={{0,8},{8,0},{16,24},{24,16},{1,9},{9,1},{17,25},{25,17},{2,10},{10... | collective-permute-start | bytes 2457608 | tf_op jit(solution)/shard_map/ppermute | solution.py:70
  295.0 32.5 %collective-permute-start.38 = (bf16[200,1600]{1,0:T(8,128)(2,1)}, bf16[200,1600]{1,0:T(8,128)(2,1)S(1)}, u32[]{:S(2)}, u32[]{:S(2)}) collective-permute-start(bf16[200,1600]{1,0:T(8,128)(2,1)} %get-tuple-element.130), channel_id=1, source_target_pairs={{0,2},{2,4},{4,6},{6,7},{7,5},{5,3},{3,1},{1,0},{8,10},{10,12},{12... | collective-permute-start | bytes 1920008 | tf_op jit(solution)/shard_map/ppermute | solution.py:125
  296.4 31.1 %collective-permute-start.39 = (bf16[200,1600]{1,0:T(8,128)(2,1)}, bf16[200,1600]{1,0:T(8,128)(2,1)}, u32[]{:S(2)}, u32[]{:S(2)}) collective-permute-start(bf16[200,1600]{1,0:T(8,128)(2,1)} %get-tuple-element.131), channel_id=1, source_target_pairs={{0,1},{2,0},{4,2},{6,4},{7,6},{5,7},{3,5},{1,3},{8,9},{10,8},{12,1... | collective-permute-start | bytes 1920008 | tf_op jit(solution)/shard_map/ppermute | solution.py:125
  346.8 29.4 %collective-permute-start.44 = (bf16[200,1600]{1,0:T(8,128)(2,1)S(1)}, bf16[200,1600]{1,0:T(8,128)(2,1)S(1)}, u32[]{:S(2)}, u32[]{:S(2)}) collective-permute-start(bf16[200,1600]{1,0:T(8,128)(2,1)S(1)} %copy-done.38), channel_id=1, source_target_pairs={{0,2},{2,4},{4,6},{6,7},{7,5},{5,3},{3,1},{1,0},{8,10},{10,12},{12... | collective-permute-start | bytes 1920008 | tf_op jit(solution)/shard_map/ppermute | solution.py:125
  347.8 28.5 %collective-permute-start.45 = (bf16[200,1600]{1,0:T(8,128)(2,1)S(1)}, bf16[200,1600]{1,0:T(8,128)(2,1)S(1)}, u32[]{:S(2)}, u32[]{:S(2)}) collective-permute-start(bf16[200,1600]{1,0:T(8,128)(2,1)S(1)} %copy-done.37), channel_id=1, source_target_pairs={{0,1},{2,0},{4,2},{6,4},{7,6},{5,7},{3,5},{1,3},{8,9},{10,8},{12,1... | collective-permute-start | bytes 1920008 | tf_op jit(solution)/shard_map/ppermute | solution.py:125
  350.8 33.3 %collective-permute-start.41 = (bf16[64,8,448]{2,1,0:T(8,128)(2,1)S(1)}, bf16[64,8,448]{2,1,0:T(8,128)(2,1)S(1)}, u32[]{:S(2)}, u32[]{:S(2)}) collective-permute-start(bf16[64,8,448]{2,1,0:T(8,128)(2,1)S(1)} %bitcast.176), channel_id=1, source_target_pairs={{0,16},{8,24},{16,0},{24,8},{1,17},{9,25},{17,1},{25,9},{2,18},{10... | collective-permute-start | bytes 1376264 | tf_op jit(solution)/shard_map/ppermute | solution.py:70
  384.2 35.5 %collective-permute-start.48 = (bf16[200,1600]{1,0:T(8,128)(2,1)}, bf16[200,1600]{1,0:T(8,128)(2,1)S(1)}, u32[]{:S(2)}, u32[]{:S(2)}) collective-permute-start(bf16[200,1600]{1,0:T(8,128)(2,1)} %get-tuple-element.150.refs_5_), channel_id=1, source_target_pairs={{0,2},{2,4},{4,6},{6,7},{7,5},{5,3},{3,1},{1,0},{8,10},{10,12},{12... | collective-permute-start | bytes 1920008 | tf_op jit(solution)/shard_map/ppermute | solution.py:125
  385.9 33.9 %collective-permute-start.49 = (bf16[200,1600]{1,0:T(8,128)(2,1)}, bf16[200,1600]{1,0:T(8,128)(2,1)}, u32[]{:S(2)}, u32[]{:S(2)}) collective-permute-start(bf16[200,1600]{1,0:T(8,128)(2,1)} %get-tuple-element.151.refs_6_), channel_id=1, source_target_pairs={{0,1},{2,0},{4,2},{6,4},{7,6},{5,7},{3,5},{1,3},{8,9},{10,8},{12,1... | collective-permute-start | bytes 1920008 | tf_op jit(solution)/shard_map/ppermute | solution.py:125
  397.5 55.2 %collective-permute-start.47 = (bf16[200,8,448]{2,1,0:T(8,128)(2,1)}, bf16[200,8,448]{2,1,0:T(8,128)(2,1)S(1)}, u32[]{:S(2)}, u32[]{:S(2)}) collective-permute-start(bf16[200,8,448]{2,1,0:T(8,128)(2,1)} %bitcast.197), channel_id=1, source_target_pairs={{0,16},{8,24},{16,0},{24,8},{1,17},{9,25},{17,1},{25,9},{2,18},{10... | collective-permute-start | bytes 4300808 | tf_op jit(solution)/shard_map/ppermute | solution.py:70
  475.5 45.2 %collective-permute-start.55 = (bf16[32,8,1600]{2,1,0:T(8,128)(2,1)}, bf16[32,8,1600]{2,1,0:T(8,128)(2,1)S(1)}, u32[]{:S(2)}, u32[]{:S(2)}) collective-permute-start(bf16[32,8,1600]{2,1,0:T(8,128)(2,1)} %bitcast.168), channel_id=1, source_target_pairs={{0,16},{8,24},{16,0},{24,8},{1,17},{9,25},{17,1},{25,9},{2,18},{10... | collective-permute-start | bytes 2457608 | tf_op jit(solution)/shard_map/ppermute | solution.py:70
  479.7 28.2 %collective-permute-start.56 = (bf16[200,1408]{1,0:T(8,128)(2,1)}, bf16[200,1408]{1,0:T(8,128)(2,1)}, u32[]{:S(2)}, u32[]{:S(2)}) collective-permute-start(bf16[200,1408]{1,0:T(8,128)(2,1)} %get-tuple-element.164.refs_5_), channel_id=1, source_target_pairs={{0,2},{2,4},{4,6},{6,7},{7,5},{5,3},{3,1},{1,0},{8,10},{10,12},{12... | collective-permute-start | bytes 1689608 | tf_op jit(solution)/shard_map/ppermute | solution.py:125
  551.1 42.7 %collective-permute-start.37 = (bf16[32,8,1600]{2,1,0:T(8,128)(2,1)S(1)}, bf16[32,8,1600]{2,1,0:T(8,128)(2,1)S(1)}, u32[]{:S(2)}, u32[]{:S(2)}) collective-permute-start(bf16[32,8,1600]{2,1,0:T(8,128)(2,1)S(1)} %bitcast.182), channel_id=1, source_target_pairs={{0,16},{8,24},{16,0},{24,8},{1,17},{9,25},{17,1},{25,9},{2,18},{10... | collective-permute-start | bytes 2457608 | tf_op jit(solution)/shard_map/ppermute | solution.py:70
  552.1 46.3 %collective-permute-start.87 = (bf16[25,8,1600]{2,1,0:T(8,128)(2,1)S(1)}, bf16[25,8,1600]{2,1,0:T(8,128)(2,1)}, u32[]{:S(2)}, u32[]{:S(2)}) collective-permute-start(bf16[25,8,1600]{2,1,0:T(8,128)(2,1)S(1)} %bitcast.173), channel_id=1, source_target_pairs={{0,8},{8,0},{16,24},{24,16},{1,9},{9,1},{17,25},{25,17},{2,10},{10... | collective-permute-start | bytes 1920008 | tf_op jit(solution)/shard_map/ppermute | solution.py:70
  556.0 31.3 %collective-permute-start.65 = (bf16[25,8,1600]{2,1,0:T(8,128)(2,1)S(1)}, bf16[25,8,1600]{2,1,0:T(8,128)(2,1)S(1)}, u32[]{:S(2)}, u32[]{:S(2)}) collective-permute-start(bf16[25,8,1600]{2,1,0:T(8,128)(2,1)S(1)} %bitcast.175), channel_id=1, source_target_pairs={{0,16},{8,24},{16,0},{24,8},{1,17},{9,25},{17,1},{25,9},{2,18},{10... | collective-permute-start | bytes 1920008 | tf_op jit(solution)/shard_map/ppermute | solution.py:70
  (138 other events, 1934.6 us)

commit v4 on v3

--- a/solution.py
+++ b/solution.py
@@ -52,6 +52,15 @@
     return with_layout_constraint(matrix, Layout(major_to_minor=tuple(range(matrix.ndim))))
 
 
+def slot(always, step):
+    empty = jax.eval_shape(step)
+    return lax.cond(
+        always,
+        step,
+        lambda: jax.tree.map(lambda leaf: jnp.zeros(leaf.shape, leaf.dtype), empty),
+    )
+
+
 def after(value, *others):
     return lax.optimization_barrier((value,) + others)[0]
 
@@ -84,22 +93,43 @@
 
 def pair_add_kernel(keep, got, kept, onward):
     rows = kept.shape[0]
-    kept[...] = added(keep[:rows], got[:rows])
+    kept[...] = added(keep[:rows], got[:rows]).astype(kept.dtype)
     onward[...] = added(keep[rows:], got[rows:]).astype(bf16)
 
 
-def scatter_near(keep, give, *gates):
+def pair_add(keep, got, kind=f32):
     rows, columns = keep.shape
     half = (rows // 2, columns)
     return call(
         pair_add_kernel,
         "pair_add",
         1,
-        (keep, ctx_swap(give, 1)),
+        (keep, got),
         [whole(keep.shape)] * 2,
-        [(half, f32), (half, bf16)],
+        [(half, kind), (half, bf16)],
         [whole(half)] * 2,
-        gates=gates,
+    )
+
+
+def pair_split_kernel(keep, got, kept, first, second):
+    rows = kept.shape[0]
+    half = rows // 2
+    kept[...] = added(keep[:rows], got[:rows]).astype(kept.dtype)
+    first[...] = added(keep[rows : rows + half], got[rows : rows + half]).astype(bf16)
+    second[...] = added(keep[rows + half :], got[rows + half :]).astype(bf16)
+
+
+def pair_split(keep, got):
+    rows, columns = keep.shape
+    half, quarter = (rows // 2, columns), (rows // 4, columns)
+    return call(
+        pair_split_kernel,
+        "pair_split",
+        1,
+        (keep, got),
+        [whole(keep.shape)] * 2,
+        [(half, bf16), (quarter, bf16), (quarter, bf16)],
+        [whole(half), whole(quarter), whole(quarter)],
     )
 
 
@@ -212,6 +242,10 @@
 PLACE = {0: 0, -1: 1, 1: 2, -2: 3, 2: 4, -3: 5, 3: 6, 4: 7}
 
 
+def half_blocks(cut, rows, width, forth, back):
+    return forth[forth.shape[0] - cut :, :width], back[back.shape[0] - (rows - cut) :, :width]
+
+
 def ring_part_kernel(distance, cut, owners, *refs):
     if distance == HALF:
         far, ahead, behind = refs
@@ -219,14 +253,17 @@
         behind[...] = far[cut:]
     elif distance == 0:
         own, forth, back, out = refs
-        out[...] = added(own[...], forth[...], back[...]).astype(bf16)
+        rows = own.shape[0]
+        out[...] = added(own[...], forth[:rows], back[:rows]).astype(bf16)
     else:
         mine_ahead, mine_behind, forth, back, ahead, behind = refs
         if distance == HALF - 1:
-            ahead[:cut] = added(mine_ahead[:cut], forth[...]).astype(bf16)
+            rows, width = mine_ahead.shape
+            from_forth, from_back = half_blocks(cut, rows, width, forth, back)
+            ahead[:cut] = added(mine_ahead[:cut], from_forth).astype(bf16)
             ahead[cut:] = mine_ahead[cut:]
             behind[:cut] = mine_behind[:cut]
-            behind[cut:] = added(mine_behind[cut:], back[...]).astype(bf16)
+            behind[cut:] = added(mine_behind[cut:], from_back).astype(bf16)
         else:
             ahead[...] = added(mine_ahead[...], forth[...]).astype(bf16)
             behind[...] = added(mine_behind[...], back[...]).astype(bf16)
@@ -256,43 +293,186 @@
     )
 
 
-class Scatter:
-    def __init__(self, blocks, owners):
-        self.blocks, self.owners = blocks, owners
-        self.cut = upper_part(blocks.shape[1])
-        self.next = HALF
-        self.moved = self.given = ()
-
-    def hop(self, *gate):
-        if not on_ring():
-            return
-        self.given = ring_part(
-            self.blocks, self.owners, self.next, self.cut, self.moved, gate
-        )
-        self.moved = [ring_hop(self.given[0], 1), ring_hop(self.given[1], -1)]
-        self.next -= 1
-
-    def result(self, *gate):
-        if not on_ring():
-            return lax.psum_scatter(self.blocks, "fsdp", scatter_dimension=0, tiled=False)
-        return ring_part(self.blocks, self.owners, 0, self.cut, self.moved, gate)[0]
-
-
-def reduce_small(table):
-    count = lax.axis_size("fsdp")
+def packed_kernel(cut, owners, mine_ahead, mine_behind, forth, back, far, ahead, behind):
+    rows, width = mine_ahead.shape
+    second = far.shape[1]
+    ahead[:rows] = added(mine_ahead[...], forth[...]).astype(bf16)
+    behind[:rows] = added(mine_behind[...], back[...]).astype(bf16)
+    ahead[rows:, :second] = far[:cut]
+    behind[rows:, :second] = far[cut:]
+    if second < width:
+        ahead[rows:, second:] = jnp.zeros((cut, width - second), bf16)
+        behind[rows:, second:] = jnp.zeros((rows - cut, width - second), bf16)
+
+
+def packed_step(blocks, others, owners, moved):
+    if not on_ring():
+        return ()
+    rows, width = blocks.shape[1:]
+    cut = upper_part(rows)
+    shapes = [(rows + cut, width), (2 * rows - cut, width)]
+    ahead, behind = call(
+        functools.partial(packed_kernel, cut),
+        "packed_part",
+        1,
+        (blocks, blocks, *moved, others),
+        [
+            pl.BlockSpec((None, rows, width), lambda i, t, p=PLACE[d]: (t[p], 0, 0))
+            for d in (1, -1)
+        ]
+        + [whole(value.shape) for value in moved]
+        + [pl.BlockSpec((None,) + others.shape[1:], lambda i, t: (t[PLACE[HALF]], 0, 0))],
+        [(shape, bf16) for shape in shapes],
+        [whole(shape) for shape in shapes],
+        table=owners,
+    )
+    return ring_hop(ahead, 1), ring_hop(behind, -1)
+
+
+def ring_step(blocks, owners, distance, moved=()):
+    if not on_ring():
+        return ()
+    ahead, behind = ring_part(blocks, owners, distance, upper_part(blocks.shape[1]), moved)
+    return ring_hop(ahead, 1), ring_hop(behind, -1)
+
+
+def twin_block(owners, place, refs):
+    kept, first, second = refs
+    low = owners[place] < HALF
+    return added(kept[...], jnp.where(low, first[...], second[...]))
+
+
+def twin_kernel(distance, lag, cut, owners, *refs):
+    width = refs[0].shape[-1]
+    if distance == 0:
+        own, forth, back, *twins = refs
+        out, ahead, behind = twins[-3:]
+        out[...] = added(own[...], forth[:, :width], back[:, :width]).astype(bf16)
+        value_ahead = twin_block(owners, PLACE[lag], twins[0:3])
+        value_behind = twin_block(owners, PLACE[-lag], twins[3:6])
+        ahead[...] = added(value_ahead, forth[:, width:]).astype(bf16)
+        behind[...] = added(value_behind, back[:, width:]).astype(bf16)
+        return
+    mine_ahead, mine_behind, forth, back, *twins = refs
+    ahead, behind = twins[-2:]
+    if distance == HALF - 1:
+        from_forth, from_back = half_blocks(cut, mine_ahead.shape[0], width, forth, back)
+        ahead[:cut, :width] = added(mine_ahead[:cut], from_forth).astype(bf16)
+        ahead[cut:, :width] = mine_ahead[cut:]
+        behind[:cut, :width] = mine_behind[:cut]
+        behind[cut:, :width] = added(mine_behind[cut:], from_back).astype(bf16)
+        value = twin_block(owners, PLACE[HALF], twins[0:3]).astype(bf16)
+        ahead[:cut, width:] = value[:cut]
+        ahead[cut:, width:] = jnp.zeros_like(value[cut:])
+        behind[:cut, width:] = jnp.zeros_like(value[:cut])
+        behind[cut:, width:] = value[cut:]
+    else:
+        ahead[:, :width] = added(mine_ahead[...], forth[:, :width]).astype(bf16)
+        behind[:, :width] = added(mine_behind[...], back[:, :width]).astype(bf16)
+        value_ahead = twin_block(owners, PLACE[lag], twins[0:3])
+        value_behind = twin_block(owners, PLACE[-lag], twins[3:6])
+        ahead[:, width:] = added(value_ahead, forth[:, width:]).astype(bf16)
+        behind[:, width:] = added(value_behind, back[:, width:]).astype(bf16)
+
+
+def twin_part(blocks, twin, owners, distance, moved):
+    rows, width = blocks.shape[1:]
+    span = twin[0].shape[2]
+    lag = distance + 1
+    mains = (distance, -distance) if distance else (0,)
+    lags = (lag, -lag) if lag < HALF else (lag,)
+    specs = [
+        pl.BlockSpec((None, rows, width), lambda i, t, p=PLACE[d]: (t[p], 0, 0)) for d in mains
+    ]
+    specs += [whole(value.shape) for value in moved]
+    for d in lags:
+        p = PLACE[d]
+        specs += [
+            pl.BlockSpec((None, rows, span), lambda i, t, p=p: (t[p], 0, 0)),
+            pl.BlockSpec(
+                (None, rows, span), lambda i, t, p=p: (jnp.minimum(t[p], HALF - 1), 0, 0)
+            ),
+            pl.BlockSpec((None, rows, span), lambda i, t, p=p: (jnp.maximum(t[p] - HALF, 0), 0, 0)),
+        ]
+    if distance:
+        shapes = [(rows, width + span)] * 2
+    else:
+        shapes = [(rows, width), (rows, span), (rows, span)]
+    return call(
+        functools.partial(twin_kernel, distance, lag, upper_part(rows)),
+        "twin_part",
+        1,
+        (*[blocks] * len(mains), *moved, *twin * len(lags)),
+        specs,
+        [(shape, bf16) for shape in shapes],
+        [whole(shape) for shape in shapes],
+        table=owners,
+    )
+
+
+def twin_last_kernel(owners, forth, back, kept, first, second, out):
+    value = twin_block(owners, PLACE[0], (kept, first, second))
+    out[...] = added(value, forth[...], back[...]).astype(bf16)
+
+
+def twin_last(twin, owners, moved):
+    if not on_ring():
+        blocks = added(twin[0], jnp.concatenate(twin[1:])).astype(bf16)
+        return ring_end(blocks, owners, moved)
+    rows, span = twin[0].shape[1:]
+    block = (None, rows, span)
+    return call(
+        twin_last_kernel,
+        "twin_last",
+        1,
+        (*moved, *twin),
+        [whole((rows, span))] * 2
+        + [
+            pl.BlockSpec(block, lambda i, t: (t[0], 0, 0)),
+            pl.BlockSpec(block, lambda i, t: (jnp.minimum(t[0], HALF - 1), 0, 0)),
+            pl.BlockSpec(block, lambda i, t: (jnp.maximum(t[0] - HALF, 0), 0, 0)),
+        ],
+        [((rows, span), bf16)],
+        [whole((rows, span))],
+        table=owners,
+    )[0]
+
+
+def twin_step(blocks, twin, owners, distance, moved):
+    if not on_ring():
+        return ()
+    ahead, behind = twin_part(blocks, twin, owners, distance, moved)
+    return ring_hop(ahead, 1), ring_hop(behind, -1)
+
+
+def twin_end(blocks, twin, owners, moved):
+    if not on_ring():
+        return ring_end(blocks, owners, moved), ()
+    out, ahead, behind = twin_part(blocks, twin, owners, 0, moved)
+    return out, (ring_hop(ahead, 1), ring_hop(behind, -1))
+
+
+def ring_end(blocks, owners, moved):
+    if not on_ring():
+        return lax.psum_scatter(blocks, "fsdp", scatter_dimension=0, tiled=False)
+    return ring_part(blocks, owners, 0, upper_part(blocks.shape[1]), moved)[0]
+
+
+def halve_small(held, bit):
     me = lax.axis_index("fsdp")
-    held = table
-    bit = count // 2
+    parts = held.reshape(2, bit, -1)
+    high = (me & bit) != 0
+    keep = jnp.where(high, parts[1], parts[0])
+    give = jnp.where(high, parts[0], parts[1])
+    pairs = [(i, i ^ bit) for i in range(lax.axis_size("fsdp"))]
+    return keep + lax.ppermute(give, "fsdp", pairs)
+
+
+def finish_small(held, bit):
     while bit:
-        halves = held.reshape(2, bit, -1)
-        high = (me & bit) != 0
-        keep = jnp.where(high, halves[1], halves[0])
-        give = jnp.where(high, halves[0], halves[1])
-        held = keep + lax.ppermute(give, "fsdp", [(i, i ^ bit) for i in range(count)])
+        held = halve_small(held, bit)
         bit //= 2
-    held = held[0]
-    held = held + ctx_swap(held, 1)
-    return held + ctx_swap(held, 2)
+    return held
 
 
 def norm_stats(values):
@@ -462,10 +642,22 @@
             put_sorted(table, out_ref, places[1 + t], 0, tile)
 
 
-def attend_back_kernel(table, qkv_ref, grad_ref, mass_ref, out_ref, acc):
+def attend_back_kernel(table, *refs):
+    grad_refs, (qkv_ref, mass_ref, out_ref, acc, held) = refs[:4], refs[4:]
     pair = pl.program_id(0)
     final = pl.num_programs(0) - 1
-    refs = (table, qkv_ref, grad_ref, mass_ref, out_ref, acc)
+
+    @pl.when(pair == 0)
+    def _():
+        span = SLOTS * HD
+        rows = grad_refs[0].shape[0]
+        for j, ref in enumerate(grad_refs):
+            for p in range(span // PAIR):
+                held[p, j * rows : (j + 1) * rows, :] = ref[:, p * PAIR : (p + 1) * PAIR]
+            tail = jnp.concatenate([ref[:, span - HD :], jnp.zeros((rows, HD), bf16)], axis=1)
+            held[span // PAIR, j * rows : (j + 1) * rows, :] = tail
+
+    refs = (table, qkv_ref, held.at[pair], mass_ref, out_ref, acc)
 
     @pl.when(pair < final)
     def _():
@@ -502,22 +694,19 @@
     )
 
 
-def attend_back(table, qkv, grad, mass, gates):
+def attend_back(table, qkv, grads, mass, gates):
     length, columns = qkv.shape
     pairs = (SLOTS + 1) // 2
     return call(
         attend_back_kernel,
         "attend_back",
         pairs,
-        (qkv, grad, mass),
-        [
-            whole((length, columns)),
-            pl.BlockSpec((length, PAIR), lambda p, t: (0, p)),
-            pl.BlockSpec((1, 8, length), lambda p, t: (p, 0, 0)),
-        ],
+        (*grads, qkv, mass),
+        [whole(grad.shape) for grad in grads]
+        + [whole((length, columns)), pl.BlockSpec((1, 8, length), lambda p, t: (p, 0, 0))],
         [((length, columns), bf16)],
         [whole((length, columns))],
-        [pltpu.VMEM((4, length, HD), f32)],
+        [pltpu.VMEM((4, length, HD), f32), pltpu.VMEM((pairs, length, PAIR), bf16)],
         table,
         gates,
     )[0]
@@ -738,23 +927,36 @@
     )
 
 
-def plain_back_kernel(left, right, out):
-    out[...] = back_product(left[...], right[...]).astype(bf16)
-
-
-def plain_back(left, right, name, gates):
+def plain_back_kernel(left, right, keep, give):
+    value = back_product(left[...], right[...]).astype(bf16)
+    first = pl.program_id(0) < pl.num_programs(0) // 2
+
+    @pl.when(first)
+    def _():
+        keep[...] = value
+
+    @pl.when(jnp.logical_not(first))
+    def _():
+        give[...] = value
+
+
+def plain_back(left, right, name):
     length, inner = left.shape
     width = right.shape[0]
+    steps = length // QB
+    half = steps // 2
     return call(
         plain_back_kernel,
         name,
-        length // QB,
+        steps,
         (left, right),
         [rows_spec(QB, inner), whole(right.shape)],
-        [((length, width), bf16)],
-        [rows_spec(QB, width)],
-        gates=gates,
-    )[0]
+        [((length // 2, width), bf16)] * 2,
+        [
+            pl.BlockSpec((QB, width), lambda i: (jnp.minimum(i, half - 1), 0)),
+            pl.BlockSpec((QB, width), lambda i: (jnp.maximum(i - half, 0), 0)),
+        ],
+    )
 
 
 VECTOR_ROWS = 8
@@ -1054,6 +1256,7 @@
     peers = [rank ^ bit for bit in PEERS]
     owners = ring_owners() if on_ring() else None
 
+    always = group_order[0] >= 0
     peer_table = jnp.stack(peers).astype(jnp.int32)
 
     slots = jnp.argsort(group_order).astype(jnp.int32)
@@ -1161,115 +1364,209 @@
     )
 
     grad_proj = row_major(outer_sum(activated, grad_all).astype(bf16))
-    proj_scatter = Scatter(grad_proj.reshape(shards, unit_rows, width), owners)
-    proj_scatter.hop()
-    before_low, grad_bias_fc = feed_back(grad_blocks, proj_weights, slope, proj_scatter.given)
-    proj_scatter.hop(before_low)
-    grad_two = plain_back(before_low, fc_weights, "feed_back_two", proj_scatter.given)
-    kept_two, onward_two = scatter_near(*halves(grad_two))
-    proj_scatter.hop()
-    branch_two = row_major(
-        product(after(activated, *proj_scatter.given), proj_weights).astype(bf16)
-    )
-    grad_fc = row_major(
-        outer_sum(after(normed_two_all, onward_two, *proj_scatter.given), before_low).astype(bf16)
-    )
-    far_two = ctx_swap(onward_two, 2)
-    kept_branch, onward_branch = scatter_near(*halves(branch_two))
-    fc_scatter = Scatter(grad_fc.reshape(shards, shard_rows, shards * unit_rows), owners)
-    fc_scatter.hop()
-    proj_scatter.hop(*fc_scatter.given)
-    grad_middle, middle_low, heads_keep, heads_give, sums_two = norm_two_back(
-        peer_table,
-        kept_two,
-        far_two,
-        middle,
-        own_grad,
-        gain_two,
-        out_weights,
-        (onward_branch, *fc_scatter.given, *proj_scatter.given),
-    )
-    far_branch = ctx_swap(after(onward_branch, far_two), 2)
-    fc_scatter.hop()
-
-    heads_near = exchange_near(heads_keep.reshape(-1, span), heads_give.reshape(-1, span))
-    out_keep, out_give = out_weight_grad(
-        peer_table,
-        attended,
-        middle_low,
-        (*heads_near[1:], *fc_scatter.given, *proj_scatter.moved),
-    )
-    heads_far = exchange_far(heads_near[0], heads_near[1], after(heads_near[2], far_branch))
-    grad_heads = jnp.pad(jnp.concatenate(heads_far), ((0, 0), (0, PAIR - span % PAIR)))
-    tokens_out = (middle + added(kept_branch, far_branch) + bias_p).astype(bf16)[None]
-    kept_out, onward_out = scatter_near(
-        out_keep.reshape(-1, span), after(out_give.reshape(-1, span), heads_far[1])
-    )
-    grad_mixed = attend_back(table, mixed, grad_heads, mass, (out_give,))
-    far_out = ctx_swap(onward_out, 2)
-    fc_scatter.hop(grad_mixed)
-    grad_qkv = row_major(
-        outer_sum(normed_all, after(grad_mixed, onward_out, *fc_scatter.given)).astype(bf16)
-    )
-    qkv_scatter = Scatter(grad_qkv.reshape(shards, shard_rows, mixed_width), owners)
-    qkv_scatter.hop()
-    fc_scatter.hop(*qkv_scatter.given)
-    qkv_scatter.hop(*fc_scatter.given)
-    grad_one = plain_back(
-        grad_mixed, qkv_weights, "mixed_back", (far_out, *fc_scatter.given, *qkv_scatter.given)
-    )
-    kept_one, onward_one = scatter_near(*halves(grad_one))
-    shard_proj = proj_scatter.result(onward_one)
-    grad_attn_out = added(kept_out, far_out).astype(bf16)
-    out_scatter = Scatter(grad_attn_out.reshape(shards, shard_rows, span), owners)
-    out_scatter.hop(onward_one)
-    far_one = ctx_swap(onward_one, 2)
-    proj_pieces = gather_ctx(after(shard_proj, far_one))
-    qkv_scatter.hop(*fc_scatter.moved)
-    out_scatter.hop(*qkv_scatter.given)
-    fc_pieces = gather_ctx(after(fc_scatter.result(*qkv_scatter.given), proj_pieces[1]))
-    grad_tokens, sums_one = norm_one_back(
-        kept_one, far_one, own_tokens, grad_middle, gain_one, qkv_scatter.given
-    )
-    grad_tokens = grad_tokens[None]
-    qkv_scatter.hop(far_one)
-    out_scatter.hop(*qkv_scatter.given)
-    grad_w_proj = whole_rows(peer_table, proj_pieces, qkv_scatter.given)
-    shard_qkv = qkv_scatter.result(proj_pieces[1])
-    out_scatter.hop(shard_qkv)
-    qkv_pieces = gather_ctx(after(shard_qkv, fc_pieces[1]))
-    grad_w_fc = whole_fc(peer_table, fc_pieces, (shard_qkv,))
-
-    bias_sums = jnp.sum(grad_mixed.astype(f32), axis=0, keepdims=True)
-
-    def all_heads(part):
-        mine = jnp.concatenate(from_pairs(bias_sums, part, True), axis=1)
-        return lax.dynamic_update_slice(jnp.zeros((1, width), f32), mine, (0, rank * step))
-
-    grad_bias_fc = lax.dynamic_update_slice(
-        jnp.zeros((shards, ctx, unit_rows), f32),
-        grad_bias_fc.reshape(shards, 1, unit_rows),
-        (0, rank, 0),
-    )
-    small_grads = [
-        all_heads(0),
-        all_heads(2),
-        sums_two[2],
-        sums_two[3],
-        sums_one[0],
-        sums_one[1],
-        sums_two[0],
-        sums_two[1],
-        grad_bias_fc,
+    proj_blocks = grad_proj.reshape(shards, unit_rows, width)
+
+    def slot_one():
+        moved = ring_step(proj_blocks, owners, 4)
+        return moved, feed_back(grad_blocks, proj_weights, slope, ())
+
+    proj_moved, (before_low, grad_bias_fc) = slot(always, slot_one)
+
+    def slot_two():
+        moved = ring_step(proj_blocks, owners, 3, proj_moved)
+
+        def beside():
+            keep, give = plain_back(before_low, fc_weights, "feed_back_two")
+            return keep, ctx_swap(give, 1)
+
+        return moved, slot(always, beside)
+
+    proj_moved, (keep_two, got_two) = slot(always, slot_two)
+
+    def slot_three():
+        moved = ring_step(proj_blocks, owners, 2, proj_moved)
+
+        def beside():
+            kept, onward = pair_add(keep_two, got_two)
+            grad_fc = row_major(outer_sum(normed_two_all, before_low).astype(bf16))
+            branch = row_major(product(activated, proj_weights).astype(bf16))
+            return kept, ctx_swap(onward, 2), grad_fc, halves(branch)
+
+        return moved, slot(always, beside)
+
+    proj_moved, (kept_two, far_two, grad_fc, branch_halves) = slot(always, slot_three)
+    fc_blocks = grad_fc.reshape(shards, shard_rows, shards * unit_rows)
+
+    def slot_four():
+        moved = packed_step(proj_blocks, fc_blocks, owners, proj_moved)
+
+        def beside():
+            grad_middle, low, keep, give, sums = norm_two_back(
+                peer_table, kept_two, far_two, middle, own_grad, gain_two, out_weights, ()
+            )
+            near = exchange_near(keep.reshape(-1, span), give.reshape(-1, span))
+            out_pair = out_weight_grad(peer_table, attended, low, ())
+            return grad_middle, low, sums, exchange_far(*near), out_pair
+
+        return moved, slot(always, beside)
+
+    proj_moved, (grad_middle, middle_low, sums_two, heads, out_pair) = slot(
+        always, slot_four
+    )
+    out_keep, out_give = [value.reshape(-1, span) for value in out_pair]
+
+    def slot_five():
+        moved = ring_step(fc_blocks, owners, 3, proj_moved)
+
+        def beside():
+            shard = ring_end(proj_blocks, owners, proj_moved)
+            far, near, got = ctx_swap(shard, 2), ctx_swap(shard, 1), ctx_swap(out_give, 1)
+            return [shard, far, near], got, attend_back(table, mixed, heads, mass, ())
+
+        return moved, slot(always, beside)
+
+    fc_moved, (proj_pieces, got_out, grad_mixed) = slot(always, slot_five)
+
+    def slot_six():
+        moved = ring_step(fc_blocks, owners, 2, fc_moved)
+
+        def beside():
+            last = ctx_swap(proj_pieces[1], 1)
+            kept, first, second = pair_split(out_keep, got_out)
+            far = ctx_swap(first, 2)
+            grad_qkv = row_major(outer_sum(normed_all, grad_mixed).astype(bf16))
+            return last, kept, second, far, grad_qkv
+
+        return moved, slot(always, beside)
+
+    fc_moved, (proj_last, kept_out, onward_out, far_first, grad_qkv) = slot(always, slot_six)
+    proj_pieces = proj_pieces + [proj_last]
+    qkv_blocks = grad_qkv.reshape(shards, shard_rows, mixed_width)
+
+    def partial_table():
+        bias_sums = jnp.sum(grad_mixed.astype(f32), axis=0, keepdims=True)
+
+        def all_heads(part):
+            mine = jnp.concatenate(from_pairs(bias_sums, part, True), axis=1)
+            return lax.dynamic_update_slice(jnp.zeros((1, width), f32), mine, (0, rank * step))
+
+        whole_bias_fc = lax.dynamic_update_slice(
+            jnp.zeros((shards, ctx, unit_rows), f32),
+            grad_bias_fc.reshape(shards, 1, unit_rows),
+            (0, rank, 0),
+        )
+        return [
+            value.reshape(shards, -1)
+            for value in (all_heads(0), all_heads(2), *sums_two, whole_bias_fc)
+        ]
+
+    def whole_table(part, sums):
+        one = [value.reshape(shards, -1) for value in sums]
+        query, value, gain_two_sum, shift_two_sum, out, down, units = part
+        return jnp.concatenate(
+            [query, value, out, down, *one, gain_two_sum, shift_two_sum, units], axis=1
+        )
+
+    def slot_seven():
+        moved = packed_step(fc_blocks, qkv_blocks, owners, fc_moved)
+
+        def beside():
+            far = ctx_swap(onward_out, 2)
+
+            def inmost():
+                keep, give = plain_back(grad_mixed, qkv_weights, "mixed_back")
+                return pair_add(keep, ctx_swap(give, 1))
+
+            return far, slot(always, inmost)
+
+        return moved, slot(always, beside)
+
+    fc_moved, (far_second, (kept_one, onward_one)) = slot(always, slot_seven)
+
+    twin = [
+        value.reshape(-1, shard_rows, span) for value in (kept_out, far_first, far_second)
     ]
-    summed = reduce_small(
-        jnp.concatenate([value.reshape(shards, -1) for value in small_grads], axis=1)
-    )
+
+    def slot_eight():
+        qkv_next = twin_step(qkv_blocks, twin, owners, 3, fc_moved)
+
+        def beside():
+            far = ctx_swap(onward_one, 2)
+            got = ctx_swap(branch_halves[1], 1)
+
+            def inmost():
+                shard = ring_end(fc_blocks, owners, fc_moved)
+                return shard, partial_table(), whole_rows(peer_table, proj_pieces, ())
+
+            return far, got, slot(always, inmost)
+
+        return qkv_next, slot(always, beside)
+
+    qkv_moved, (far_one, got_branch, (shard_fc, table_part, grad_w_proj)) = slot(
+        always, slot_eight
+    )
+
+    def slot_nine():
+        qkv_next = twin_step(qkv_blocks, twin, owners, 2, qkv_moved)
+
+        def beside():
+            far, near = ctx_swap(shard_fc, 2), ctx_swap(shard_fc, 1)
+
+            def inmost():
+                kept, onward = pair_add(branch_halves[0], got_branch)
+                back, sums = norm_one_back(
+                    kept_one, far_one, own_tokens, grad_middle, gain_one, ()
+                )
+                return kept, onward, back, whole_table(table_part, sums)
+
+            return [shard_fc, far, near], slot(always, inmost)
+
+        return qkv_next, slot(always, beside)
+
+    qkv_moved, (fc_pieces, beside_nine) = slot(always, slot_nine)
+    kept_branch, onward_branch, grad_tokens, small = beside_nine
+
+    def slot_ten():
+        held = halve_small(small, shards // 2)
+        qkv_next = twin_step(qkv_blocks, twin, owners, 1, qkv_moved)
+        far, last = ctx_swap(onward_branch, 2), ctx_swap(fc_pieces[1], 1)
+        return qkv_next, held, far, last
+
+    qkv_moved, held, far_branch, fc_last = slot(always, slot_ten)
+
+    def slot_eleven():
+        shard_qkv, out_next = twin_end(qkv_blocks, twin, owners, qkv_moved)
+        far, near = ctx_swap(shard_qkv, 2), ctx_swap(shard_qkv, 1)
+        next_held = halve_small(held, shards // 4)
+
+        def beside():
+            out = (middle + added(kept_branch, far_branch) + bias_p).astype(bf16)[None]
+            return whole_fc(peer_table, fc_pieces + [fc_last], ()), out
+
+        return [shard_qkv, far, near], out_next, next_held, slot(always, beside)
+
+    qkv_pieces, out_moved, held, (grad_w_fc, tokens_out) = slot(always, slot_eleven)
+    def slot_twelve():
+        shard_out = twin_last(twin, owners, out_moved)
+        swaps = [ctx_swap(shard_out, 2), ctx_swap(shard_out, 1)]
+        return [shard_out, *swaps], ctx_swap(qkv_pieces[1], 1), halve_small(held, shards // 8)
+
+    out_pieces, qkv_last, held = slot(always, slot_twelve)
+    held = finish_small(held, shards // 16)
+
+    def slot_thirteen():
+        last = ctx_swap(out_pieces[1], 1)
+        total = held[0] + ctx_swap(held[0], 1)
+        return last, total, slot(
+            always, lambda: whole_qkv(peer_table, qkv_pieces + [qkv_last], width)
+        )
+
+    out_last, summed, grad_w_qkv = slot(always, slot_thirteen)
+    summed = summed + ctx_swap(summed, 2)
+    whole_attn_out = join_windows(peer_table, out_pieces + [out_last], width).astype(f32)
     shares = [summed[t * shard_rows : (t + 1) * shard_rows] for t in range(8)]
     share_fc = summed[8 * shard_rows :]
-
-    whole_attn_out = join_windows(peer_table, gather_ctx(out_scatter.result()), width).astype(f32)
-    grad_w_qkv = whole_qkv(peer_table, qkv_pieces, width)
+    grad_tokens = grad_tokens[None]
 
     return (
         tokens_out,

time: 633 us -> 557 us (0.88)
  waiting for transfers between devices: 173 us -> 147 us
  Pallas kernels: 244 us -> 220 us
  starting transfers between devices: 85.8 us -> 69.3 us
  local copies, waits for them, and re-layouts: 67.6 us -> 52.8 us
    ppermute x48 -> x38, waiting for transfers between devices: 130 us -> 86.8 us  [ring_hop(): return row_major(lax.ppermute(row_major(value), 'fsdp', pairs))]
    pallas_call x43 -> x37, Pallas kernels: 244 us -> 220 us  [call(): pl.pallas_call(body, grid_spec=pltpu.PrefetchScalarGridSpec(num_scalar_pr...]
    unnamed x150 -> x50, local copies, waits for them, and re-layouts: 28.8 us -> 6.03 us
    ppermute x48 -> x38, starting transfers between devices: 61.4 us -> 39.6 us  [ring_hop(): return row_major(lax.ppermute(row_major(value), 'fsdp', pairs))]
    ppermute x3, waiting for transfers between devices: 3.58 us -> 15.4 us  [halve_small(): return keep + lax.ppermute(give, 'fsdp', pairs)]
    reshape x4 -> x1, local copies, waits for them, and re-layouts: 11.1 us -> 1.08 us  [tiled(): return block.reshape(-1, 8, block.shape[1])]
    cond x0 -> x17, local copies, waits for them, and re-layouts: none -> 6.44 us
    ppermute x38 -> x39, waiting for transfers between devices: 39.1 us -> 45 us  [ctx_swap(): got = row_major(lax.ppermute(row_major(tiled(block)), 'ctx', pairs))]
  transfers between devices with their start and end apart: 89 -> 80, of which waited for: 31 -> 24; matrix products, arithmetic and copies ran while one was open for 14% -> 16% of each run, Pallas kernels for 33% -> 33%
where the time goes in v4:
time: 557 us; the launch traced here: 547 us
  Pallas kernels  220 us (39%)
  waiting for transfers between devices  147 us (26%)
  starting transfers between devices  69.3 us (12%)
  local copies, waits for them, and re-layouts  52.8 us (9%)
  matrix products  39.5 us (7%)
  other arithmetic  14.5 us (3%)
    pallas_call x37, Pallas kernels, call(): pl.pallas_call(body, grid_spec=pltpu.PrefetchScalarGridSpec(num_scalar_pr...  220 us
    ppermute x38, waiting for transfers between devices, ring_hop(): return row_major(lax.ppermute(row_major(value), 'fsdp', pairs))  86.8 us
    ppermute x39, waiting for transfers between devices, ctx_swap(): got = row_major(lax.ppermute(row_major(tiled(block)), 'ctx', pairs))  45 us
    ppermute x38, starting transfers between devices, ring_hop(): return row_major(lax.ppermute(row_major(value), 'fsdp', pairs))  39.6 us
    dot_general x3, matrix products, outer_sum(): lax.dot_general(left_op, right_op, (((0,), (0,)), ((), ())), preferred_el...  32.6 us
    ppermute x39, starting transfers between devices, ctx_swap(): got = row_major(lax.ppermute(row_major(tiled(block)), 'ctx', pairs))  26.7 us
    ppermute x3, waiting for transfers between devices, halve_small(): return keep + lax.ppermute(give, 'fsdp', pairs)  15.4 us
  transfers between devices with their start and end apart: 80, of which 24 were waited for; matrix products, arithmetic and copies ran while one was open for 16% of the time, Pallas kernels for 33%

profile of v4, /device:TPU:0, one launch (start us, length us, event | category | flops | bytes accessed | tf_op | source)
XLA Modules:
  0.0 546.7 jit_solution(4152717065354959632)
XLA Ops:
  6.7 18.1 %collective-permute-done.55.refs_3_ = bf16[208,1856]{1,0:T(8,128)(2,1)} collective-permute-done((bf16[208,1856]{1,0:T(8,128)(2,1)}, bf16[208,1856]{1,0:T(8,128)(2,1)}, u32[]{:S(2)}, u32[]{:S(2)}) %collective-permute-start.55) | collective-permute-done | bytes 772128 | tf_op jit(solution)/shard_map/ppermute | solution.py:155
  73.0 27.6 %collective-permute-done.60.refs_8_ = bf16[104,1856]{1,0:T(8,128)(2,1)} collective-permute-done((bf16[104,1856]{1,0:T(8,128)(2,1)S(1)}, bf16[104,1856]{1,0:T(8,128)(2,1)}, u32[]{:S(2)}, u32[]{:S(2)}) %collective-permute-start.60) | collective-permute-done | bytes 386080 | tf_op jit(solution)/shard_map/ppermute | solution.py:155
  234.5 16.3 %conditional.26 = (bf16[96,1600]{1,0:T(8,128)(2,1)}, bf16[104,1600]{1,0:T(8,128)(2,1)}, bf16[1024,1600]{1,0:T(8,128)(2,1)}, f32[1,1600]{1,0:T(1,128)S(1)}) conditional(s32[]{:T(128)} %convert_element_type.82, () %tuple.269, (s32[8]{0:T(128)S(1)}, bf16[8,200,1600]{2,1,0:T(8,128)(2,1)}, bf16[256,1600]{1,0:T(8,128)(2,1)}, bf16[256,1600]{1,0:T(8,128)(2,1)}, ...), branch_computations={%region_1.2_spmd, %region_2.3_spmd} | conditional | flops 2097152 | bytes 3923242 | solution.py:57
  250.8 21.0 %conditional.27 = (bf16[200,1600]{1,0:T(8,128)(2,1)}, bf16[200,1600]{1,0:T(8,128)(2,1)}, bf16[512,1600]{1,0:T(8,128)(2,1)}, bf16[512,1600]{1,0:T(8,128)(2,1)}) conditional(s32[]{:T(128)} %convert_element_type.82, () %tuple.268, (s32[8]{0:T(128)S(1)}, bf16[8,200,1600]{2,1,0:T(8,128)(2,1)}, bf16[96,1600]{1,0:T(8,128)(2,1)}, ...), branch_computations={%region_3.4_spmd, %region_4.7_spmd} | conditional | flops 2097153 | bytes 11804861 | solution.py:57
  256.0 15.8 %conditional = (bf16[512,1600]{1,0:T(8,128)(2,1)}, bf16[512,1600]{1,0:T(8,128)(2,1)}) conditional(s32[]{:T(128)} %convert_element_type.5, () %tuple.145, (bf16[1024,1600]{1,0:T(8,128)(2,1)}, bf16[1600,1600]{1,0:T(8,128)(2,1)}) %tuple.146), branch_computations={%region_5.5_spmd, %region_6.6_spmd} | conditional | flops 1048576 | bytes 6619192 | solution.py:57
  271.8 31.1 %conditional.28 = (bf16[200,1600]{1,0:T(8,128)(2,1)}, bf16[200,1600]{1,0:T(8,128)(2,1)}, f32[256,1600]{1,0:T(8,128)}, bf16[256,1600]{1,0:T(8,128)(2,1)}, bf16[51...) conditional(s32[]{:T(128)} %convert_element_type.82, () %tuple.256, ...), branch_computations={%region_7.8_spmd, %region_8.11_spmd} | conditional | flops 10492055552 | bytes 67510616 | solution.py:57
  277.3 25.4 %conditional.1 = (f32[256,1600]{1,0:T(8,128)}, bf16[256,1600]{1,0:T(8,128)(2,1)}, bf16[512,1600]{1,0:T(8,128)(2,1)}, bf16[512,1600]{1,0:T(8,128)(2,1)}, bf16[8,200,1600]{2,1,0:T(8,128)(2,1)}) conditional(s32[]{:T(128)} %convert_element_type.20, () %tuple.151, (bf16[512,1600]{1,0:T(8,128)(2,1)}, bf16[512,1600]{1,0:T(8,128)(2,1)}, ...), branch_computations={%region_9.9_spmd, %region_10.10_spmd} | conditional | flops 10491006976 | bytes 62324892 | solution.py:57
  302.9 32.8 %conditional.29 = (bf16[296,1600]{1,0:T(8,128)(2,1)}, bf16[304,1600]{1,0:T(8,128)(2,1)}, f32[256,1600]{1,0:T(8,128)}, f32[4,1600]{1,0:T(4,128)}, bf16[256,448]{1...) conditional(s32[]{:T(128)} %convert_element_type.82, () %tuple.274, ...), branch_computations={%region_11.12_spmd, %region_12.15_spmd} | conditional | flops 4063233 | bytes 16061753 | solution.py:57
  308.9 26.8 %conditional.2 = (f32[256,1600]{1,0:T(8,128)}, f32[4,1600]{1,0:T(4,128)}, bf16[256,448]{1,0:T(8,128)(2,1)}, bf16[256,448]{1,0:T(8,128)(2,1)}, bf16[256,448]{1,0:...) conditional(s32[]{:T(128)} %convert_element_type.25, () %tuple.157, ...), branch_computations={%region_13.13_spmd, %region_14.14_spmd} | conditional | flops 3014656 | bytes 8315988 | solution.py:57
  335.7 30.7 %conditional.30 = (bf16[200,1600]{1,0:T(8,128)(2,1)}, bf16[200,1600]{1,0:T(8,128)(2,1)}, bf16[200,1600]{1,0:T(8,128)(2,1)}, bf16[200,1600]{1,0:T(8,128)(2,1)}, b...) conditional(s32[]{:T(128)} %convert_element_type.82, () %tuple.273, ...), branch_computations={%region_15.16_spmd, %region_16.19_spmd} | conditional | flops 3145729 | bytes 33964484 | solution.py:57
  341.4 24.8 %conditional.3 = (bf16[200,1600]{1,0:T(8,128)(2,1)}, bf16[200,1600]{1,0:T(8,128)(2,1)}, bf16[200,1600]{1,0:T(8,128)(2,1)}, bf16[3200,448]{1,0:T(8,128)(2,1)}, bf16[1024,1408]{1,0:T(8,128)(2,1)}) conditional(s32[]{:T(128)} %convert_element_type.30, () %tuple.163, (s32[8]{0:T(128)S(1)}, bf16[8,200,1600]{2,1,0:T(8,128)(2,1)}, ...), branch_computations={%region_17.17_spmd, %region_18.18_spmd} | conditional | flops 2097152 | bytes 28254396 | solution.py:57
  346.9 19.3 %attend_back.1 = bf16[1024,1408]{1,0:T(8,128)(2,1)} custom-call(s32[9]{0:T(128)S(1)} %get-tuple-element.661.refs_0_, bf16[256,448]{1,0:T(8,128)(2,1)} %get-tuple-element.662.refs_1_, bf16[256,448]{1,0:T(8,128)(2,1)} %get-tuple-element.663.refs_2_, bf16[256,448]{1,0:T(8,128)(2,1)} %get-tuple-element.664.refs_3_, bf16[256,448]{1,0:T(8,128)(2,1)} %get-tuple-element.665.refs_4_, ...), custom_call_target="tpu_custom_call" | custom-call | flops 1048576 | bytes 65536 | tf_op jit(solution)/shard_map/cond/branch_1_fun/cond/branch_1_fun/attend_back/pallas_call | solution.py:731
  366.4 32.7 %conditional.31 = (bf16[200,1600]{1,0:T(8,128)(2,1)}, bf16[200,1600]{1,0:T(8,128)(2,1)}, bf16[200,1600]{1,0:T(8,128)(2,1)}, bf16[800,448]{1,0:T(8,128)(2,1)}, bf...) conditional(s32[]{:T(128)} %convert_element_type.82, () %tuple.255, ...), branch_computations={%region_19.20_spmd, %region_20.23_spmd} | conditional | flops 4618084352 | bytes 34451784 | solution.py:57
  371.9 27.2 %conditional.4 = (bf16[200,1600]{1,0:T(8,128)(2,1)}, bf16[800,448]{1,0:T(8,128)(2,1)}, bf16[8,200,448]{2,1,0:T(8,128)(2,1)}, bf16[4,200,448]{2,1,0:T(8,128)(2,1)}, bf16[8,200,1408]{2,1,0:T(8,128)(2,1)}) conditional(s32[]{:T(128)} %convert_element_type.39, () %tuple.169, (bf16[200,1600]{1,0:T(8,128)(2,1)}, bf16[3200,448]{1,0:T(8,128)(2,1)}, ...), branch_computations={%region_21.21_spmd, %region_22.22_spmd} | conditional | flops 4617035776 | bytes 29266068 | solution.py:57
  399.2 28.1 %conditional.32 = (bf16[296,1600]{1,0:T(8,128)(2,1)}, bf16[304,1600]{1,0:T(8,128)(2,1)}, f32[256,1600]{1,0:T(8,128)}, bf16[256,1600]{1,0:T(8,128)(2,1)}, bf16[4,200,448]{2,1,0:T(8,128)(2,1)}) conditional(s32[]{:T(128)} %convert_element_type.82, () %tuple.281, (s32[8]{0:T(128)S(1)}, bf16[8,200,1600]{2,1,0:T(8,128)(2,1)}, ...), branch_computations={%region_23.24_spmd, %region_24.29_spmd} | conditional | flops 3145730 | bytes 23851326 | solution.py:57
  405.2 20.9 %conditional.6 = (f32[256,1600]{1,0:T(8,128)}, bf16[256,1600]{1,0:T(8,128)(2,1)}, bf16[4,200,448]{2,1,0:T(8,128)(2,1)}) conditional(s32[]{:T(128)} %convert_element_type.50, () %tuple.178, (pred[]{:T(512)}, bf16[1024,1408]{1,0:T(8,128)(2,1)}, bf16[1600,1408]{1,0:T(8,128)(2,1)}, bf16[800,448]{1,0:T(8,128)(2,1)}) %tuple.179), branch_computations={%region_25.25_spmd, %region_26.28_spmd} | conditional | flops 2097153 | bytes 16105633 | solution.py:57
  406.9 19.2 %conditional.5 = ((f32[256,1600]{1,0:T(8,128)}, bf16[256,1600]{1,0:T(8,128)(2,1)})) conditional(s32[]{:T(128)} %convert_element_type.46, () %tuple.175, (bf16[1024,1408]{1,0:T(8,128)(2,1)}, bf16[1600,1408]{1,0:T(8,128)(2,1)}) %tuple.176), branch_computations={%region_27.26_spmd, %region_28.27_spmd} | conditional | flops 2097152 | bytes 13238348 | solution.py:57
  427.2 27.8 %conditional.33 = (bf16[200,1856]{1,0:T(8,128)(2,1)}, bf16[200,1856]{1,0:T(8,128)(2,1)}, bf16[256,1600]{1,0:T(8,128)(2,1)}, bf16[512,1600]{1,0:T(8,128)(2,1)}, b...) conditional(s32[]{:T(128)} %convert_element_type.82, () %tuple.280, ...), branch_computations={%region_29.30_spmd, %region_30.36_spmd} | conditional | flops 6030601 | bytes 21659836 | solution.py:57
  433.1 21.7 %conditional.8 = (bf16[256,1600]{1,0:T(8,128)(2,1)}, bf16[512,1600]{1,0:T(8,128)(2,1)}, bf16[200,1600]{1,0:T(8,128)(2,1)}, f32[8,200]{1,0:T(8,128)}, f32[8,200]{...) conditional(s32[]{:T(128)} %convert_element_type.54, () %tuple.188, ...), branch_computations={%region_31.31_spmd, %region_32.35_spmd} | conditional | flops 4982024 | bytes 15654783 | solution.py:57
  434.5 17.1 %conditional.7 = (bf16[200,1600]{1,0:T(8,128)(2,1)}, f32[8,200]{1,0:T(8,128)}, f32[8,200]{1,0:T(8,128)}, f32[8,200]{1,0:T(8,128)}, f32[8,200]{1,0:T(8,128)}, /*i...) conditional(s32[]{:T(128)} %convert_element_type.52, () %tuple.185, ...), branch_computations={%region_33.32_spmd, %region_34.34_spmd} | conditional | flops 4982023 | bytes 5824106 | solution.py:57
  455.0 25.1 %conditional.34 = (bf16[200,1856]{1,0:T(8,128)(2,1)}, bf16[200,1856]{1,0:T(8,128)(2,1)}, bf16[200,1600]{1,0:T(8,128)(2,1)}, bf16[200,1600]{1,0:T(8,128)(2,1)}, b...) conditional(s32[]{:T(128)} %convert_element_type.82, () %tuple.279, ...), branch_computations={%region_36.37_spmd, %region_37.42_spmd} | conditional | flops 3145730 | bytes 19867720 | solution.py:57
  461.1 16.3 %conditional.10 = (bf16[200,1600]{1,0:T(8,128)(2,1)}, bf16[200,1600]{1,0:T(8,128)(2,1)}, bf16[200,1600]{1,0:T(8,128)(2,1)}, f32[256,1600]{1,0:T(8,128)}, bf16[25...) conditional(s32[]{:T(128)} %convert_element_type.73, () %tuple.198, ...), branch_computations={%region_38.38_spmd, %region_39.41_spmd} | conditional | flops 2097153 | bytes 10585899 | solution.py:57
  480.1 27.3 %conditional.35 = (bf16[200,1856]{1,0:T(8,128)(2,1)}, bf16[200,1856]{1,0:T(8,128)(2,1)}, f32[4,2400]{1,0:T(4,128)S(1)}, bf16[256,1600]{1,0:T(8,128)(2,1)}, bf16[200,1600]{1,0:T(8,128)(2,1)}) conditional(s32[]{:T(128)} %convert_element_type.82, () %tuple.278, (s32[8]{0:T(128)S(1)}, bf16[8,200,1408]{2,1,0:T(8,128)(2,1)}, ...), branch_computations={%region_42.43_spmd, %region_43.44_spmd} | conditional | flops 1077380 | bytes 12264219 | solution.py:57
  507.4 16.5 %conditional.36 = (bf16[200,1408]{1,0:T(8,128)(2,1)}, bf16[200,1408]{1,0:T(8,128)(2,1)}, bf16[200,1408]{1,0:T(8,128)(2,1)}, bf16[200,448]{1,0:T(8,128)(2,1)}, bf...) conditional(s32[]{:T(128)} %convert_element_type.82, () %tuple.254, ...), branch_computations={%region_44.45_spmd, %region_45.48_spmd} | conditional | flops 4159557 | bytes 13793942 | solution.py:57
  (370 shorter events, 517.3 us)
Async XLA Ops:
  63.7 37.6 %collective-permute-start.62 = (bf16[400,1600]{1,0:T(8,128)(2,1)}, bf16[400,1600]{1,0:T(8,128)(2,1)S(1)}, u32[]{:S(2)}, u32[]{:S(2)}) collective-permute-start(bf16[400,1600]{1,0:T(8,128)(2,1)} %pad_maximum_fusion.3.refs_1_), channel_id=1, source_target_pairs={{0,2},{2,4},{4,6},{6,7},{7,5},{5,3},{3,1},{1,0},{8,10},{10,12},{12... | collective-permute-start | bytes 3840008 | tf_op jit(solution)/shard_map/ppermute | solution.py:155
  64.9 36.4 %collective-permute-start.63 = (bf16[400,1600]{1,0:T(8,128)(2,1)}, bf16[400,1600]{1,0:T(8,128)(2,1)}, u32[]{:S(2)}, u32[]{:S(2)}) collective-permute-start(bf16[400,1600]{1,0:T(8,128)(2,1)} %pad_maximum_fusion.3.refs_1_), channel_id=1, source_target_pairs={{0,1},{2,0},{4,2},{6,4},{7,6},{5,7},{3,5},{1,3},{8,9},{10,8},{12,1... | collective-permute-start | bytes 3840008 | tf_op jit(solution)/shard_map/ppermute | solution.py:155
  67.1 46.1 %collective-permute-start.51 = (bf16[32,8,1600]{2,1,0:T(8,128)(2,1)}, bf16[32,8,1600]{2,1,0:T(8,128)(2,1)}, u32[]{:S(2)}, u32[]{:S(2)}) collective-permute-start(bf16[32,8,1600]{2,1,0:T(8,128)(2,1)} %collective-permute-done.50), channel_id=1, source_target_pairs={{0,8},{8,0},{16,24},{24,16},{1,9},{9,1},{17,25},{25,17},{2,10},{10... | collective-permute-start | bytes 2457608 | tf_op jit(solution)/shard_map/ppermute | solution.py:79
  67.1 33.5 %collective-permute-start.60 = (bf16[104,1856]{1,0:T(8,128)(2,1)S(1)}, bf16[104,1856]{1,0:T(8,128)(2,1)}, u32[]{:S(2)}, u32[]{:S(2)}) collective-permute-start(bf16[104,1856]{1,0:T(8,128)(2,1)S(1)} %slice.290), channel_id=1, source_target_pairs={{0,2},{2,4},{4,6},{6,7},{7,5},{5,3},{3,1},{1,0},{8,10},{10,12},{12... | collective-permute-start | bytes 1158152 | tf_op jit(solution)/shard_map/ppermute | solution.py:155
  70.0 31.2 %collective-permute-start.61 = (bf16[104,1856]{1,0:T(8,128)(2,1)}, bf16[104,1856]{1,0:T(8,128)(2,1)}, u32[]{:S(2)}, u32[]{:S(2)}) collective-permute-start(bf16[104,1856]{1,0:T(8,128)(2,1)} %slice.291), channel_id=1, source_target_pairs={{0,1},{2,0},{4,2},{6,4},{7,6},{5,7},{3,5},{1,3},{8,9},{10,8},{12,1... | collective-permute-start | bytes 1158152 | tf_op jit(solution)/shard_map/ppermute | solution.py:155
  108.6 34.2 %collective-permute-start.64 = (bf16[200,8,448]{2,1,0:T(8,128)(2,1)}, bf16[200,8,448]{2,1,0:T(8,128)(2,1)}, u32[]{:S(2)}, u32[]{:S(2)}) collective-permute-start(bf16[200,8,448]{2,1,0:T(8,128)(2,1)} %bitcast.131), channel_id=1, source_target_pairs={{0,16},{8,24},{16,0},{24,8},{1,17},{9,25},{17,1},{25,9},{2,18},{10... | collective-permute-start | bytes 4300808 | tf_op jit(solution)/shard_map/ppermute | solution.py:79
  111.6 32.9 %collective-permute-start.69 = (bf16[400,1600]{1,0:T(8,128)(2,1)}, bf16[400,1600]{1,0:T(8,128)(2,1)}, u32[]{:S(2)}, u32[]{:S(2)}) collective-permute-start(bf16[400,1600]{1,0:T(8,128)(2,1)} %copy-done.8), channel_id=1, source_target_pairs={{0,2},{2,4},{4,6},{6,7},{7,5},{5,3},{3,1},{1,0},{8,10},{10,12},{12... | collective-permute-start | bytes 3840008 | tf_op jit(solution)/shard_map/ppermute | solution.py:155
  113.2 32.9 %collective-permute-start.70 = (bf16[400,1600]{1,0:T(8,128)(2,1)}, bf16[400,1600]{1,0:T(8,128)(2,1)}, u32[]{:S(2)}, u32[]{:S(2)}) collective-permute-start(bf16[400,1600]{1,0:T(8,128)(2,1)} %collective-permute-done.63.refs_11_.refs_3_), channel_id=1, source_target_pairs={{0,1},{2,0},{4,2},{6,4},{7,6},{5,7},{3,5},{1,3},{8,9},{10,8},{12,1... | collective-permute-start | bytes 3840008 | tf_op jit(solution)/shard_map/ppermute | solution.py:155
  144.5 31.9 %collective-permute-start.74 = (bf16[400,1600]{1,0:T(8,128)(2,1)}, bf16[400,1600]{1,0:T(8,128)(2,1)}, u32[]{:S(2)}, u32[]{:S(2)}) collective-permute-start(bf16[400,1600]{1,0:T(8,128)(2,1)} %collective-permute-done.69.refs_4_), channel_id=1, source_target_pairs={{0,2},{2,4},{4,6},{6,7},{7,5},{5,3},{3,1},{1,0},{8,10},{10,12},{12... | collective-permute-start | bytes 3840008 | tf_op jit(solution)/shard_map/ppermute | solution.py:155
  146.1 33.1 %collective-permute-start.76 = (bf16[400,1600]{1,0:T(8,128)(2,1)}, bf16[400,1600]{1,0:T(8,128)(2,1)}, u32[]{:S(2)}, u32[]{:S(2)}) collective-permute-start(bf16[400,1600]{1,0:T(8,128)(2,1)} %collective-permute-done.70.refs_5_), channel_id=1, source_target_pairs={{0,1},{2,0},{4,2},{6,4},{7,6},{5,7},{3,5},{1,3},{8,9},{10,8},{12,1... | collective-permute-start | bytes 3840008 | tf_op jit(solution)/shard_map/ppermute | solution.py:155
  173.1 23.6 %collective-permute-start.72 = (bf16[32,8,1600]{2,1,0:T(8,128)(2,1)}, bf16[32,8,1600]{2,1,0:T(8,128)(2,1)}, u32[]{:S(2)}, u32[]{:S(2)}) collective-permute-start(bf16[32,8,1600]{2,1,0:T(8,128)(2,1)} %bitcast.138), channel_id=1, source_target_pairs={{0,16},{8,24},{16,0},{24,8},{1,17},{9,25},{17,1},{25,9},{2,18},{10... | collective-permute-start | bytes 2457608 | tf_op jit(solution)/shard_map/ppermute | solution.py:79
  180.8 27.0 %collective-permute-start.73 = (bf16[32,8,1600]{2,1,0:T(8,128)(2,1)}, bf16[32,8,1600]{2,1,0:T(8,128)(2,1)}, u32[]{:S(2)}, u32[]{:S(2)}) collective-permute-start(bf16[32,8,1600]{2,1,0:T(8,128)(2,1)} %bitcast.139), channel_id=1, source_target_pairs={{0,8},{8,0},{16,24},{24,16},{1,9},{9,1},{17,25},{25,17},{2,10},{10... | collective-permute-start | bytes 2457608 | tf_op jit(solution)/shard_map/ppermute | solution.py:79
  197.5 25.3 %collective-permute-start.71 = (bf16[32,8,1600]{2,1,0:T(8,128)(2,1)}, bf16[32,8,1600]{2,1,0:T(8,128)(2,1)}, u32[]{:S(2)}, u32[]{:S(2)}) collective-permute-start(bf16[32,8,1600]{2,1,0:T(8,128)(2,1)} %bitcast.64), channel_id=1, source_target_pairs={{0,8},{8,0},{16,24},{24,16},{1,9},{9,1},{17,25},{25,17},{2,10},{10... | collective-permute-start | bytes 2457608 | tf_op jit(solution)/shard_map/ppermute | solution.py:79
  275.3 27.4 %collective-permute-start.43 = (bf16[200,1600]{1,0:T(8,128)(2,1)}, bf16[200,1600]{1,0:T(8,128)(2,1)}, u32[]{:S(2)}, u32[]{:S(2)}) collective-permute-start(bf16[200,1600]{1,0:T(8,128)(2,1)} %get-tuple-element.603), channel_id=1, source_target_pairs={{0,2},{2,4},{4,6},{6,7},{7,5},{5,3},{3,1},{1,0},{8,10},{10,12},{12... | collective-permute-start | bytes 1920008 | tf_op jit(solution)/shard_map/cond/branch_1_fun/ppermute | solution.py:155
  276.7 25.9 %collective-permute-start.44 = (bf16[200,1600]{1,0:T(8,128)(2,1)}, bf16[200,1600]{1,0:T(8,128)(2,1)}, u32[]{:S(2)}, u32[]{:S(2)}) collective-permute-start(bf16[200,1600]{1,0:T(8,128)(2,1)} %get-tuple-element.604), channel_id=1, source_target_pairs={{0,1},{2,0},{4,2},{6,4},{7,6},{5,7},{3,5},{1,3},{8,9},{10,8},{12,1... | collective-permute-start | bytes 1920008 | tf_op jit(solution)/shard_map/cond/branch_1_fun/ppermute | solution.py:155
  306.9 28.8 %collective-permute-start.28 = (bf16[304,1600]{1,0:T(8,128)(2,1)}, bf16[304,1600]{1,0:T(8,128)(2,1)}, u32[]{:S(2)}, u32[]{:S(2)}) collective-permute-start(bf16[304,1600]{1,0:T(8,128)(2,1)} %get-tuple-element.638), channel_id=1, source_target_pairs={{0,1},{2,0},{4,2},{6,4},{7,6},{5,7},{3,5},{1,3},{8,9},{10,8},{12,1... | collective-permute-start | bytes 2918408 | tf_op jit(solution)/shard_map/cond/branch_1_fun/ppermute | solution.py:155
  307.4 28.3 %collective-permute-start.27 = (bf16[296,1600]{1,0:T(8,128)(2,1)}, bf16[296,1600]{1,0:T(8,128)(2,1)}, u32[]{:S(2)}, u32[]{:S(2)}) collective-permute-start(bf16[296,1600]{1,0:T(8,128)(2,1)} %get-tuple-element.637), channel_id=1, source_target_pairs={{0,2},{2,4},{4,6},{6,7},{7,5},{5,3},{3,1},{1,0},{8,10},{10,12},{12... | collective-permute-start | bytes 2841608 | tf_op jit(solution)/shard_map/cond/branch_1_fun/ppermute | solution.py:155
  339.4 26.8 %collective-permute-start.8 = (bf16[200,1600]{1,0:T(8,128)(2,1)}, bf16[200,1600]{1,0:T(8,128)(2,1)}, u32[]{:S(2)}, u32[]{:S(2)}) collective-permute-start(bf16[200,1600]{1,0:T(8,128)(2,1)} %get-tuple-element.672), channel_id=1, source_target_pairs={{0,2},{2,4},{4,6},{6,7},{7,5},{5,3},{3,1},{1,0},{8,10},{10,12},{12... | collective-permute-start | bytes 1920008 | tf_op jit(solution)/shard_map/cond/branch_1_fun/ppermute | solution.py:155
  340.8 25.4 %collective-permute-start.9 = (bf16[200,1600]{1,0:T(8,128)(2,1)}, bf16[200,1600]{1,0:T(8,128)(2,1)}, u32[]{:S(2)}, u32[]{:S(2)}) collective-permute-start(bf16[200,1600]{1,0:T(8,128)(2,1)} %get-tuple-element.673), channel_id=1, source_target_pairs={{0,1},{2,0},{4,2},{6,4},{7,6},{5,7},{3,5},{1,3},{8,9},{10,8},{12,1... | collective-permute-start | bytes 1920008 | tf_op jit(solution)/shard_map/cond/branch_1_fun/ppermute | solution.py:155
  341.8 24.4 %collective-permute-start.7 = (bf16[400,8,448]{2,1,0:T(8,128)(2,1)}, bf16[400,8,448]{2,1,0:T(8,128)(2,1)}, u32[]{:S(2)}, u32[]{:S(2)}) collective-permute-start(bf16[400,8,448]{2,1,0:T(8,128)(2,1)} %bitcast.17), channel_id=1, source_target_pairs={{0,8},{8,0},{16,24},{24,16},{1,9},{9,1},{17,25},{25,17},{2,10},{10... | collective-permute-start | bytes 8601608 | tf_op jit(solution)/shard_map/cond/branch_1_fun/cond/branch_1_fun/ppermute | solution.py:79
  369.9 29.3 %collective-permute-start.47 = (bf16[200,1600]{1,0:T(8,128)(2,1)}, bf16[200,1600]{1,0:T(8,128)(2,1)}, u32[]{:S(2)}, u32[]{:S(2)}) collective-permute-start(bf16[200,1600]{1,0:T(8,128)(2,1)} %get-tuple-element.701), channel_id=1, source_target_pairs={{0,2},{2,4},{4,6},{6,7},{7,5},{5,3},{3,1},{1,0},{8,10},{10,12},{12... | collective-permute-start | bytes 1920008 | tf_op jit(solution)/shard_map/cond/branch_1_fun/ppermute | solution.py:155
  371.4 27.8 %collective-permute-start.48 = (bf16[200,1600]{1,0:T(8,128)(2,1)}, bf16[200,1600]{1,0:T(8,128)(2,1)}, u32[]{:S(2)}, u32[]{:S(2)}) collective-permute-start(bf16[200,1600]{1,0:T(8,128)(2,1)} %get-tuple-element.702), channel_id=1, source_target_pairs={{0,1},{2,0},{4,2},{6,4},{7,6},{5,7},{3,5},{1,3},{8,9},{10,8},{12,1... | collective-permute-start | bytes 1920008 | tf_op jit(solution)/shard_map/cond/branch_1_fun/ppermute | solution.py:155
  403.2 24.1 %collective-permute-start.13 = (bf16[304,1600]{1,0:T(8,128)(2,1)}, bf16[304,1600]{1,0:T(8,128)(2,1)}, u32[]{:S(2)}, u32[]{:S(2)}) collective-permute-start(bf16[304,1600]{1,0:T(8,128)(2,1)} %get-tuple-element.730), channel_id=1, source_target_pairs={{0,1},{2,0},{4,2},{6,4},{7,6},{5,7},{3,5},{1,3},{8,9},{10,8},{12,1... | collective-permute-start | bytes 2918408 | tf_op jit(solution)/shard_map/cond/branch_1_fun/ppermute | solution.py:155
  431.1 23.7 %collective-permute-start.40 = (bf16[200,1856]{1,0:T(8,128)(2,1)}, bf16[200,1856]{1,0:T(8,128)(2,1)}, u32[]{:S(2)}, u32[]{:S(2)}) collective-permute-start(bf16[200,1856]{1,0:T(8,128)(2,1)} %get-tuple-element.783), channel_id=1, source_target_pairs={{0,2},{2,4},{4,6},{6,7},{7,5},{5,3},{3,1},{1,0},{8,10},{10,12},{12... | collective-permute-start | bytes 2227208 | tf_op jit(solution)/shard_map/cond/branch_1_fun/ppermute | solution.py:155
  (87 other events, 1385.0 us)

commit v5 on v4

--- a/solution.py
+++ b/solution.py
@@ -20,7 +20,7 @@
 norm_eps = 1e-05
 masked_low = -1e30
 LIGHT = pl.CostEstimate(flops=1 << 20, transcendentals=0, bytes_accessed=1 << 16)
-VMEM_LIMIT = 56 << 20
+VMEM_LIMIT = 40 << 20
 f32 = jnp.float32
 bf16 = jnp.bfloat16
 
@@ -177,17 +177,21 @@
         self.pieces = [block]
         self.forth = self.back = block
 
-    def hop(self, *gate):
+    def step(self):
         if not on_ring():
-            return
-        k = (len(self.pieces) + 1) // 2
+            return ()
         forth, back = self.forth, self.back
-        if k == HALF:
+        if len(self.pieces) == 2 * HALF - 1:
             forth, back = forth[: self.cut], back[self.cut :]
-        if gate:
-            forth, back = after(forth, *gate), after(back, *gate)
-        self.forth, self.back = ring_hop(forth, 1), ring_hop(back, -1)
-        self.pieces += [self.forth, self.back]
+        return ring_hop(forth, 1), ring_hop(back, -1)
+
+    def take(self, moved):
+        if moved:
+            self.forth, self.back = moved
+            self.pieces += list(moved)
+
+    def hop(self):
+        self.take(self.step())
 
     def arrived(self):
         return (self.forth, self.back) if on_ring() else ()
@@ -197,6 +201,12 @@
             whole = lax.all_gather(self.block, "fsdp", axis=0, tiled=False)
             return [whole[:, top : top + n, c : c + w] for c, w, top, n in columns]
         return collect(self.pieces, owners, self.cut, columns, gates)
+
+
+def spread_small(held, bit):
+    got = lax.ppermute(held, "fsdp", [(i, i ^ bit) for i in range(lax.axis_size("fsdp"))])
+    low = (lax.axis_index("fsdp") & bit) == 0
+    return jnp.concatenate([jnp.where(low, held, got), jnp.where(low, got, held)])
 
 
 def collect_kernel(cut, columns, owners, *refs):
@@ -720,7 +730,19 @@
     return pl.BlockSpec((rows, columns), lambda i, *_: (i, 0))
 
 
-def call(kernel, name, grid, operands, specs, outs, out_specs, scratch=(), table=None, gates=()):
+def call(
+    kernel,
+    name,
+    grid,
+    operands,
+    specs,
+    outs,
+    out_specs,
+    scratch=(),
+    table=None,
+    gates=(),
+    limit=VMEM_LIMIT,
+):
     tables = () if table is None else (table,)
     first = len(tables) + len(operands)
     count = len(gates)
@@ -738,7 +760,7 @@
             scratch_shapes=list(scratch),
         ),
         out_shape=[jax.ShapeDtypeStruct(shape, kind) for shape, kind in outs],
-        compiler_params=pltpu.CompilerParams(vmem_limit_bytes=VMEM_LIMIT),
+        compiler_params=pltpu.CompilerParams(vmem_limit_bytes=limit),
         cost_estimate=LIGHT,
         name=name,
     )(*tables, *operands, *gates)
@@ -961,10 +983,11 @@
 
 VECTOR_ROWS = 8
 FC_START = 2 * PAIR
+VECTOR_WIDTH = 9 * PAIR
 
 
 def attn_block_kernel(place, qkv, out_weights, *refs):
-    vectors, bias_fc, block = refs[:VECTOR_ROWS], refs[VECTOR_ROWS], refs[VECTOR_ROWS + 1]
+    vectors, (bias_fc, block, lines_out) = refs[:VECTOR_ROWS], refs[VECTOR_ROWS:]
     step, span = BASE * HD, SLOTS * HD
     width = out_weights.shape[1]
     rows = qkv.shape[0]
@@ -976,21 +999,21 @@
     for p in range(SLOTS // 2):
         for t in range(3):
             first = (3 * p + t) * PAIR
-            block[:rows, first : first + PAIR] = parts[t][:, p * PAIR : (p + 1) * PAIR]
+            block[:, first : first + PAIR] = parts[t][:, p * PAIR : (p + 1) * PAIR]
     rest = [part[:, (SLOTS - 1) * HD :] for part in parts] + [jnp.zeros((rows, HD), bf16)]
     first = 3 * (SLOTS // 2) * PAIR
     for p in range(2):
-        block[:rows, first + p * PAIR : first + (p + 1) * PAIR] = jnp.concatenate(
+        block[:, first + p * PAIR : first + (p + 1) * PAIR] = jnp.concatenate(
             rest[2 * p : 2 * p + 2], axis=1
         )
     start = pl.multiple_of(place[0] * step, PAIR)
-    block[:rows, first + 2 * PAIR :] = out_weights[:, pl.ds(start, span)]
-    block[rows:, :] = jnp.zeros((VECTOR_ROWS, block.shape[1]), bf16)
+    block[:, first + 2 * PAIR :] = out_weights[:, pl.ds(start, span)]
     lines = jnp.stack([vector[...].astype(f32) for vector in vectors])
-    block[rows:, : lines.shape[1]] = lines.astype(bf16)
+    lines_out[...] = jnp.zeros_like(lines_out)
+    lines_out[:, : lines.shape[1]] = lines.astype(bf16)
     units = bias_fc.shape[0]
     line = jnp.broadcast_to(bias_fc[...].astype(f32)[None], (VECTOR_ROWS, units))
-    block[rows:, FC_START : FC_START + units] = line.astype(bf16)
+    lines_out[:, FC_START : FC_START + units] = line.astype(bf16)
 
 
 def form_attn_block(place, qkv, out_weights, vectors, bias_fc):
@@ -1003,10 +1026,11 @@
         1,
         (qkv, out_weights, *vectors),
         [whole(value.shape) for value in (qkv, out_weights, *vectors)],
-        [((rows + VECTOR_ROWS, columns), bf16)],
-        [whole((rows + VECTOR_ROWS, columns))],
+        [((rows, columns), bf16), ((VECTOR_ROWS, VECTOR_WIDTH), bf16)],
+        [whole((rows, columns)), whole((VECTOR_ROWS, VECTOR_WIDTH))],
         table=place,
-    )[0]
+        limit=56 << 20,
+    )
 
 
 def whole_rows_kernel(table, *refs):
@@ -1264,7 +1288,7 @@
     slot_rows = (place * 2 + slots % 2) * GROUP
     table = jnp.concatenate([slot_rows, (rank == ctx - 1).astype(jnp.int32)[None]])
 
-    attn_block = form_attn_block(
+    attn_block, vectors = form_attn_block(
         rank[None].astype(jnp.int32),
         w_qkv,
         w_attn_out,
@@ -1275,6 +1299,10 @@
     own_grad = out_grad[0]
     attn_gather = Gather(attn_block)
     attn_gather.hop()
+    small, bit = vectors[None], 1
+    while bit < shards:
+        small = spread_small(small, bit)
+        bit *= 2
     w_fc = after(w_fc, attn_block)
     fc_block = jnp.concatenate(
         [
@@ -1290,36 +1318,42 @@
     token_blocks = gather_ctx(own_tokens)
     grad_blocks = gather_ctx(after(own_grad, token_blocks[1]))
     attn_gather.hop()
-    attn_gather.hop(feed_block)
-    feed_gather = Gather(after(feed_block, *attn_gather.arrived()))
-    feed_gather.hop()
     attn_gather.hop()
-
-    qkv_weights, out_columns, small = attn_gather.result(
-        owners,
-        (
-            (0, mixed_width, 0, shard_rows),
-            (mixed_width, span, 0, shard_rows),
-            (0, attn_width, shard_rows, VECTOR_ROWS),
-        ),
-        feed_gather.arrived(),
-    )
-    qkv_weights = qkv_weights.reshape(width, mixed_width)
-    small = small.astype(f32)
-    bias_q, bias_v, bias_o, bias_p, gain_one, shift_one, gain_two, shift_two = [
-        small[:, t, :shard_rows].reshape(-1) for t in range(VECTOR_ROWS)
-    ]
-    bias_fc = lax.dynamic_index_in_dim(
-        small[:, 0, FC_START : FC_START + ctx * unit_rows].reshape(shards, ctx, unit_rows),
-        rank,
-        1,
-        False,
-    ).reshape(-1)
+    feed_gather = Gather(feed_block)
 
     def my_bias(vector):
         return lax.dynamic_slice(vector, (rank * step,), (span,))[None]
 
-    bias_mixed = to_pairs([my_bias(bias_q), jnp.zeros((1, span), f32), my_bias(bias_v)])
+    def slot_zero():
+        moved = attn_gather.step(), feed_gather.step()
+
+        def beside():
+            lines = small.astype(f32)
+            values = [lines[:, t, :shard_rows].reshape(-1) for t in range(VECTOR_ROWS)]
+            units = lax.dynamic_index_in_dim(
+                lines[:, 0, FC_START : FC_START + ctx * unit_rows].reshape(
+                    shards, ctx, unit_rows
+                ),
+                rank,
+                1,
+                False,
+            ).reshape(-1)
+            mixed_bias = to_pairs(
+                [my_bias(values[0]), jnp.zeros((1, span), f32), my_bias(values[1])]
+            )
+            return mixed_bias, values[2:], units
+
+        return moved, slot(always, beside)
+
+    (attn_moved, feed_moved), (bias_mixed, values, bias_fc) = slot(always, slot_zero)
+    attn_gather.take(attn_moved)
+    feed_gather.take(feed_moved)
+    bias_o, bias_p, gain_one, shift_one, gain_two, shift_two = values
+    qkv_weights, out_columns = attn_gather.result(
+        owners, ((0, mixed_width, 0, shard_rows), (mixed_width, span, 0, shard_rows))
+    )
+    qkv_weights = qkv_weights.reshape(width, mixed_width)
+
     normed_all, mixed = norm_mixed(
         [after(token_blocks[0], grad_blocks[3])] + token_blocks[1:],
         gain_one,

time: 557 us -> 524 us (0.941)
  Pallas kernels: 220 us -> 195 us
  starting transfers between devices: 69.3 us -> 85.2 us
  local copies, waits for them, and re-layouts: 52.8 us -> 42.4 us
  waiting for transfers between devices: 147 us -> 141 us
    pallas_call x37, Pallas kernels: 220 us -> 195 us  [call(): pl.pallas_call(body, grid_spec=pltpu.PrefetchScalarGridSpec(num_scalar_pr...]
    ppermute x38, waiting for transfers between devices: 86.8 us -> 62.9 us  [ring_hop(): return row_major(lax.ppermute(row_major(value), 'fsdp', pairs))]
    ppermute x39, waiting for transfers between devices: 45 us -> 55.5 us  [ctx_swap(): got = row_major(lax.ppermute(row_major(tiled(block)), 'ctx', pairs))]
    ppermute x0 -> x3, waiting for transfers between devices: none -> 7.94 us  [spread_small(): lax.ppermute(held, 'fsdp', [(i, i ^ bit) for i in range(lax.axis_size('fs...]
    ppermute x38, starting transfers between devices: 39.6 us -> 47.3 us  [ring_hop(): return row_major(lax.ppermute(row_major(value), 'fsdp', pairs))]
    ppermute x0 -> x3, starting transfers between devices: none -> 6.46 us  [spread_small(): lax.ppermute(held, 'fsdp', [(i, i ^ bit) for i in range(lax.axis_size('fs...]
    another operation x17 -> x5, local copies, waits for them, and re-layouts: 5.76 us -> 0.02 us  [the longest x1 0.69 us: norm_mixed(): shift[None]]
  transfers between devices with their start and end apart: 80 -> 83, of which waited for: 24 -> 26; matrix products, arithmetic and copies ran while one was open for 16% -> 16% of each run, Pallas kernels for 33% -> 32%
where the time goes in v5:
time: 524 us; the launch traced here: 518 us
  Pallas kernels  195 us (37%)
  waiting for transfers between devices  141 us (27%)
  starting transfers between devices  85.2 us (16%)
  local copies, waits for them, and re-layouts  42.4 us (8%)
  matrix products  38.2 us (7%)
  other arithmetic  13.1 us (2%)
    pallas_call x37, Pallas kernels, call(): pl.pallas_call(body, grid_spec=pltpu.PrefetchScalarGridSpec(num_scalar_pr...  195 us
    ppermute x38, waiting for transfers between devices, ring_hop(): return row_major(lax.ppermute(row_major(value), 'fsdp', pairs))  62.9 us
    ppermute x39, waiting for transfers between devices, ctx_swap(): got = row_major(lax.ppermute(row_major(tiled(block)), 'ctx', pairs))  55.5 us
    ppermute x38, starting transfers between devices, ring_hop(): return row_major(lax.ppermute(row_major(value), 'fsdp', pairs))  47.3 us
    dot_general x3, matrix products, outer_sum(): lax.dot_general(left_op, right_op, (((0,), (0,)), ((), ())), preferred_el...  31.3 us
    ppermute x39, starting transfers between devices, ctx_swap(): got = row_major(lax.ppermute(row_major(tiled(block)), 'ctx', pairs))  26.6 us
    ppermute x3, waiting for transfers between devices, halve_small(): return keep + lax.ppermute(give, 'fsdp', pairs)  14.3 us
  transfers between devices with their start and end apart: 83, of which 26 were waited for; matrix products, arithmetic and copies ran while one was open for 16% of the time, Pallas kernels for 32%

profile of v5, /device:TPU:0, one launch (start us, length us, event | category | flops | bytes accessed | tf_op | source)
XLA Modules:
  0.0 517.6 jit_solution(17232138671985746288)
XLA Ops:
  64.8 38.5 %conditional.28 = (bf16[96,1856]{1,0:T(8,128)(2,1)}, bf16[104,1856]{1,0:T(8,128)(2,1)}, bf16[400,1600]{1,0:T(8,128)(2,1)}, bf16[400,1600]{1,0:T(8,128)(2,1)}, f3...) conditional(s32[]{:T(128)} %convert_element_type.86, () %tuple.292, ...), branch_computations={%region_1.2_spmd, %region_2.5_spmd} | conditional | flops 73736 | bytes 15522009 | solution.py:57
  82.0 18.5 %collective-permute-done.42 = bf16[96,1856]{1,0:T(8,128)(2,1)} collective-permute-done((bf16[96,1856]{1,0:T(8,128)(2,1)}, bf16[96,1856]{1,0:T(8,128)(2,1)}, u32[]{:S(2)}, u32[]{:S(2)}) %collective-permute-start.42) | collective-permute-done | bytes 356384 | tf_op jit(solution)/shard_map/cond/branch_1_fun/ppermute | solution.py:155
  219.7 14.6 %conditional.29 = (bf16[96,1600]{1,0:T(8,128)(2,1)}, bf16[104,1600]{1,0:T(8,128)(2,1)}, bf16[1024,1600]{1,0:T(8,128)(2,1)}, f32[1,1600]{1,0:T(1,128)S(1)}) conditional(s32[]{:T(128)} %convert_element_type.86, () %tuple.301, (s32[8]{0:T(128)S(1)}, bf16[8,200,1600]{2,1,0:T(8,128)(2,1)}, bf16[256,1600]{1,0:T(8,128)(2,1)S(1)}, ...), branch_computations={%region_5.6_spmd, %region_6.7_spmd} | conditional | flops 2097152 | bytes 3923242 | solution.py:57
  234.3 19.7 %conditional.30 = (bf16[200,1600]{1,0:T(8,128)(2,1)}, bf16[200,1600]{1,0:T(8,128)(2,1)}, bf16[512,1600]{1,0:T(8,128)(2,1)}, bf16[512,1600]{1,0:T(8,128)(2,1)}) conditional(s32[]{:T(128)} %convert_element_type.86, () %tuple.300, (s32[8]{0:T(128)S(1)}, bf16[8,200,1600]{2,1,0:T(8,128)(2,1)}, bf16[96,1600]{1,0:T(8,128)(2,1)}, ...), branch_computations={%region_7.8_spmd, %region_8.11_spmd} | conditional | flops 2097153 | bytes 11804861 | solution.py:57
  238.6 15.2 %conditional.1 = (bf16[512,1600]{1,0:T(8,128)(2,1)}, bf16[512,1600]{1,0:T(8,128)(2,1)}) conditional(s32[]{:T(128)} %convert_element_type.22, () %tuple.179, (bf16[1024,1600]{1,0:T(8,128)(2,1)}, bf16[1600,1600]{1,0:T(8,128)(2,1)}) %tuple.180), branch_computations={%region_9.9_spmd, %region_10.10_spmd} | conditional | flops 1048576 | bytes 6619192 | solution.py:57
  254.0 29.4 %conditional.31 = (bf16[200,1600]{1,0:T(8,128)(2,1)}, bf16[200,1600]{1,0:T(8,128)(2,1)}, f32[256,1600]{1,0:T(8,128)}, bf16[256,1600]{1,0:T(8,128)(2,1)}, bf16[51...) conditional(s32[]{:T(128)} %convert_element_type.86, () %tuple.289, ...), branch_computations={%region_11.12_spmd, %region_12.15_spmd} | conditional | flops 10492055552 | bytes 80617848 | solution.py:57
  258.6 24.7 %conditional.2 = (f32[256,1600]{1,0:T(8,128)}, bf16[256,1600]{1,0:T(8,128)(2,1)}, bf16[512,1600]{1,0:T(8,128)(2,1)}, bf16[512,1600]{1,0:T(8,128)(2,1)}, bf16[8,200,1600]{2,1,0:T(8,128)(2,1)}) conditional(s32[]{:T(128)} %convert_element_type.37, () %tuple.185, (bf16[512,1600]{1,0:T(8,128)(2,1)}, bf16[512,1600]{1,0:T(8,128)(2,1)}, ...), branch_computations={%region_13.13_spmd, %region_14.14_spmd} | conditional | flops 10491006976 | bytes 75432120 | solution.py:57
  283.4 31.7 %conditional.32 = (bf16[296,1600]{1,0:T(8,128)(2,1)}, bf16[304,1600]{1,0:T(8,128)(2,1)}, f32[256,1600]{1,0:T(8,128)}, f32[4,1600]{1,0:T(4,128)}, bf16[256,448]{1...) conditional(s32[]{:T(128)} %convert_element_type.86, () %tuple.306, ...), branch_computations={%region_15.16_spmd, %region_16.19_spmd} | conditional | flops 4063233 | bytes 18506640 | solution.py:57
  288.3 26.6 %conditional.3 = (f32[256,1600]{1,0:T(8,128)}, f32[4,1600]{1,0:T(4,128)}, bf16[256,448]{1,0:T(8,128)(2,1)}, bf16[256,448]{1,0:T(8,128)(2,1)}, bf16[256,448]{1,0:...) conditional(s32[]{:T(128)} %convert_element_type.42, () %tuple.191, ...), branch_computations={%region_17.17_spmd, %region_18.18_spmd} | conditional | flops 3014656 | bytes 10760876 | solution.py:57
  315.2 28.8 %conditional.33 = (bf16[200,1600]{1,0:T(8,128)(2,1)}, bf16[200,1600]{1,0:T(8,128)(2,1)}, bf16[200,1600]{1,0:T(8,128)(2,1)}, bf16[200,1600]{1,0:T(8,128)(2,1)}, b...) conditional(s32[]{:T(128)} %convert_element_type.86, () %tuple.305, ...), branch_computations={%region_19.20_spmd, %region_20.23_spmd} | conditional | flops 3145729 | bytes 33440168 | solution.py:57
  319.9 24.0 %conditional.4 = (bf16[200,1600]{1,0:T(8,128)(2,1)}, bf16[200,1600]{1,0:T(8,128)(2,1)}, bf16[200,1600]{1,0:T(8,128)(2,1)}, bf16[3200,448]{1,0:T(8,128)(2,1)}, bf16[1024,1408]{1,0:T(8,128)(2,1)}) conditional(s32[]{:T(128)} %convert_element_type.48, () %tuple.197, (s32[8]{0:T(128)S(1)}, bf16[8,200,1600]{2,1,0:T(8,128)(2,1)}, ...), branch_computations={%region_21.21_spmd, %region_22.22_spmd} | conditional | flops 2097152 | bytes 28254396 | solution.py:57
  324.5 19.4 %attend_back.1 = bf16[1024,1408]{1,0:T(8,128)(2,1)} custom-call(s32[9]{0:T(128)S(1)} %get-tuple-element.701.refs_0_, bf16[256,448]{1,0:T(8,128)(2,1)} %get-tuple-element.702.refs_1_, bf16[256,448]{1,0:T(8,128)(2,1)} %get-tuple-element.703.refs_2_, bf16[256,448]{1,0:T(8,128)(2,1)} %get-tuple-element.704.refs_3_, bf16[256,448]{1,0:T(8,128)(2,1)} %get-tuple-element.705.refs_4_, ...), custom_call_target="tpu_custom_call" | custom-call | flops 1048576 | bytes 65536 | tf_op jit(solution)/shard_map/cond/branch_1_fun/cond/branch_1_fun/attend_back/pallas_call | solution.py:753
  343.9 32.5 %conditional.34 = (bf16[200,1600]{1,0:T(8,128)(2,1)}, bf16[200,1600]{1,0:T(8,128)(2,1)}, bf16[200,1600]{1,0:T(8,128)(2,1)}, bf16[800,448]{1,0:T(8,128)(2,1)}, bf...) conditional(s32[]{:T(128)} %convert_element_type.86, () %tuple.288, ...), branch_computations={%region_23.24_spmd, %region_24.27_spmd} | conditional | flops 4618084352 | bytes 34451784 | solution.py:57
  348.6 27.7 %conditional.5 = (bf16[200,1600]{1,0:T(8,128)(2,1)}, bf16[800,448]{1,0:T(8,128)(2,1)}, bf16[8,200,448]{2,1,0:T(8,128)(2,1)}, bf16[4,200,448]{2,1,0:T(8,128)(2,1)}, bf16[8,200,1408]{2,1,0:T(8,128)(2,1)}) conditional(s32[]{:T(128)} %convert_element_type.50, () %tuple.203, (bf16[200,1600]{1,0:T(8,128)(2,1)}, bf16[3200,448]{1,0:T(8,128)(2,1)}, ...), branch_computations={%region_25.25_spmd, %region_26.26_spmd} | conditional | flops 4617035776 | bytes 29266068 | solution.py:57
  376.5 26.8 %conditional.35 = (bf16[296,1600]{1,0:T(8,128)(2,1)}, bf16[304,1600]{1,0:T(8,128)(2,1)}, f32[256,1600]{1,0:T(8,128)}, bf16[256,1600]{1,0:T(8,128)(2,1)}, bf16[4,200,448]{2,1,0:T(8,128)(2,1)}) conditional(s32[]{:T(128)} %convert_element_type.86, () %tuple.313, (s32[8]{0:T(128)S(1)}, bf16[8,200,1600]{2,1,0:T(8,128)(2,1)}, ...), branch_computations={%region_27.28_spmd, %region_28.33_spmd} | conditional | flops 3145730 | bytes 17297698 | solution.py:57
  381.3 19.4 %conditional.7 = (f32[256,1600]{1,0:T(8,128)}, bf16[256,1600]{1,0:T(8,128)(2,1)}, bf16[4,200,448]{2,1,0:T(8,128)(2,1)}) conditional(s32[]{:T(128)} %convert_element_type.55, () %tuple.212, (pred[]{:T(512)}, bf16[1024,1408]{1,0:T(8,128)(2,1)}, bf16[1600,1408]{1,0:T(8,128)(2,1)}, bf16[800,448]{1,0:T(8,128)(2,1)}) %tuple.213), branch_computations={%region_29.29_spmd, %region_30.32_spmd} | conditional | flops 2097153 | bytes 9552005 | solution.py:57
  383.1 14.6 %conditional.6 = ((f32[256,1600]{1,0:T(8,128)}, bf16[256,1600]{1,0:T(8,128)(2,1)})) conditional(s32[]{:T(128)} %convert_element_type.54, () %tuple.209, (bf16[1024,1408]{1,0:T(8,128)(2,1)}, bf16[1600,1408]{1,0:T(8,128)(2,1)}) %tuple.210), branch_computations={%region_31.30_spmd, %region_32.31_spmd} | conditional | flops 2097152 | bytes 6684720 | solution.py:57
  403.3 26.5 %conditional.36 = (bf16[200,1856]{1,0:T(8,128)(2,1)}, bf16[200,1856]{1,0:T(8,128)(2,1)}, bf16[256,1600]{1,0:T(8,128)(2,1)}, bf16[512,1600]{1,0:T(8,128)(2,1)}, b...) conditional(s32[]{:T(128)} %convert_element_type.86, () %tuple.312, ...), branch_computations={%region_33.34_spmd, %region_34.40_spmd} | conditional | flops 6030601 | bytes 21659836 | solution.py:57
  408.1 21.7 %conditional.9 = (bf16[256,1600]{1,0:T(8,128)(2,1)}, bf16[512,1600]{1,0:T(8,128)(2,1)}, bf16[200,1600]{1,0:T(8,128)(2,1)}, f32[8,200]{1,0:T(8,128)}, f32[8,200]{...) conditional(s32[]{:T(128)} %convert_element_type.76, () %tuple.222, ...), branch_computations={%region_35.35_spmd, %region_36.39_spmd} | conditional | flops 4982024 | bytes 15654783 | solution.py:57
  409.6 17.1 %conditional.8 = (bf16[200,1600]{1,0:T(8,128)(2,1)}, f32[8,200]{1,0:T(8,128)}, f32[8,200]{1,0:T(8,128)}, f32[8,200]{1,0:T(8,128)}, f32[8,200]{1,0:T(8,128)}, /*i...) conditional(s32[]{:T(128)} %convert_element_type.58, () %tuple.219, ...), branch_computations={%region_37.36_spmd, %region_38.38_spmd} | conditional | flops 4982023 | bytes 5824106 | solution.py:57
  429.8 24.3 %conditional.37 = (bf16[200,1856]{1,0:T(8,128)(2,1)}, bf16[200,1856]{1,0:T(8,128)(2,1)}, bf16[200,1600]{1,0:T(8,128)(2,1)}, bf16[200,1600]{1,0:T(8,128)(2,1)}, b...) conditional(s32[]{:T(128)} %convert_element_type.86, () %tuple.311, ...), branch_computations={%region_40.41_spmd, %region_41.46_spmd} | conditional | flops 3145730 | bytes 19854920 | solution.py:57
  434.9 16.3 %conditional.11 = (bf16[200,1600]{1,0:T(8,128)(2,1)}, bf16[200,1600]{1,0:T(8,128)(2,1)}, bf16[200,1600]{1,0:T(8,128)(2,1)}, f32[256,1600]{1,0:T(8,128)}, bf16[25...) conditional(s32[]{:T(128)} %convert_element_type.78, () %tuple.232, ...), branch_computations={%region_42.42_spmd, %region_43.45_spmd} | conditional | flops 2097153 | bytes 10573099 | solution.py:57
  454.1 25.0 %conditional.38 = (bf16[200,1856]{1,0:T(8,128)(2,1)}, bf16[200,1856]{1,0:T(8,128)(2,1)}, f32[4,2400]{1,0:T(4,128)S(1)}, bf16[256,1600]{1,0:T(8,128)(2,1)}, bf16[200,1600]{1,0:T(8,128)(2,1)}) conditional(s32[]{:T(128)} %convert_element_type.86, () %tuple.310, (s32[8]{0:T(128)S(1)}, bf16[8,200,1408]{2,1,0:T(8,128)(2,1)}, ...), branch_computations={%region_46.47_spmd, %region_47.48_spmd} | conditional | flops 1077380 | bytes 12264219 | solution.py:57
  479.1 16.7 %conditional.39 = (bf16[200,1408]{1,0:T(8,128)(2,1)}, bf16[200,1408]{1,0:T(8,128)(2,1)}, bf16[200,1408]{1,0:T(8,128)(2,1)}, bf16[200,448]{1,0:T(8,128)(2,1)}, bf...) conditional(s32[]{:T(128)} %convert_element_type.86, () %tuple.287, ...), branch_computations={%region_48.49_spmd, %region_49.52_spmd} | conditional | flops 4159557 | bytes 20347570 | solution.py:57
  (376 shorter events, 523.3 us)
Async XLA Ops:
  26.6 23.2 %collective-permute-start.62 = (bf16[200,1856]{1,0:T(8,128)(2,1)}, bf16[200,1856]{1,0:T(8,128)(2,1)S(1)}, u32[]{:S(2)}, u32[]{:S(2)}) collective-permute-start(bf16[200,1856]{1,0:T(8,128)(2,1)} %collective-permute-done.61.refs_3_), channel_id=1, source_target_pairs={{0,1},{2,0},{4,2},{6,4},{7,6},{5,7},{3,5},{1,3},{8,9},{10,8},{12,1... | collective-permute-start | bytes 2227208 | tf_op jit(solution)/shard_map/ppermute | solution.py:155
  53.1 59.5 %collective-permute-start.55 = (bf16[32,8,1600]{2,1,0:T(8,128)(2,1)}, bf16[32,8,1600]{2,1,0:T(8,128)(2,1)}, u32[]{:S(2)}, u32[]{:S(2)}) collective-permute-start(bf16[32,8,1600]{2,1,0:T(8,128)(2,1)} %collective-permute-done.54), channel_id=1, source_target_pairs={{0,8},{8,0},{16,24},{24,16},{1,9},{9,1},{17,25},{25,17},{2,10},{10... | collective-permute-start | bytes 2457608 | tf_op jit(solution)/shard_map/ppermute | solution.py:79
  64.8 38.5 %collective-permute-start.44 = (bf16[400,1600]{1,0:T(8,128)(2,1)}, bf16[400,1600]{1,0:T(8,128)(2,1)}, u32[]{:S(2)}, u32[]{:S(2)}) collective-permute-start(bf16[400,1600]{1,0:T(8,128)(2,1)} %get-tuple-element.592), channel_id=1, source_target_pairs={{0,2},{2,4},{4,6},{6,7},{7,5},{5,3},{3,1},{1,0},{8,10},{10,12},{12... | collective-permute-start | bytes 3840008 | tf_op jit(solution)/shard_map/cond/branch_1_fun/ppermute | solution.py:155
  68.8 34.5 %collective-permute-start.45 = (bf16[400,1600]{1,0:T(8,128)(2,1)}, bf16[400,1600]{1,0:T(8,128)(2,1)}, u32[]{:S(2)}, u32[]{:S(2)}) collective-permute-start(bf16[400,1600]{1,0:T(8,128)(2,1)} %get-tuple-element.592), channel_id=1, source_target_pairs={{0,1},{2,0},{4,2},{6,4},{7,6},{5,7},{3,5},{1,3},{8,9},{10,8},{12,1... | collective-permute-start | bytes 3840008 | tf_op jit(solution)/shard_map/cond/branch_1_fun/ppermute | solution.py:155
  70.6 32.7 %collective-permute-start.43 = (bf16[104,1856]{1,0:T(8,128)(2,1)}, bf16[104,1856]{1,0:T(8,128)(2,1)}, u32[]{:S(2)}, u32[]{:S(2)}) collective-permute-start(bf16[104,1856]{1,0:T(8,128)(2,1)} %slice.175), channel_id=1, source_target_pairs={{0,1},{2,0},{4,2},{6,4},{7,6},{5,7},{3,5},{1,3},{8,9},{10,8},{12,1... | collective-permute-start | bytes 1158152 | tf_op jit(solution)/shard_map/cond/branch_1_fun/ppermute | solution.py:155
  72.4 28.1 %collective-permute-start.42 = (bf16[96,1856]{1,0:T(8,128)(2,1)}, bf16[96,1856]{1,0:T(8,128)(2,1)}, u32[]{:S(2)}, u32[]{:S(2)}) collective-permute-start(bf16[96,1856]{1,0:T(8,128)(2,1)} %slice.174), channel_id=1, source_target_pairs={{0,2},{2,4},{4,6},{6,7},{7,5},{5,3},{3,1},{1,0},{8,10},{10,12},{12... | collective-permute-start | bytes 1069064 | tf_op jit(solution)/shard_map/cond/branch_1_fun/ppermute | solution.py:155
  108.8 31.7 %collective-permute-start.67 = (bf16[200,8,448]{2,1,0:T(8,128)(2,1)}, bf16[200,8,448]{2,1,0:T(8,128)(2,1)}, u32[]{:S(2)}, u32[]{:S(2)}) collective-permute-start(bf16[200,8,448]{2,1,0:T(8,128)(2,1)} %bitcast.72), channel_id=1, source_target_pairs={{0,16},{8,24},{16,0},{24,8},{1,17},{9,25},{17,1},{25,9},{2,18},{10... | collective-permute-start | bytes 4300808 | tf_op jit(solution)/shard_map/ppermute | solution.py:79
  110.9 31.4 %collective-permute-start.72 = (bf16[400,1600]{1,0:T(8,128)(2,1)}, bf16[400,1600]{1,0:T(8,128)(2,1)}, u32[]{:S(2)}, u32[]{:S(2)}) collective-permute-start(bf16[400,1600]{1,0:T(8,128)(2,1)} %get-tuple-element.1138.refs_2_), channel_id=1, source_target_pairs={{0,2},{2,4},{4,6},{6,7},{7,5},{5,3},{3,1},{1,0},{8,10},{10,12},{12... | collective-permute-start | bytes 3840008 | tf_op jit(solution)/shard_map/ppermute | solution.py:155
  112.5 31.6 %collective-permute-start.73 = (bf16[400,1600]{1,0:T(8,128)(2,1)}, bf16[400,1600]{1,0:T(8,128)(2,1)}, u32[]{:S(2)}, u32[]{:S(2)}) collective-permute-start(bf16[400,1600]{1,0:T(8,128)(2,1)} %get-tuple-element.1139.refs_3_), channel_id=1, source_target_pairs={{0,1},{2,0},{4,2},{6,4},{7,6},{5,7},{3,5},{1,3},{8,9},{10,8},{12,1... | collective-permute-start | bytes 3840008 | tf_op jit(solution)/shard_map/ppermute | solution.py:155
  142.4 31.6 %collective-permute-start.77 = (bf16[400,1600]{1,0:T(8,128)(2,1)}, bf16[400,1600]{1,0:T(8,128)(2,1)S(1)}, u32[]{:S(2)}, u32[]{:S(2)}) collective-permute-start(bf16[400,1600]{1,0:T(8,128)(2,1)} %collective-permute-done.72.refs_4_), channel_id=1, source_target_pairs={{0,2},{2,4},{4,6},{6,7},{7,5},{5,3},{3,1},{1,0},{8,10},{10,12},{12... | collective-permute-start | bytes 3840008 | tf_op jit(solution)/shard_map/ppermute | solution.py:155
  144.1 31.9 %collective-permute-start.79 = (bf16[400,1600]{1,0:T(8,128)(2,1)}, bf16[400,1600]{1,0:T(8,128)(2,1)S(1)}, u32[]{:S(2)}, u32[]{:S(2)}) collective-permute-start(bf16[400,1600]{1,0:T(8,128)(2,1)} %collective-permute-done.73.refs_5_), channel_id=1, source_target_pairs={{0,1},{2,0},{4,2},{6,4},{7,6},{5,7},{3,5},{1,3},{8,9},{10,8},{12,1... | collective-permute-start | bytes 3840008 | tf_op jit(solution)/shard_map/ppermute | solution.py:155
  169.5 23.2 %collective-permute-start.75 = (bf16[32,8,1600]{2,1,0:T(8,128)(2,1)S(1)}, bf16[32,8,1600]{2,1,0:T(8,128)(2,1)S(1)}, u32[]{:S(2)}, u32[]{:S(2)}) collective-permute-start(bf16[32,8,1600]{2,1,0:T(8,128)(2,1)S(1)} %bitcast.122), channel_id=1, source_target_pairs={{0,16},{8,24},{16,0},{24,8},{1,17},{9,25},{17,1},{25,9},{2,18},{10... | collective-permute-start | bytes 2457608 | tf_op jit(solution)/shard_map/ppermute | solution.py:79
  256.5 26.8 %collective-permute-start.47 = (bf16[200,1600]{1,0:T(8,128)(2,1)S(1)}, bf16[200,1600]{1,0:T(8,128)(2,1)}, u32[]{:S(2)}, u32[]{:S(2)}) collective-permute-start(bf16[200,1600]{1,0:T(8,128)(2,1)S(1)} %get-tuple-element.643), channel_id=1, source_target_pairs={{0,2},{2,4},{4,6},{6,7},{7,5},{5,3},{3,1},{1,0},{8,10},{10,12},{12... | collective-permute-start | bytes 1920008 | tf_op jit(solution)/shard_map/cond/branch_1_fun/ppermute | solution.py:155
  257.6 25.8 %collective-permute-start.48 = (bf16[200,1600]{1,0:T(8,128)(2,1)S(1)}, bf16[200,1600]{1,0:T(8,128)(2,1)}, u32[]{:S(2)}, u32[]{:S(2)}) collective-permute-start(bf16[200,1600]{1,0:T(8,128)(2,1)S(1)} %get-tuple-element.644), channel_id=1, source_target_pairs={{0,1},{2,0},{4,2},{6,4},{7,6},{5,7},{3,5},{1,3},{8,9},{10,8},{12,1... | collective-permute-start | bytes 1920008 | tf_op jit(solution)/shard_map/cond/branch_1_fun/ppermute | solution.py:155
  286.2 28.7 %collective-permute-start.19 = (bf16[304,1600]{1,0:T(8,128)(2,1)S(1)}, bf16[304,1600]{1,0:T(8,128)(2,1)}, u32[]{:S(2)}, u32[]{:S(2)}) collective-permute-start(bf16[304,1600]{1,0:T(8,128)(2,1)S(1)} %get-tuple-element.678), channel_id=1, source_target_pairs={{0,1},{2,0},{4,2},{6,4},{7,6},{5,7},{3,5},{1,3},{8,9},{10,8},{12,1... | collective-permute-start | bytes 2918408 | tf_op jit(solution)/shard_map/cond/branch_1_fun/ppermute | solution.py:155
  287.2 27.7 %collective-permute-start.18 = (bf16[296,1600]{1,0:T(8,128)(2,1)S(1)}, bf16[296,1600]{1,0:T(8,128)(2,1)}, u32[]{:S(2)}, u32[]{:S(2)}) collective-permute-start(bf16[296,1600]{1,0:T(8,128)(2,1)S(1)} %get-tuple-element.677), channel_id=1, source_target_pairs={{0,2},{2,4},{4,6},{6,7},{7,5},{5,3},{3,1},{1,0},{8,10},{10,12},{12... | collective-permute-start | bytes 2841608 | tf_op jit(solution)/shard_map/cond/branch_1_fun/ppermute | solution.py:155
  317.8 26.1 %collective-permute-start.8 = (bf16[200,1600]{1,0:T(8,128)(2,1)S(1)}, bf16[200,1600]{1,0:T(8,128)(2,1)}, u32[]{:S(2)}, u32[]{:S(2)}) collective-permute-start(bf16[200,1600]{1,0:T(8,128)(2,1)S(1)} %get-tuple-element.712), channel_id=1, source_target_pairs={{0,2},{2,4},{4,6},{6,7},{7,5},{5,3},{3,1},{1,0},{8,10},{10,12},{12... | collective-permute-start | bytes 1920008 | tf_op jit(solution)/shard_map/cond/branch_1_fun/ppermute | solution.py:155
  318.8 25.1 %collective-permute-start.9 = (bf16[200,1600]{1,0:T(8,128)(2,1)S(1)}, bf16[200,1600]{1,0:T(8,128)(2,1)}, u32[]{:S(2)}, u32[]{:S(2)}) collective-permute-start(bf16[200,1600]{1,0:T(8,128)(2,1)S(1)} %get-tuple-element.713), channel_id=1, source_target_pairs={{0,1},{2,0},{4,2},{6,4},{7,6},{5,7},{3,5},{1,3},{8,9},{10,8},{12,1... | collective-permute-start | bytes 1920008 | tf_op jit(solution)/shard_map/cond/branch_1_fun/ppermute | solution.py:155
  319.9 24.0 %collective-permute-start.7 = (bf16[400,8,448]{2,1,0:T(8,128)(2,1)}, bf16[400,8,448]{2,1,0:T(8,128)(2,1)}, u32[]{:S(2)}, u32[]{:S(2)}) collective-permute-start(bf16[400,8,448]{2,1,0:T(8,128)(2,1)} %bitcast.19), channel_id=1, source_target_pairs={{0,8},{8,0},{16,24},{24,16},{1,9},{9,1},{17,25},{25,17},{2,10},{10... | collective-permute-start | bytes 8601608 | tf_op jit(solution)/shard_map/cond/branch_1_fun/cond/branch_1_fun/ppermute | solution.py:79
  346.5 29.8 %collective-permute-start.51 = (bf16[200,1600]{1,0:T(8,128)(2,1)S(1)}, bf16[200,1600]{1,0:T(8,128)(2,1)}, u32[]{:S(2)}, u32[]{:S(2)}) collective-permute-start(bf16[200,1600]{1,0:T(8,128)(2,1)S(1)} %get-tuple-element.741), channel_id=1, source_target_pairs={{0,2},{2,4},{4,6},{6,7},{7,5},{5,3},{3,1},{1,0},{8,10},{10,12},{12... | collective-permute-start | bytes 1920008 | tf_op jit(solution)/shard_map/cond/branch_1_fun/ppermute | solution.py:155
  347.3 29.0 %collective-permute-start.52 = (bf16[200,1600]{1,0:T(8,128)(2,1)S(1)}, bf16[200,1600]{1,0:T(8,128)(2,1)}, u32[]{:S(2)}, u32[]{:S(2)}) collective-permute-start(bf16[200,1600]{1,0:T(8,128)(2,1)S(1)} %get-tuple-element.742), channel_id=1, source_target_pairs={{0,1},{2,0},{4,2},{6,4},{7,6},{5,7},{3,5},{1,3},{8,9},{10,8},{12,1... | collective-permute-start | bytes 1920008 | tf_op jit(solution)/shard_map/cond/branch_1_fun/ppermute | solution.py:155
  379.2 24.1 %collective-permute-start.13 = (bf16[304,1600]{1,0:T(8,128)(2,1)S(1)}, bf16[304,1600]{1,0:T(8,128)(2,1)}, u32[]{:S(2)}, u32[]{:S(2)}) collective-permute-start(bf16[304,1600]{1,0:T(8,128)(2,1)S(1)} %get-tuple-element.770), channel_id=1, source_target_pairs={{0,1},{2,0},{4,2},{6,4},{7,6},{5,7},{3,5},{1,3},{8,9},{10,8},{12,1... | collective-permute-start | bytes 2918408 | tf_op jit(solution)/shard_map/cond/branch_1_fun/ppermute | solution.py:155
  380.3 23.0 %collective-permute-start.12 = (bf16[296,1600]{1,0:T(8,128)(2,1)S(1)}, bf16[296,1600]{1,0:T(8,128)(2,1)}, u32[]{:S(2)}, u32[]{:S(2)}) collective-permute-start(bf16[296,1600]{1,0:T(8,128)(2,1)S(1)} %get-tuple-element.769), channel_id=1, source_target_pairs={{0,2},{2,4},{4,6},{6,7},{7,5},{5,3},{3,1},{1,0},{8,10},{10,12},{12... | collective-permute-start | bytes 2841608 | tf_op jit(solution)/shard_map/cond/branch_1_fun/ppermute | solution.py:155
  406.0 23.8 %collective-permute-start.40 = (bf16[200,1856]{1,0:T(8,128)(2,1)S(1)}, bf16[200,1856]{1,0:T(8,128)(2,1)}, u32[]{:S(2)}, u32[]{:S(2)}) collective-permute-start(bf16[200,1856]{1,0:T(8,128)(2,1)S(1)} %get-tuple-element.823), channel_id=1, source_target_pairs={{0,2},{2,4},{4,6},{6,7},{7,5},{5,3},{3,1},{1,0},{8,10},{10,12},{12... | collective-permute-start | bytes 2227208 | tf_op jit(solution)/shard_map/cond/branch_1_fun/ppermute | solution.py:155
  (87 other events, 1275.3 us)

commit v6 on v5

--- a/solution.py
+++ b/solution.py
@@ -1153,6 +1153,33 @@
     )
 
 
+def whole_out_kernel(table, *refs):
+    pieces, out = refs[:4], refs[4]
+    step, span = BASE * HD, SLOTS * HD
+    width = out.shape[1]
+    for j, piece in enumerate(pieces):
+        start = pl.multiple_of(table[j] * step, PAIR)
+        out[:, pl.ds(start, step)] = piece[:, :step].astype(f32)
+
+        @pl.when(table[j] == len(pieces) - 1)
+        def _(piece=piece):
+            out[:, width - (span - step) :] = piece[:, step:].astype(f32)
+
+
+def whole_out(table, pieces, width):
+    rows = pieces[0].shape[0]
+    return call(
+        whole_out_kernel,
+        "whole_out",
+        1,
+        pieces,
+        [whole(piece.shape) for piece in pieces],
+        [((rows, width), f32)],
+        [whole((rows, width))],
+        table=table,
+    )[0]
+
+
 def whole_fc_kernel(table, *refs):
     pieces, out, held, sems = refs[:4], refs[4], refs[5], refs[6]
     copies = [
@@ -1581,23 +1608,26 @@
 
     qkv_pieces, out_moved, held, (grad_w_fc, tokens_out) = slot(always, slot_eleven)
     def slot_twelve():
-        shard_out = twin_last(twin, owners, out_moved)
-        swaps = [ctx_swap(shard_out, 2), ctx_swap(shard_out, 1)]
-        return [shard_out, *swaps], ctx_swap(qkv_pieces[1], 1), halve_small(held, shards // 8)
-
-    out_pieces, qkv_last, held = slot(always, slot_twelve)
+        last = ctx_swap(qkv_pieces[1], 1)
+        return last, slot(always, lambda: twin_last(twin, owners, out_moved))
+
+    qkv_last, shard_out = slot(always, slot_twelve)
+
+    def slot_thirteen():
+        far, near = ctx_swap(shard_out, 2), ctx_swap(shard_out, 1)
+        next_held = halve_small(held, shards // 8)
+
+        def beside():
+            return whole_qkv(peer_table, qkv_pieces + [qkv_last], width)
+
+        return [shard_out, far, near], next_held, slot(always, beside)
+
+    out_pieces, held, grad_w_qkv = slot(always, slot_thirteen)
     held = finish_small(held, shards // 16)
-
-    def slot_thirteen():
-        last = ctx_swap(out_pieces[1], 1)
-        total = held[0] + ctx_swap(held[0], 1)
-        return last, total, slot(
-            always, lambda: whole_qkv(peer_table, qkv_pieces + [qkv_last], width)
-        )
-
-    out_last, summed, grad_w_qkv = slot(always, slot_thirteen)
+    out_last = ctx_swap(out_pieces[1], 1)
+    summed = held[0] + ctx_swap(held[0], 1)
     summed = summed + ctx_swap(summed, 2)
-    whole_attn_out = join_windows(peer_table, out_pieces + [out_last], width).astype(f32)
+    whole_attn_out = whole_out(peer_table, out_pieces + [out_last], width)
     shares = [summed[t * shard_rows : (t + 1) * shard_rows] for t in range(8)]
     share_fc = summed[8 * shard_rows :]
     grad_tokens = grad_tokens[None]

time: 524 us -> 522 us (level)
  transfers between devices with their start and end apart: 83 -> 83, of which waited for: 26 -> 27; matrix products, arithmetic and copies ran while one was open for 16% -> 16% of each run, Pallas kernels for 32% -> 32%
where the time goes in v6:
time: 522 us; the launch traced here: 516 us
  Pallas kernels  196 us (38%)
  waiting for transfers between devices  139 us (27%)
  starting transfers between devices  84.1 us (16%)
  local copies, waits for them, and re-layouts  43.3 us (8%)
  matrix products  38.2 us (7%)
  other arithmetic  11.9 us (2%)
    pallas_call x37, Pallas kernels, call(): pl.pallas_call(body, grid_spec=pltpu.PrefetchScalarGridSpec(num_scalar_pr...  196 us
    ppermute x38, waiting for transfers between devices, ring_hop(): return row_major(lax.ppermute(row_major(value), 'fsdp', pairs))  63 us
    ppermute x39, waiting for transfers between devices, ctx_swap(): got = row_major(lax.ppermute(row_major(tiled(block)), 'ctx', pairs))  54.1 us
    ppermute x38, starting transfers between devices, ring_hop(): return row_major(lax.ppermute(row_major(value), 'fsdp', pairs))  47.3 us
    dot_general x3, matrix products, outer_sum(): lax.dot_general(left_op, right_op, (((0,), (0,)), ((), ())), preferred_el...  31.3 us
    ppermute x39, starting transfers between devices, ctx_swap(): got = row_major(lax.ppermute(row_major(tiled(block)), 'ctx', pairs))  25.6 us
    ppermute x3, waiting for transfers between devices, halve_small(): return keep + lax.ppermute(give, 'fsdp', pairs)  14.3 us
  transfers between devices with their start and end apart: 83, of which 27 were waited for; matrix products, arithmetic and copies ran while one was open for 16% of the time, Pallas kernels for 32%

profile of v6, /device:TPU:0, one launch (start us, length us, event | category | flops | bytes accessed | tf_op | source)
XLA Modules:
  0.0 515.9 jit_solution(15482420220040056467)
XLA Ops:
  64.8 38.5 %conditional.29 = (bf16[96,1856]{1,0:T(8,128)(2,1)}, bf16[104,1856]{1,0:T(8,128)(2,1)}, bf16[400,1600]{1,0:T(8,128)(2,1)}, bf16[400,1600]{1,0:T(8,128)(2,1)}, f3...) conditional(s32[]{:T(128)} %convert_element_type.86, () %tuple.300, ...), branch_computations={%region_1.2_spmd, %region_2.5_spmd} | conditional | flops 73736 | bytes 15522009 | solution.py:57
  82.0 18.5 %collective-permute-done.40 = bf16[96,1856]{1,0:T(8,128)(2,1)} collective-permute-done((bf16[96,1856]{1,0:T(8,128)(2,1)}, bf16[96,1856]{1,0:T(8,128)(2,1)}, u32[]{:S(2)}, u32[]{:S(2)}) %collective-permute-start.40) | collective-permute-done | bytes 356384 | tf_op jit(solution)/shard_map/cond/branch_1_fun/ppermute | solution.py:155
  219.7 14.6 %conditional.30 = (bf16[96,1600]{1,0:T(8,128)(2,1)}, bf16[104,1600]{1,0:T(8,128)(2,1)}, bf16[1024,1600]{1,0:T(8,128)(2,1)}, f32[1,1600]{1,0:T(1,128)S(1)}) conditional(s32[]{:T(128)} %convert_element_type.86, () %tuple.309, (s32[8]{0:T(128)S(1)}, bf16[8,200,1600]{2,1,0:T(8,128)(2,1)}, bf16[256,1600]{1,0:T(8,128)(2,1)S(1)}, ...), branch_computations={%region_5.6_spmd, %region_6.7_spmd} | conditional | flops 2097152 | bytes 3923242 | solution.py:57
  234.3 19.6 %conditional.31 = (bf16[200,1600]{1,0:T(8,128)(2,1)}, bf16[200,1600]{1,0:T(8,128)(2,1)}, bf16[512,1600]{1,0:T(8,128)(2,1)}, bf16[512,1600]{1,0:T(8,128)(2,1)}) conditional(s32[]{:T(128)} %convert_element_type.86, () %tuple.308, (s32[8]{0:T(128)S(1)}, bf16[8,200,1600]{2,1,0:T(8,128)(2,1)}, bf16[96,1600]{1,0:T(8,128)(2,1)}, ...), branch_computations={%region_7.8_spmd, %region_8.11_spmd} | conditional | flops 2097153 | bytes 11804861 | solution.py:57
  238.6 15.2 %conditional.1 = (bf16[512,1600]{1,0:T(8,128)(2,1)}, bf16[512,1600]{1,0:T(8,128)(2,1)}) conditional(s32[]{:T(128)} %convert_element_type.22, () %tuple.185, (bf16[1024,1600]{1,0:T(8,128)(2,1)}, bf16[1600,1600]{1,0:T(8,128)(2,1)}) %tuple.186), branch_computations={%region_9.9_spmd, %region_10.10_spmd} | conditional | flops 1048576 | bytes 6619192 | solution.py:57
  254.0 29.4 %conditional.32 = (bf16[200,1600]{1,0:T(8,128)(2,1)}, bf16[200,1600]{1,0:T(8,128)(2,1)}, f32[256,1600]{1,0:T(8,128)}, bf16[256,1600]{1,0:T(8,128)(2,1)}, bf16[51...) conditional(s32[]{:T(128)} %convert_element_type.86, () %tuple.297, ...), branch_computations={%region_11.12_spmd, %region_12.15_spmd} | conditional | flops 10492055552 | bytes 80617848 | solution.py:57
  258.6 24.8 %conditional.2 = (f32[256,1600]{1,0:T(8,128)}, bf16[256,1600]{1,0:T(8,128)(2,1)}, bf16[512,1600]{1,0:T(8,128)(2,1)}, bf16[512,1600]{1,0:T(8,128)(2,1)}, bf16[8,200,1600]{2,1,0:T(8,128)(2,1)}) conditional(s32[]{:T(128)} %convert_element_type.37, () %tuple.191, (bf16[512,1600]{1,0:T(8,128)(2,1)}, bf16[512,1600]{1,0:T(8,128)(2,1)}, ...), branch_computations={%region_13.13_spmd, %region_14.14_spmd} | conditional | flops 10491006976 | bytes 75432120 | solution.py:57
  283.4 31.7 %conditional.33 = (bf16[296,1600]{1,0:T(8,128)(2,1)}, bf16[304,1600]{1,0:T(8,128)(2,1)}, f32[256,1600]{1,0:T(8,128)}, f32[4,1600]{1,0:T(4,128)}, bf16[256,448]{1...) conditional(s32[]{:T(128)} %convert_element_type.86, () %tuple.314, ...), branch_computations={%region_15.16_spmd, %region_16.19_spmd} | conditional | flops 4063233 | bytes 18506640 | solution.py:57
  288.3 26.6 %conditional.3 = (f32[256,1600]{1,0:T(8,128)}, f32[4,1600]{1,0:T(4,128)}, bf16[256,448]{1,0:T(8,128)(2,1)}, bf16[256,448]{1,0:T(8,128)(2,1)}, bf16[256,448]{1,0:...) conditional(s32[]{:T(128)} %convert_element_type.42, () %tuple.197, ...), branch_computations={%region_17.17_spmd, %region_18.18_spmd} | conditional | flops 3014656 | bytes 10760876 | solution.py:57
  315.2 28.8 %conditional.34 = (bf16[200,1600]{1,0:T(8,128)(2,1)}, bf16[200,1600]{1,0:T(8,128)(2,1)}, bf16[200,1600]{1,0:T(8,128)(2,1)}, bf16[200,1600]{1,0:T(8,128)(2,1)}, b...) conditional(s32[]{:T(128)} %convert_element_type.86, () %tuple.313, ...), branch_computations={%region_19.20_spmd, %region_20.23_spmd} | conditional | flops 3145729 | bytes 33440168 | solution.py:57
  319.9 24.0 %conditional.4 = (bf16[200,1600]{1,0:T(8,128)(2,1)}, bf16[200,1600]{1,0:T(8,128)(2,1)}, bf16[200,1600]{1,0:T(8,128)(2,1)}, bf16[3200,448]{1,0:T(8,128)(2,1)}, bf16[1024,1408]{1,0:T(8,128)(2,1)}) conditional(s32[]{:T(128)} %convert_element_type.48, () %tuple.203, (s32[8]{0:T(128)S(1)}, bf16[8,200,1600]{2,1,0:T(8,128)(2,1)}, ...), branch_computations={%region_21.21_spmd, %region_22.22_spmd} | conditional | flops 2097152 | bytes 28254396 | solution.py:57
  324.5 19.5 %attend_back.1 = bf16[1024,1408]{1,0:T(8,128)(2,1)} custom-call(s32[9]{0:T(128)S(1)} %get-tuple-element.717.refs_0_, bf16[256,448]{1,0:T(8,128)(2,1)} %get-tuple-element.718.refs_1_, bf16[256,448]{1,0:T(8,128)(2,1)} %get-tuple-element.719.refs_2_, bf16[256,448]{1,0:T(8,128)(2,1)} %get-tuple-element.720.refs_3_, bf16[256,448]{1,0:T(8,128)(2,1)} %get-tuple-element.721.refs_4_, ...), custom_call_target="tpu_custom_call" | custom-call | flops 1048576 | bytes 65536 | tf_op jit(solution)/shard_map/cond/branch_1_fun/cond/branch_1_fun/attend_back/pallas_call | solution.py:753
  344.0 32.5 %conditional.35 = (bf16[200,1600]{1,0:T(8,128)(2,1)}, bf16[200,1600]{1,0:T(8,128)(2,1)}, bf16[200,1600]{1,0:T(8,128)(2,1)}, bf16[800,448]{1,0:T(8,128)(2,1)}, bf...) conditional(s32[]{:T(128)} %convert_element_type.86, () %tuple.296, ...), branch_computations={%region_23.24_spmd, %region_24.27_spmd} | conditional | flops 4618084352 | bytes 34451784 | solution.py:57
  348.6 27.7 %conditional.5 = (bf16[200,1600]{1,0:T(8,128)(2,1)}, bf16[800,448]{1,0:T(8,128)(2,1)}, bf16[8,200,448]{2,1,0:T(8,128)(2,1)}, bf16[4,200,448]{2,1,0:T(8,128)(2,1)}, bf16[8,200,1408]{2,1,0:T(8,128)(2,1)}) conditional(s32[]{:T(128)} %convert_element_type.50, () %tuple.209, (bf16[200,1600]{1,0:T(8,128)(2,1)}, bf16[3200,448]{1,0:T(8,128)(2,1)}, ...), branch_computations={%region_25.25_spmd, %region_26.26_spmd} | conditional | flops 4617035776 | bytes 29266068 | solution.py:57
  376.5 26.8 %conditional.36 = (bf16[296,1600]{1,0:T(8,128)(2,1)}, bf16[304,1600]{1,0:T(8,128)(2,1)}, f32[256,1600]{1,0:T(8,128)}, bf16[256,1600]{1,0:T(8,128)(2,1)}, bf16[4,200,448]{2,1,0:T(8,128)(2,1)}) conditional(s32[]{:T(128)} %convert_element_type.86, () %tuple.321, (s32[8]{0:T(128)S(1)}, bf16[8,200,1600]{2,1,0:T(8,128)(2,1)}, ...), branch_computations={%region_27.28_spmd, %region_28.33_spmd} | conditional | flops 3145730 | bytes 17297698 | solution.py:57
  381.3 19.4 %conditional.7 = (f32[256,1600]{1,0:T(8,128)}, bf16[256,1600]{1,0:T(8,128)(2,1)}, bf16[4,200,448]{2,1,0:T(8,128)(2,1)}) conditional(s32[]{:T(128)} %convert_element_type.55, () %tuple.218, (pred[]{:T(512)}, bf16[1024,1408]{1,0:T(8,128)(2,1)}, bf16[1600,1408]{1,0:T(8,128)(2,1)}, bf16[800,448]{1,0:T(8,128)(2,1)}) %tuple.219), branch_computations={%region_29.29_spmd, %region_30.32_spmd} | conditional | flops 2097153 | bytes 9552005 | solution.py:57
  383.1 14.6 %conditional.6 = ((f32[256,1600]{1,0:T(8,128)}, bf16[256,1600]{1,0:T(8,128)(2,1)})) conditional(s32[]{:T(128)} %convert_element_type.54, () %tuple.215, (bf16[1024,1408]{1,0:T(8,128)(2,1)}, bf16[1600,1408]{1,0:T(8,128)(2,1)}) %tuple.216), branch_computations={%region_31.30_spmd, %region_32.31_spmd} | conditional | flops 2097152 | bytes 6684720 | solution.py:57
  403.3 26.5 %conditional.37 = (bf16[200,1856]{1,0:T(8,128)(2,1)}, bf16[200,1856]{1,0:T(8,128)(2,1)}, bf16[256,1600]{1,0:T(8,128)(2,1)}, bf16[512,1600]{1,0:T(8,128)(2,1)}, b...) conditional(s32[]{:T(128)} %convert_element_type.86, () %tuple.320, ...), branch_computations={%region_33.34_spmd, %region_34.40_spmd} | conditional | flops 6030601 | bytes 21659836 | solution.py:57
  408.2 21.7 %conditional.9 = (bf16[256,1600]{1,0:T(8,128)(2,1)}, bf16[512,1600]{1,0:T(8,128)(2,1)}, bf16[200,1600]{1,0:T(8,128)(2,1)}, f32[8,200]{1,0:T(8,128)}, f32[8,200]{...) conditional(s32[]{:T(128)} %convert_element_type.76, () %tuple.228, ...), branch_computations={%region_35.35_spmd, %region_36.39_spmd} | conditional | flops 4982024 | bytes 15654783 | solution.py:57
  409.6 17.1 %conditional.8 = (bf16[200,1600]{1,0:T(8,128)(2,1)}, f32[8,200]{1,0:T(8,128)}, f32[8,200]{1,0:T(8,128)}, f32[8,200]{1,0:T(8,128)}, f32[8,200]{1,0:T(8,128)}, /*i...) conditional(s32[]{:T(128)} %convert_element_type.58, () %tuple.225, ...), branch_computations={%region_37.36_spmd, %region_38.38_spmd} | conditional | flops 4982023 | bytes 5824106 | solution.py:57
  429.9 24.3 %conditional.38 = (bf16[200,1856]{1,0:T(8,128)(2,1)}, bf16[200,1856]{1,0:T(8,128)(2,1)}, bf16[200,1600]{1,0:T(8,128)(2,1)}, bf16[200,1600]{1,0:T(8,128)(2,1)}, b...) conditional(s32[]{:T(128)} %convert_element_type.86, () %tuple.319, ...), branch_computations={%region_40.41_spmd, %region_41.46_spmd} | conditional | flops 3145730 | bytes 19854920 | solution.py:57
  435.0 16.3 %conditional.11 = (bf16[200,1600]{1,0:T(8,128)(2,1)}, bf16[200,1600]{1,0:T(8,128)(2,1)}, bf16[200,1600]{1,0:T(8,128)(2,1)}, f32[256,1600]{1,0:T(8,128)}, bf16[25...) conditional(s32[]{:T(128)} %convert_element_type.78, () %tuple.238, ...), branch_computations={%region_42.42_spmd, %region_43.45_spmd} | conditional | flops 2097153 | bytes 10573099 | solution.py:57
  454.1 25.0 %conditional.39 = (bf16[200,1856]{1,0:T(8,128)(2,1)}, bf16[200,1856]{1,0:T(8,128)(2,1)}, f32[4,2400]{1,0:T(4,128)S(1)}, bf16[256,1600]{1,0:T(8,128)(2,1)}, bf16[200,1600]{1,0:T(8,128)(2,1)}) conditional(s32[]{:T(128)} %convert_element_type.86, () %tuple.318, (s32[8]{0:T(128)S(1)}, bf16[8,200,1408]{2,1,0:T(8,128)(2,1)}, ...), branch_computations={%region_46.47_spmd, %region_47.48_spmd} | conditional | flops 1077380 | bytes 12264219 | solution.py:57
  479.1 16.7 %conditional.40 = (bf16[200,1408]{1,0:T(8,128)(2,1)}, bf16[200,1408]{1,0:T(8,128)(2,1)}, bf16[200,1408]{1,0:T(8,128)(2,1)}, bf16[200,448]{1,0:T(8,128)(2,1)}, bf...) conditional(s32[]{:T(128)} %convert_element_type.86, () %tuple.295, ...), branch_computations={%region_48.49_spmd, %region_49.52_spmd} | conditional | flops 4159557 | bytes 20347570 | solution.py:57
  (376 shorter events, 518.9 us)
Async XLA Ops:
  26.6 23.2 %collective-permute-start.60 = (bf16[200,1856]{1,0:T(8,128)(2,1)}, bf16[200,1856]{1,0:T(8,128)(2,1)S(1)}, u32[]{:S(2)}, u32[]{:S(2)}) collective-permute-start(bf16[200,1856]{1,0:T(8,128)(2,1)} %collective-permute-done.59.refs_3_), channel_id=1, source_target_pairs={{0,1},{2,0},{4,2},{6,4},{7,6},{5,7},{3,5},{1,3},{8,9},{10,8},{12,1... | collective-permute-start | bytes 2227208 | tf_op jit(solution)/shard_map/ppermute | solution.py:155
  53.1 59.5 %collective-permute-start.53 = (bf16[32,8,1600]{2,1,0:T(8,128)(2,1)}, bf16[32,8,1600]{2,1,0:T(8,128)(2,1)}, u32[]{:S(2)}, u32[]{:S(2)}) collective-permute-start(bf16[32,8,1600]{2,1,0:T(8,128)(2,1)} %collective-permute-done.52), channel_id=1, source_target_pairs={{0,8},{8,0},{16,24},{24,16},{1,9},{9,1},{17,25},{25,17},{2,10},{10... | collective-permute-start | bytes 2457608 | tf_op jit(solution)/shard_map/ppermute | solution.py:79
  64.8 38.5 %collective-permute-start.42 = (bf16[400,1600]{1,0:T(8,128)(2,1)}, bf16[400,1600]{1,0:T(8,128)(2,1)}, u32[]{:S(2)}, u32[]{:S(2)}) collective-permute-start(bf16[400,1600]{1,0:T(8,128)(2,1)} %get-tuple-element.608), channel_id=1, source_target_pairs={{0,2},{2,4},{4,6},{6,7},{7,5},{5,3},{3,1},{1,0},{8,10},{10,12},{12... | collective-permute-start | bytes 3840008 | tf_op jit(solution)/shard_map/cond/branch_1_fun/ppermute | solution.py:155
  68.8 34.5 %collective-permute-start.43 = (bf16[400,1600]{1,0:T(8,128)(2,1)}, bf16[400,1600]{1,0:T(8,128)(2,1)}, u32[]{:S(2)}, u32[]{:S(2)}) collective-permute-start(bf16[400,1600]{1,0:T(8,128)(2,1)} %get-tuple-element.608), channel_id=1, source_target_pairs={{0,1},{2,0},{4,2},{6,4},{7,6},{5,7},{3,5},{1,3},{8,9},{10,8},{12,1... | collective-permute-start | bytes 3840008 | tf_op jit(solution)/shard_map/cond/branch_1_fun/ppermute | solution.py:155
  70.6 32.7 %collective-permute-start.41 = (bf16[104,1856]{1,0:T(8,128)(2,1)}, bf16[104,1856]{1,0:T(8,128)(2,1)}, u32[]{:S(2)}, u32[]{:S(2)}) collective-permute-start(bf16[104,1856]{1,0:T(8,128)(2,1)} %slice.175), channel_id=1, source_target_pairs={{0,1},{2,0},{4,2},{6,4},{7,6},{5,7},{3,5},{1,3},{8,9},{10,8},{12,1... | collective-permute-start | bytes 1158152 | tf_op jit(solution)/shard_map/cond/branch_1_fun/ppermute | solution.py:155
  72.4 28.1 %collective-permute-start.40 = (bf16[96,1856]{1,0:T(8,128)(2,1)}, bf16[96,1856]{1,0:T(8,128)(2,1)}, u32[]{:S(2)}, u32[]{:S(2)}) collective-permute-start(bf16[96,1856]{1,0:T(8,128)(2,1)} %slice.174), channel_id=1, source_target_pairs={{0,2},{2,4},{4,6},{6,7},{7,5},{5,3},{3,1},{1,0},{8,10},{10,12},{12... | collective-permute-start | bytes 1069064 | tf_op jit(solution)/shard_map/cond/branch_1_fun/ppermute | solution.py:155
  108.8 31.7 %collective-permute-start.65 = (bf16[200,8,448]{2,1,0:T(8,128)(2,1)}, bf16[200,8,448]{2,1,0:T(8,128)(2,1)}, u32[]{:S(2)}, u32[]{:S(2)}) collective-permute-start(bf16[200,8,448]{2,1,0:T(8,128)(2,1)} %bitcast.70), channel_id=1, source_target_pairs={{0,16},{8,24},{16,0},{24,8},{1,17},{9,25},{17,1},{25,9},{2,18},{10... | collective-permute-start | bytes 4300808 | tf_op jit(solution)/shard_map/ppermute | solution.py:79
  110.9 31.4 %collective-permute-start.70 = (bf16[400,1600]{1,0:T(8,128)(2,1)}, bf16[400,1600]{1,0:T(8,128)(2,1)}, u32[]{:S(2)}, u32[]{:S(2)}) collective-permute-start(bf16[400,1600]{1,0:T(8,128)(2,1)} %get-tuple-element.1159.refs_2_), channel_id=1, source_target_pairs={{0,2},{2,4},{4,6},{6,7},{7,5},{5,3},{3,1},{1,0},{8,10},{10,12},{12... | collective-permute-start | bytes 3840008 | tf_op jit(solution)/shard_map/ppermute | solution.py:155
  112.5 31.6 %collective-permute-start.71 = (bf16[400,1600]{1,0:T(8,128)(2,1)}, bf16[400,1600]{1,0:T(8,128)(2,1)}, u32[]{:S(2)}, u32[]{:S(2)}) collective-permute-start(bf16[400,1600]{1,0:T(8,128)(2,1)} %get-tuple-element.1160.refs_3_), channel_id=1, source_target_pairs={{0,1},{2,0},{4,2},{6,4},{7,6},{5,7},{3,5},{1,3},{8,9},{10,8},{12,1... | collective-permute-start | bytes 3840008 | tf_op jit(solution)/shard_map/ppermute | solution.py:155
  142.4 31.6 %collective-permute-start.75 = (bf16[400,1600]{1,0:T(8,128)(2,1)}, bf16[400,1600]{1,0:T(8,128)(2,1)S(1)}, u32[]{:S(2)}, u32[]{:S(2)}) collective-permute-start(bf16[400,1600]{1,0:T(8,128)(2,1)} %collective-permute-done.70.refs_4_), channel_id=1, source_target_pairs={{0,2},{2,4},{4,6},{6,7},{7,5},{5,3},{3,1},{1,0},{8,10},{10,12},{12... | collective-permute-start | bytes 3840008 | tf_op jit(solution)/shard_map/ppermute | solution.py:155
  144.1 31.9 %collective-permute-start.77 = (bf16[400,1600]{1,0:T(8,128)(2,1)}, bf16[400,1600]{1,0:T(8,128)(2,1)S(1)}, u32[]{:S(2)}, u32[]{:S(2)}) collective-permute-start(bf16[400,1600]{1,0:T(8,128)(2,1)} %collective-permute-done.71.refs_5_), channel_id=1, source_target_pairs={{0,1},{2,0},{4,2},{6,4},{7,6},{5,7},{3,5},{1,3},{8,9},{10,8},{12,1... | collective-permute-start | bytes 3840008 | tf_op jit(solution)/shard_map/ppermute | solution.py:155
  169.5 23.2 %collective-permute-start.73 = (bf16[32,8,1600]{2,1,0:T(8,128)(2,1)S(1)}, bf16[32,8,1600]{2,1,0:T(8,128)(2,1)S(1)}, u32[]{:S(2)}, u32[]{:S(2)}) collective-permute-start(bf16[32,8,1600]{2,1,0:T(8,128)(2,1)S(1)} %bitcast.122), channel_id=1, source_target_pairs={{0,16},{8,24},{16,0},{24,8},{1,17},{9,25},{17,1},{25,9},{2,18},{10... | collective-permute-start | bytes 2457608 | tf_op jit(solution)/shard_map/ppermute | solution.py:79
  256.5 26.8 %collective-permute-start.45 = (bf16[200,1600]{1,0:T(8,128)(2,1)S(1)}, bf16[200,1600]{1,0:T(8,128)(2,1)}, u32[]{:S(2)}, u32[]{:S(2)}) collective-permute-start(bf16[200,1600]{1,0:T(8,128)(2,1)S(1)} %get-tuple-element.659), channel_id=1, source_target_pairs={{0,2},{2,4},{4,6},{6,7},{7,5},{5,3},{3,1},{1,0},{8,10},{10,12},{12... | collective-permute-start | bytes 1920008 | tf_op jit(solution)/shard_map/cond/branch_1_fun/ppermute | solution.py:155
  257.6 25.8 %collective-permute-start.46 = (bf16[200,1600]{1,0:T(8,128)(2,1)S(1)}, bf16[200,1600]{1,0:T(8,128)(2,1)}, u32[]{:S(2)}, u32[]{:S(2)}) collective-permute-start(bf16[200,1600]{1,0:T(8,128)(2,1)S(1)} %get-tuple-element.660), channel_id=1, source_target_pairs={{0,1},{2,0},{4,2},{6,4},{7,6},{5,7},{3,5},{1,3},{8,9},{10,8},{12,1... | collective-permute-start | bytes 1920008 | tf_op jit(solution)/shard_map/cond/branch_1_fun/ppermute | solution.py:155
  286.2 28.7 %collective-permute-start.18 = (bf16[304,1600]{1,0:T(8,128)(2,1)S(1)}, bf16[304,1600]{1,0:T(8,128)(2,1)}, u32[]{:S(2)}, u32[]{:S(2)}) collective-permute-start(bf16[304,1600]{1,0:T(8,128)(2,1)S(1)} %get-tuple-element.694), channel_id=1, source_target_pairs={{0,1},{2,0},{4,2},{6,4},{7,6},{5,7},{3,5},{1,3},{8,9},{10,8},{12,1... | collective-permute-start | bytes 2918408 | tf_op jit(solution)/shard_map/cond/branch_1_fun/ppermute | solution.py:155
  287.3 27.7 %collective-permute-start.17 = (bf16[296,1600]{1,0:T(8,128)(2,1)S(1)}, bf16[296,1600]{1,0:T(8,128)(2,1)}, u32[]{:S(2)}, u32[]{:S(2)}) collective-permute-start(bf16[296,1600]{1,0:T(8,128)(2,1)S(1)} %get-tuple-element.693), channel_id=1, source_target_pairs={{0,2},{2,4},{4,6},{6,7},{7,5},{5,3},{3,1},{1,0},{8,10},{10,12},{12... | collective-permute-start | bytes 2841608 | tf_op jit(solution)/shard_map/cond/branch_1_fun/ppermute | solution.py:155
  317.8 26.1 %collective-permute-start.8 = (bf16[200,1600]{1,0:T(8,128)(2,1)S(1)}, bf16[200,1600]{1,0:T(8,128)(2,1)}, u32[]{:S(2)}, u32[]{:S(2)}) collective-permute-start(bf16[200,1600]{1,0:T(8,128)(2,1)S(1)} %get-tuple-element.728), channel_id=1, source_target_pairs={{0,2},{2,4},{4,6},{6,7},{7,5},{5,3},{3,1},{1,0},{8,10},{10,12},{12... | collective-permute-start | bytes 1920008 | tf_op jit(solution)/shard_map/cond/branch_1_fun/ppermute | solution.py:155
  318.9 25.1 %collective-permute-start.9 = (bf16[200,1600]{1,0:T(8,128)(2,1)S(1)}, bf16[200,1600]{1,0:T(8,128)(2,1)}, u32[]{:S(2)}, u32[]{:S(2)}) collective-permute-start(bf16[200,1600]{1,0:T(8,128)(2,1)S(1)} %get-tuple-element.729), channel_id=1, source_target_pairs={{0,1},{2,0},{4,2},{6,4},{7,6},{5,7},{3,5},{1,3},{8,9},{10,8},{12,1... | collective-permute-start | bytes 1920008 | tf_op jit(solution)/shard_map/cond/branch_1_fun/ppermute | solution.py:155
  319.9 24.0 %collective-permute-start.7 = (bf16[400,8,448]{2,1,0:T(8,128)(2,1)}, bf16[400,8,448]{2,1,0:T(8,128)(2,1)}, u32[]{:S(2)}, u32[]{:S(2)}) collective-permute-start(bf16[400,8,448]{2,1,0:T(8,128)(2,1)} %bitcast.19), channel_id=1, source_target_pairs={{0,8},{8,0},{16,24},{24,16},{1,9},{9,1},{17,25},{25,17},{2,10},{10... | collective-permute-start | bytes 8601608 | tf_op jit(solution)/shard_map/cond/branch_1_fun/cond/branch_1_fun/ppermute | solution.py:79
  346.5 29.8 %collective-permute-start.49 = (bf16[200,1600]{1,0:T(8,128)(2,1)S(1)}, bf16[200,1600]{1,0:T(8,128)(2,1)}, u32[]{:S(2)}, u32[]{:S(2)}) collective-permute-start(bf16[200,1600]{1,0:T(8,128)(2,1)S(1)} %get-tuple-element.757), channel_id=1, source_target_pairs={{0,2},{2,4},{4,6},{6,7},{7,5},{5,3},{3,1},{1,0},{8,10},{10,12},{12... | collective-permute-start | bytes 1920008 | tf_op jit(solution)/shard_map/cond/branch_1_fun/ppermute | solution.py:155
  347.4 29.0 %collective-permute-start.50 = (bf16[200,1600]{1,0:T(8,128)(2,1)S(1)}, bf16[200,1600]{1,0:T(8,128)(2,1)}, u32[]{:S(2)}, u32[]{:S(2)}) collective-permute-start(bf16[200,1600]{1,0:T(8,128)(2,1)S(1)} %get-tuple-element.758), channel_id=1, source_target_pairs={{0,1},{2,0},{4,2},{6,4},{7,6},{5,7},{3,5},{1,3},{8,9},{10,8},{12,1... | collective-permute-start | bytes 1920008 | tf_op jit(solution)/shard_map/cond/branch_1_fun/ppermute | solution.py:155
  379.3 24.1 %collective-permute-start.13 = (bf16[304,1600]{1,0:T(8,128)(2,1)S(1)}, bf16[304,1600]{1,0:T(8,128)(2,1)}, u32[]{:S(2)}, u32[]{:S(2)}) collective-permute-start(bf16[304,1600]{1,0:T(8,128)(2,1)S(1)} %get-tuple-element.786), channel_id=1, source_target_pairs={{0,1},{2,0},{4,2},{6,4},{7,6},{5,7},{3,5},{1,3},{8,9},{10,8},{12,1... | collective-permute-start | bytes 2918408 | tf_op jit(solution)/shard_map/cond/branch_1_fun/ppermute | solution.py:155
  380.3 23.0 %collective-permute-start.12 = (bf16[296,1600]{1,0:T(8,128)(2,1)S(1)}, bf16[296,1600]{1,0:T(8,128)(2,1)}, u32[]{:S(2)}, u32[]{:S(2)}) collective-permute-start(bf16[296,1600]{1,0:T(8,128)(2,1)S(1)} %get-tuple-element.785), channel_id=1, source_target_pairs={{0,2},{2,4},{4,6},{6,7},{7,5},{5,3},{3,1},{1,0},{8,10},{10,12},{12... | collective-permute-start | bytes 2841608 | tf_op jit(solution)/shard_map/cond/branch_1_fun/ppermute | solution.py:155
  406.1 23.8 %collective-permute-start.38 = (bf16[200,1856]{1,0:T(8,128)(2,1)S(1)}, bf16[200,1856]{1,0:T(8,128)(2,1)}, u32[]{:S(2)}, u32[]{:S(2)}) collective-permute-start(bf16[200,1856]{1,0:T(8,128)(2,1)S(1)} %get-tuple-element.839), channel_id=1, source_target_pairs={{0,2},{2,4},{4,6},{6,7},{7,5},{5,3},{3,1},{1,0},{8,10},{10,12},{12... | collective-permute-start | bytes 2227208 | tf_op jit(solution)/shard_map/cond/branch_1_fun/ppermute | solution.py:155
  (87 other events, 1274.2 us)

commit v7 on v6

--- a/solution.py
+++ b/solution.py
@@ -20,7 +20,7 @@
 norm_eps = 1e-05
 masked_low = -1e30
 LIGHT = pl.CostEstimate(flops=1 << 20, transcendentals=0, bytes_accessed=1 << 16)
-VMEM_LIMIT = 40 << 20
+VMEM_LIMIT = 30 << 20
 f32 = jnp.float32
 bf16 = jnp.bfloat16
 

time: 522 us -> 521 us (level)
  no operation moved by 1% of the time
where the time goes in v7:
time: 521 us; the launch traced here: 515 us
  Pallas kernels  195 us (37%)
  waiting for transfers between devices  139 us (27%)
  starting transfers between devices  84.3 us (16%)
  local copies, waits for them, and re-layouts  43.3 us (8%)
  matrix products  38.2 us (7%)
  other arithmetic  11.9 us (2%)
    pallas_call x37, Pallas kernels, call(): pl.pallas_call(body, grid_spec=pltpu.PrefetchScalarGridSpec(num_scalar_pr...  195 us
    ppermute x38, waiting for transfers between devices, ring_hop(): return row_major(lax.ppermute(row_major(value), 'fsdp', pairs))  62.9 us
    ppermute x39, waiting for transfers between devices, ctx_swap(): got = row_major(lax.ppermute(row_major(tiled(block)), 'ctx', pairs))  54 us
    ppermute x38, starting transfers between devices, ring_hop(): return row_major(lax.ppermute(row_major(value), 'fsdp', pairs))  47.3 us
    dot_general x3, matrix products, outer_sum(): lax.dot_general(left_op, right_op, (((0,), (0,)), ((), ())), preferred_el...  31.2 us
    ppermute x39, starting transfers between devices, ctx_swap(): got = row_major(lax.ppermute(row_major(tiled(block)), 'ctx', pairs))  25.7 us
    ppermute x3, waiting for transfers between devices, halve_small(): return keep + lax.ppermute(give, 'fsdp', pairs)  14.3 us
  transfers between devices with their start and end apart: 83, of which 27 were waited for; matrix products, arithmetic and copies ran while one was open for 16% of the time, Pallas kernels for 32%

profile of v7, /device:TPU:0, one launch (start us, length us, event | category | flops | bytes accessed | tf_op | source)
XLA Modules:
  0.0 515.1 jit_solution(3133121358315368684)
XLA Ops:
  64.8 38.5 %conditional.29 = (bf16[96,1856]{1,0:T(8,128)(2,1)}, bf16[104,1856]{1,0:T(8,128)(2,1)}, bf16[400,1600]{1,0:T(8,128)(2,1)}, bf16[400,1600]{1,0:T(8,128)(2,1)}, f3...) conditional(s32[]{:T(128)} %convert_element_type.86, () %tuple.300, ...), branch_computations={%region_1.2_spmd, %region_2.5_spmd} | conditional | flops 73736 | bytes 15522009 | solution.py:57
  82.0 18.5 %collective-permute-done.40 = bf16[96,1856]{1,0:T(8,128)(2,1)} collective-permute-done((bf16[96,1856]{1,0:T(8,128)(2,1)}, bf16[96,1856]{1,0:T(8,128)(2,1)}, u32[]{:S(2)}, u32[]{:S(2)}) %collective-permute-start.40) | collective-permute-done | bytes 356384 | tf_op jit(solution)/shard_map/cond/branch_1_fun/ppermute | solution.py:155
  176.9 14.4 %collective-permute-done.76.refs_8_ = bf16[200,1600]{1,0:T(8,128)(2,1)S(1)} collective-permute-done((bf16[200,1600]{1,0:T(8,128)(2,1)S(1)}, bf16[200,1600]{1,0:T(8,128)(2,1)S(1)}, u32[]{:S(2)}, u32[]{:S(2)}) %collective-permute-start.76) | collective-permute-done | bytes 640032 | tf_op jit(solution)/shard_map/ppermute | solution.py:155
  233.8 19.5 %conditional.31 = (bf16[200,1600]{1,0:T(8,128)(2,1)}, bf16[200,1600]{1,0:T(8,128)(2,1)}, bf16[512,1600]{1,0:T(8,128)(2,1)}, bf16[512,1600]{1,0:T(8,128)(2,1)}) conditional(s32[]{:T(128)} %convert_element_type.86, () %tuple.308, (s32[8]{0:T(128)S(1)}, bf16[8,200,1600]{2,1,0:T(8,128)(2,1)}, bf16[96,1600]{1,0:T(8,128)(2,1)}, ...), branch_computations={%region_7.8_spmd, %region_8.11_spmd} | conditional | flops 2097153 | bytes 11804861 | solution.py:57
  238.1 15.2 %conditional.1 = (bf16[512,1600]{1,0:T(8,128)(2,1)}, bf16[512,1600]{1,0:T(8,128)(2,1)}) conditional(s32[]{:T(128)} %convert_element_type.22, () %tuple.185, (bf16[1024,1600]{1,0:T(8,128)(2,1)}, bf16[1600,1600]{1,0:T(8,128)(2,1)}) %tuple.186), branch_computations={%region_9.9_spmd, %region_10.10_spmd} | conditional | flops 1048576 | bytes 6619192 | solution.py:57
  253.2 29.5 %conditional.32 = (bf16[200,1600]{1,0:T(8,128)(2,1)}, bf16[200,1600]{1,0:T(8,128)(2,1)}, f32[256,1600]{1,0:T(8,128)}, bf16[256,1600]{1,0:T(8,128)(2,1)}, bf16[51...) conditional(s32[]{:T(128)} %convert_element_type.86, () %tuple.297, ...), branch_computations={%region_11.12_spmd, %region_12.15_spmd} | conditional | flops 10492055552 | bytes 80617848 | solution.py:57
  258.1 24.7 %conditional.2 = (f32[256,1600]{1,0:T(8,128)}, bf16[256,1600]{1,0:T(8,128)(2,1)}, bf16[512,1600]{1,0:T(8,128)(2,1)}, bf16[512,1600]{1,0:T(8,128)(2,1)}, bf16[8,200,1600]{2,1,0:T(8,128)(2,1)}) conditional(s32[]{:T(128)} %convert_element_type.37, () %tuple.191, (bf16[512,1600]{1,0:T(8,128)(2,1)}, bf16[512,1600]{1,0:T(8,128)(2,1)}, ...), branch_computations={%region_13.13_spmd, %region_14.14_spmd} | conditional | flops 10491006976 | bytes 75432120 | solution.py:57
  282.8 31.5 %conditional.33 = (bf16[296,1600]{1,0:T(8,128)(2,1)}, bf16[304,1600]{1,0:T(8,128)(2,1)}, f32[256,1600]{1,0:T(8,128)}, f32[4,1600]{1,0:T(4,128)}, bf16[256,448]{1...) conditional(s32[]{:T(128)} %convert_element_type.86, () %tuple.314, ...), branch_computations={%region_15.16_spmd, %region_16.19_spmd} | conditional | flops 4063233 | bytes 18506640 | solution.py:57
  287.7 26.4 %conditional.3 = (f32[256,1600]{1,0:T(8,128)}, f32[4,1600]{1,0:T(4,128)}, bf16[256,448]{1,0:T(8,128)(2,1)}, bf16[256,448]{1,0:T(8,128)(2,1)}, bf16[256,448]{1,0:...) conditional(s32[]{:T(128)} %convert_element_type.42, () %tuple.197, ...), branch_computations={%region_17.17_spmd, %region_18.18_spmd} | conditional | flops 3014656 | bytes 10760876 | solution.py:57
  314.3 28.8 %conditional.34 = (bf16[200,1600]{1,0:T(8,128)(2,1)}, bf16[200,1600]{1,0:T(8,128)(2,1)}, bf16[200,1600]{1,0:T(8,128)(2,1)}, bf16[200,1600]{1,0:T(8,128)(2,1)}, b...) conditional(s32[]{:T(128)} %convert_element_type.86, () %tuple.313, ...), branch_computations={%region_19.20_spmd, %region_20.23_spmd} | conditional | flops 3145729 | bytes 33440168 | solution.py:57
  319.0 24.1 %conditional.4 = (bf16[200,1600]{1,0:T(8,128)(2,1)}, bf16[200,1600]{1,0:T(8,128)(2,1)}, bf16[200,1600]{1,0:T(8,128)(2,1)}, bf16[3200,448]{1,0:T(8,128)(2,1)}, bf16[1024,1408]{1,0:T(8,128)(2,1)}) conditional(s32[]{:T(128)} %convert_element_type.48, () %tuple.203, (s32[8]{0:T(128)S(1)}, bf16[8,200,1600]{2,1,0:T(8,128)(2,1)}, ...), branch_computations={%region_21.21_spmd, %region_22.22_spmd} | conditional | flops 2097152 | bytes 28254396 | solution.py:57
  323.7 19.4 %attend_back.1 = bf16[1024,1408]{1,0:T(8,128)(2,1)} custom-call(s32[9]{0:T(128)S(1)} %get-tuple-element.717.refs_0_, bf16[256,448]{1,0:T(8,128)(2,1)} %get-tuple-element.718.refs_1_, bf16[256,448]{1,0:T(8,128)(2,1)} %get-tuple-element.719.refs_2_, bf16[256,448]{1,0:T(8,128)(2,1)} %get-tuple-element.720.refs_3_, bf16[256,448]{1,0:T(8,128)(2,1)} %get-tuple-element.721.refs_4_, ...), custom_call_target="tpu_custom_call" | custom-call | flops 1048576 | bytes 65536 | tf_op jit(solution)/shard_map/cond/branch_1_fun/cond/branch_1_fun/attend_back/pallas_call | solution.py:753
  343.2 32.4 %conditional.35 = (bf16[200,1600]{1,0:T(8,128)(2,1)}, bf16[200,1600]{1,0:T(8,128)(2,1)}, bf16[200,1600]{1,0:T(8,128)(2,1)}, bf16[800,448]{1,0:T(8,128)(2,1)}, bf...) conditional(s32[]{:T(128)} %convert_element_type.86, () %tuple.296, ...), branch_computations={%region_23.24_spmd, %region_24.27_spmd} | conditional | flops 4618084352 | bytes 34451784 | solution.py:57
  347.8 27.6 %conditional.5 = (bf16[200,1600]{1,0:T(8,128)(2,1)}, bf16[800,448]{1,0:T(8,128)(2,1)}, bf16[8,200,448]{2,1,0:T(8,128)(2,1)}, bf16[4,200,448]{2,1,0:T(8,128)(2,1)}, bf16[8,200,1408]{2,1,0:T(8,128)(2,1)}) conditional(s32[]{:T(128)} %convert_element_type.50, () %tuple.209, (bf16[200,1600]{1,0:T(8,128)(2,1)}, bf16[3200,448]{1,0:T(8,128)(2,1)}, ...), branch_computations={%region_25.25_spmd, %region_26.26_spmd} | conditional | flops 4617035776 | bytes 29266068 | solution.py:57
  375.6 26.8 %conditional.36 = (bf16[296,1600]{1,0:T(8,128)(2,1)}, bf16[304,1600]{1,0:T(8,128)(2,1)}, f32[256,1600]{1,0:T(8,128)}, bf16[256,1600]{1,0:T(8,128)(2,1)}, bf16[4,200,448]{2,1,0:T(8,128)(2,1)}) conditional(s32[]{:T(128)} %convert_element_type.86, () %tuple.321, (s32[8]{0:T(128)S(1)}, bf16[8,200,1600]{2,1,0:T(8,128)(2,1)}, ...), branch_computations={%region_27.28_spmd, %region_28.33_spmd} | conditional | flops 3145730 | bytes 17297698 | solution.py:57
  380.4 19.4 %conditional.7 = (f32[256,1600]{1,0:T(8,128)}, bf16[256,1600]{1,0:T(8,128)(2,1)}, bf16[4,200,448]{2,1,0:T(8,128)(2,1)}) conditional(s32[]{:T(128)} %convert_element_type.55, () %tuple.218, (pred[]{:T(512)}, bf16[1024,1408]{1,0:T(8,128)(2,1)}, bf16[1600,1408]{1,0:T(8,128)(2,1)}, bf16[800,448]{1,0:T(8,128)(2,1)}) %tuple.219), branch_computations={%region_29.29_spmd, %region_30.32_spmd} | conditional | flops 2097153 | bytes 9552005 | solution.py:57
  382.1 14.6 %conditional.6 = ((f32[256,1600]{1,0:T(8,128)}, bf16[256,1600]{1,0:T(8,128)(2,1)})) conditional(s32[]{:T(128)} %convert_element_type.54, () %tuple.215, (bf16[1024,1408]{1,0:T(8,128)(2,1)}, bf16[1600,1408]{1,0:T(8,128)(2,1)}) %tuple.216), branch_computations={%region_31.30_spmd, %region_32.31_spmd} | conditional | flops 2097152 | bytes 6684720 | solution.py:57
  402.4 26.5 %conditional.37 = (bf16[200,1856]{1,0:T(8,128)(2,1)}, bf16[200,1856]{1,0:T(8,128)(2,1)}, bf16[256,1600]{1,0:T(8,128)(2,1)}, bf16[512,1600]{1,0:T(8,128)(2,1)}, b...) conditional(s32[]{:T(128)} %convert_element_type.86, () %tuple.320, ...), branch_computations={%region_33.34_spmd, %region_34.40_spmd} | conditional | flops 6030601 | bytes 21659836 | solution.py:57
  407.2 21.7 %conditional.9 = (bf16[256,1600]{1,0:T(8,128)(2,1)}, bf16[512,1600]{1,0:T(8,128)(2,1)}, bf16[200,1600]{1,0:T(8,128)(2,1)}, f32[8,200]{1,0:T(8,128)}, f32[8,200]{...) conditional(s32[]{:T(128)} %convert_element_type.76, () %tuple.228, ...), branch_computations={%region_35.35_spmd, %region_36.39_spmd} | conditional | flops 4982024 | bytes 15654783 | solution.py:57
  408.6 17.1 %conditional.8 = (bf16[200,1600]{1,0:T(8,128)(2,1)}, f32[8,200]{1,0:T(8,128)}, f32[8,200]{1,0:T(8,128)}, f32[8,200]{1,0:T(8,128)}, f32[8,200]{1,0:T(8,128)}, /*i...) conditional(s32[]{:T(128)} %convert_element_type.58, () %tuple.225, ...), branch_computations={%region_37.36_spmd, %region_38.38_spmd} | conditional | flops 4982023 | bytes 5824106 | solution.py:57
  428.9 24.3 %conditional.38 = (bf16[200,1856]{1,0:T(8,128)(2,1)}, bf16[200,1856]{1,0:T(8,128)(2,1)}, bf16[200,1600]{1,0:T(8,128)(2,1)}, bf16[200,1600]{1,0:T(8,128)(2,1)}, b...) conditional(s32[]{:T(128)} %convert_element_type.86, () %tuple.319, ...), branch_computations={%region_40.41_spmd, %region_41.46_spmd} | conditional | flops 3145730 | bytes 19854920 | solution.py:57
  434.0 16.3 %conditional.11 = (bf16[200,1600]{1,0:T(8,128)(2,1)}, bf16[200,1600]{1,0:T(8,128)(2,1)}, bf16[200,1600]{1,0:T(8,128)(2,1)}, f32[256,1600]{1,0:T(8,128)}, bf16[25...) conditional(s32[]{:T(128)} %convert_element_type.78, () %tuple.238, ...), branch_computations={%region_42.42_spmd, %region_43.45_spmd} | conditional | flops 2097153 | bytes 10573099 | solution.py:57
  453.2 24.9 %conditional.39 = (bf16[200,1856]{1,0:T(8,128)(2,1)}, bf16[200,1856]{1,0:T(8,128)(2,1)}, f32[4,2400]{1,0:T(4,128)S(1)}, bf16[256,1600]{1,0:T(8,128)(2,1)}, bf16[200,1600]{1,0:T(8,128)(2,1)}) conditional(s32[]{:T(128)} %convert_element_type.86, () %tuple.318, (s32[8]{0:T(128)S(1)}, bf16[8,200,1408]{2,1,0:T(8,128)(2,1)}, ...), branch_computations={%region_46.47_spmd, %region_47.48_spmd} | conditional | flops 1077380 | bytes 12264219 | solution.py:57
  478.1 16.8 %conditional.40 = (bf16[200,1408]{1,0:T(8,128)(2,1)}, bf16[200,1408]{1,0:T(8,128)(2,1)}, bf16[200,1408]{1,0:T(8,128)(2,1)}, bf16[200,448]{1,0:T(8,128)(2,1)}, bf...) conditional(s32[]{:T(128)} %convert_element_type.86, () %tuple.295, ...), branch_computations={%region_48.49_spmd, %region_49.52_spmd} | conditional | flops 4159557 | bytes 20347570 | solution.py:57
  (378 shorter events, 518.4 us)
Async XLA Ops:
  26.6 23.2 %collective-permute-start.60 = (bf16[200,1856]{1,0:T(8,128)(2,1)}, bf16[200,1856]{1,0:T(8,128)(2,1)S(1)}, u32[]{:S(2)}, u32[]{:S(2)}) collective-permute-start(bf16[200,1856]{1,0:T(8,128)(2,1)} %collective-permute-done.59.refs_3_), channel_id=1, source_target_pairs={{0,1},{2,0},{4,2},{6,4},{7,6},{5,7},{3,5},{1,3},{8,9},{10,8},{12,1... | collective-permute-start | bytes 2227208 | tf_op jit(solution)/shard_map/ppermute | solution.py:155
  53.1 59.5 %collective-permute-start.53 = (bf16[32,8,1600]{2,1,0:T(8,128)(2,1)}, bf16[32,8,1600]{2,1,0:T(8,128)(2,1)}, u32[]{:S(2)}, u32[]{:S(2)}) collective-permute-start(bf16[32,8,1600]{2,1,0:T(8,128)(2,1)} %collective-permute-done.52), channel_id=1, source_target_pairs={{0,8},{8,0},{16,24},{24,16},{1,9},{9,1},{17,25},{25,17},{2,10},{10... | collective-permute-start | bytes 2457608 | tf_op jit(solution)/shard_map/ppermute | solution.py:79
  64.8 38.5 %collective-permute-start.42 = (bf16[400,1600]{1,0:T(8,128)(2,1)}, bf16[400,1600]{1,0:T(8,128)(2,1)}, u32[]{:S(2)}, u32[]{:S(2)}) collective-permute-start(bf16[400,1600]{1,0:T(8,128)(2,1)} %get-tuple-element.608), channel_id=1, source_target_pairs={{0,2},{2,4},{4,6},{6,7},{7,5},{5,3},{3,1},{1,0},{8,10},{10,12},{12... | collective-permute-start | bytes 3840008 | tf_op jit(solution)/shard_map/cond/branch_1_fun/ppermute | solution.py:155
  68.8 34.5 %collective-permute-start.43 = (bf16[400,1600]{1,0:T(8,128)(2,1)}, bf16[400,1600]{1,0:T(8,128)(2,1)}, u32[]{:S(2)}, u32[]{:S(2)}) collective-permute-start(bf16[400,1600]{1,0:T(8,128)(2,1)} %get-tuple-element.608), channel_id=1, source_target_pairs={{0,1},{2,0},{4,2},{6,4},{7,6},{5,7},{3,5},{1,3},{8,9},{10,8},{12,1... | collective-permute-start | bytes 3840008 | tf_op jit(solution)/shard_map/cond/branch_1_fun/ppermute | solution.py:155
  70.6 32.7 %collective-permute-start.41 = (bf16[104,1856]{1,0:T(8,128)(2,1)}, bf16[104,1856]{1,0:T(8,128)(2,1)}, u32[]{:S(2)}, u32[]{:S(2)}) collective-permute-start(bf16[104,1856]{1,0:T(8,128)(2,1)} %slice.175), channel_id=1, source_target_pairs={{0,1},{2,0},{4,2},{6,4},{7,6},{5,7},{3,5},{1,3},{8,9},{10,8},{12,1... | collective-permute-start | bytes 1158152 | tf_op jit(solution)/shard_map/cond/branch_1_fun/ppermute | solution.py:155
  72.4 28.1 %collective-permute-start.40 = (bf16[96,1856]{1,0:T(8,128)(2,1)}, bf16[96,1856]{1,0:T(8,128)(2,1)}, u32[]{:S(2)}, u32[]{:S(2)}) collective-permute-start(bf16[96,1856]{1,0:T(8,128)(2,1)} %slice.174), channel_id=1, source_target_pairs={{0,2},{2,4},{4,6},{6,7},{7,5},{5,3},{3,1},{1,0},{8,10},{10,12},{12... | collective-permute-start | bytes 1069064 | tf_op jit(solution)/shard_map/cond/branch_1_fun/ppermute | solution.py:155
  108.8 31.7 %collective-permute-start.65 = (bf16[200,8,448]{2,1,0:T(8,128)(2,1)}, bf16[200,8,448]{2,1,0:T(8,128)(2,1)}, u32[]{:S(2)}, u32[]{:S(2)}) collective-permute-start(bf16[200,8,448]{2,1,0:T(8,128)(2,1)} %bitcast.70), channel_id=1, source_target_pairs={{0,16},{8,24},{16,0},{24,8},{1,17},{9,25},{17,1},{25,9},{2,18},{10... | collective-permute-start | bytes 4300808 | tf_op jit(solution)/shard_map/ppermute | solution.py:79
  110.9 31.4 %collective-permute-start.70 = (bf16[400,1600]{1,0:T(8,128)(2,1)}, bf16[400,1600]{1,0:T(8,128)(2,1)}, u32[]{:S(2)}, u32[]{:S(2)}) collective-permute-start(bf16[400,1600]{1,0:T(8,128)(2,1)} %get-tuple-element.1159.refs_2_), channel_id=1, source_target_pairs={{0,2},{2,4},{4,6},{6,7},{7,5},{5,3},{3,1},{1,0},{8,10},{10,12},{12... | collective-permute-start | bytes 3840008 | tf_op jit(solution)/shard_map/ppermute | solution.py:155
  112.5 31.6 %collective-permute-start.71 = (bf16[400,1600]{1,0:T(8,128)(2,1)}, bf16[400,1600]{1,0:T(8,128)(2,1)}, u32[]{:S(2)}, u32[]{:S(2)}) collective-permute-start(bf16[400,1600]{1,0:T(8,128)(2,1)} %get-tuple-element.1160.refs_3_), channel_id=1, source_target_pairs={{0,1},{2,0},{4,2},{6,4},{7,6},{5,7},{3,5},{1,3},{8,9},{10,8},{12,1... | collective-permute-start | bytes 3840008 | tf_op jit(solution)/shard_map/ppermute | solution.py:155
  142.4 31.6 %collective-permute-start.75 = (bf16[400,1600]{1,0:T(8,128)(2,1)}, bf16[400,1600]{1,0:T(8,128)(2,1)S(1)}, u32[]{:S(2)}, u32[]{:S(2)}) collective-permute-start(bf16[400,1600]{1,0:T(8,128)(2,1)} %collective-permute-done.70.refs_4_), channel_id=1, source_target_pairs={{0,2},{2,4},{4,6},{6,7},{7,5},{5,3},{3,1},{1,0},{8,10},{10,12},{12... | collective-permute-start | bytes 3840008 | tf_op jit(solution)/shard_map/ppermute | solution.py:155
  144.1 31.9 %collective-permute-start.77 = (bf16[400,1600]{1,0:T(8,128)(2,1)}, bf16[400,1600]{1,0:T(8,128)(2,1)S(1)}, u32[]{:S(2)}, u32[]{:S(2)}) collective-permute-start(bf16[400,1600]{1,0:T(8,128)(2,1)} %collective-permute-done.71.refs_5_), channel_id=1, source_target_pairs={{0,1},{2,0},{4,2},{6,4},{7,6},{5,7},{3,5},{1,3},{8,9},{10,8},{12,1... | collective-permute-start | bytes 3840008 | tf_op jit(solution)/shard_map/ppermute | solution.py:155
  169.5 23.3 %collective-permute-start.73 = (bf16[32,8,1600]{2,1,0:T(8,128)(2,1)S(1)}, bf16[32,8,1600]{2,1,0:T(8,128)(2,1)S(1)}, u32[]{:S(2)}, u32[]{:S(2)}) collective-permute-start(bf16[32,8,1600]{2,1,0:T(8,128)(2,1)S(1)} %bitcast.122), channel_id=1, source_target_pairs={{0,16},{8,24},{16,0},{24,8},{1,17},{9,25},{17,1},{25,9},{2,18},{10... | collective-permute-start | bytes 2457608 | tf_op jit(solution)/shard_map/ppermute | solution.py:79
  256.0 26.8 %collective-permute-start.45 = (bf16[200,1600]{1,0:T(8,128)(2,1)S(1)}, bf16[200,1600]{1,0:T(8,128)(2,1)}, u32[]{:S(2)}, u32[]{:S(2)}) collective-permute-start(bf16[200,1600]{1,0:T(8,128)(2,1)S(1)} %get-tuple-element.659), channel_id=1, source_target_pairs={{0,2},{2,4},{4,6},{6,7},{7,5},{5,3},{3,1},{1,0},{8,10},{10,12},{12... | collective-permute-start | bytes 1920008 | tf_op jit(solution)/shard_map/cond/branch_1_fun/ppermute | solution.py:155
  257.0 25.8 %collective-permute-start.46 = (bf16[200,1600]{1,0:T(8,128)(2,1)S(1)}, bf16[200,1600]{1,0:T(8,128)(2,1)}, u32[]{:S(2)}, u32[]{:S(2)}) collective-permute-start(bf16[200,1600]{1,0:T(8,128)(2,1)S(1)} %get-tuple-element.660), channel_id=1, source_target_pairs={{0,1},{2,0},{4,2},{6,4},{7,6},{5,7},{3,5},{1,3},{8,9},{10,8},{12,1... | collective-permute-start | bytes 1920008 | tf_op jit(solution)/shard_map/cond/branch_1_fun/ppermute | solution.py:155
  285.6 28.5 %collective-permute-start.18 = (bf16[304,1600]{1,0:T(8,128)(2,1)S(1)}, bf16[304,1600]{1,0:T(8,128)(2,1)}, u32[]{:S(2)}, u32[]{:S(2)}) collective-permute-start(bf16[304,1600]{1,0:T(8,128)(2,1)S(1)} %get-tuple-element.694), channel_id=1, source_target_pairs={{0,1},{2,0},{4,2},{6,4},{7,6},{5,7},{3,5},{1,3},{8,9},{10,8},{12,1... | collective-permute-start | bytes 2918408 | tf_op jit(solution)/shard_map/cond/branch_1_fun/ppermute | solution.py:155
  286.6 27.5 %collective-permute-start.17 = (bf16[296,1600]{1,0:T(8,128)(2,1)S(1)}, bf16[296,1600]{1,0:T(8,128)(2,1)}, u32[]{:S(2)}, u32[]{:S(2)}) collective-permute-start(bf16[296,1600]{1,0:T(8,128)(2,1)S(1)} %get-tuple-element.693), channel_id=1, source_target_pairs={{0,2},{2,4},{4,6},{6,7},{7,5},{5,3},{3,1},{1,0},{8,10},{10,12},{12... | collective-permute-start | bytes 2841608 | tf_op jit(solution)/shard_map/cond/branch_1_fun/ppermute | solution.py:155
  317.0 26.2 %collective-permute-start.8 = (bf16[200,1600]{1,0:T(8,128)(2,1)S(1)}, bf16[200,1600]{1,0:T(8,128)(2,1)}, u32[]{:S(2)}, u32[]{:S(2)}) collective-permute-start(bf16[200,1600]{1,0:T(8,128)(2,1)S(1)} %get-tuple-element.728), channel_id=1, source_target_pairs={{0,2},{2,4},{4,6},{6,7},{7,5},{5,3},{3,1},{1,0},{8,10},{10,12},{12... | collective-permute-start | bytes 1920008 | tf_op jit(solution)/shard_map/cond/branch_1_fun/ppermute | solution.py:155
  318.0 25.2 %collective-permute-start.9 = (bf16[200,1600]{1,0:T(8,128)(2,1)S(1)}, bf16[200,1600]{1,0:T(8,128)(2,1)}, u32[]{:S(2)}, u32[]{:S(2)}) collective-permute-start(bf16[200,1600]{1,0:T(8,128)(2,1)S(1)} %get-tuple-element.729), channel_id=1, source_target_pairs={{0,1},{2,0},{4,2},{6,4},{7,6},{5,7},{3,5},{1,3},{8,9},{10,8},{12,1... | collective-permute-start | bytes 1920008 | tf_op jit(solution)/shard_map/cond/branch_1_fun/ppermute | solution.py:155
  319.0 24.1 %collective-permute-start.7 = (bf16[400,8,448]{2,1,0:T(8,128)(2,1)}, bf16[400,8,448]{2,1,0:T(8,128)(2,1)}, u32[]{:S(2)}, u32[]{:S(2)}) collective-permute-start(bf16[400,8,448]{2,1,0:T(8,128)(2,1)} %bitcast.19), channel_id=1, source_target_pairs={{0,8},{8,0},{16,24},{24,16},{1,9},{9,1},{17,25},{25,17},{2,10},{10... | collective-permute-start | bytes 8601608 | tf_op jit(solution)/shard_map/cond/branch_1_fun/cond/branch_1_fun/ppermute | solution.py:79
  345.7 29.7 %collective-permute-start.49 = (bf16[200,1600]{1,0:T(8,128)(2,1)S(1)}, bf16[200,1600]{1,0:T(8,128)(2,1)}, u32[]{:S(2)}, u32[]{:S(2)}) collective-permute-start(bf16[200,1600]{1,0:T(8,128)(2,1)S(1)} %get-tuple-element.757), channel_id=1, source_target_pairs={{0,2},{2,4},{4,6},{6,7},{7,5},{5,3},{3,1},{1,0},{8,10},{10,12},{12... | collective-permute-start | bytes 1920008 | tf_op jit(solution)/shard_map/cond/branch_1_fun/ppermute | solution.py:155
  346.4 29.0 %collective-permute-start.50 = (bf16[200,1600]{1,0:T(8,128)(2,1)S(1)}, bf16[200,1600]{1,0:T(8,128)(2,1)}, u32[]{:S(2)}, u32[]{:S(2)}) collective-permute-start(bf16[200,1600]{1,0:T(8,128)(2,1)S(1)} %get-tuple-element.758), channel_id=1, source_target_pairs={{0,1},{2,0},{4,2},{6,4},{7,6},{5,7},{3,5},{1,3},{8,9},{10,8},{12,1... | collective-permute-start | bytes 1920008 | tf_op jit(solution)/shard_map/cond/branch_1_fun/ppermute | solution.py:155
  378.3 24.0 %collective-permute-start.13 = (bf16[304,1600]{1,0:T(8,128)(2,1)S(1)}, bf16[304,1600]{1,0:T(8,128)(2,1)}, u32[]{:S(2)}, u32[]{:S(2)}) collective-permute-start(bf16[304,1600]{1,0:T(8,128)(2,1)S(1)} %get-tuple-element.786), channel_id=1, source_target_pairs={{0,1},{2,0},{4,2},{6,4},{7,6},{5,7},{3,5},{1,3},{8,9},{10,8},{12,1... | collective-permute-start | bytes 2918408 | tf_op jit(solution)/shard_map/cond/branch_1_fun/ppermute | solution.py:155
  379.3 23.0 %collective-permute-start.12 = (bf16[296,1600]{1,0:T(8,128)(2,1)S(1)}, bf16[296,1600]{1,0:T(8,128)(2,1)}, u32[]{:S(2)}, u32[]{:S(2)}) collective-permute-start(bf16[296,1600]{1,0:T(8,128)(2,1)S(1)} %get-tuple-element.785), channel_id=1, source_target_pairs={{0,2},{2,4},{4,6},{6,7},{7,5},{5,3},{3,1},{1,0},{8,10},{10,12},{12... | collective-permute-start | bytes 2841608 | tf_op jit(solution)/shard_map/cond/branch_1_fun/ppermute | solution.py:155
  405.1 23.8 %collective-permute-start.38 = (bf16[200,1856]{1,0:T(8,128)(2,1)S(1)}, bf16[200,1856]{1,0:T(8,128)(2,1)}, u32[]{:S(2)}, u32[]{:S(2)}) collective-permute-start(bf16[200,1856]{1,0:T(8,128)(2,1)S(1)} %get-tuple-element.839), channel_id=1, source_target_pairs={{0,2},{2,4},{4,6},{6,7},{7,5},{5,3},{3,1},{1,0},{8,10},{10,12},{12... | collective-permute-start | bytes 2227208 | tf_op jit(solution)/shard_map/cond/branch_1_fun/ppermute | solution.py:155
  (88 other events, 1284.0 us)
